TPU v7x, 32 devices: a whole 2x2x4 slice. The times are simulated.
32 devices in a mesh: dp: 4 (over y, x), row: 2 (over core), col: 4 (over z).
Axes of the slice: x: 2, y: 2, z: 4, core: 2. Of those that a mesh axis runs over, the one named last changes fastest.
Arguments:
- states: bfloat16 [25088, 1024], P(('dp', 'row', 'col')), may hold values from -6 to 6
- ln1_gain: bfloat16 [1024], P('row'), may hold values from 0.5 to 1.5
- ln1_bias: bfloat16 [1024], P('row'), may hold values from -0.59765625 to 0.59765625
- w_qkv: bfloat16 [1024, 3, 1024], P('row', None, 'col'), may hold values from -0.1875 to 0.1875
- q_bias: bfloat16 [1024], P('col'), may hold values from -1.796875 to 1.796875
- v_bias: bfloat16 [1024], P('col'), may hold values from -0.29882812 to 0.29882812
- w_proj: bfloat16 [1024, 1024], P('col', 'row'), may hold values from -0.75 to 0.75
- proj_bias: bfloat16 [1024], P('row'), may hold values from -0.59765625 to 0.59765625
- ln2_gain: bfloat16 [1024], P('row'), may hold values from 0.5 to 1.5
- ln2_bias: bfloat16 [1024], P('row'), may hold values from -0.59765625 to 0.59765625
- w_fc1: bfloat16 [1024, 4096], P('row', 'col'), may hold values from -0.1875 to 0.1875
- fc1_bias: bfloat16 [4096], P('col'), may hold values from -0.59765625 to 0.59765625
- w_fc2: bfloat16 [4096, 1024], P('col', 'row'), may hold values from -0.09375 to 0.09375
- fc2_bias: bfloat16 [1024], P('row'), may hold values from -0.59765625 to 0.59765625
- teacher: bfloat16 [25088, 1024], P(('dp', 'row', 'col')), may hold values from -6 to 6
- loss_mask: int32 [25088], replicated, may hold values 0 or 1
- lengths: int32 [16], replicated, may hold values from 784 to 1568, as said below
Outputs:
- states_out: bfloat16 [25088, 1024], P(('dp', 'row', 'col'))
- loss: float32 [], replicated
- grad_states: bfloat16 [25088, 1024], P(('dp', 'row', 'col'))
- grad_ln1_gain: float32 [1024], P('row')
- grad_ln1_bias: float32 [1024], P('row')
- grad_w_qkv: float32 [1024, 3, 1024], P('row', None, 'col')
- grad_q_bias: float32 [1024], P('col')
- grad_v_bias: float32 [1024], P('col')
- grad_w_proj: float32 [1024, 1024], P('col', 'row')
- grad_proj_bias: float32 [1024], P('row')
- grad_ln2_gain: float32 [1024], P('row')
- grad_ln2_bias: float32 [1024], P('row')
- grad_w_fc1: float32 [1024, 4096], P('row', 'col')
- grad_fc1_bias: float32 [4096], P('col')
- grad_w_fc2: float32 [4096, 1024], P('col', 'row')
- grad_fc2_bias: float32 [1024], P('row')
Inputs may be any that keep to these rules, and one draw needn't show every extreme that they name: `lengths`: each entry is the number of real tube tokens of one clip, from 784 to 1568; some clip has all 1568. Positions at or beyond it are padding.
All inputs are finite; a program needn't handle non-finite values.
Results may differ from a plain program's by a relative error of at most 0.012.
The roundings to bfloat16 on the way count: a program that leaves them out, or rounds other values in their place, can miss the bound.
Values may be sent and summed in bfloat16 or wider, within the bound.
No kernel may reach another device: no remote copies, remote signals or barrier semaphores. Data moves between devices by JAX's collectives and lax.ppermute only.
A program may use at most 320 MiB of HBM per device.

v0:
```python
import jax
import jax.numpy as jnp
from jax import lax
from jax.sharding import PartitionSpec as P

HD = 64
L = 1568


EPSILON = 1e-06
MASKED = -1e30
ROOT_HALF = 0.7071067811865476
DENSITY_FACTOR = 0.3989422804014327


def normalize(values, factor, offset):
    centered = values - jnp.mean(values, axis=-1, keepdims=True)
    spread = lax.rsqrt(jnp.mean(centered * centered, axis=-1, keepdims=True) + EPSILON)
    normal = centered * spread
    return (normal * factor + offset, normal, spread)


def norm_back(upstream, normal, spread, factor):
    inner = upstream * factor
    center_term = jnp.mean(inner, axis=-1, keepdims=True)
    slope_term = jnp.mean(inner * normal, axis=-1, keepdims=True)
    back = spread * (inner - center_term - normal * slope_term)
    return (back, jnp.sum(upstream * normal, axis=0), jnp.sum(upstream, axis=0))


def gelu_value(values):
    return values * (0.5 * (1.0 + lax.erf(values * ROOT_HALF)))


def gelu_slope(values):
    normal_cdf = 0.5 * (1.0 + lax.erf(values * ROOT_HALF))
    return normal_cdf + values * jnp.exp(-0.5 * values * values) * DENSITY_FACTOR


def masked_scores(queries, key_rows, length, score_scale):
    logits = (
        jnp.einsum("ihd,jhd->hij", queries, key_rows, preferred_element_type=jnp.float32)
        * score_scale
    )
    keep = jnp.arange(key_rows.shape[0]) < length
    return jnp.where(keep[None, None, :], logits, MASKED)


def attend_clip(packed, length, score_scale):
    half_span = packed.shape[0] // 2
    key_rows = packed[:, 1]
    value_rows = packed[:, 2]
    pieces = []
    totals = []
    for block_index in range(2):
        queries = packed[block_index * half_span : (block_index + 1) * half_span, 0]
        logits = masked_scores(queries, key_rows, length, score_scale)
        peak = jnp.max(logits, axis=-1, keepdims=True)
        total = peak + jnp.log(jnp.sum(jnp.exp(logits - peak), axis=-1, keepdims=True))
        weights = jnp.exp(logits - total).astype(jnp.bfloat16)
        pieces.append(
            jnp.einsum("hij,jhd->ihd", weights, value_rows, preferred_element_type=jnp.float32)
        )
        totals.append(total[..., 0])
    return (jnp.concatenate(pieces, 0), jnp.concatenate(totals, 1))


def attend_clip_back(packed, length, totals, upstream, score_scale):
    half_span = packed.shape[0] // 2
    key_rows = packed[:, 1]
    value_rows = packed[:, 2]
    grad_keys = jnp.zeros(key_rows.shape, jnp.float32)
    grad_values = jnp.zeros(value_rows.shape, jnp.float32)
    grad_queries = []
    for block_index in range(2):
        first = block_index * half_span
        queries = packed[first : first + half_span, 0]
        logits = masked_scores(queries, key_rows, length, score_scale)
        probs = jnp.exp(logits - totals[:, first : first + half_span][..., None])
        incoming = upstream[first : first + half_span]
        grad_values = grad_values + jnp.einsum(
            "hij,ihd->jhd", probs.astype(jnp.bfloat16), incoming, preferred_element_type=jnp.float32
        )
        grad_probs = jnp.einsum(
            "ihd,jhd->hij", incoming, value_rows, preferred_element_type=jnp.float32
        )
        grad_logits = (
            probs * (grad_probs - jnp.sum(probs * grad_probs, axis=-1, keepdims=True))
        ).astype(jnp.bfloat16)
        grad_queries.append(
            jnp.einsum("hij,jhd->ihd", grad_logits, key_rows, preferred_element_type=jnp.float32)
            * score_scale
        )
        grad_keys = (
            grad_keys
            + jnp.einsum("hij,ihd->jhd", grad_logits, queries, preferred_element_type=jnp.float32)
            * score_scale
        )
    return jnp.stack([jnp.concatenate(grad_queries, 0), grad_keys, grad_values], axis=1)


def local(
    states,
    ln1_gain,
    ln1_bias,
    w_qkv,
    q_bias,
    v_bias,
    w_proj,
    proj_bias,
    ln2_gain,
    ln2_bias,
    w_fc1,
    fc1_bias,
    w_fc2,
    fc2_bias,
    teacher,
    loss_mask,
    lengths,
):
    row_count = lax.axis_size("row")
    col_count = lax.axis_size("col")
    col_index = lax.axis_index("col")
    group_index = lax.axis_index("dp") * row_count + lax.axis_index("row")
    local_rows = states.shape[0]
    width = states.shape[1]
    group_rows = local_rows * col_count
    clip_count = group_rows // L
    head_width = w_qkv.shape[2]
    heads_here = head_width // HD
    hidden_width = w_fc1.shape[1]
    score_scale = HD ** (-0.5)
    vectors = jnp.stack([ln1_gain, ln1_bias, proj_bias, ln2_gain, ln2_bias, fc2_bias])
    qkv_full, proj_full, fc1_full, fc2_full, vector_full = (
        lax.all_gather(w_qkv, "row", axis=0, tiled=True),
        lax.all_gather(w_proj, "row", axis=1, tiled=True),
        lax.all_gather(w_fc1, "row", axis=0, tiled=True),
        lax.all_gather(w_fc2, "row", axis=1, tiled=True),
        lax.all_gather(vectors, "row", axis=1, tiled=True),
    )
    vector_full = vector_full.astype(jnp.float32)
    gain_one = vector_full[0]
    shift_one = vector_full[1]
    bias_proj = vector_full[2]
    gain_two = vector_full[3]
    shift_two = vector_full[4]
    bias_two = vector_full[5]
    all_clips = lengths.shape[0]
    valid_all = (
        loss_mask.reshape(all_clips, L) * (jnp.arange(L)[None, :] < lengths[:, None])
    ).astype(jnp.float32)
    valid_total = jnp.maximum(jnp.sum(valid_all), 1.0)
    first_row = (group_index * col_count + col_index) * local_rows
    valid = lax.dynamic_slice_in_dim(valid_all.reshape(all_clips * L), first_row, local_rows)
    my_lengths = lax.dynamic_slice_in_dim(lengths, group_index * clip_count, clip_count)
    inputs = states.astype(jnp.float32)
    norm_one, unit_one, spread_one = normalize(inputs, gain_one, shift_one)
    norm_one = norm_one.astype(jnp.bfloat16)
    tokens_one = lax.all_gather(norm_one, "col", axis=0, tiled=True)
    qkv_matrix = qkv_full.reshape(width, 3 * head_width)
    projected = jnp.dot(tokens_one, qkv_matrix, preferred_element_type=jnp.float32).reshape(
        group_rows, 3, head_width
    )
    bias_rows = jnp.stack(
        [
            q_bias.astype(jnp.float32),
            jnp.zeros((head_width,), jnp.float32),
            v_bias.astype(jnp.float32),
        ]
    )
    packed = (projected + bias_rows[None]).astype(jnp.bfloat16)
    clips_packed = packed.reshape(clip_count, L, 3, heads_here, HD)
    attended, totals = lax.map(
        lambda element: attend_clip(element[0], element[1], score_scale), (clips_packed, my_lengths)
    )
    attended = attended.reshape(group_rows, head_width).astype(jnp.bfloat16)
    proj_whole, qkv_whole = (
        lax.all_gather(proj_full, "col", axis=0, tiled=True),
        lax.all_gather(qkv_full, "col", axis=2, tiled=True),
    )
    attended_rows = lax.all_to_all(attended, "col", split_axis=0, concat_axis=1, tiled=True)
    middle = inputs + (
        jnp.dot(attended_rows, proj_whole, preferred_element_type=jnp.float32) + bias_proj
    )
    norm_two, unit_two, spread_two = normalize(middle, gain_two, shift_two)
    norm_two = norm_two.astype(jnp.bfloat16)
    fc1_whole, fc2_whole, fc1_bias_whole = (
        lax.all_gather(fc1_full, "col", axis=1, tiled=True),
        lax.all_gather(fc2_full, "col", axis=0, tiled=True),
        lax.all_gather(fc1_bias, "col", axis=0, tiled=True),
    )
    hidden_pre = jnp.dot(
        norm_two, fc1_whole, preferred_element_type=jnp.float32
    ) + fc1_bias_whole.astype(jnp.float32)
    hidden = gelu_value(hidden_pre).astype(jnp.bfloat16)
    outputs = middle + (jnp.dot(hidden, fc2_whole, preferred_element_type=jnp.float32) + bias_two)
    differ = outputs - teacher.astype(jnp.float32)
    numerator = jnp.sum(valid[:, None] * differ * differ)
    loss_scale = all_clips * L * width / 2.0
    grad_out = loss_scale * 2.0 / (valid_total * width) * valid[:, None] * differ
    grad_low = grad_out.astype(jnp.bfloat16)
    grad_hidden = jnp.dot(grad_low, fc2_whole.T, preferred_element_type=jnp.float32)
    grad_pre = (grad_hidden * gelu_slope(hidden_pre)).astype(jnp.bfloat16)
    wide_fc2 = jnp.dot(hidden.T, grad_low, preferred_element_type=jnp.float32)
    wide_fc1 = jnp.dot(norm_two.T, grad_pre, preferred_element_type=jnp.float32)
    fc1_grad_part, fc2_grad_part = (
        lax.psum_scatter(
            wide_fc1.astype(jnp.bfloat16), "col", scatter_dimension=1, tiled=True
        ).astype(jnp.float32),
        lax.psum_scatter(
            wide_fc2.astype(jnp.bfloat16), "col", scatter_dimension=0, tiled=True
        ).astype(jnp.float32),
    )
    fc1_bias_sum = jnp.sum(grad_pre, axis=0, dtype=jnp.float32)
    grad_norm_two = jnp.dot(grad_pre, fc1_whole.T, preferred_element_type=jnp.float32)
    back_two, gain_two_grad, shift_two_grad = norm_back(
        grad_norm_two, unit_two, spread_two, gain_two
    )
    grad_mid = grad_out + back_two
    mid_low = grad_mid.astype(jnp.bfloat16)
    wide_proj = jnp.dot(attended_rows.T, mid_low, preferred_element_type=jnp.float32)
    proj_grad_part = lax.psum_scatter(
        wide_proj.astype(jnp.bfloat16), "col", scatter_dimension=0, tiled=True
    )
    grad_attended_rows = jnp.dot(mid_low, proj_whole.T, preferred_element_type=jnp.float32).astype(
        jnp.bfloat16
    )
    grad_attended = lax.all_to_all(
        grad_attended_rows, "col", split_axis=1, concat_axis=0, tiled=True
    )
    grads_packed = lax.map(
        lambda element: attend_clip_back(
            element[0], element[1], element[2], element[3], score_scale
        ),
        (clips_packed, my_lengths, totals, grad_attended.reshape(clip_count, L, heads_here, HD)),
    )
    grads_packed = grads_packed.reshape(group_rows, 3 * head_width).astype(jnp.bfloat16)
    qkv_grad_part = jnp.dot(tokens_one.T, grads_packed, preferred_element_type=jnp.float32).reshape(
        width, 3, head_width
    )
    bias_sums = jnp.sum(grads_packed.reshape(group_rows, 3, head_width), axis=0, dtype=jnp.float32)
    grads_rows = lax.all_to_all(
        grads_packed.reshape(group_rows, 3, head_width),
        "col",
        split_axis=0,
        concat_axis=2,
        tiled=True,
    )
    grad_norm_one = jnp.dot(
        grads_rows.reshape(local_rows, 3 * width),
        qkv_whole.reshape(width, 3 * width).T,
        preferred_element_type=jnp.float32,
    )
    back_one, gain_one_grad, shift_one_grad = norm_back(
        grad_norm_one, unit_one, spread_one, gain_one
    )
    grad_states = (grad_mid + back_one).astype(jnp.bfloat16)
    proj_bias_grad = jnp.sum(mid_low, axis=0, dtype=jnp.float32)
    fc2_bias_grad = jnp.sum(grad_low, axis=0, dtype=jnp.float32)
    token_vectors = jnp.stack(
        [
            gain_one_grad,
            shift_one_grad,
            proj_bias_grad,
            gain_two_grad,
            shift_two_grad,
            fc2_bias_grad,
        ]
    )
    head_vectors = lax.dynamic_update_slice(
        jnp.zeros((2, width), jnp.float32),
        jnp.stack([bias_sums[0], bias_sums[2]]),
        (0, col_index * head_width),
    )
    token_sums, head_sums, fc1_sums, loss_sum = lax.psum(
        (token_vectors, head_vectors, fc1_bias_sum, numerator), ("dp", "row", "col")
    )
    qkv_rows, proj_cols, fc1_rows, fc2_cols = (
        lax.psum_scatter(
            qkv_grad_part.astype(jnp.bfloat16), "row", scatter_dimension=0, tiled=True
        ).astype(jnp.float32),
        lax.psum_scatter(proj_grad_part, "row", scatter_dimension=1, tiled=True).astype(
            jnp.float32
        ),
        lax.psum_scatter(
            fc1_grad_part.astype(jnp.bfloat16), "row", scatter_dimension=0, tiled=True
        ).astype(jnp.float32),
        lax.psum_scatter(
            fc2_grad_part.astype(jnp.bfloat16), "row", scatter_dimension=1, tiled=True
        ).astype(jnp.float32),
    )
    qkv_grad, proj_grad, fc1_grad, fc2_grad = (
        lax.psum(qkv_rows.astype(jnp.bfloat16), "dp").astype(jnp.float32),
        lax.psum(proj_cols.astype(jnp.bfloat16), "dp").astype(jnp.float32),
        lax.psum(fc1_rows.astype(jnp.bfloat16), "dp").astype(jnp.float32),
        lax.psum(fc2_cols.astype(jnp.bfloat16), "dp").astype(jnp.float32),
    )
    half_width = width // row_count
    token_part = lax.dynamic_slice_in_dim(
        token_sums, lax.axis_index("row") * half_width, half_width, 1
    )
    head_part = lax.dynamic_slice_in_dim(head_sums, col_index * head_width, head_width, 1)
    fc1_part = lax.dynamic_slice_in_dim(fc1_sums, col_index * hidden_width, hidden_width, 0)
    loss_value = loss_sum / (valid_total * width)
    return (
        outputs.astype(jnp.bfloat16),
        loss_value,
        grad_states,
        token_part[0],
        token_part[1],
        qkv_grad,
        head_part[0],
        head_part[1],
        proj_grad,
        token_part[2],
        token_part[3],
        token_part[4],
        fc1_grad,
        fc1_part,
        fc2_grad,
        token_part[5],
    )


def solution(mesh):
    in_specs = (
        P(("dp", "row", "col"), None),
        P("row"),
        P("row"),
        P("row", None, "col"),
        P("col"),
        P("col"),
        P("col", "row"),
        P("row"),
        P("row"),
        P("row"),
        P("row", "col"),
        P("col"),
        P("col", "row"),
        P("row"),
        P(("dp", "row", "col"), None),
        P(),
        P(),
    )
    out_specs = (
        P(("dp", "row", "col"), None),
        P(),
        P(("dp", "row", "col"), None),
        P("row"),
        P("row"),
        P("row", None, "col"),
        P("col"),
        P("col"),
        P("col", "row"),
        P("row"),
        P("row"),
        P("row"),
        P("row", "col"),
        P("col"),
        P("col", "row"),
        P("row"),
    )
    return jax.shard_map(local, mesh=mesh, in_specs=in_specs, out_specs=out_specs, check_vma=False)
```

profile of v0, /device:TPU:0, one launch (start us, length us, event | category | flops | bytes accessed | tf_op | source)
XLA Modules:
  0.0 1376.4 jit_solution(3440307325007686870)
XLA Ops:
  49.4 120.7 %all-gather.9.cloned.1.call-done = bf16[3136,1024]{1,0:T(8,128)(2,1)} async-done(((bf16[784,1024]{1,0:T(8,128)(2,1)}), bf16[3136,1024]{1,0:T(8,128)(2,1)}) %all-gather.9.cloned.1.call-update) | async-done | bytes 6422544 | tf_op jit(solution)/shard_map/all_gather | solution.py:159
  179.4 14.6 %reshape.167 = bf16[2,1568,3,4,64]{4,3,1,0,2:T(4,128)(2,1)} reshape(bf16[3136,3,256]{2,0,1:T(8,128)(2,1)} %add_convert_fusion) | data formatting | bytes 9633792 | tf_op jit(solution)/shard_map/reshape | solution.py:172
  194.0 15.6 %copy.62 = bf16[2,1568,3,4,64]{1,4,3,2,0:T(8,128)(2,1)} copy(bf16[2,1568,3,4,64]{4,3,1,0,2:T(4,128)(2,1)} %reshape.167) | data formatting | bytes 9633792 | tf_op jit(solution)/shard_map/while | solution.py:173
  209.5 100.1 %while.22 = (s32[]{:T(128)}, bf16[2,1568,4,64]{1,3,2,0:T(8,128)(2,1)S(1)}, f32[2,4,1568]{2,1,0:T(4,128)S(1)}, bf16[2,1568,3,4,64]{1,4,3,2,0:T(8,128)(2,1)}, s32[2]{0:T(128)S(1)}, /*index=5*/s32[]{:T(128)}) while((s32[]{:T(128)}, bf16[2,1568,4,64]{1,3,2,0:T(8,128)(2,1)S(1)}, f32[2,4,1568]{2,1,0:T(4,128)S(1)}, ...), condition=%wide.region_7.8_spmd, body=%wide.region_2.7_spmd.sunk | while | flops 2588079616 | bytes 208644768 | solution.py:173
  324.3 78.0 %all_gather.40 = bf16[4096]{0:T(1024)(128)(2,1)S(1)} all-gather(bf16[1024]{0:T(1024)(128)(2,1)S(1)} %copy-done.38), channel_id=1, replica_groups=mesh['dp'=4,'row'=2,'col'=4] {'col'}, dimensions={0}, use_global_device_ids=true | all-gather | bytes 10240 | tf_op jit(solution)/shard_map/all_gather | solution.py:190
  412.1 15.9 %multiply_convert_fusion.2 = (bf16[784,4096]{1,0:T(8,128)(2,1)}, f32[784,4096]{1,0:T(8,128)}) fusion(f32[4096]{0:T(1024)S(1)} %convert_element_type.142, bf16[1024,4096]{1,0:T(8,128)(2,1)} %all-gather.17.cloned.1.call-done, f32[784,1024]{1,0:T(8,128)} %copy-done.10, f32[1024]{0:T(1024)S(1)} %bitcast.272, f32[1024]{0:T(1024)S(1)} %bitcast.262, ...), kind=kOutput, calls=%fused_computation.70 | convolution fusion | flops 6599950336 | bytes 30898304 | tf_op jit(solution)/shard_map/dot_general | solution.py:192
  428.0 121.4 %all-gather.21.cloned.1.call-done = bf16[4096,1024]{1,0:T(8,128)(2,1)} async-done(((bf16[1024,1024]{1,0:T(8,128)(2,1)}), bf16[4096,1024]{1,0:T(8,128)(2,1)}) %all-gather.21.cloned.1.call-update) | async-done | bytes 8388624 | tf_op jit(solution)/shard_map/all_gather | solution.py:189
  561.7 17.8 %convert_reduce_fusion = (f32[4096]{0:T(1024)}, bf16[784,4096]{1,0:T(8,128)(2,1)}) fusion(f32[784,4096]{1,0:T(8,128)} %get-tuple-element.202, f32[4096]{0:T(1024)S(1)} %convert_element_type.142, bf16[784,1024]{1,0:T(8,128)(2,1)S(1)} %get-tuple-element.162, bf16[4096,1024]{1,0:T(8,128)(2,1)} %all-gather.21.cloned.1.call-done), kind=kOutput, calls=%fused_computation.69 | convolution fusion | flops 6618411008 | bytes 29294592 | tf_op jit(solution)/shard_map/dot_general | solution.py:202
  598.9 15.1 %convolution_convert_fusion = bf16[1024,4096]{1,0:T(8,128)(2,1)} fusion(bf16[784,4096]{1,0:T(8,128)(2,1)} %get-tuple-element.207, f32[784,1024]{1,0:T(8,128)} %copy-done.10, f32[1024]{0:T(1024)S(1)} %bitcast.273, f32[1024]{0:T(1024)S(1)} %bitcast.265, f32[784]{0:T(1024)S(1)} %add_rsqrt_fusion, f32[784]{0:T(1024)S(1)} %broadcast_multiply_fusion.5), kind=kOutput, calls=%fused_computation.74 | convolution fusion | flops 6584877056 | bytes 18036864 | tf_op jit(solution)/shard_map/dot_general | solution.py:205
  622.4 14.2 %convolution_convert_fusion.1 = bf16[4096,1024]{1,0:T(8,128)(2,1)} fusion(bf16[784,4096]{1,0:T(8,128)(2,1)} %get-tuple-element.201, bf16[784,1024]{1,0:T(8,128)(2,1)S(1)} %copy-done.52), kind=kOutput, calls=%fused_computation.75 | convolution fusion | flops 6580862976 | bytes 16416768 | tf_op jit(solution)/shard_map/dot_general | solution.py:204
  636.7 61.9 %all-to-all-done.1 = bf16[784,4,256]{2,0,1:T(8,128)(2,1)S(1)} async-done(((bf16[784,4,256]{2,0,1:T(8,128)(2,1)}), bf16[784,4,256]{2,0,1:T(8,128)(2,1)S(1)}, u32[]{:S(2)}, u32[]{:S(2)}) %all-to-all-start.1) | async-done | bytes 1605664 | tf_op jit(solution)/shard_map/all_to_all | solution.py:228
  708.9 258.5 %while.23 = (s32[]{:T(128)}, bf16[2,1568,3,4,64]{1,4,3,2,0:T(8,128)(2,1)}, bf16[2,1568,3,4,64]{1,4,3,2,0:T(8,128)(2,1)}, s32[2]{0:T(128)S(1)}, f32[2,4,1568]{2,1...) while((s32[]{:T(128)}, bf16[2,1568,3,4,64]{1,4,3,2,0:T(8,128)(2,1)}, ...), condition=%wide.region_18.19_spmd, body=%wide.region_15.18_spmd.sunk | while | flops 6394224128 | bytes 484584864 | solution.py:231
  740.5 14.7 %multiply_reduce_fusion.9 = (f32[4,784]{1,0:T(4,128)S(1)}, f32[4,784,1568]{2,1,0:T(8,128)}) fusion(f32[4,784,1568]{2,1,0:T(8,128)} %fusion.126, f32[4,784]{1,0:T(4,128)S(1)} %get-tuple-element.296, bf16[1568,3,4,64]{0,3,2,1:T(8,128)(2,1)S(1)} %dynamic-slice_bitcast_fusion.21, pred[1568]{0:T(1024)(128)(4,1)S(1)} %iota_compare_fusion.6), kind=kOutput, calls=%fused_computation.25.clone.1 | convolution fusion | flops 653990848 | bytes 40677632 | tf_op jit(solution)/shard_map/while/body/eval_jaxpr/ihd,jhd->hij/dot_general | solution.py:42
  755.2 13.8 %multiply_convert_fusion.8 = bf16[4,784,1568]{2,1,0:T(8,128)(2,1)S(1)} fusion(f32[4,784,1568]{2,1,0:T(8,128)} %get-tuple-element.297, f32[4,784,1568]{2,1,0:T(8,128)} %fusion.126, f32[4,784]{1,0:T(4,128)S(1)} %get-tuple-element.301), kind=kLoop, calls=%fused_computation.24.clone.1 | loop fusion | flops 14751744 | bytes 49185024 | tf_op jit(solution)/shard_map/while/body/eval_jaxpr/convert_element_type | solution.py:89
  783.9 14.1 %multiply_reduce_fusion.10 = (f32[4,784]{1,0:T(4,128)S(1)}, f32[4,784,1568]{2,1,0:T(8,128)}) fusion(f32[4,784,1568]{2,1,0:T(8,128)} %fusion.129, f32[4,784]{1,0:T(4,128)S(1)} %get-tuple-element.298, bf16[1568,3,4,64]{0,3,2,1:T(8,128)(2,1)S(1)} %dynamic-slice_bitcast_fusion.21, pred[1568]{0:T(1024)(128)(4,1)S(1)} %iota_compare_fusion.6), kind=kOutput, calls=%fused_computation.28.clone.1 | convolution fusion | flops 653990848 | bytes 40677632 | tf_op jit(solution)/shard_map/while/body/eval_jaxpr/ihd,jhd->hij/dot_general | solution.py:42
  798.0 13.9 %multiply_convert_fusion.7 = bf16[4,784,1568]{2,1,0:T(8,128)(2,1)S(1)} fusion(f32[4,784,1568]{2,1,0:T(8,128)} %get-tuple-element.299, f32[4,784,1568]{2,1,0:T(8,128)} %fusion.129, f32[4,784]{1,0:T(4,128)S(1)} %get-tuple-element.300), kind=kLoop, calls=%fused_computation.27.clone.1 | loop fusion | flops 14751744 | bytes 49185024 | tf_op jit(solution)/shard_map/while/body/eval_jaxpr/convert_element_type | solution.py:89
  861.6 14.5 %multiply_reduce_fusion.9 = (f32[4,784]{1,0:T(4,128)S(1)}, f32[4,784,1568]{2,1,0:T(8,128)}) fusion(f32[4,784,1568]{2,1,0:T(8,128)} %fusion.126, f32[4,784]{1,0:T(4,128)S(1)} %get-tuple-element.296, bf16[1568,3,4,64]{0,3,2,1:T(8,128)(2,1)S(1)} %dynamic-slice_bitcast_fusion.21, pred[1568]{0:T(1024)(128)(4,1)S(1)} %iota_compare_fusion.6), kind=kOutput, calls=%fused_computation.25.clone.1 | convolution fusion | flops 653990848 | bytes 40677632 | tf_op jit(solution)/shard_map/while/body/eval_jaxpr/ihd,jhd->hij/dot_general | solution.py:42
  876.1 14.5 %multiply_convert_fusion.8 = bf16[4,784,1568]{2,1,0:T(8,128)(2,1)S(1)} fusion(f32[4,784,1568]{2,1,0:T(8,128)} %get-tuple-element.297, f32[4,784,1568]{2,1,0:T(8,128)} %fusion.126, f32[4,784]{1,0:T(4,128)S(1)} %get-tuple-element.301), kind=kLoop, calls=%fused_computation.24.clone.1 | loop fusion | flops 14751744 | bytes 49185024 | tf_op jit(solution)/shard_map/while/body/eval_jaxpr/convert_element_type | solution.py:89
  905.5 13.9 %multiply_reduce_fusion.10 = (f32[4,784]{1,0:T(4,128)S(1)}, f32[4,784,1568]{2,1,0:T(8,128)}) fusion(f32[4,784,1568]{2,1,0:T(8,128)} %fusion.129, f32[4,784]{1,0:T(4,128)S(1)} %get-tuple-element.298, bf16[1568,3,4,64]{0,3,2,1:T(8,128)(2,1)S(1)} %dynamic-slice_bitcast_fusion.21, pred[1568]{0:T(1024)(128)(4,1)S(1)} %iota_compare_fusion.6), kind=kOutput, calls=%fused_computation.28.clone.1 | convolution fusion | flops 653990848 | bytes 40677632 | tf_op jit(solution)/shard_map/while/body/eval_jaxpr/ihd,jhd->hij/dot_general | solution.py:42
  919.5 13.9 %multiply_convert_fusion.7 = bf16[4,784,1568]{2,1,0:T(8,128)(2,1)S(1)} fusion(f32[4,784,1568]{2,1,0:T(8,128)} %get-tuple-element.299, f32[4,784,1568]{2,1,0:T(8,128)} %fusion.129, f32[4,784]{1,0:T(4,128)S(1)} %get-tuple-element.300), kind=kLoop, calls=%fused_computation.27.clone.1 | loop fusion | flops 14751744 | bytes 49185024 | tf_op jit(solution)/shard_map/while/body/eval_jaxpr/convert_element_type | solution.py:89
  1000.4 16.0 %copy.80 = bf16[2,1568,3,4,64]{4,3,2,1,0:T(4,128)(2,1)} copy(bf16[2,1568,3,4,64]{1,4,3,2,0:T(8,128)(2,1)} %get-tuple-element.78) | data formatting | bytes 9633792 | tf_op jit(solution)/shard_map/convert_element_type | solution.py:237
  1016.4 20.6 %reshape.166 = bf16[3136,3,256]{2,1,0:T(4,128)(2,1)} reshape(bf16[2,1568,3,4,64]{4,3,2,1,0:T(4,128)(2,1)} %copy.80) | data formatting | bytes 9633792 | tf_op jit(solution)/shard_map/convert_element_type | solution.py:237
  1046.6 234.9 %all-to-all-done.2 = bf16[3136,3,256]{2,1,0:T(4,128)(2,1)} async-done(((bf16[3136,3,256]{2,1,0:T(4,128)(2,1)}), bf16[3136,3,256]{2,1,0:T(4,128)(2,1)}, u32[]{:S(2)}, u32[]{:S(2)}) %all-to-all-start.2) | async-done | bytes 4816928 | tf_op jit(solution)/shard_map/all_to_all | solution.py:242
  1310.0 39.1 %all-reduce = (f32[]{:T(128)}, f32[6,1024]{1,0:T(8,128)S(1)}, f32[2,1024]{1,0:T(2,128)S(1)}, f32[4096]{0:T(1024)S(1)}) all-reduce(f32[]{:T(128)} %get-tuple-element.181, f32[6,1024]{1,0:T(8,128)S(1)} %stack.90, f32[2,1024]{1,0:T(2,128)S(1)} %maximum_dynamic-update-slice_fusion, ...), channel_id=1, replica_groups=mesh['dp'=4,'row'=2,'col'=4] {'dp','row','col'}, use_global_device_ids=true, to_apply=%region_11.12 | all-reduce | flops 12289 | bytes 98312 | tf_op jit(solution)/shard_map/psum | solution.py:275
  (319 shorter events, 442.6 us)
Async XLA Ops:
  7.3 15.7 %all-gather.15.cloned.1.call-start = ((), (), s32[]{:S(2)}) async-start(), calls=%async_computation.13 | async-start | bytes 3145728 | tf_op jit(solution)/shard_map/all_gather | solution.py:137
  8.0 28.3 %all-gather.19.cloned.1.call-start = ((), (), s32[]{:S(2)}) async-start(), calls=%async_computation.15 | async-start | bytes 3145728 | tf_op jit(solution)/shard_map/all_gather | solution.py:138
  8.7 40.7 %all-gather.11.cloned.1.call-start = ((), (), s32[]{:S(2)}) async-start(), calls=%async_computation.11 | async-start | bytes 2359296 | tf_op jit(solution)/shard_map/all_gather | solution.py:135
  11.1 159.0 %all-gather.9.cloned.1.call-start = ((), (), s32[]{:S(2)}) async-start(), calls=%async_computation.10 | async-start | bytes 8028160 | tf_op jit(solution)/shard_map/all_gather | solution.py:159
  17.2 388.1 %all-gather.13.cloned.1.call-start = ((), (), s32[]{:S(2)}) async-start(), calls=%async_computation.12 | async-start | bytes 2621440 | tf_op jit(solution)/shard_map/all_gather | solution.py:178
  19.6 392.4 %all-gather.17.cloned.1.call-start = ((), (), s32[]{:S(2)}) async-start(), calls=%async_computation.14 | async-start | bytes 10485760 | tf_op jit(solution)/shard_map/all_gather | solution.py:188
  23.0 526.3 %all-gather.21.cloned.1.call-start = ((), (), s32[]{:S(2)}) async-start(), calls=%async_computation.16 | async-start | bytes 10485760 | tf_op jit(solution)/shard_map/all_gather | solution.py:189
  317.5 84.8 %copy-start.46 = (s32[16]{0:T(128)S(1)}, s32[16]{0:T(128)}, u32[]{:S(2)}) copy-start(s32[16]{0:T(128)} %param.37) | copy-start | bytes 196
  317.5 85.0 %copy-start.22 = (s32[25088]{0:T(1024)S(1)}, s32[25088]{0:T(1024)}, u32[]{:S(2)}) copy-start(s32[25088]{0:T(1024)} %param.36) | copy-start | bytes 301060
  320.5 84.8 %copy-start.37 = (f32[1,1024]{1,0:T(1,128)S(1)}, f32[1,1024]{1,0:T(1,128)}, u32[]{:S(2)}) copy-start(f32[1,1024]{1,0:T(1,128)} %get-tuple-element.192) | copy-start | bytes 12292
  320.5 83.4 %all-to-all-start = ((bf16[4,784,256]{2,1,0:T(8,128)(2,1)}), bf16[4,784,256]{2,1,0:T(8,128)(2,1)S(1)}, u32[]{:S(2)}, u32[]{:S(2)}) async-start(bf16[4,784,256]{2,1,0:T(8,128)(2,1)} %reshape.164), calls=%async_computation | async-start | bytes 3211264 | tf_op jit(solution)/shard_map/all_to_all | solution.py:181
  324.2 664.1 %reduce-scatter.10.cloned.1.call-start = ((), (), s32[]{:S(2)}) async-start(), calls=%async_computation.19 | async-start | bytes 2621440 | tf_op jit(solution)/shard_map/reduce_scatter | solution.py:222
  412.1 137.2 %copy-start.11 = (f32[784,1024]{1,0:T(8,128)S(1)}, f32[784,1024]{1,0:T(8,128)}, u32[]{:S(2)}) copy-start(f32[784,1024]{1,0:T(8,128)} %copy-done.10) | copy-start | bytes 9633796
  412.1 137.2 %copy-start.36 = (f32[1,1024]{1,0:T(1,128)S(1)}, f32[1,1024]{1,0:T(1,128)}, u32[]{:S(2)}) copy-start(f32[1,1024]{1,0:T(1,128)} %get-tuple-element.191) | copy-start | bytes 12292
  598.9 399.6 %reduce-scatter.14.cloned.1.call-start = ((), (), s32[]{:S(2)}) async-start(), calls=%async_computation.21 | async-start | bytes 10485760 | tf_op jit(solution)/shard_map/reduce_scatter | solution.py:207
  618.8 79.8 %all-to-all-start.1 = ((bf16[784,4,256]{2,0,1:T(8,128)(2,1)}), bf16[784,4,256]{2,0,1:T(8,128)(2,1)S(1)}, u32[]{:S(2)}, u32[]{:S(2)}) async-start(bf16[784,4,256]{2,0,1:T(8,128)(2,1)} %bitcast.170), calls=%async_computation.1 | async-start | bytes 3211264 | tf_op jit(solution)/shard_map/all_to_all | solution.py:228
  622.3 376.9 %reduce-scatter.18.cloned.1.call-start = ((), (), s32[]{:S(2)}) async-start(), calls=%async_computation.23 | async-start | bytes 10485760 | tf_op jit(solution)/shard_map/reduce_scatter | solution.py:210
  636.6 409.9 %reduce-scatter.12.cloned.1.call-start = ((), (), s32[]{:S(2)}) async-start(), calls=%async_computation.20 | async-start | bytes 786432 | tf_op jit(solution)/shard_map/reduce_scatter | solution.py:282
  988.4 58.2 %reduce-scatter.8.cloned.1.call-start = ((), (), s32[]{:S(2)}) async-start(), calls=%async_computation.18 | async-start | bytes 2359296 | tf_op jit(solution)/shard_map/reduce_scatter | solution.py:279
  998.4 48.1 %reduce-scatter.16.cloned.1.call-start = ((), (), s32[]{:S(2)}) async-start(), calls=%async_computation.22 | async-start | bytes 3145728 | tf_op jit(solution)/shard_map/reduce_scatter | solution.py:285
  999.2 47.4 %reduce-scatter.20.cloned.1.call-start = ((), (), s32[]{:S(2)}) async-start(), calls=%async_computation.24 | async-start | bytes 3145728 | tf_op jit(solution)/shard_map/reduce_scatter | solution.py:288
  999.8 299.5 %all-gather.23.cloned.1.call-start = ((), (), s32[]{:S(2)}) async-start(), calls=%async_computation.17 | async-start | bytes 7864320 | tf_op jit(solution)/shard_map/all_gather | solution.py:179
  1037.0 244.6 %all-to-all-start.2 = ((bf16[3136,3,256]{2,1,0:T(4,128)(2,1)}), bf16[3136,3,256]{2,1,0:T(4,128)(2,1)}, u32[]{:S(2)}, u32[]{:S(2)}) async-start(bf16[3136,3,256]{2,1,0:T(4,128)(2,1)} %reshape.166), calls=%async_computation.2 | async-start | bytes 12845056 | tf_op jit(solution)/shard_map/all_to_all | solution.py:242
  1042.3 319.6 %all-reduce.4.cloned.1.call-start = ((), (), s32[]{:S(2)}) async-start(), calls=%async_computation.25 | async-start | bytes 6291456 | tf_op jit(solution)/shard_map/psum | solution.py:293
  (66 other events, 710.8 us)
Sparse Core Ops, SparseCore 0:
  9.6 13.2 all-gather.14
  24.5 11.7 all-gather.18
  38.4 10.9 all-gather.10
  51.4 118.6 all-gather.8
  171.5 44.1 all-gather.12
  217.1 182.7 all-gather.16
  401.5 147.7 all-gather.20
  599.0 55.7 reduce-scatter.9
  657.3 151.0 reduce-scatter.13
  810.7 145.4 reduce-scatter.17
  988.5 6.2 reduce-scatter.11
  998.6 9.0 reduce-scatter.7
  1010.0 10.8 reduce-scatter.15
  1023.0 10.7 reduce-scatter.19
  1035.3 229.2 all-gather.22
  1268.2 93.6 all-reduce.3
where the time goes:
time: 1380 us
  waiting for transfers between devices  577 us (42%)
  matrix products  359 us (26%)
  local copies, waits for them, and re-layouts  159 us (12%)
  blocking collectives  121 us (9%)
  other arithmetic  112 us (8%)
  loops' own time  17.3 us (1%)
  between operations  17.3 us (1%)
    all_to_all x1, waiting for transfers between devices, local(): lax.all_to_all(grads_packed.reshape(group_rows, 3, head_width), 'col', sp...  235 us
    all_gather x1, waiting for transfers between devices, local(): lax.all_gather(fc2_full, 'col', axis=0, tiled=True)  121 us
    all_gather x1, waiting for transfers between devices, local(): tokens_one = lax.all_gather(norm_one, 'col', axis=0, tiled=True)  121 us
    dot_general x8, matrix products, masked_scores(): jnp.einsum('ihd,jhd->hij', queries, key_rows, preferred_element_type=jnp....  82.4 us
    all_gather x1, blocking collectives, local(): lax.all_gather(fc1_bias, 'col', axis=0, tiled=True)  78 us
    all_to_all x1, waiting for transfers between devices, local(): lax.all_to_all(grad_attended_rows, 'col', split_axis=1, concat_axis=0, ti...  61.9 us
    convert_element_type x4, local copies, waits for them, and re-layouts, local(): grads_packed.reshape(group_rows, 3 * head_width).astype(jnp.bfloat16)  57.5 us
    convert_element_type x4, other arithmetic, attend_clip_back(): grad_logits = (probs * (grad_probs - jnp.sum(probs * grad_probs, axis=-1,...  56.2 us
  transfers between devices with their start and end apart: 19, of which 8 were waited for; matrix products, arithmetic and copies ran while one was open for 41% of the time, Pallas kernels for 0%

commit v1 on v0

--- a/solution.py
+++ b/solution.py
@@ -1,6 +1,8 @@
 import jax
 import jax.numpy as jnp
 from jax import lax
+from jax.experimental import pallas as pl
+from jax.experimental.pallas import tpu as pltpu
 from jax.sharding import PartitionSpec as P
 
 HD = 64
@@ -99,7 +101,7 @@
     return jnp.stack([jnp.concatenate(grad_queries, 0), grad_keys, grad_values], axis=1)
 
 
-def local(
+def local_general(
     states,
     ln1_gain,
     ln1_bias,
@@ -322,7 +324,540 @@
     )
 
 
+PAIRED_MESH = (4, 2, 4)
+GROUP = 4
+QT = 128
+
+
+def dot_nn(a, b):
+    return lax.dot_general(a, b, (((1,), (0,)), ((), ())), preferred_element_type=jnp.float32)
+
+
+def dot_nt(a, b):
+    return lax.dot_general(a, b, (((1,), (1,)), ((), ())), preferred_element_type=jnp.float32)
+
+
+def dot_tn(a, b):
+    return lax.dot_general(a, b, (((0,), (0,)), ((), ())), preferred_element_type=jnp.float32)
+
+
+def head_stack(values, zero):
+    lane_head = lax.broadcasted_iota(jnp.int32, values.shape, 1) // HD
+    return jnp.concatenate([jnp.where(lane_head == h, values, zero) for h in range(GROUP)], axis=0)
+
+
+def head_unstack(wide, count):
+    return jnp.concatenate(
+        [wide[h * HD : (h + 1) * HD, h * count : (h + 1) * count] for h in range(GROUP)], axis=0
+    ).T
+
+
+def attend_kernel(packed_ref, bias_ref, out_ref, lse_ref, vt_ref):
+    width = GROUP * HD
+    tokens = packed_ref.shape[0]
+    vt_ref[...] = packed_ref[:, 2 * width : 3 * width].T
+
+    def tile(start, count, index):
+        stacked = head_stack(packed_ref[pl.ds(start, count), 0:width], jnp.zeros((), jnp.bfloat16))
+        keys = packed_ref[:, width : 2 * width]
+        bias = bias_ref[...]
+        scores = dot_nt(keys, stacked) + jnp.concatenate([bias] * (GROUP * count // 128), axis=1)
+        peak = jnp.max(scores, axis=0, keepdims=True)
+        weights = jnp.exp(scores - peak)
+        total = jnp.sum(weights, axis=0, keepdims=True)
+        wide = dot_nn(vt_ref[...], weights.astype(jnp.bfloat16)) * (1.0 / total)
+        out_ref[pl.ds(start, count), :] = head_unstack(wide, count).astype(jnp.bfloat16)
+        lse_ref[index, :, 0 : GROUP * count] = jnp.broadcast_to(
+            peak + jnp.log(total), (8, GROUP * count)
+        )
+
+    full = tokens // QT
+    rest = tokens - full * QT
+
+    @pl.loop(0, full)
+    def _(index):
+        tile(pl.multiple_of(index * QT, QT), QT, index)
+
+    if rest:
+        tile(full * QT, rest, full)
+
+
+def attend_back_kernel(
+    packed_ref, bias_ref, lse_ref, att_ref, up_ref, out_ref, kt_ref, dk_ref, dv_ref
+):
+    width = GROUP * HD
+    tokens = packed_ref.shape[0]
+    kt_ref[...] = packed_ref[:, width : 2 * width].T
+    dk_ref[...] = jnp.zeros_like(dk_ref)
+    dv_ref[...] = jnp.zeros_like(dv_ref)
+
+    def tile(start, count, index):
+        cols = GROUP * count
+        zero = jnp.zeros((), jnp.bfloat16)
+        up = up_ref[pl.ds(start, count), :]
+        stacked = head_stack(packed_ref[pl.ds(start, count), 0:width], zero)
+        up_stacked = head_stack(up, zero)
+        product = head_stack(
+            up.astype(jnp.float32) * att_ref[pl.ds(start, count), :].astype(jnp.float32),
+            jnp.zeros((), jnp.float32),
+        )
+        high = product.astype(jnp.bfloat16)
+        low = (product - high.astype(jnp.float32)).astype(jnp.bfloat16)
+        ones = jnp.ones((8, width), jnp.bfloat16)
+        delta = (dot_nt(ones, high) + dot_nt(ones, low))[0:1]
+        keys = packed_ref[:, width : 2 * width]
+        values = packed_ref[:, 2 * width : 3 * width]
+        bias = bias_ref[...]
+        scores = dot_nt(keys, stacked) + jnp.concatenate([bias] * (cols // 128), axis=1)
+        weights = jnp.exp(scores - lse_ref[index, 0:1, 0:cols])
+        dv_ref[...] += dot_nn(weights.astype(jnp.bfloat16), up_stacked)
+        grad = (weights * (dot_nt(values, up_stacked) - delta)).astype(jnp.bfloat16)
+        dk_ref[...] += dot_nn(grad, stacked)
+        wide = dot_nn(kt_ref[...], grad) * (HD**-0.5)
+        out_ref[pl.ds(start, count), 0:width] = head_unstack(wide, count).astype(jnp.bfloat16)
+
+    full = tokens // QT
+    rest = tokens - full * QT
+
+    @pl.loop(0, full)
+    def _(index):
+        tile(pl.multiple_of(index * QT, QT), QT, index)
+
+    if rest:
+        tile(full * QT, rest, full)
+    out_ref[:, width : 2 * width] = dk_ref[...].astype(jnp.bfloat16)
+    out_ref[:, 2 * width : 3 * width] = dv_ref[...].astype(jnp.bfloat16)
+
+
+def attend(packed, bias):
+    tokens, width = packed.shape[0], GROUP * HD
+    tiles = -(-tokens // QT)
+    return pl.pallas_call(
+        attend_kernel,
+        out_shape=(
+            jax.ShapeDtypeStruct((tokens, width), jnp.bfloat16),
+            jax.ShapeDtypeStruct((tiles, 8, GROUP * QT), jnp.float32),
+        ),
+        in_specs=[pl.BlockSpec(memory_space=pltpu.VMEM)] * 2,
+        out_specs=[pl.BlockSpec(memory_space=pltpu.VMEM)] * 2,
+        scratch_shapes=[pltpu.VMEM((width, tokens), jnp.bfloat16)],
+        compiler_params=pltpu.CompilerParams(vmem_limit_bytes=48 << 20),
+        cost_estimate=pl.CostEstimate(
+            flops=4 * tokens * tokens * width * 4, bytes_accessed=8 << 20, transcendentals=0
+        ),
+        name="attend",
+    )(packed, bias)
+
+
+def attend_back(packed, bias, lse, att, upstream):
+    tokens, width = packed.shape[0], GROUP * HD
+    return pl.pallas_call(
+        attend_back_kernel,
+        out_shape=jax.ShapeDtypeStruct((tokens, 3 * width), jnp.bfloat16),
+        in_specs=[pl.BlockSpec(memory_space=pltpu.VMEM)] * 5,
+        out_specs=pl.BlockSpec(memory_space=pltpu.VMEM),
+        scratch_shapes=[
+            pltpu.VMEM((width, tokens), jnp.bfloat16),
+            pltpu.VMEM((tokens, width), jnp.float32),
+            pltpu.VMEM((tokens, width), jnp.float32),
+        ],
+        compiler_params=pltpu.CompilerParams(vmem_limit_bytes=56 << 20),
+        cost_estimate=pl.CostEstimate(
+            flops=10 * tokens * tokens * width * 4, bytes_accessed=10 << 20, transcendentals=0
+        ),
+        name="attend_back",
+    )(packed, bias, lse, att, upstream)
+
+
+def swap(values, axis, mask, size):
+    return lax.ppermute(values, axis, [(i, i ^ mask) for i in range(size)])
+
+
+def over_row(values):
+    return swap(values, "row", 1, 2)
+
+
+def over_dp(values, mask):
+    return swap(values, "dp", mask, 4)
+
+
+def over_col(values, mask):
+    return swap(values, "col", mask, 4)
+
+
+def cut(values, index, size, axis=0):
+    return lax.dynamic_slice_in_dim(values, index * size, size, axis)
+
+
+def place(pieces, index_of, axis):
+    size = pieces[0].shape[axis]
+    shape = list(pieces[0].shape)
+    shape[axis] = size * len(pieces)
+    whole = jnp.zeros(shape, pieces[0].dtype)
+    for s, piece in enumerate(pieces):
+        whole = lax.dynamic_update_slice_in_dim(whole, piece, index_of(s) * size, axis)
+    return whole
+
+
+SUB_ORDER = (0, 2, 1, 3)
+
+
+def local_paired(
+    states,
+    ln1_gain,
+    ln1_bias,
+    w_qkv,
+    q_bias,
+    v_bias,
+    w_proj,
+    proj_bias,
+    ln2_gain,
+    ln2_bias,
+    w_fc1,
+    fc1_bias,
+    w_fc2,
+    fc2_bias,
+    teacher,
+    loss_mask,
+    lengths,
+):
+    f32, bf16 = jnp.float32, jnp.bfloat16
+    dp = lax.axis_index("dp")
+    row = lax.axis_index("row")
+    col = lax.axis_index("col")
+    local_rows, width = states.shape
+    half = width // 2
+    head_width = w_qkv.shape[2]
+    hidden_width = w_fc1.shape[1]
+    sub = hidden_width // 4
+    group_index = dp * 2 + row
+    clip = group_index * 2 + col // 2
+    second = col % 2
+
+    def quarter(s):
+        return dp ^ s
+
+    def frame(values):
+        return jnp.where(
+            row == 0, values, jnp.concatenate([values[:, half:], values[:, :half]], axis=1)
+        )
+
+    w_qkv2 = w_qkv.reshape(half, 3 * head_width)
+    vectors = jnp.stack([ln1_gain, ln1_bias, proj_bias, ln2_gain, ln2_bias, fc2_bias])
+    vectors_other = over_row(vectors)
+    vector_full = jnp.concatenate([vectors, vectors_other], axis=1).astype(f32)
+    gain_one, shift_one, bias_proj, gain_two, shift_two, bias_two = (vector_full[i] for i in range(6))
+
+    inputs = frame(states).astype(f32)
+    norm_one, unit_one, spread_one = normalize(inputs, gain_one, shift_one)
+    norm_one = norm_one.astype(bf16)
+    norm_other = over_col(norm_one, 1)
+
+    qkv_other = over_row(w_qkv2)
+    qkv_quarter = over_col(cut(w_qkv2, dp, half // 4), 2)
+    qkv_pieces = [qkv_quarter] + [over_dp(qkv_quarter, s) for s in (1, 2, 3)]
+    qkv_far = place(qkv_pieces, quarter, 0)
+    qkv_far_other = over_row(qkv_far)
+    qkv_near = jnp.concatenate([w_qkv2, qkv_other], axis=0)
+    qkv_far = jnp.concatenate([qkv_far, qkv_far_other], axis=0)
+
+    fc1_own = [cut(w_fc1, quarter(s), sub, 1) for s in range(4)]
+    fc2_own = [cut(w_fc2, quarter(s), sub, 0) for s in range(4)]
+    proj_cut = cut(w_proj, dp, head_width // 4, 0)
+    slab = jnp.concatenate(
+        [
+            fc1_own[0],
+            fc2_own[0][:, :sub],
+            fc2_own[0][:, sub:],
+            proj_cut[:, :sub],
+            proj_cut[:, sub:],
+        ],
+        axis=0,
+    )
+    slab_rows = slab.shape[0]
+    own = jnp.concatenate(
+        [
+            jnp.concatenate(fc1_own, axis=0),
+            jnp.concatenate([f[:, i * sub : (i + 1) * sub] for f in fc2_own for i in range(2)], axis=0),
+            w_proj[:, :sub],
+            w_proj[:, sub:],
+        ],
+        axis=0,
+    )
+    own_other = over_row(own)
+    near, far = [None], [None]
+    for j in (1, 2, 3):
+        first = over_col(slab, j)
+        pieces = jnp.concatenate([first] + [over_dp(first, s) for s in (1, 2, 3)], axis=0)
+        near.append(pieces)
+        far.append(over_row(pieces))
+
+    quarter_rows = head_width // 4
+
+    def own_parts(block):
+        fc1 = [block[s * half : (s + 1) * half] for s in range(4)]
+        at = 4 * half
+        fc2 = [
+            jnp.concatenate(
+                [block[at + (2 * s + i) * sub : at + (2 * s + i + 1) * sub] for i in range(2)], axis=1
+            )
+            for s in range(4)
+        ]
+        at += 8 * sub
+        proj = jnp.concatenate([block[at : at + head_width], block[at + head_width :]], axis=1)
+        return fc1, fc2, proj
+
+    def far_parts(block):
+        fc1, fc2, proj = [], [], []
+        for s in range(4):
+            at = s * slab_rows
+            fc1.append(block[at : at + half])
+            at += half
+            fc2.append(jnp.concatenate([block[at : at + sub], block[at + sub : at + 2 * sub]], axis=1))
+            at += 2 * sub
+            proj.append(
+                jnp.concatenate(
+                    [block[at : at + quarter_rows], block[at + quarter_rows : at + 2 * quarter_rows]],
+                    axis=1,
+                )
+            )
+        return fc1, fc2, place(proj, quarter, 0)
+
+    mine = [own_parts(own)] + [far_parts(near[j]) for j in (1, 2, 3)]
+    theirs = [own_parts(own_other)] + [far_parts(far[j]) for j in (1, 2, 3)]
+    order = [(s, j) for s in SUB_ORDER for j in range(4)]
+    fc1_whole = jnp.concatenate(
+        [
+            jnp.concatenate([mine[j][0][s] for s, j in order], axis=1),
+            jnp.concatenate([theirs[j][0][s] for s, j in order], axis=1),
+        ],
+        axis=0,
+    )
+    fc2_whole = jnp.concatenate(
+        [
+            jnp.concatenate([mine[j][1][s] for s, j in order], axis=0),
+            jnp.concatenate([theirs[j][1][s] for s, j in order], axis=0),
+        ],
+        axis=1,
+    )
+    proj_whole = jnp.concatenate(
+        [
+            jnp.concatenate([mine[j][2] for j in range(4)], axis=0),
+            jnp.concatenate([theirs[j][2] for j in range(4)], axis=0),
+        ],
+        axis=1,
+    )
+    fc1_biases = [fc1_bias] + [over_col(fc1_bias, j) for j in (1, 2, 3)]
+    fc1_bias_whole = jnp.concatenate([cut(fc1_biases[j], quarter(s), sub) for s, j in order]).astype(f32)
+
+    all_clips = lengths.shape[0]
+    valid_all = (
+        loss_mask.reshape(all_clips, L) * (jnp.arange(L)[None, :] < lengths[:, None])
+    ).astype(f32)
+    valid_total = jnp.maximum(jnp.sum(valid_all), 1.0)
+    first_row = (group_index * 4 + col) * local_rows
+    valid = lax.dynamic_slice_in_dim(valid_all.reshape(all_clips * L), first_row, local_rows)
+    my_length = lax.dynamic_slice_in_dim(lengths, clip, 1)
+    spot = jnp.arange(L)
+    position = jnp.where(
+        spot < local_rows, second * local_rows + spot, (1 - second) * local_rows + spot - local_rows
+    )
+    key_bias = jnp.where(position < my_length, 0.0, MASKED).astype(f32)
+    key_bias = jnp.broadcast_to(key_bias[:, None], (L, 128))
+
+    tokens_one = jnp.concatenate([norm_one, norm_other], axis=0)
+    zero_bias = jnp.zeros((head_width,), f32)
+    score_scale = HD**-0.5
+    packs, atts, lses, att_others = [], [], [], []
+    biases = [(q_bias, v_bias), tuple(over_col(jnp.stack([q_bias, v_bias]), 2))]
+    for matrix, (q_add, v_add) in zip((qkv_near, qkv_far), biases, strict=True):
+        projected = jnp.dot(tokens_one, matrix, preferred_element_type=f32)
+        packed = (
+            projected + jnp.concatenate([q_add.astype(f32), zero_bias, v_add.astype(f32)])[None]
+        ).astype(bf16)
+        scale = jnp.where(jnp.arange(3 * head_width) < head_width, score_scale, 1.0).astype(bf16)
+        packed = packed * scale[None]
+        att, lse = attend(packed, key_bias)
+        packs.append(packed)
+        atts.append(att)
+        lses.append(lse)
+        att_others.append(over_col(att[local_rows:], 1))
+    attended_rows = jnp.concatenate(
+        [atts[0][:local_rows], att_others[0], atts[1][:local_rows], att_others[1]], axis=1
+    )
+    middle = inputs + (jnp.dot(attended_rows, proj_whole, preferred_element_type=f32) + bias_proj)
+    norm_two, unit_two, spread_two = normalize(middle, gain_two, shift_two)
+    norm_two = norm_two.astype(bf16)
+    hidden_pre = jnp.dot(norm_two, fc1_whole, preferred_element_type=f32) + fc1_bias_whole
+    hidden = gelu_value(hidden_pre).astype(bf16)
+    outputs = middle + (jnp.dot(hidden, fc2_whole, preferred_element_type=f32) + bias_two)
+    differ = outputs - frame(teacher).astype(f32)
+    numerator = jnp.sum(valid[:, None] * differ * differ)
+    loss_scale = all_clips * L * width / 2.0
+    grad_out = loss_scale * 2.0 / (valid_total * width) * valid[:, None] * differ
+    grad_low = grad_out.astype(bf16)
+
+    def both_halves(left, right, split_left):
+        if split_left:
+            given = dot_tn(left[:, half:], right)
+            kept = dot_tn(left[:, :half], right)
+        else:
+            given = dot_tn(left, right[:, half:])
+            kept = dot_tn(left, right[:, :half])
+        taken = over_row(given.astype(bf16))
+        return (kept + taken.astype(f32)).astype(bf16)
+
+    wide_fc2 = both_halves(hidden, grad_low, False)
+    grad_hidden = jnp.dot(grad_low, fc2_whole.T, preferred_element_type=f32)
+    grad_pre = (grad_hidden * gelu_slope(hidden_pre)).astype(bf16)
+    fc1_bias_sum = jnp.sum(grad_pre, axis=0, dtype=f32)
+    grad_norm_two = jnp.dot(grad_pre, fc1_whole.T, preferred_element_type=f32)
+    back_two, gain_two_grad, shift_two_grad = norm_back(grad_norm_two, unit_two, spread_two, gain_two)
+    grad_mid = grad_out + back_two
+    mid_low = grad_mid.astype(bf16)
+    grad_att_rows = jnp.dot(mid_low, proj_whole.T, preferred_element_type=f32).astype(bf16)
+    ups = []
+    for b in range(2):
+        at = 2 * b * head_width
+        ups.append(
+            jnp.concatenate(
+                [
+                    grad_att_rows[:, at : at + head_width],
+                    over_col(grad_att_rows[:, at + head_width : at + 2 * head_width], 1),
+                ],
+                axis=0,
+            )
+        )
+    wide_fc1 = both_halves(norm_two, grad_pre, True)
+    wide_proj = both_halves(attended_rows, mid_low, False)
+
+    span = 4 * sub
+
+    def fc1_part(s):
+        at = SUB_ORDER.index(s) * span
+        return wide_fc1[:, at : at + span]
+
+    def fc2_part(s):
+        at = SUB_ORDER.index(s) * span
+        return wide_fc2[at : at + span]
+
+    def proj_part(s):
+        return jnp.concatenate(
+            [
+                cut(wide_proj[j * head_width : (j + 1) * head_width], quarter(s), quarter_rows)
+                for j in range(4)
+            ],
+            axis=0,
+        )
+
+    def gather_sum(own_part, taken):
+        total = own_part.astype(f32)
+        for piece in taken:
+            total = total + piece.astype(f32)
+        return total.astype(bf16)
+
+    def reduce_parts(part, block, axis):
+        plane = gather_sum(part(0), [over_dp(part(s), s) for s in (1, 2, 3)])
+        cuts = [lax.slice_in_dim(plane, j * block, (j + 1) * block, axis=axis) for j in range(4)]
+        mine_sum = gather_sum(cuts[0], [over_col(cuts[j], j) for j in (1, 2, 3)])
+        pieces = [mine_sum] + [over_dp(mine_sum, s) for s in (1, 2, 3)]
+        return place(pieces, quarter, axis).astype(f32)
+
+    fc2_grad = reduce_parts(fc2_part, sub, 0)
+    fc1_grad = reduce_parts(fc1_part, sub, 1)
+    proj_grad = reduce_parts(proj_part, quarter_rows, 0)
+
+    grads, wide_qkv, grad_norm_one = [], [], None
+    for b, matrix in enumerate((qkv_near, qkv_far)):
+        grad = attend_back(packs[b], key_bias, lses[b], atts[b], ups[b])
+        grads.append(grad)
+        wide_qkv.append(both_halves(tokens_one, grad, True))
+        part = dot_nt(grad, matrix)
+        grad_norm_one = part if grad_norm_one is None else grad_norm_one + part
+    norm_taken = over_col(grad_norm_one[local_rows:].astype(bf16), 1)
+    grad_norm_one = grad_norm_one[:local_rows] + norm_taken.astype(f32)
+    back_one, gain_one_grad, shift_one_grad = norm_back(grad_norm_one, unit_one, spread_one, gain_one)
+    grad_states = frame((grad_mid + back_one).astype(bf16))
+
+    qkv_sum = gather_sum(wide_qkv[0], [over_col(wide_qkv[1], 2)])
+    quarter_deep = half // 4
+    qkv_parts = gather_sum(
+        cut(qkv_sum, dp, quarter_deep),
+        [over_dp(cut(qkv_sum, quarter(s), quarter_deep), s) for s in (1, 2, 3)],
+    )
+    qkv_grad = place([qkv_parts] + [over_dp(qkv_parts, s) for s in (1, 2, 3)], quarter, 0)
+    qkv_grad = qkv_grad.astype(f32).reshape(half, 3, head_width)
+
+    def row_half(stacked):
+        return stacked[:, :half] + over_row(stacked[:, half:])
+
+    early = jnp.stack(
+        [
+            gain_two_grad,
+            shift_two_grad,
+            jnp.sum(mid_low, axis=0, dtype=f32),
+            jnp.sum(grad_low, axis=0, dtype=f32),
+        ]
+    )
+    early = jnp.concatenate([row_half(early).reshape(-1), jnp.zeros((128,), f32).at[0].set(0.0)])
+    tail_mask = jnp.arange(early.shape[0]) == early.shape[0] - 128
+    numerator = numerator + over_row(numerator.reshape(1))[0]
+    early = jnp.where(tail_mask, numerator, early)
+    bias_sum = fc1_bias_sum + over_row(fc1_bias_sum)
+    bias_parts = [bias_sum[SUB_ORDER.index(s) * span : (SUB_ORDER.index(s) + 1) * span] for s in range(4)]
+    joined = jnp.concatenate([early, bias_parts[0]])
+    for s in (1, 2, 3):
+        joined = joined + over_dp(jnp.concatenate([early, bias_parts[s]]), s)
+    early, bias_sum = joined[: early.shape[0]], joined[early.shape[0] :]
+    joined = jnp.concatenate([early, bias_sum[:sub]])
+    for j in (1, 2, 3):
+        joined = joined + over_col(jnp.concatenate([early, bias_sum[j * sub : (j + 1) * sub]]), j)
+    early, bias_sum = joined[: early.shape[0]], joined[early.shape[0] :]
+    fc1_bias_grad = place([bias_sum] + [over_dp(bias_sum, s) for s in (1, 2, 3)], quarter, 0)
+    loss_sum = early[early.shape[0] - 128]
+    early = early[: early.shape[0] - 128].reshape(4, half)
+
+    late = row_half(jnp.stack([gain_one_grad, shift_one_grad])).reshape(-1)
+    head_sums = [
+        jnp.concatenate([jnp.sum(g[:, i : i + head_width], axis=0, dtype=f32) for i in (0, 2 * head_width)])
+        for g in grads
+    ]
+    heads = jnp.concatenate(head_sums)
+    heads = heads + over_row(heads)
+    late = jnp.concatenate([late, heads])
+    late = late + over_dp(late, 1)
+    late = late + over_dp(late, 2)
+    cut_at = 2 * half
+    late_heads = late[cut_at : cut_at + 2 * head_width] + over_col(late[cut_at + 2 * head_width :], 2)
+    late = late[:cut_at]
+    late = late + over_col(late, 1)
+    late = late + over_col(late, 2)
+    late = late.reshape(2, half)
+
+    loss_value = loss_sum / (valid_total * width)
+    return (
+        frame(outputs.astype(bf16)),
+        loss_value,
+        grad_states,
+        late[0],
+        late[1],
+        qkv_grad,
+        late_heads[:head_width],
+        late_heads[head_width:],
+        proj_grad,
+        early[2],
+        early[0],
+        early[1],
+        fc1_grad,
+        fc1_bias_grad,
+        fc2_grad,
+        early[3],
+    )
+
+
 def solution(mesh):
+    sizes = (mesh.shape["dp"], mesh.shape["row"], mesh.shape["col"])
+    body = local_paired if sizes == PAIRED_MESH else local_general
     in_specs = (
         P(("dp", "row", "col"), None),
         P("row"),
@@ -360,4 +895,4 @@
         P("col", "row"),
         P("row"),
     )
-    return jax.shard_map(local, mesh=mesh, in_specs=in_specs, out_specs=out_specs, check_vma=False)
+    return jax.shard_map(body, mesh=mesh, in_specs=in_specs, out_specs=out_specs, check_vma=False)

time: 1380 us -> 765 us (0.55)
  waiting for transfers between devices: 577 us -> 260 us
  matrix products: 359 us -> 136 us
  Pallas kernels: 0 us -> 121 us
  blocking collectives: 121 us -> 0 us
  starting transfers between devices: 13.4 us -> 97.8 us
  local copies, waits for them, and re-layouts: 159 us -> 89.5 us
  other arithmetic: 112 us -> 47.4 us
  loops' own time: 17.3 us -> 0 us
    all_to_all x3 -> x0, waiting for transfers between devices: 297 us -> none  [the longest x1 235 us: local(): lax.all_to_all(grads_packed.reshape(group_rows, 3, head_width), 'col', sp...]
    all_gather x8 -> x0, waiting for transfers between devices: 271 us -> none  [the longest x1 121 us: local(): lax.all_gather(fc2_full, 'col', axis=0, tiled=True)]
    ppermute x0 -> x91, waiting for transfers between devices: none -> 260 us  [swap(): return lax.ppermute(values, axis, [(i, i ^ mask) for i in range(size)])]
    dot_general x40 -> x20, matrix products: 359 us -> 136 us  [the longest x10 49.1 us: dot_tn(): lax.dot_general(a, b, (((0,), (0,)), ((), ())), preferred_element_type=jn...]
    pallas_call x0 -> x4, Pallas kernels: none -> 121 us  [the longest x2 74.7 us: attend_back(): pl.pallas_call(attend_back_kernel, out_shape=jax.ShapeDtypeStruct((tokens...]
    ppermute x0 -> x91, starting transfers between devices: none -> 97.8 us  [swap(): return lax.ppermute(values, axis, [(i, i ^ mask) for i in range(size)])]
    all_gather x3 -> x0, blocking collectives: 82.3 us -> none  [the longest x1 78 us: local(): lax.all_gather(fc1_bias, 'col', axis=0, tiled=True)]
    convert_element_type x6 -> x1, local copies, waits for them, and re-layouts: 66.1 us -> 0.82 us  [gather_sum(): return total.astype(bf16)]
  transfers between devices with their start and end apart: 19 -> 91, of which waited for: 8 -> 39; matrix products, arithmetic and copies ran while one was open for 41% -> 22% of each run, Pallas kernels for 0% -> 16%
where the time goes in v1:
time: 765 us; the launch traced here: 760 us
  waiting for transfers between devices  260 us (34%)
  matrix products  136 us (18%)
  Pallas kernels  121 us (16%)
  starting transfers between devices  97.8 us (13%)
  local copies, waits for them, and re-layouts  89.5 us (12%)
  other arithmetic  47.4 us (6%)
    ppermute x91, waiting for transfers between devices, swap(): return lax.ppermute(values, axis, [(i, i ^ mask) for i in range(size)])  260 us
    ppermute x91, starting transfers between devices, swap(): return lax.ppermute(values, axis, [(i, i ^ mask) for i in range(size)])  97.8 us
    pallas_call x2, Pallas kernels, attend_back(): pl.pallas_call(attend_back_kernel, out_shape=jax.ShapeDtypeStruct((tokens...  74.7 us
    unnamed x256, local copies, waits for them, and re-layouts  50.2 us
    dot_general x10, matrix products, dot_tn(): lax.dot_general(a, b, (((0,), (0,)), ((), ())), preferred_element_type=jn...  49.1 us
    pallas_call x2, Pallas kernels, attend(): pl.pallas_call(attend_kernel, out_shape=(jax.ShapeDtypeStruct((tokens, wi...  46.3 us
    dot_general x1, matrix products, local_paired(): grad_hidden = jnp.dot(grad_low, fc2_whole.T, preferred_element_type=f32)  15.5 us
  transfers between devices with their start and end apart: 91, of which 39 were waited for; matrix products, arithmetic and copies ran while one was open for 22% of the time, Pallas kernels for 16%

profile of v1, /device:TPU:0, one launch (start us, length us, event | category | flops | bytes accessed | tf_op | source)
XLA Modules:
  0.0 759.7 jit_solution(14761102937070948230)
XLA Ops:
  40.7 24.8 %collective-permute-done.9 = bf16[2,256]{1,0:T(2,128)(2,1)} collective-permute-done((bf16[2,256]{1,0:T(2,128)(2,1)}, bf16[2,256]{1,0:T(2,128)(2,1)}, u32[]{:S(2)}, u32[]{:S(2)}) %collective-permute-start.9) | collective-permute-done | bytes 1056 | tf_op jit(solution)/shard_map/ppermute | solution.py:473
  110.4 8.4 %collective-permute-done.13 = bf16[1152,256]{1,0:T(8,128)(2,1)S(1)} collective-permute-done((bf16[1152,256]{1,0:T(8,128)(2,1)}, bf16[1152,256]{1,0:T(8,128)(2,1)S(1)}, u32[]{:S(2)}, u32[]{:S(2)}) %collective-permute-start.13) | collective-permute-done | bytes 589856 | tf_op jit(solution)/shard_map/ppermute | solution.py:473
  121.0 10.4 %collective-permute-done.17 = bf16[1152,256]{1,0:T(8,128)(2,1)S(1)} collective-permute-done((bf16[1152,256]{1,0:T(8,128)(2,1)}, bf16[1152,256]{1,0:T(8,128)(2,1)S(1)}, u32[]{:S(2)}, u32[]{:S(2)}) %collective-permute-start.17) | collective-permute-done | bytes 589856 | tf_op jit(solution)/shard_map/ppermute | solution.py:473
  133.6 7.9 %collective-permute-done.21 = bf16[1152,256]{1,0:T(8,128)(2,1)S(1)} collective-permute-done((bf16[1152,256]{1,0:T(8,128)(2,1)}, bf16[1152,256]{1,0:T(8,128)(2,1)S(1)}, u32[]{:S(2)}, u32[]{:S(2)}) %collective-permute-start.21) | collective-permute-done | bytes 589856 | tf_op jit(solution)/shard_map/ppermute | solution.py:473
  147.6 10.5 %collective-permute-done.20 = bf16[1152,256]{1,0:T(8,128)(2,1)S(1)} collective-permute-done((bf16[1152,256]{1,0:T(8,128)(2,1)}, bf16[1152,256]{1,0:T(8,128)(2,1)S(1)}, u32[]{:S(2)}, u32[]{:S(2)}) %collective-permute-start.20) | collective-permute-done | bytes 589856 | tf_op jit(solution)/shard_map/ppermute | solution.py:473
  174.5 9.7 %collective-permute-done.18 = bf16[1152,256]{1,0:T(8,128)(2,1)S(1)} collective-permute-done((bf16[1152,256]{1,0:T(8,128)(2,1)}, bf16[1152,256]{1,0:T(8,128)(2,1)S(1)}, u32[]{:S(2)}, u32[]{:S(2)}) %collective-permute-start.18) | collective-permute-done | bytes 589856 | tf_op jit(solution)/shard_map/ppermute | solution.py:473
  205.4 23.4 %attend.3 = (bf16[1568,256]{1,0:T(8,128)(2,1)S(1)}, f32[13,8,512]{2,1,0:T(8,128)S(1)}) custom-call(bf16[1568,768]{1,0:T(8,128)(2,1)S(1)} %fusion.26.packed_ref, f32[1568,128]{1,0:T(8,128)S(1)} %broadcast_in_dim.63.bias_ref), custom_call_target="tpu_custom_call" | custom-call | flops 10070523904 | bytes 8388608 | tf_op jit(solution)/shard_map/attend/pallas_call | solution.py:435
  235.4 22.9 %attend.2 = (bf16[1568,256]{1,0:T(8,128)(2,1)S(1)}, f32[13,8,512]{2,1,0:T(8,128)S(1)}) custom-call(bf16[1568,768]{1,0:T(8,128)(2,1)S(1)} %fusion.25.packed_ref, f32[1568,128]{1,0:T(8,128)S(1)} %broadcast_in_dim.63.bias_ref), custom_call_target="tpu_custom_call" | custom-call | flops 10070523904 | bytes 8388608 | tf_op jit(solution)/shard_map/attend/pallas_call | solution.py:435
  262.0 7.9 %collective-permute-done.3 = bf16[784,256]{1,0:T(8,128)(2,1)S(1)} collective-permute-done((bf16[784,256]{1,0:T(8,128)(2,1)S(1)}, bf16[784,256]{1,0:T(8,128)(2,1)S(1)}, u32[]{:S(2)}, u32[]{:S(2)}) %collective-permute-start.3) | collective-permute-done | bytes 401440 | tf_op jit(solution)/shard_map/ppermute | solution.py:473
  287.8 11.6 %multiply_convert_fusion = (bf16[784,4096]{1,0:T(8,128)(2,1)}, f32[784,4096]{1,0:T(8,128)}) fusion(f32[4096]{0:T(1024)S(1)} %convert_element_type.290, bf16[784,1024]{1,0:T(8,128)(2,1)S(1)} %add_convert_fusion.4, bf16[512,4096]{1,0:T(8,128)(2,1)S(1)} %slice_dynamic-update-slice_fusion, bf16[512,4096]{1,0:T(8,128)(2,1)S(1)} %copy-done.77), kind=kOutput, calls=%fused_computation.8 | convolution fusion | flops 6612713472 | bytes 29278208 | tf_op jit(solution)/shard_map/dot_general | solution.py:691
  299.4 14.3 %fusion.24 = (f32[]{:T(128)}, f32[784,1024]{1,0:T(8,128)S(1)}, bf16[784,1024]{1,0:T(8,128)(2,1)}) fusion(f32[784]{0:T(1024)S(1)} %copy-done.79, bf16[784,1024]{1,0:T(8,128)(2,1)S(1)} %copy-done.24, bf16[784,512]{1,0:T(8,128)(2,1)S(1)} %copy-done.32, bf16[784,512]{1,0:T(8,128)(2,1)S(1)} %get-tuple-element.154, pred[]{:T(512)S(6)} %eq.14, ...), kind=kOutput, calls=%fused_computation.46 | convolution fusion | flops 6603882496 | bytes 26057796 | tf_op jit(solution)/shard_map/dot_general | solution.py:693
  314.0 9.8 %convolution_convert_fusion = bf16[4096,512]{1,0:T(8,128)(2,1)} fusion(bf16[784,4096]{1,0:T(8,128)(2,1)} %get-tuple-element.299, bf16[784,1024]{1,0:T(8,128)(2,1)S(1)} %get-tuple-element.76), kind=kOutput, calls=%fused_computation.14 | convolution fusion | flops 3290431488 | bytes 11419648 | tf_op jit(solution)/shard_map/dot_general | solution.py:341
  323.8 15.5 %convert_reduce_fusion = (f32[4096]{0:T(1024)S(1)}, bf16[784,4096]{1,0:T(8,128)(2,1)}) fusion(f32[784,4096]{1,0:T(8,128)} %get-tuple-element.300, f32[4096]{0:T(1024)S(1)} %convert_element_type.290, bf16[784,1024]{1,0:T(8,128)(2,1)S(1)} %get-tuple-element.76, bf16[4096,512]{1,0:T(8,128)(2,1)S(1)} %copy-done.75, bf16[4096,512]{1,0:T(8,128)(2,1)S(1)} %copy-done.73), kind=kOutput, calls=%fused_computation.7 | convolution fusion | flops 6635188224 | bytes 29294592 | tf_op jit(solution)/shard_map/dot_general | solution.py:711
  339.3 14.3 %multiply_reduce_fusion.1 = (f32[1024]{0:T(1024)S(1)}, f32[784]{0:T(1024)S(1)}, f32[784]{0:T(1024)S(1)}, f32[1024]{0:T(1024)S(1)}, f32[784,1024]{1,0:T(8,128)}) fusion(f32[784,1024]{1,0:T(8,128)S(1)} %get-tuple-element.298, f32[784]{0:T(1024)S(1)} %add_rsqrt_fusion, f32[784]{0:T(1024)S(1)} %broadcast_multiply_fusion.5, f32[1024]{0:T(1024)S(1)} %bitcast.53, ...), kind=kOutput, calls=%fused_computation.53 | convolution fusion | flops 6600667136 | bytes 21258496 | tf_op jit(solution)/shard_map/dot_general | solution.py:714
  353.6 9.1 %convolution_convert_fusion.1 = bf16[512,4096]{1,0:T(8,128)(2,1)} fusion(bf16[784,4096]{1,0:T(8,128)(2,1)} %get-tuple-element.304, bf16[784,1024]{1,0:T(8,128)(2,1)S(1)} %add_convert_fusion.4), kind=kOutput, calls=%fused_computation.15 | convolution fusion | flops 3290431488 | bytes 11419648 | tf_op jit(solution)/shard_map/dot_general | solution.py:341
  365.1 14.5 %convolution_convert_fusion.2 = bf16[784,1024]{1,0:T(8,128)(2,1)S(1)} fusion(bf16[784,1024]{1,0:T(8,128)(2,1)S(1)} %get-tuple-element.73, bf16[256,512]{1,0:T(8,128)(2,1)S(1)} %copy-done.57, bf16[256,512]{1,0:T(8,128)(2,1)S(1)} %copy-done.55, bf16[256,512]{1,0:T(8,128)(2,1)S(1)} %copy-done.53, bf16[256,256]{1,0:T(8,128)(2,1)S(1)} %copy-done.62, ...), kind=kOutput, calls=%fused_computation.71 | convolution fusion | flops 1663844352 | bytes 5308416 | tf_op jit(solution)/shard_map/dot_general | solution.py:718
  412.0 37.2 %attend_back.2 = bf16[1568,768]{1,0:T(8,128)(2,1)} custom-call(bf16[1568,768]{1,0:T(8,128)(2,1)} %copy-done.4, f32[1568,128]{1,0:T(8,128)} %copy-done, f32[13,8,512]{2,1,0:T(8,128)} %copy-done.6, bf16[1568,256]{1,0:T(8,128)(2,1)} %copy-done.2, bf16[1568,256]{1,0:T(8,128)(2,1)} %pad_maximum_fusion.21.up_ref), custom_call_target="tpu_custom_call" | custom-call | flops 25176309760 | bytes 10485760 | tf_op jit(solution)/shard_map/attend_back/pallas_call | solution.py:454
  452.8 37.5 %attend_back.3 = bf16[1568,768]{1,0:T(8,128)(2,1)} custom-call(bf16[1568,768]{1,0:T(8,128)(2,1)} %copy-done.3, f32[1568,128]{1,0:T(8,128)} %copy-done, f32[13,8,512]{2,1,0:T(8,128)} %copy-done.5, bf16[1568,256]{1,0:T(8,128)(2,1)} %copy-done.1, bf16[1568,256]{1,0:T(8,128)(2,1)} %pad_maximum_fusion.22.up_ref), custom_call_target="tpu_custom_call" | custom-call | flops 25176309760 | bytes 10485760 | tf_op jit(solution)/shard_map/attend_back/pallas_call | solution.py:454
  527.6 23.9 %collective-permute-done.62 = bf16[64,512]{1,0:T(8,128)(2,1)S(1)} collective-permute-done((bf16[64,512]{1,0:T(8,128)(2,1)S(1)}, bf16[64,512]{1,0:T(8,128)(2,1)S(1)}, u32[]{:S(2)}, u32[]{:S(2)}) %collective-permute-start.62) | collective-permute-done | bytes 65568 | tf_op jit(solution)/shard_map/ppermute | solution.py:473
  569.1 20.6 %collective-permute-done.50 = bf16[512,768]{1,0:T(8,128)(2,1)S(1)} collective-permute-done((bf16[512,768]{1,0:T(8,128)(2,1)S(1)}, bf16[512,768]{1,0:T(8,128)(2,1)S(1)}, u32[]{:S(2)}, u32[]{:S(2)}) %collective-permute-start.50) | collective-permute-done | bytes 786464 | tf_op jit(solution)/shard_map/ppermute | solution.py:473
  626.6 8.8 %add_convert_fusion = bf16[4096,512]{1,0:T(8,128)(2,1)S(1)} fusion(bf16[4096,512]{1,0:T(8,128)(2,1)} %collective-permute-done.81, bf16[784,4096]{1,0:T(8,128)(2,1)} %get-tuple-element.299, bf16[784,1024]{1,0:T(8,128)(2,1)} %copy-done.27), kind=kOutput, calls=%fused_computation.12 | convolution fusion | flops 3294625792 | bytes 15613952 | tf_op jit(solution)/shard_map/dot_general | solution.py:341
  651.4 38.8 %collective-permute-done.56 = bf16[128,768]{1,0:T(8,128)(2,1)S(1)} collective-permute-done((bf16[128,768]{1,0:T(8,128)(2,1)S(1)}, bf16[128,768]{1,0:T(8,128)(2,1)S(1)}, u32[]{:S(2)}, u32[]{:S(2)}) %collective-permute-start.56) | collective-permute-done | bytes 196640 | tf_op jit(solution)/shard_map/ppermute | solution.py:473
  701.8 10.6 %collective-permute-done.69 = bf16[512,1024]{1,0:T(8,128)(2,1)S(1)} collective-permute-done((bf16[512,1024]{1,0:T(8,128)(2,1)}, bf16[512,1024]{1,0:T(8,128)(2,1)S(1)}, u32[]{:S(2)}, u32[]{:S(2)}) %collective-permute-start.69) | collective-permute-done | bytes 1048608 | tf_op jit(solution)/shard_map/ppermute | solution.py:473
  713.6 15.5 %collective-permute-done.70 = bf16[512,1024]{1,0:T(8,128)(2,1)} collective-permute-done((bf16[512,1024]{1,0:T(8,128)(2,1)}, bf16[512,1024]{1,0:T(8,128)(2,1)}, u32[]{:S(2)}, u32[]{:S(2)}) %collective-permute-start.70) | collective-permute-done | bytes 1048608 | tf_op jit(solution)/shard_map/ppermute | solution.py:473
  (679 shorter events, 344.3 us)
Async XLA Ops:
  8.4 86.6 %collective-permute-start.11 = (bf16[1152,256]{1,0:T(8,128)(2,1)}, bf16[1152,256]{1,0:T(8,128)(2,1)}, u32[]{:S(2)}, u32[]{:S(2)}) collective-permute-start(bf16[1152,256]{1,0:T(8,128)(2,1)} %constant_dynamic-update-slice_fusion), channel_id=1, source_target_pairs={{0,1},{1,0},{2,3},{3,2},{4,5},{5,4},{6,7},{7,6},{8,9},{9,8},{10,11... | collective-permute-start | bytes 1769480 | tf_op jit(solution)/shard_map/ppermute | solution.py:473
  11.5 85.5 %collective-permute-start.15 = (bf16[1152,256]{1,0:T(8,128)(2,1)}, bf16[1152,256]{1,0:T(8,128)(2,1)}, u32[]{:S(2)}, u32[]{:S(2)}) collective-permute-start(bf16[1152,256]{1,0:T(8,128)(2,1)} %constant_dynamic-update-slice_fusion), channel_id=1, source_target_pairs={{0,2},{1,3},{2,0},{3,1},{4,6},{5,7},{6,4},{7,5},{8,10},{9,11},{10,... | collective-permute-start | bytes 1769480 | tf_op jit(solution)/shard_map/ppermute | solution.py:473
  14.1 84.7 %collective-permute-start.19 = (bf16[1152,256]{1,0:T(8,128)(2,1)}, bf16[1152,256]{1,0:T(8,128)(2,1)}, u32[]{:S(2)}, u32[]{:S(2)}) collective-permute-start(bf16[1152,256]{1,0:T(8,128)(2,1)} %constant_dynamic-update-slice_fusion), channel_id=1, source_target_pairs={{0,3},{1,2},{2,1},{3,0},{4,7},{5,6},{6,5},{7,4},{8,11},{9,10},{10,... | collective-permute-start | bytes 1769480 | tf_op jit(solution)/shard_map/ppermute | solution.py:473
  15.9 49.5 %collective-permute-start.9 = (bf16[2,256]{1,0:T(2,128)(2,1)}, bf16[2,256]{1,0:T(2,128)(2,1)}, u32[]{:S(2)}, u32[]{:S(2)}) collective-permute-start(bf16[2,256]{1,0:T(2,128)(2,1)} %pad_maximum_fusion.40), channel_id=1, source_target_pairs={{0,2},{1,3},{2,0},{3,1},{4,6},{5,7},{6,4},{7,5},{8,10},{9,11},{10,... | collective-permute-start | bytes 3080 | tf_op jit(solution)/shard_map/ppermute | solution.py:473
  17.9 49.6 %collective-permute-start.27 = (bf16[1024]{0:T(1024)(128)(2,1)}, bf16[1024]{0:T(1024)(128)(2,1)}, u32[]{:S(2)}, u32[]{:S(2)}) collective-permute-start(bf16[1024]{0:T(1024)(128)(2,1)} %param.30), channel_id=1, source_target_pairs={{0,1},{1,0},{2,3},{3,2},{4,5},{5,4},{6,7},{7,6},{8,9},{9,8},{10,11... | collective-permute-start | bytes 6152 | tf_op jit(solution)/shard_map/ppermute | solution.py:473
  89.6 141.1 %collective-permute-start.2 = (bf16[512,768]{0,1:T(8,128)(2,1)S(1)}, bf16[512,768]{0,1:T(8,128)(2,1)}, u32[]{:S(2)}, u32[]{:S(2)}) collective-permute-start(bf16[512,768]{0,1:T(8,128)(2,1)S(1)} %bitcast.46), channel_id=1, source_target_pairs={{0,4},{4,0},{1,5},{5,1},{2,6},{6,2},{3,7},{7,3},{8,12},{12,8},{9,1... | collective-permute-start | bytes 2359304 | tf_op jit(solution)/shard_map/ppermute | solution.py:473
  93.9 108.3 %collective-permute-start.1 = (bf16[784,1024]{1,0:T(8,128)(2,1)S(1)}, bf16[784,1024]{1,0:T(8,128)(2,1)S(1)}, u32[]{:S(2)}, u32[]{:S(2)}) collective-permute-start(bf16[784,1024]{1,0:T(8,128)(2,1)S(1)} %fusion.16), channel_id=1, source_target_pairs={{0,1},{1,0},{2,3},{3,2},{4,5},{5,4},{6,7},{7,6},{8,9},{9,8},{10,11... | collective-permute-start | bytes 4816904 | tf_op jit(solution)/shard_map/ppermute | solution.py:473
  144.6 57.1 %collective-permute-start.8 = (bf16[512,768]{0,1:T(8,128)(2,1)S(1)}, bf16[512,768]{0,1:T(8,128)(2,1)S(1)}, u32[]{:S(2)}, u32[]{:S(2)}) collective-permute-start(bf16[512,768]{0,1:T(8,128)(2,1)S(1)} %constant_dynamic-update-slice_fusion.30), channel_id=1, source_target_pairs={{0,4},{4,0},{1,5},{5,1},{2,6},{6,2},{3,7},{7,3},{8,12},{12,8},{9,1... | collective-permute-start | bytes 2359304 | tf_op jit(solution)/shard_map/ppermute | solution.py:473
  184.3 77.6 %collective-permute-start.23 = (bf16[4608,256]{1,0:T(8,128)(2,1)}, bf16[4608,256]{1,0:T(8,128)(2,1)S(1)}, u32[]{:S(2)}, u32[]{:S(2)}) collective-permute-start(bf16[4608,256]{1,0:T(8,128)(2,1)} %constant_dynamic-update-slice_fusion.4), channel_id=1, source_target_pairs={{0,4},{4,0},{1,5},{5,1},{2,6},{6,2},{3,7},{7,3},{8,12},{12,8},{9,1... | collective-permute-start | bytes 7077896 | tf_op jit(solution)/shard_map/ppermute | solution.py:473
  193.5 64.9 %collective-permute-start.24 = (bf16[4608,256]{1,0:T(8,128)(2,1)}, bf16[4608,256]{1,0:T(8,128)(2,1)S(1)}, u32[]{:S(2)}, u32[]{:S(2)}) collective-permute-start(bf16[4608,256]{1,0:T(8,128)(2,1)} %pad_maximum_fusion.7), channel_id=1, source_target_pairs={{0,4},{4,0},{1,5},{5,1},{2,6},{6,2},{3,7},{7,3},{8,12},{12,8},{9,1... | collective-permute-start | bytes 7077896 | tf_op jit(solution)/shard_map/ppermute | solution.py:473
  201.7 58.7 %collective-permute-start.25 = (bf16[4608,256]{1,0:T(8,128)(2,1)}, bf16[4608,256]{1,0:T(8,128)(2,1)S(1)}, u32[]{:S(2)}, u32[]{:S(2)}) collective-permute-start(bf16[4608,256]{1,0:T(8,128)(2,1)} %pad_maximum_fusion.8), channel_id=1, source_target_pairs={{0,4},{4,0},{1,5},{5,1},{2,6},{6,2},{3,7},{7,3},{8,12},{12,8},{9,1... | collective-permute-start | bytes 7077896 | tf_op jit(solution)/shard_map/ppermute | solution.py:473
  202.2 58.4 %collective-permute-start.26 = (bf16[4608,256]{1,0:T(8,128)(2,1)}, bf16[4608,256]{1,0:T(8,128)(2,1)}, u32[]{:S(2)}, u32[]{:S(2)}) collective-permute-start(bf16[4608,256]{1,0:T(8,128)(2,1)} %pad_maximum_fusion.9), channel_id=1, source_target_pairs={{0,4},{4,0},{1,5},{5,1},{2,6},{6,2},{3,7},{7,3},{8,12},{12,8},{9,1... | collective-permute-start | bytes 7077896 | tf_op jit(solution)/shard_map/ppermute | solution.py:473
  382.9 120.1 %collective-permute-start.58 = (bf16[1024,512]{1,0:T(8,128)(2,1)}, bf16[1024,512]{1,0:T(8,128)(2,1)}, u32[]{:S(2)}, u32[]{:S(2)}) collective-permute-start(bf16[1024,512]{1,0:T(8,128)(2,1)} %convolution_convert_fusion.3), channel_id=1, source_target_pairs={{0,4},{4,0},{1,5},{5,1},{2,6},{6,2},{3,7},{7,3},{8,12},{12,8},{9,1... | collective-permute-start | bytes 3145736 | tf_op jit(solution)/shard_map/ppermute | solution.py:473
  408.5 42.4 %collective-permute-start.40 = (bf16[784,256]{1,0:T(8,128)(2,1)}, bf16[784,256]{1,0:T(8,128)(2,1)}, u32[]{:S(2)}, u32[]{:S(2)}) collective-permute-start(bf16[784,256]{1,0:T(8,128)(2,1)} %get-tuple-element.151), channel_id=1, source_target_pairs={{0,1},{1,0},{2,3},{3,2},{4,5},{5,4},{6,7},{7,6},{8,9},{9,8},{10,11... | collective-permute-start | bytes 1204232 | tf_op jit(solution)/shard_map/ppermute | solution.py:473
  511.6 80.4 %collective-permute-start.41 = (bf16[784,1024]{1,0:T(8,128)(2,1)S(1)}, bf16[784,1024]{1,0:T(8,128)(2,1)S(1)}, u32[]{:S(2)}, u32[]{:S(2)}) collective-permute-start(bf16[784,1024]{1,0:T(8,128)(2,1)S(1)} %slice.1284), channel_id=1, source_target_pairs={{0,1},{1,0},{2,3},{3,2},{4,5},{5,4},{6,7},{7,6},{8,9},{9,8},{10,11... | collective-permute-start | bytes 4816904 | tf_op jit(solution)/shard_map/ppermute | solution.py:473
  515.1 39.3 %collective-permute-start.48 = (bf16[512,768]{1,0:T(8,128)(2,1)S(1)}, bf16[512,768]{1,0:T(8,128)(2,1)S(1)}, u32[]{:S(2)}, u32[]{:S(2)}) collective-permute-start(bf16[512,768]{1,0:T(8,128)(2,1)S(1)} %convolution_convert_fusion.5), channel_id=1, source_target_pairs={{0,4},{4,0},{1,5},{5,1},{2,6},{6,2},{3,7},{7,3},{8,12},{12,8},{9,1... | collective-permute-start | bytes 2359304 | tf_op jit(solution)/shard_map/ppermute | solution.py:473
  551.5 75.1 %collective-permute-start.81 = (bf16[4096,512]{1,0:T(8,128)(2,1)}, bf16[4096,512]{1,0:T(8,128)(2,1)}, u32[]{:S(2)}, u32[]{:S(2)}) collective-permute-start(bf16[4096,512]{1,0:T(8,128)(2,1)} %convolution_convert_fusion), channel_id=1, source_target_pairs={{0,4},{4,0},{1,5},{5,1},{2,6},{6,2},{3,7},{7,3},{8,12},{12,8},{9,1... | collective-permute-start | bytes 12582920 | tf_op jit(solution)/shard_map/ppermute | solution.py:473
  551.5 87.7 %collective-permute-start.68 = (bf16[512,4096]{1,0:T(8,128)(2,1)}, bf16[512,4096]{1,0:T(8,128)(2,1)}, u32[]{:S(2)}, u32[]{:S(2)}) collective-permute-start(bf16[512,4096]{1,0:T(8,128)(2,1)} %convolution_convert_fusion.1), channel_id=1, source_target_pairs={{0,4},{4,0},{1,5},{5,1},{2,6},{6,2},{3,7},{7,3},{8,12},{12,8},{9,1... | collective-permute-start | bytes 12582920 | tf_op jit(solution)/shard_map/ppermute | solution.py:473
  637.1 54.3 %collective-permute-start.82 = (bf16[1024,512]{1,0:T(8,128)(2,1)S(1)}, bf16[1024,512]{1,0:T(8,128)(2,1)S(1)}, u32[]{:S(2)}, u32[]{:S(2)}) collective-permute-start(bf16[1024,512]{1,0:T(8,128)(2,1)S(1)} %get-tuple-element.83), channel_id=1, source_target_pairs={{0,8},{8,0},{16,24},{24,16},{1,9},{9,1},{17,25},{25,17},{2,10},{10... | collective-permute-start | bytes 3145736 | tf_op jit(solution)/shard_map/ppermute | solution.py:473
  637.9 60.1 %collective-permute-start.83 = (bf16[1024,512]{1,0:T(8,128)(2,1)}, bf16[1024,512]{1,0:T(8,128)(2,1)}, u32[]{:S(2)}, u32[]{:S(2)}) collective-permute-start(bf16[1024,512]{1,0:T(8,128)(2,1)} %get-tuple-element.85), channel_id=1, source_target_pairs={{0,16},{8,24},{16,0},{24,8},{1,17},{9,25},{17,1},{25,9},{2,18},{10... | collective-permute-start | bytes 3145736 | tf_op jit(solution)/shard_map/ppermute | solution.py:473
  639.2 58.8 %collective-permute-start.84 = (bf16[1024,512]{1,0:T(8,128)(2,1)}, bf16[1024,512]{1,0:T(8,128)(2,1)}, u32[]{:S(2)}, u32[]{:S(2)}) collective-permute-start(bf16[1024,512]{1,0:T(8,128)(2,1)} %get-tuple-element.84), channel_id=1, source_target_pairs={{0,24},{8,16},{16,8},{24,0},{1,25},{9,17},{17,9},{25,1},{2,26},{10... | collective-permute-start | bytes 3145736 | tf_op jit(solution)/shard_map/ppermute | solution.py:473
  647.3 42.9 %collective-permute-start.56 = (bf16[128,768]{1,0:T(8,128)(2,1)S(1)}, bf16[128,768]{1,0:T(8,128)(2,1)S(1)}, u32[]{:S(2)}, u32[]{:S(2)}) collective-permute-start(bf16[128,768]{1,0:T(8,128)(2,1)S(1)} %add_convert_fusion.14), channel_id=1, source_target_pairs={{0,24},{8,16},{16,8},{24,0},{1,25},{9,17},{17,9},{25,1},{2,26},{10... | collective-permute-start | bytes 589832 | tf_op jit(solution)/shard_map/ppermute | solution.py:473
  650.7 61.7 %collective-permute-start.69 = (bf16[512,1024]{1,0:T(8,128)(2,1)}, bf16[512,1024]{1,0:T(8,128)(2,1)S(1)}, u32[]{:S(2)}, u32[]{:S(2)}) collective-permute-start(bf16[512,1024]{1,0:T(8,128)(2,1)} %get-tuple-element.86), channel_id=1, source_target_pairs={{0,8},{8,0},{16,24},{24,16},{1,9},{9,1},{17,25},{25,17},{2,10},{10... | collective-permute-start | bytes 3145736 | tf_op jit(solution)/shard_map/ppermute | solution.py:473
  690.2 38.9 %collective-permute-start.70 = (bf16[512,1024]{1,0:T(8,128)(2,1)}, bf16[512,1024]{1,0:T(8,128)(2,1)}, u32[]{:S(2)}, u32[]{:S(2)}) collective-permute-start(bf16[512,1024]{1,0:T(8,128)(2,1)} %get-tuple-element.88), channel_id=1, source_target_pairs={{0,16},{8,24},{16,0},{24,8},{1,17},{9,25},{17,1},{25,9},{2,18},{10... | collective-permute-start | bytes 3145736 | tf_op jit(solution)/shard_map/ppermute | solution.py:473
  (161 other events, 2807.3 us)

commit v2 on v0

--- a/solution.py
+++ b/solution.py
@@ -1,6 +1,10 @@
+import functools
+
 import jax
 import jax.numpy as jnp
 from jax import lax
+from jax.experimental import pallas as pl
+from jax.experimental.pallas import tpu as pltpu
 from jax.sharding import PartitionSpec as P
 
 HD = 64
@@ -99,7 +103,7 @@
     return jnp.stack([jnp.concatenate(grad_queries, 0), grad_keys, grad_values], axis=1)
 
 
-def local(
+def local_general(
     states,
     ln1_gain,
     ln1_bias,
@@ -322,7 +326,795 @@
     )
 
 
+PAIRED_MESH = (4, 2, 4)
+GROUP = 4
+QT = 128
+
+
+def dot_nn(a, b):
+    return lax.dot_general(a, b, (((1,), (0,)), ((), ())), preferred_element_type=jnp.float32)
+
+
+def dot_nt(a, b):
+    return lax.dot_general(a, b, (((1,), (1,)), ((), ())), preferred_element_type=jnp.float32)
+
+
+def dot_tn(a, b):
+    return lax.dot_general(a, b, (((0,), (0,)), ((), ())), preferred_element_type=jnp.float32)
+
+
+def head_stack(values, zero):
+    lane_head = lax.broadcasted_iota(jnp.int32, values.shape, 1) // HD
+    return jnp.concatenate([jnp.where(lane_head == h, values, zero) for h in range(GROUP)], axis=0)
+
+
+def head_unstack(wide, count):
+    return jnp.concatenate(
+        [wide[h * HD : (h + 1) * HD, h * count : (h + 1) * count] for h in range(GROUP)], axis=0
+    ).T
+
+
+def tiles_of(rows, tile):
+    full = rows // QT
+
+    @pl.loop(0, full)
+    def _(index):
+        tile(pl.multiple_of(index * QT, QT), QT, index)
+
+    if rows > full * QT:
+        tile(full * QT, rows - full * QT, full)
+
+
+def attend_kernel(first, packed_ref, bias_ref, out_ref, lse_ref, vt_ref):
+    width = GROUP * HD
+    vt_ref[...] = packed_ref[:, 2 * width : 3 * width].T
+
+    def tile(start, count, index):
+        cols = GROUP * count
+        stacked = head_stack(
+            packed_ref[pl.ds(first + start, count), 0:width], jnp.zeros((), jnp.bfloat16)
+        )
+        keys = packed_ref[:, width : 2 * width]
+        bias = bias_ref[...]
+        scores = dot_nt(keys, stacked) + jnp.concatenate([bias] * (cols // 128), axis=1)
+        peak = jnp.max(scores, axis=0, keepdims=True)
+        weights = jnp.exp(scores - peak)
+        total = jnp.sum(weights, axis=0, keepdims=True)
+        wide = dot_nn(vt_ref[...], weights.astype(jnp.bfloat16)) * (1.0 / total)
+        out_ref[pl.ds(start, count), :] = head_unstack(wide, count).astype(jnp.bfloat16)
+        lse_ref[index, :, 0:cols] = jnp.broadcast_to(peak + jnp.log(total), (8, cols))
+
+    tiles_of(out_ref.shape[0], tile)
+
+
+def attend_back_kernel(first, last, packed_ref, bias_ref, lse_ref, att_ref, up_ref, *refs):
+    width = GROUP * HD
+    if last:
+        dq_in, dk_in, dv_in, out_ref, kt_ref, dk_ref, dv_ref = refs
+        dk_ref[...] = dk_in[...]
+        dv_ref[...] = dv_in[...]
+        out_ref[0:first, 0:width] = dq_in[...]
+        rows = out_ref.shape[0] - first
+    else:
+        out_ref, dk_ref, dv_ref, kt_ref = refs
+        dk_ref[...] = jnp.zeros_like(dk_ref)
+        dv_ref[...] = jnp.zeros_like(dv_ref)
+        rows = out_ref.shape[0]
+    kt_ref[...] = packed_ref[:, width : 2 * width].T
+
+    def tile(start, count, index):
+        cols = GROUP * count
+        zero = jnp.zeros((), jnp.bfloat16)
+        up = up_ref[pl.ds(start, count), :]
+        stacked = head_stack(packed_ref[pl.ds(first + start, count), 0:width], zero)
+        up_stacked = head_stack(up, zero)
+        product = head_stack(
+            up.astype(jnp.float32) * att_ref[pl.ds(start, count), :].astype(jnp.float32),
+            jnp.zeros((), jnp.float32),
+        )
+        high = product.astype(jnp.bfloat16)
+        low = (product - high.astype(jnp.float32)).astype(jnp.bfloat16)
+        ones = jnp.ones((8, width), jnp.bfloat16)
+        delta = (dot_nt(ones, high) + dot_nt(ones, low))[0:1]
+        keys = packed_ref[:, width : 2 * width]
+        values = packed_ref[:, 2 * width : 3 * width]
+        bias = bias_ref[...]
+        scores = dot_nt(keys, stacked) + jnp.concatenate([bias] * (cols // 128), axis=1)
+        weights = jnp.exp(scores - lse_ref[index, 0:1, 0:cols])
+        dv_ref[...] += dot_nn(weights.astype(jnp.bfloat16), up_stacked)
+        grad = (weights * (dot_nt(values, up_stacked) - delta)).astype(jnp.bfloat16)
+        dk_ref[...] += dot_nn(grad, stacked)
+        wide = dot_nn(kt_ref[...], grad) * (HD**-0.5)
+        at = pl.ds(first + start if last else start, count)
+        out_ref[at, 0:width] = head_unstack(wide, count).astype(jnp.bfloat16)
+
+    tiles_of(rows, tile)
+    if last:
+        out_ref[:, width : 2 * width] = dk_ref[...].astype(jnp.bfloat16)
+        out_ref[:, 2 * width : 3 * width] = dv_ref[...].astype(jnp.bfloat16)
+
+
+def attend(packed, bias, first, rows):
+    tokens, width = packed.shape[0], GROUP * HD
+    tiles = -(-rows // QT)
+    return pl.pallas_call(
+        functools.partial(attend_kernel, first),
+        out_shape=(
+            jax.ShapeDtypeStruct((rows, width), jnp.bfloat16),
+            jax.ShapeDtypeStruct((tiles, 8, GROUP * QT), jnp.float32),
+        ),
+        in_specs=[pl.BlockSpec(memory_space=pltpu.VMEM)] * 2,
+        out_specs=[pl.BlockSpec(memory_space=pltpu.VMEM)] * 2,
+        scratch_shapes=[pltpu.VMEM((width, tokens), jnp.bfloat16)],
+        compiler_params=pltpu.CompilerParams(vmem_limit_bytes=32 << 20),
+        cost_estimate=pl.CostEstimate(
+            flops=10 * rows * tokens * width * 4, bytes_accessed=6 << 20, transcendentals=0
+        ),
+        name="attend",
+    )(packed, bias)
+
+
+def attend_back(packed, bias, lse, att, upstream, first, before=None):
+    tokens, width = packed.shape[0], GROUP * HD
+    rows = att.shape[0]
+    total = jax.ShapeDtypeStruct((tokens, width), jnp.float32)
+    vmem = pl.BlockSpec(memory_space=pltpu.VMEM)
+    turned = pltpu.VMEM((width, tokens), jnp.bfloat16)
+    if before is None:
+        extra = ()
+        out_shape = (jax.ShapeDtypeStruct((rows, width), jnp.bfloat16), total, total)
+        scratch = [turned]
+        out_specs = (vmem,) * 3
+    else:
+        extra = before
+        out_shape = jax.ShapeDtypeStruct((tokens, 3 * width), jnp.bfloat16)
+        scratch = [turned] + [pltpu.VMEM((tokens, width), jnp.float32)] * 2
+        out_specs = vmem
+    return pl.pallas_call(
+        functools.partial(attend_back_kernel, first, before is not None),
+        out_shape=out_shape,
+        in_specs=[vmem] * (5 + len(extra)),
+        out_specs=out_specs,
+        scratch_shapes=scratch,
+        compiler_params=pltpu.CompilerParams(vmem_limit_bytes=48 << 20),
+        cost_estimate=pl.CostEstimate(
+            flops=20 * rows * tokens * width * 4, bytes_accessed=10 << 20, transcendentals=0
+        ),
+        name="attend_back",
+    )(packed, bias, lse, att, upstream, *extra)
+
+
+FF_CHUNK = 512
+
+
+def ffn_kernel(
+    table_ref,
+    factor_ref,
+    norm_ref,
+    middle_ref,
+    target_ref,
+    valid_ref,
+    bias_one_ref,
+    bias_two_ref,
+    fc1_own,
+    fc1_other,
+    fc2_own,
+    fc2_other,
+    two_mine,
+    two_theirs,
+    one_mine,
+    one_theirs,
+    out_ref,
+    hidden_ref,
+    pre_ref,
+    grad_out_ref,
+    grad_low_ref,
+    grad_norm_ref,
+    hidden_sum_ref,
+    sums_ref,
+    fc1_v,
+    fc2_v,
+    sem_one,
+    sem_two,
+):
+    half = fc1_own.shape[0]
+    sub = fc1_own.shape[1] // 4
+    hidden_total = hidden_ref.shape[1]
+    step = one_mine.shape[0] // 4
+
+    def fc1_place(side, at):
+        return fc1_v.at[side * half : (side + 1) * half, pl.ds(pl.multiple_of(at * sub, sub), sub)]
+
+    def fc2_place(side, i, at):
+        lane = side * half + i * sub
+        return fc2_v.at[pl.ds(pl.multiple_of(at * sub, sub), sub), lane : lane + sub]
+
+    def pieces():
+        for a in range(4):
+            at = table_ref[16 + a]
+            rows = slice(a * sub, (a + 1) * sub)
+            for side, (one, two) in enumerate(((fc1_own, fc2_own), (fc1_other, fc2_other))):
+                yield side, at, one.at[:, rows], [two.at[rows, i * sub : (i + 1) * sub] for i in range(2)]
+        for s in range(4):
+            for j in (1, 2, 3):
+                at = table_ref[4 * s + j]
+                for side in range(2):
+                    ref = (one_mine, one_theirs)[side] if j == 3 else (two_mine, two_theirs)[side]
+                    base = s * step if j == 3 else (2 * s + j - 1) * step
+                    low = base + half
+                    yield (
+                        side,
+                        at,
+                        ref.at[base : base + half, :],
+                        [ref.at[low + i * sub : low + (i + 1) * sub, :] for i in range(2)],
+                    )
+
+    listed = list(pieces())
+    for side, at, one, _ in listed:
+        pltpu.make_async_copy(one, fc1_place(side, at), sem_one.at[side, at]).start()
+    for side, at, _, two in listed:
+        for i in range(2):
+            pltpu.make_async_copy(two[i], fc2_place(side, i, at), sem_two.at[side, i, at]).start()
+    grad_norm_ref[...] = jnp.zeros_like(grad_norm_ref)
+
+    @pl.loop(0, hidden_total // FF_CHUNK)
+    def _(k):
+        for i in range(FF_CHUNK // sub):
+            for side in range(2):
+                at = k * (FF_CHUNK // sub) + i
+                pltpu.make_async_copy(
+                    fc1_own.at[:, 0:sub], fc1_place(side, at), sem_one.at[side, at]
+                ).wait()
+        span = pl.ds(pl.multiple_of(k * FF_CHUNK, FF_CHUNK), FF_CHUNK)
+        pre = dot_nn(norm_ref[...], fc1_v[:, span]) + bias_one_ref[0:1, span]
+        cdf = 0.5 * (1.0 + lax.erf(pre * ROOT_HALF))
+        hidden_ref[:, span] = (pre * cdf).astype(jnp.bfloat16)
+        slope = cdf + pre * jnp.exp(-0.5 * pre * pre) * DENSITY_FACTOR
+        pre_ref[:, span] = slope.astype(jnp.bfloat16)
+
+    @pl.loop(0, hidden_total // sub)
+    def _(at):
+        for side in range(2):
+            for i in range(2):
+                pltpu.make_async_copy(
+                    fc2_own.at[0:sub, 0:sub], fc2_place(side, i, at), sem_two.at[side, i, at]
+                ).wait()
+
+    for i in range(2):
+        cols = slice(i * half, (i + 1) * half)
+        total = dot_nn(hidden_ref[...], fc2_v[:, cols]) + (middle_ref[:, cols] + bias_two_ref[0:1, cols])
+        out_ref[:, cols] = total.astype(jnp.bfloat16)
+        differ = total - target_ref[:, cols].astype(jnp.float32)
+        weighted = valid_ref[...] * differ
+        sums_ref[0:1, cols] = jnp.sum(weighted * differ, axis=0, keepdims=True)
+        grad = factor_ref[0] * weighted
+        grad_out_ref[:, cols] = grad
+        low = grad.astype(jnp.bfloat16)
+        grad_low_ref[:, cols] = low
+        sums_ref[1:2, cols] = jnp.sum(low.astype(jnp.float32), axis=0, keepdims=True)
+
+    @pl.loop(0, hidden_total // FF_CHUNK)
+    def _(k):
+        span = pl.ds(pl.multiple_of(k * FF_CHUNK, FF_CHUNK), FF_CHUNK)
+        back = dot_nt(grad_low_ref[...], fc2_v[span, :])
+        back = (back * pre_ref[:, span].astype(jnp.float32)).astype(jnp.bfloat16)
+        pre_ref[:, span] = back
+        hidden_sum_ref[0:1, span] = jnp.sum(back.astype(jnp.float32), axis=0, keepdims=True)
+        grad_norm_ref[...] += dot_nt(back, fc1_v[:, span])
+
+
+def feed_forward(table, factor, norm, middle, target, valid, bias_one, bias_two, pieces):
+    rows, width = norm.shape
+    hidden = bias_one.shape[1]
+    vmem = pl.BlockSpec(memory_space=pltpu.VMEM)
+    smem = pl.BlockSpec(memory_space=pltpu.SMEM)
+    anywhere = pl.BlockSpec(memory_space=pl.ANY)
+    f32, bf16 = jnp.float32, jnp.bfloat16
+    return pl.pallas_call(
+        ffn_kernel,
+        out_shape=(
+            jax.ShapeDtypeStruct((rows, width), bf16),
+            jax.ShapeDtypeStruct((rows, hidden), bf16),
+            jax.ShapeDtypeStruct((rows, hidden), bf16),
+            jax.ShapeDtypeStruct((rows, width), f32),
+            jax.ShapeDtypeStruct((rows, width), bf16),
+            jax.ShapeDtypeStruct((rows, width), f32),
+            jax.ShapeDtypeStruct((1, hidden), f32),
+            jax.ShapeDtypeStruct((2, width), f32),
+        ),
+        in_specs=[smem] * 2 + [vmem] * 6 + [anywhere] * 8,
+        out_specs=[vmem] * 8,
+        scratch_shapes=[
+            pltpu.VMEM((width, hidden), bf16),
+            pltpu.VMEM((hidden, width), bf16),
+            pltpu.SemaphoreType.DMA((2, 16)),
+            pltpu.SemaphoreType.DMA((2, 2, 16)),
+        ],
+        compiler_params=pltpu.CompilerParams(vmem_limit_bytes=62 << 20),
+        cost_estimate=pl.CostEstimate(
+            flops=8 * rows * width * hidden, bytes_accessed=44 << 20, transcendentals=0
+        ),
+        name="feed_forward",
+    )(table, factor, norm, middle, target, valid, bias_one, bias_two, *pieces)
+
+
+def swap(values, axis, mask, size):
+    return lax.ppermute(values, axis, [(i, i ^ mask) for i in range(size)])
+
+
+def over_row(values):
+    return swap(values, "row", 1, 2)
+
+
+def over_dp(values, mask):
+    return swap(values, "dp", mask, 4)
+
+
+def over_col(values, mask):
+    return swap(values, "col", mask, 4)
+
+
+def cut(values, index, size, axis=0):
+    return lax.dynamic_slice_in_dim(values, index * size, size, axis)
+
+
+def place(pieces, index_of, axis):
+    size = pieces[0].shape[axis]
+    shape = list(pieces[0].shape)
+    shape[axis] = size * len(pieces)
+    whole = jnp.zeros(shape, pieces[0].dtype)
+    for s, piece in enumerate(pieces):
+        whole = lax.dynamic_update_slice_in_dim(whole, piece, index_of(s) * size, axis)
+    return whole
+
+
+def finish_kernel(part_rows, places_ref, *refs):
+    pieces, (fc2_ref, fc1_ref, proj_ref) = refs[:4], refs[4:]
+    sub = fc2_ref.shape[0] // 4
+    for s, piece in enumerate(pieces):
+        at = places_ref[s]
+        rows = pl.ds(pl.multiple_of(at * sub, sub), sub)
+        fc2_ref[rows, :] = piece[0:sub, :].astype(jnp.float32)
+        fc1_ref[:, rows] = piece[sub : 2 * sub, :].astype(jnp.float32).T
+        rows = pl.ds(pl.multiple_of(at * part_rows, part_rows), part_rows)
+        proj_ref[rows, :] = piece[2 * sub :, :].astype(jnp.float32)
+
+
+def finish_qkv_kernel(places_ref, *refs):
+    out_ref = refs[4]
+    deep, width = refs[0].shape[0], out_ref.shape[2]
+    for s in range(4):
+        rows = pl.ds(pl.multiple_of(places_ref[s] * deep, deep), deep)
+        for k in range(3):
+            out_ref[k, rows, :] = refs[s][:, k * width : (k + 1) * width].astype(jnp.float32)
+
+
+def finish(places, pieces, part_rows):
+    rows, half = pieces[0].shape
+    sub = (rows - part_rows) // 2
+    vmem = pl.BlockSpec(memory_space=pltpu.VMEM)
+    return pl.pallas_call(
+        functools.partial(finish_kernel, part_rows),
+        out_shape=(
+            jax.ShapeDtypeStruct((4 * sub, half), jnp.float32),
+            jax.ShapeDtypeStruct((half, 4 * sub), jnp.float32),
+            jax.ShapeDtypeStruct((4 * part_rows, half), jnp.float32),
+        ),
+        in_specs=[pl.BlockSpec(memory_space=pltpu.SMEM)] + [vmem] * 4,
+        out_specs=[vmem] * 3,
+        name="finish",
+    )(places, *pieces)
+
+
+def finish_qkv(places, pieces):
+    deep, width = pieces[0].shape
+    vmem = pl.BlockSpec(memory_space=pltpu.VMEM)
+    return pl.pallas_call(
+        finish_qkv_kernel,
+        out_shape=jax.ShapeDtypeStruct((3, 4 * deep, width // 3), jnp.float32),
+        in_specs=[pl.BlockSpec(memory_space=pltpu.SMEM)] + [vmem] * 4,
+        out_specs=vmem,
+        name="finish_qkv",
+    )(places, *pieces)
+
+
+def tie(value, *others):
+    return lax.optimization_barrier((value, *others))[0]
+
+
+def add_up(own, taken):
+    total = own.astype(jnp.float32)
+    for piece in taken:
+        total = total + piece.astype(jnp.float32)
+    return total
+
+
+def local_paired(
+    states,
+    ln1_gain,
+    ln1_bias,
+    w_qkv,
+    q_bias,
+    v_bias,
+    w_proj,
+    proj_bias,
+    ln2_gain,
+    ln2_bias,
+    w_fc1,
+    fc1_bias,
+    w_fc2,
+    fc2_bias,
+    teacher,
+    loss_mask,
+    lengths,
+):
+    f32, bf16 = jnp.float32, jnp.bfloat16
+    dp = lax.axis_index("dp")
+    row = lax.axis_index("row")
+    col = lax.axis_index("col")
+    local_rows, width = states.shape
+    half = width // 2
+    head_width = w_qkv.shape[2]
+    hidden_width = w_fc1.shape[1]
+    sub = hidden_width // 4
+    span = 4 * sub
+    part_rows = head_width // 4
+    clip = (dp * 2 + row) * 2 + col // 2
+    second = col % 2
+
+    def quarter(s):
+        return dp ^ s
+
+    def frame(values):
+        return jnp.where(
+            row == 0, values, jnp.concatenate([values[:, half:], values[:, :half]], axis=1)
+        )
+
+    states_other = over_col(states, 1)
+    proj_cut = cut(w_proj, dp, part_rows, 0)
+    fc2_cut = cut(w_fc2, dp, sub, 0)
+    slab = jnp.concatenate(
+        [
+            cut(w_fc1, dp, sub, 1),
+            fc2_cut[:, :sub],
+            fc2_cut[:, sub:],
+            proj_cut[:, :sub],
+            proj_cut[:, sub:],
+        ],
+        axis=0,
+    )
+    slab_rows = slab.shape[0]
+    w_qkv2 = w_qkv.reshape(half, 3 * head_width)
+    qkv_cut = cut(w_qkv2, dp, half // 4)
+    qkv_quarter = over_col(qkv_cut, 2)
+    two = jnp.concatenate([over_col(slab, 1), over_col(slab, 2)], axis=0)
+    two_x, two_y = over_dp(two, 1), over_dp(two, 2)
+    states_other = tie(states_other, two)
+
+    vectors = jnp.stack([ln1_gain, ln1_bias, proj_bias, ln2_gain, ln2_bias, fc2_bias])
+    vectors, fc1_bias, states, teacher, loss_mask = lax.optimization_barrier(
+        (vectors, fc1_bias, states, teacher, loss_mask, slab, qkv_cut)
+    )[:5]
+    vector_full = jnp.concatenate([vectors, over_row(vectors)], axis=1).astype(f32)
+    gain_one, shift_one, bias_proj, gain_two, shift_two, bias_two = (vector_full[i] for i in range(6))
+
+    qkv_near = jnp.concatenate([w_qkv2, over_row(w_qkv2)], axis=0)
+    qkv_pieces = [qkv_quarter] + [over_dp(qkv_quarter, s) for s in (1, 2, 3)]
+    qkv_far = place(qkv_pieces, quarter, 0)
+    qkv_far = jnp.concatenate([qkv_far, over_row(qkv_far)], axis=0)
+    small = jnp.concatenate([fc1_bias, q_bias, v_bias])
+    smalls = [small] + [over_col(small, j) for j in (1, 2, 3)]
+    fc1_other = over_row(w_fc1)
+    fc2_other = over_row(w_fc2)
+    proj_other = over_row(w_proj)
+
+    one = over_col(tie(slab, states_other), 3)
+
+    all_clips = lengths.shape[0]
+    valid_all = (
+        loss_mask.reshape(all_clips, L) * (jnp.arange(L)[None, :] < lengths[:, None])
+    ).astype(f32)
+    valid_total = jnp.maximum(jnp.sum(valid_all), 1.0)
+    first_row = ((dp * 2 + row) * 4 + col) * local_rows
+    valid = lax.dynamic_slice_in_dim(valid_all.reshape(all_clips * L), first_row, local_rows)
+    my_length = lax.dynamic_slice_in_dim(lengths, clip, 1)
+    spot = jnp.arange(L)
+    position = jnp.where(
+        spot < local_rows, second * local_rows + spot, (1 - second) * local_rows + spot - local_rows
+    )
+    key_bias = jnp.where(position < my_length, 0.0, MASKED).astype(f32)
+    key_bias = jnp.broadcast_to(key_bias[:, None], (L, 128))
+
+    inputs = frame(states).astype(f32)
+    norm_one, unit_one, spread_one = normalize(inputs, gain_one, shift_one)
+    norm_other, unit_other, _ = normalize(frame(states_other).astype(f32), gain_one, shift_one)
+    tokens_one = jnp.concatenate([norm_one.astype(bf16), norm_other.astype(bf16)], axis=0)
+
+    zero_bias = jnp.zeros((head_width,), f32)
+    score_scale = HD**-0.5
+    scale = jnp.where(jnp.arange(3 * head_width) < head_width, score_scale, 1.0).astype(bf16)
+    split = local_rows // QT * QT
+    later = L - split
+    over = local_rows - split
+
+    def project(matrix, extra):
+        q_add = extra[span : span + head_width].astype(f32)
+        v_add = extra[span + head_width :].astype(f32)
+        projected = jnp.dot(tokens_one, matrix, preferred_element_type=f32)
+        packed = (projected + jnp.concatenate([q_add, zero_bias, v_add])[None]).astype(bf16)
+        return packed * scale[None]
+
+    packed_near = project(qkv_near, small)
+    near_late, near_late_lse = attend(packed_near, key_bias, split, later)
+    near_other = over_col(near_late[over:], 1)
+    two_x, two_y = tie(two_x, near_late), tie(two_y, near_late)
+    middle_row = two.shape[0] // 2
+    two_low, two_high = over_dp(two_y[:middle_row], 1), over_dp(two_x[middle_row:], 2)
+    near_soon, near_soon_lse = attend(tie(packed_near, two_x, two_y), key_bias, 0, split)
+    one = tie(one, near_soon)
+    one_x, one_y = over_dp(one, 1), over_dp(one, 2)
+    packed_far = tie(project(qkv_far, smalls[2]), one, near_other)
+    far_late, far_late_lse = attend(packed_far, key_bias, split, later)
+    far_other = over_col(far_late[over:], 1)
+    two_low, two_high = tie(two_low, far_late), tie(two_high, far_late)
+    two_all = jnp.concatenate([two, two_x, two_y, two_low, two_high], axis=0)
+    two_theirs = over_row(two_all)
+    one_x, one_y = tie(one_x, far_late), tie(one_y, far_late)
+    middle_row = one.shape[0] // 2
+    one_low, one_high = over_dp(one_y[:middle_row], 1), over_dp(one_x[middle_row:], 2)
+    far_soon, far_soon_lse = attend(tie(packed_far, two_all, one_x, one_y), key_bias, 0, split)
+    one_low, one_high = tie(one_low, far_soon), tie(one_high, far_soon)
+    one_all = jnp.concatenate([one, one_x, one_y, one_low, one_high], axis=0)
+    one_theirs = over_row(one_all)
+
+    def proj_rows(block, index, count):
+        rows = []
+        for s in range(4):
+            at = (s * count + index) * slab_rows + half + 2 * sub
+            rows.append(
+                jnp.concatenate(
+                    [block[at : at + part_rows], block[at + part_rows : at + 2 * part_rows]], axis=1
+                )
+            )
+        return place(rows, quarter, 0)
+
+    proj_whole = jnp.concatenate(
+        [
+            jnp.concatenate(
+                [w, proj_rows(b, 0, 2), proj_rows(b, 1, 2), proj_rows(c, 0, 1)], axis=0
+            )
+            for w, b, c in ((w_proj, two_all, one_all), (proj_other, two_theirs, one_theirs))
+        ],
+        axis=1,
+    )
+    attended_rows = jnp.concatenate(
+        [
+            jnp.concatenate([near_soon, near_late[:over]], axis=0),
+            near_other,
+            jnp.concatenate([far_soon, far_late[:over]], axis=0),
+            far_other,
+        ],
+        axis=1,
+    )
+    middle = inputs + (jnp.dot(attended_rows, proj_whole, preferred_element_type=f32) + bias_proj)
+    norm_two, unit_two, spread_two = normalize(middle, gain_two, shift_two)
+    norm_two = norm_two.astype(bf16)
+
+    table = jnp.stack(
+        [(dp ^ s) * 4 + (col ^ j) for s in range(4) for j in range(4)]
+        + [a * 4 + col for a in range(4)]
+    ).astype(jnp.int32)
+    bias_blocks = jnp.stack([b[:span].reshape(4, sub) for b in smalls], axis=1)
+    bias_blocks = jnp.concatenate(
+        [lax.dynamic_index_in_dim(bias_blocks, col ^ b, 1) for b in range(4)], axis=1
+    )
+    loss_scale = all_clips * L * width / 2.0
+    factor = (loss_scale * 2.0 / (valid_total * width)).reshape(1)
+    outputs, hidden, grad_pre, grad_out, grad_low, grad_norm_two, fc1_bias_sum, sums = feed_forward(
+        table,
+        factor,
+        norm_two,
+        middle,
+        frame(teacher),
+        valid[:, None],
+        bias_blocks.reshape(1, 4 * span).astype(f32),
+        bias_two[None],
+        (w_fc1, fc1_other, w_fc2, fc2_other, two_all, two_theirs, one_all, one_theirs),
+    )
+    numerator = jnp.sum(sums[0])
+    back_two, gain_two_grad, shift_two_grad = norm_back(grad_norm_two, unit_two, spread_two, gain_two)
+    grad_mid = grad_out + back_two
+    mid_low = grad_mid.astype(bf16)
+    grad_att_rows = jnp.dot(mid_low, proj_whole.T, preferred_element_type=f32).astype(bf16)
+    ups = [
+        grad_att_rows[:, 0:head_width],
+        over_col(grad_att_rows[:, head_width : 2 * head_width], 1),
+        grad_att_rows[:, 2 * head_width : 3 * head_width],
+        over_col(grad_att_rows[:, 3 * head_width :], 1),
+    ]
+
+    def joined(kept, taken):
+        return (kept + taken.astype(f32)).astype(bf16)
+
+    give_fc2 = over_row(dot_tn(hidden, grad_low[:, half:]).astype(bf16))
+    give_fc1 = over_row(dot_tn(grad_pre, norm_two[:, half:]).astype(bf16))
+    give_proj = over_row(dot_tn(attended_rows, mid_low[:, half:]).astype(bf16))
+    wide_fc2 = joined(dot_tn(hidden, grad_low[:, :half]), give_fc2)
+    wide_fc1 = joined(dot_tn(grad_pre, norm_two[:, :half]), give_fc1)
+    wide_proj = joined(dot_tn(attended_rows, mid_low[:, :half]), give_proj)
+
+    def fc2_part(s, side):
+        return cut(wide_fc2[:, side * sub : (side + 1) * sub], quarter(s), span, 0)
+
+    def fc1_part(s, side):
+        lanes = slice(side * sub, (side + 1) * sub)
+        proj = [
+            cut(wide_proj[j * head_width : (j + 1) * head_width, lanes], quarter(s), part_rows, 0)
+            for j in range(4)
+        ]
+        return jnp.concatenate([cut(wide_fc1[:, lanes], quarter(s), span, 0), *proj], axis=0)
+
+    STAY, GO = ((0, 2), (0, 1)), ((1, 3), (2, 3))
+
+    def plane_first(part):
+        give = [jnp.concatenate([part(s, side) for s in GO[side]], axis=0) for side in range(2)]
+        return [over_dp(give[0], 1), over_dp(give[1], 2)], give
+
+    def plane_second(part, taken):
+        rows = taken[0].shape[0] // 2
+        keep, give = [], []
+        for side in range(2):
+            first, second = STAY[side]
+            keep.append(joined(part(first, side).astype(f32), taken[side][:rows]))
+            give.append(joined(part(second, side).astype(f32), taken[side][rows:]))
+        return keep, [over_dp(give[0], 2), over_dp(give[1], 1)], give
+
+    fc2_taken, fc2_give = plane_first(fc2_part)
+    fc1_taken, fc1_give = plane_first(fc1_part)
+
+    def row_half(stacked):
+        return stacked[:, :half].reshape(-1), stacked[:, half:].reshape(-1)
+
+    keep, give = row_half(
+        jnp.stack([gain_two_grad, shift_two_grad, jnp.sum(mid_low, axis=0, dtype=f32), sums[1]])
+    )
+    rest = jnp.concatenate([fc1_bias_sum[0], jnp.full((128,), numerator)])
+    early = jnp.concatenate([keep, rest]) + over_row(jnp.concatenate([give, rest]))
+
+    def cols_out(block_of):
+        return [over_col(block_of(j), j) for j in (1, 2, 3)]
+
+    packed_near = tie(packed_near, *fc2_give, *fc1_give)
+    part_near = attend_back(packed_near, key_bias, near_soon_lse, near_soon, ups[0][:split], 0)
+    fc2_taken = [tie(t, part_near[0]) for t in fc2_taken]
+    fc2_keep, fc2_taken, fc2_give = plane_second(fc2_part, fc2_taken)
+    early = early + over_dp(tie(early, part_near[0]), 1)
+
+    packed_far = tie(packed_far, *fc2_give, early)
+    part_far = attend_back(packed_far, key_bias, far_soon_lse, far_soon, ups[2][:split], 0)
+    fc2_taken = [tie(t, part_far[0]) for t in fc2_taken]
+    fc2_sum = jnp.concatenate(
+        [joined(k.astype(f32), t) for k, t in zip(fc2_keep, fc2_taken, strict=True)], axis=1
+    )
+    fc2_cols = cols_out(lambda j: cut(fc2_sum, col ^ j, sub, 0))
+    fc1_taken = [tie(t, part_far[0]) for t in fc1_taken]
+    fc1_keep, fc1_taken, fc1_give = plane_second(fc1_part, fc1_taken)
+    early = early + over_dp(tie(early, part_far[0]), 2)
+
+    packed_near = tie(packed_near, fc2_sum, early, *fc1_give)
+    up = jnp.concatenate([ups[0][split:], ups[1]], axis=0)
+    grad_near = attend_back(packed_near, key_bias, near_late_lse, near_late, up, split, part_near)
+    fc1_taken = [tie(t, grad_near) for t in fc1_taken]
+    fc1_sum = jnp.concatenate(
+        [joined(k.astype(f32), t) for k, t in zip(fc1_keep, fc1_taken, strict=True)], axis=1
+    )
+
+    def fc1_block(j):
+        proj = fc1_sum[span + j * part_rows : span + (j + 1) * part_rows]
+        return jnp.concatenate([cut(fc1_sum[:span], col ^ j, sub, 0), proj], axis=0)
+
+    fc1_cols = cols_out(fc1_block)
+    early = early + over_col(tie(early, grad_near), 1)
+
+    def qkv_halves(grad):
+        taken = over_row(dot_tn(tokens_one[:, half:], grad).astype(bf16))
+        return joined(dot_tn(tokens_one[:, :half], grad), taken)
+
+    deep = half // 4
+
+    def plane_out(wide):
+        return cut(wide, dp, deep), [over_dp(cut(wide, quarter(s), deep), s) for s in (1, 2, 3)]
+
+    wide_near = qkv_halves(grad_near)
+    near_keep, near_taken = plane_out(wide_near)
+    norm_near = dot_nt(grad_near, qkv_near)
+
+    packed_far = tie(packed_far, fc1_sum, wide_near, norm_near, early)
+    up = jnp.concatenate([ups[2][split:], ups[3]], axis=0)
+    grad_far = attend_back(packed_far, key_bias, far_late_lse, far_late, up, split, part_far)
+
+    grad_norm_one = norm_near + dot_nt(grad_far, qkv_far)
+    norm_give = grad_norm_one[local_rows:].astype(bf16)
+    norm_taken = over_col(norm_give, 1)
+    grad_far = tie(grad_far, norm_give)
+    taken_far = over_row(dot_tn(tokens_one[:, half:], grad_far).astype(bf16))
+    fc2_cols = [tie(t, grad_far) for t in fc2_cols]
+    fc1_cols = [tie(t, grad_far) for t in fc1_cols]
+    mine = jnp.concatenate(
+        [add_up(cut(fc2_sum, col, sub, 0), fc2_cols), add_up(fc1_block(0), fc1_cols)], axis=0
+    ).astype(bf16)
+    mine_back = [over_dp(mine, s) for s in (1, 2, 3)]
+    near_sum = add_up(near_keep, [tie(t, grad_far) for t in near_taken]).astype(bf16)
+    early = early + over_col(tie(early, grad_far), 2)
+    both = jnp.stack(
+        [
+            jnp.sum(grad_norm_one[:local_rows] * unit_one, axis=0)
+            + jnp.sum(grad_norm_one[local_rows:] * unit_other, axis=0),
+            jnp.sum(grad_norm_one, axis=0),
+        ]
+    )
+    keep, give = row_half(both)
+    heads = [
+        jnp.sum(g[:, i : i + head_width], axis=0, dtype=f32)
+        for g in (grad_near, grad_far)
+        for i in (0, 2 * head_width)
+    ]
+    late_keep, late_give = jnp.concatenate([keep, *heads]), jnp.concatenate([give, *heads])
+    late_taken = over_row(tie(late_give, mine))
+
+    wide_far = joined(dot_tn(tokens_one[:, :half], grad_far), tie(taken_far, mine, late_give))
+    far_keep, far_taken = plane_out(wide_far)
+    late = late_keep + tie(late_taken, wide_far)
+    late_parts = [over_dp(late, s) for s in (1, 2, 3)]
+    far_taken = [tie(t, late) for t in far_taken]
+    far_sum = add_up(far_keep, far_taken).astype(bf16)
+    far_other = over_col(far_sum, 2)
+    late_parts = [tie(t, far_sum) for t in late_parts]
+    late = add_up(late, late_parts)
+    flat, _, theirs = jnp.split(late, [2 * half, 2 * half + 2 * head_width])
+    moved = [over_col(flat, 1), over_col(jnp.concatenate([flat, theirs]), 2), over_col(flat, 3)]
+    qkv_sum = add_up(near_sum, [tie(far_other, flat, theirs)]).astype(bf16)
+    qkv_back = [over_dp(qkv_sum, s) for s in (1, 2, 3)]
+
+    norm_taken, *mine_back = lax.optimization_barrier((norm_taken, *mine_back, qkv_sum))[:4]
+    places = jnp.stack([dp, dp ^ 1, dp ^ 2, dp ^ 3]).astype(jnp.int32)
+    fc2_grad, fc1_grad, proj_grad = finish(places, [mine, *mine_back], part_rows)
+    grad_norm_one = grad_norm_one[:local_rows] + norm_taken.astype(f32)
+    back_one, _, _ = norm_back(grad_norm_one, unit_one, spread_one, gain_one)
+    grad_states = frame((grad_mid + back_one).astype(bf16))
+    moved = [tie(t, grad_states) for t in moved]
+    heads = late[2 * half : 2 * half + 2 * head_width] + moved[1][2 * half :]
+    late = (flat + moved[0] + moved[1][: 2 * half] + moved[2]).reshape(2, half)
+    qkv_back = [tie(t, grad_states) for t in qkv_back]
+    qkv_grad = finish_qkv(places, [qkv_sum, *qkv_back]).transpose(1, 0, 2)
+    flat = early[: 4 * half].reshape(4, half)
+    fc1_bias_grad = lax.dynamic_index_in_dim(
+        early[4 * half : 4 * half + 4 * span].reshape(4, 4, sub), col, 1, False
+    ).reshape(span)
+    loss_value = early[4 * half + 4 * span] / (valid_total * width)
+    return (
+        frame(outputs),
+        loss_value,
+        grad_states,
+        late[0],
+        late[1],
+        qkv_grad,
+        heads[:head_width],
+        heads[head_width:],
+        proj_grad,
+        flat[2],
+        flat[0],
+        flat[1],
+        fc1_grad,
+        fc1_bias_grad,
+        fc2_grad,
+        flat[3],
+    )
+
+
 def solution(mesh):
+    sizes = (mesh.shape["dp"], mesh.shape["row"], mesh.shape["col"])
+    body = local_paired if sizes == PAIRED_MESH else local_general
     in_specs = (
         P(("dp", "row", "col"), None),
         P("row"),
@@ -360,4 +1152,4 @@
         P("col", "row"),
         P("row"),
     )
-    return jax.shard_map(local, mesh=mesh, in_specs=in_specs, out_specs=out_specs, check_vma=False)
+    return jax.shard_map(body, mesh=mesh, in_specs=in_specs, out_specs=out_specs, check_vma=False)

time: 1380 us -> 597 us (0.43)
  waiting for transfers between devices: 577 us -> 151 us
  matrix products: 359 us -> 73.9 us
  Pallas kernels: 0 us -> 180 us
  blocking collectives: 121 us -> 0 us
  local copies, waits for them, and re-layouts: 159 us -> 41.9 us
  starting transfers between devices: 13.4 us -> 84.2 us
  other arithmetic: 112 us -> 50 us
  loops' own time: 17.3 us -> 0 us
    all_to_all x3 -> x0, waiting for transfers between devices: 297 us -> none  [the longest x1 235 us: local(): lax.all_to_all(grads_packed.reshape(group_rows, 3, head_width), 'col', sp...]
    dot_general x40 -> x16, matrix products: 359 us -> 73.9 us  [the longest x10 39 us: dot_tn(): lax.dot_general(a, b, (((0,), (0,)), ((), ())), preferred_element_type=jn...]
    all_gather x8 -> x0, waiting for transfers between devices: 271 us -> none  [the longest x1 121 us: local(): lax.all_gather(fc2_full, 'col', axis=0, tiled=True)]
    pallas_call x0 -> x11, Pallas kernels: none -> 180 us  [the longest x4 77.7 us: attend_back(): pl.pallas_call(functools.partial(attend_back_kernel, first, before is not...]
    ppermute x0 -> x76, waiting for transfers between devices: none -> 151 us  [swap(): return lax.ppermute(values, axis, [(i, i ^ mask) for i in range(size)])]
    ppermute x0 -> x76, starting transfers between devices: none -> 84.2 us  [swap(): return lax.ppermute(values, axis, [(i, i ^ mask) for i in range(size)])]
    all_gather x3 -> x0, blocking collectives: 82.3 us -> none  [the longest x1 78 us: local(): lax.all_gather(fc1_bias, 'col', axis=0, tiled=True)]
    convert_element_type x6 -> x2, local copies, waits for them, and re-layouts: 66.1 us -> 0.64 us  [local_paired(): bias_blocks.reshape(1, 4 * span).astype(f32)]
  transfers between devices with their start and end apart: 19 -> 76, of which waited for: 8 -> 23; matrix products, arithmetic and copies ran while one was open for 41% -> 23% of each run, Pallas kernels for 0% -> 21%
where the time goes in v2:
time: 597 us; the launch traced here: 587 us
  Pallas kernels  180 us (30%)
  waiting for transfers between devices  151 us (25%)
  starting transfers between devices  84.2 us (14%)
  matrix products  73.9 us (12%)
  other arithmetic  50 us (8%)
  local copies, waits for them, and re-layouts  41.9 us (7%)
  between operations  6.5 us (1%)
    ppermute x76, waiting for transfers between devices, swap(): return lax.ppermute(values, axis, [(i, i ^ mask) for i in range(size)])  151 us
    ppermute x76, starting transfers between devices, swap(): return lax.ppermute(values, axis, [(i, i ^ mask) for i in range(size)])  84.2 us
    pallas_call x4, Pallas kernels, attend_back(): pl.pallas_call(functools.partial(attend_back_kernel, first, before is not...  77.7 us
    pallas_call x1, Pallas kernels, feed_forward(): pl.pallas_call(ffn_kernel, out_shape=(jax.ShapeDtypeStruct((rows, width),...  48.3 us
    pallas_call x4, Pallas kernels, attend(): pl.pallas_call(functools.partial(attend_kernel, first), out_shape=(jax.Sh...  47 us
    dot_general x10, matrix products, dot_tn(): lax.dot_general(a, b, (((0,), (0,)), ((), ())), preferred_element_type=jn...  39 us
    unnamed x273, local copies, waits for them, and re-layouts  23.3 us
    dot_general x2, matrix products, dot_nt(): lax.dot_general(a, b, (((1,), (1,)), ((), ())), preferred_element_type=jn...  14.6 us
  transfers between devices with their start and end apart: 76, of which 23 were waited for; matrix products, arithmetic and copies ran while one was open for 23% of the time, Pallas kernels for 21%

profile of v2, /device:TPU:0, one launch (start us, length us, event | category | flops | bytes accessed | tf_op | source)
XLA Modules:
  0.0 587.3 jit_solution(12891367880030550082)
XLA Ops:
  41.8 35.8 %collective-permute-done.8 = bf16[128,768]{0,1:T(8,128)(2,1)} collective-permute-done((bf16[128,768]{0,1:T(8,128)(2,1)S(1)}, bf16[128,768]{0,1:T(8,128)(2,1)}, u32[]{:S(2)}, u32[]{:S(2)}) %collective-permute-start.8) | collective-permute-done | bytes 196640 | tf_op jit(solution)/shard_map/ppermute | solution.py:642
  104.2 12.4 %attend.4 = (bf16[800,256]{1,0:T(8,128)(2,1)S(1)}, f32[7,8,512]{2,1,0:T(8,128)S(1)}) custom-call(bf16[1568,768]{1,0:T(8,128)(2,1)S(1)} %fusion.23.packed_ref, f32[1568,128]{1,0:T(8,128)S(1)} %broadcast_in_dim.31.bias_ref), custom_call_target="tpu_custom_call" | custom-call | flops 12845056000 | bytes 6291456 | tf_op jit(solution)/shard_map/attend/pallas_call | solution.py:440
  124.5 10.9 %attend.5 = (bf16[768,256]{1,0:T(8,128)(2,1)S(1)}, f32[6,8,512]{2,1,0:T(8,128)S(1)}) custom-call(bf16[1568,768]{1,0:T(8,128)(2,1)S(1)} %fusion.23.packed_ref, f32[1568,128]{1,0:T(8,128)S(1)} %broadcast_in_dim.31.bias_ref), custom_call_target="tpu_custom_call" | custom-call | flops 12331253760 | bytes 6291456 | tf_op jit(solution)/shard_map/attend/pallas_call | solution.py:440
  142.5 12.2 %attend.6 = (bf16[800,256]{1,0:T(8,128)(2,1)S(1)}, f32[7,8,512]{2,1,0:T(8,128)S(1)}) custom-call(bf16[1568,768]{1,0:T(8,128)(2,1)S(1)} %fusion.24.packed_ref, f32[1568,128]{1,0:T(8,128)S(1)} %broadcast_in_dim.31.bias_ref), custom_call_target="tpu_custom_call" | custom-call | flops 12845056000 | bytes 6291456 | tf_op jit(solution)/shard_map/attend/pallas_call | solution.py:440
  155.6 6.9 %collective-permute-done.17 = bf16[1152,256]{1,0:T(8,128)(2,1)S(1)} collective-permute-done((bf16[1152,256]{1,0:T(8,128)(2,1)S(1)}, bf16[1152,256]{1,0:T(8,128)(2,1)S(1)}, u32[]{:S(2)}, u32[]{:S(2)}) %collective-permute-start.17) | collective-permute-done | bytes 589856 | tf_op jit(solution)/shard_map/ppermute | solution.py:642
  166.1 11.3 %attend.7 = (bf16[768,256]{1,0:T(8,128)(2,1)S(1)}, f32[6,8,512]{2,1,0:T(8,128)S(1)}) custom-call(bf16[1568,768]{1,0:T(8,128)(2,1)S(1)} %fusion.24.packed_ref, f32[1568,128]{1,0:T(8,128)S(1)} %broadcast_in_dim.31.bias_ref), custom_call_target="tpu_custom_call" | custom-call | flops 12331253760 | bytes 6291456 | tf_op jit(solution)/shard_map/attend/pallas_call | solution.py:440
  178.7 5.0 collective-permute-done.24.one_theirs
  187.7 9.1 %collective-permute-done.19 = bf16[784,256]{1,0:T(8,128)(2,1)S(1)} collective-permute-done((bf16[784,256]{1,0:T(8,128)(2,1)S(1)}, bf16[784,256]{1,0:T(8,128)(2,1)S(1)}, u32[]{:S(2)}, u32[]{:S(2)}) %collective-permute-start.19) | collective-permute-done | bytes 401440 | tf_op jit(solution)/shard_map/ppermute | solution.py:642
  203.2 48.3 %feed_forward.1 = (bf16[784,1024]{1,0:T(8,128)(2,1)}, bf16[784,4096]{1,0:T(8,128)(2,1)}, bf16[784,4096]{1,0:T(8,128)(2,1)}, f32[784,1024]{1,0:T(8,128)}, bf16[78...) custom-call(s32[20]{0:T(128)} %stack.141.table_ref, f32[1]{0:T(128)} %bitcast.21.factor_ref, ...), custom_call_target="tpu_custom_call" | custom-call | flops 26306674688 | bytes 46137344 | tf_op jit(solution)/shard_map/feed_forward/pallas_call | solution.py:613
  255.8 8.0 %convolution_convert_fusion = bf16[4096,512]{1,0:T(8,128)(2,1)S(1)} fusion(bf16[784,4096]{1,0:T(8,128)(2,1)} %get-tuple-element.136, bf16[784,1024]{1,0:T(8,128)(2,1)S(1)} %copy-done.27), kind=kOutput, calls=%fused_computation.2 | convolution fusion | flops 3290431488 | bytes 11419648 | tf_op jit(solution)/shard_map/dot_general | solution.py:343
  266.6 12.9 %convolution_convert_fusion.2 = bf16[784,1024]{1,0:T(8,128)(2,1)S(1)} fusion(bf16[784,1024]{1,0:T(8,128)(2,1)S(1)} %get-tuple-element.209, bf16[256,512]{1,0:T(8,128)(2,1)S(1)} %copy-done.53, bf16[256,512]{1,0:T(8,128)(2,1)S(1)} %copy-done.45, bf16[256,512]{1,0:T(8,128)(2,1)S(1)} %copy-done.55, bf16[256,512]{1,0:T(8,128)(2,1)S(1)} %copy-done.108, ...), kind=kOutput, calls=%fused_computation.65 | convolution fusion | flops 1661747200 | bytes 5308416 | tf_op jit(solution)/shard_map/dot_general | solution.py:928
  285.9 4.9 convolution_convert_fusion.1
  294.3 7.9 %add_convert_fusion = bf16[4096,512]{1,0:T(8,128)(2,1)S(1)} fusion(bf16[4096,512]{1,0:T(8,128)(2,1)S(1)} %collective-permute-done.31, bf16[784,4096]{1,0:T(8,128)(2,1)} %get-tuple-element.136, bf16[784,1024]{1,0:T(8,128)(2,1)S(1)} %copy-done.27), kind=kOutput, calls=%fused_computation | convolution fusion | flops 3294625792 | bytes 15613952 | tf_op jit(solution)/shard_map/dot_general | solution.py:343
  304.3 8.9 %add_convert_fusion.1 = bf16[4096,512]{1,0:T(8,128)(2,1)S(1)} fusion(bf16[4096,512]{1,0:T(8,128)(2,1)} %collective-permute-done.30, bf16[784,4096]{1,0:T(8,128)(2,1)} %get-tuple-element.134, bf16[784,1024]{1,0:T(8,128)(2,1)S(1)} %copy-done.110), kind=kOutput, calls=%fused_computation.1 | convolution fusion | flops 3294625792 | bytes 15613952 | tf_op jit(solution)/shard_map/dot_general | solution.py:343
  319.5 17.8 %attend_back.4 = (bf16[768,256]{1,0:T(8,128)(2,1)S(1)}, f32[1568,256]{1,0:T(8,128)S(1)}, f32[1568,256]{1,0:T(8,128)S(1)}) custom-call(bf16[1568,768]{1,0:T(8,128)(2,1)} %copy-done.5, f32[1568,128]{1,0:T(8,128)S(1)} %broadcast_in_dim.31.bias_ref, f32[6,8,512]{2,1,0:T(8,128)S(1)} %get-tuple-element.138.lse_ref, ...), custom_call_target="tpu_custom_call" | custom-call | flops 24662507520 | bytes 10485760 | tf_op jit(solution)/shard_map/attend_back/pallas_call | solution.py:473
  346.1 17.8 %attend_back.5 = (bf16[768,256]{1,0:T(8,128)(2,1)S(1)}, f32[1568,256]{1,0:T(8,128)S(1)}, f32[1568,256]{1,0:T(8,128)S(1)}) custom-call(bf16[1568,768]{1,0:T(8,128)(2,1)} %copy-done.4, f32[1568,128]{1,0:T(8,128)S(1)} %broadcast_in_dim.31.bias_ref, f32[6,8,512]{2,1,0:T(8,128)S(1)} %get-tuple-element.144.lse_ref, ...), custom_call_target="tpu_custom_call" | custom-call | flops 24662507520 | bytes 10485760 | tf_op jit(solution)/shard_map/attend_back/pallas_call | solution.py:473
  379.0 20.9 %attend_back.6 = bf16[1568,768]{1,0:T(8,128)(2,1)} custom-call(bf16[1568,768]{1,0:T(8,128)(2,1)} %copy-done.5, f32[1568,128]{1,0:T(8,128)S(1)} %broadcast_in_dim.31.bias_ref, f32[7,8,512]{2,1,0:T(8,128)S(1)} %get-tuple-element.152.lse_ref, bf16[800,256]{1,0:T(8,128)(2,1)S(1)} %copy-done.3, bf16[800,256]{1,0:T(8,128)(2,1)S(1)} %pad_maximum_fusion.15.up_ref, ...), custom_call_target="tpu_custom_call" | custom-call | flops 25690112000 | bytes 10485760 | tf_op jit(solution)/shard_map/attend_back/pallas_call | solution.py:473
  404.6 7.5 %fusion.28 = f32[1568,1024]{1,0:T(8,128)} fusion(bf16[1568,768]{1,0:T(8,128)(2,1)} %attend_back.6, bf16[512,768]{0,1:T(8,128)(2,1)} %copy-done.102, bf16[512,768]{0,1:T(8,128)(2,1)} %bitcast.67), kind=kOutput, calls=%fused_computation.109 | convolution fusion | flops 2469396480 | bytes 10403840 | tf_op jit(solution)/shard_map/dot_general | solution.py:339
  420.2 6.5 %collective-permute-done.43 = bf16[1280,256]{1,0:T(8,128)(2,1)S(1)} collective-permute-done((bf16[1280,256]{1,0:T(8,128)(2,1)S(1)}, bf16[1280,256]{1,0:T(8,128)(2,1)S(1)}, u32[]{:S(2)}, u32[]{:S(2)}) %collective-permute-start.43) | collective-permute-done | bytes 655392 | tf_op jit(solution)/shard_map/ppermute | solution.py:642
  432.3 21.2 %attend_back.7 = bf16[1568,768]{1,0:T(8,128)(2,1)} custom-call(bf16[1568,768]{1,0:T(8,128)(2,1)} %copy-done.4, f32[1568,128]{1,0:T(8,128)S(1)} %broadcast_in_dim.31.bias_ref, f32[7,8,512]{2,1,0:T(8,128)S(1)} %get-tuple-element.159.lse_ref, bf16[800,256]{1,0:T(8,128)(2,1)S(1)} %copy-done.1, bf16[800,256]{1,0:T(8,128)(2,1)S(1)} %pad_maximum_fusion.16.up_ref, ...), custom_call_target="tpu_custom_call" | custom-call | flops 25690112000 | bytes 10485760 | tf_op jit(solution)/shard_map/attend_back/pallas_call | solution.py:473
  453.6 7.1 %fusion.92 = (f32[1024]{0:T(1024)S(1)}, f32[1568,1024]{1,0:T(8,128)S(1)}) fusion(f32[1568,1024]{1,0:T(8,128)} %fusion.28, bf16[1568,768]{1,0:T(8,128)(2,1)} %attend_back.7, bf16[512,768]{0,1:T(8,128)(2,1)S(1)} %copy-done.101, bf16[512,768]{0,1:T(8,128)(2,1)S(1)} %copy-done.38), kind=kOutput, calls=%fused_computation.342 | convolution fusion | flops 2472606720 | bytes 16830464 | tf_op jit(solution)/shard_map/dot_general | solution.py:339
  473.0 29.4 %collective-permute-done.47 = f32[6272]{0:T(1024)S(1)} collective-permute-done((f32[6272]{0:T(1024)S(1)}, f32[6272]{0:T(1024)S(1)}, u32[]{:S(2)}, u32[]{:S(2)}) %collective-permute-start.47) | collective-permute-done | bytes 25120 | tf_op jit(solution)/shard_map/ppermute | solution.py:642
  529.9 19.2 %collective-permute-done.69 = f32[2048]{0:T(1024)S(1)} collective-permute-done((f32[2048]{0:T(1024)S(1)}, f32[2048]{0:T(1024)S(1)}, u32[]{:S(2)}, u32[]{:S(2)}) %collective-permute-start.69) | collective-permute-done | bytes 8224 | tf_op jit(solution)/shard_map/ppermute | solution.py:642
  551.4 6.4 %collective-permute-done.66 = bf16[128,768]{1,0:T(8,128)(2,1)S(1)} collective-permute-done((bf16[128,768]{1,0:T(8,128)(2,1)S(1)}, bf16[128,768]{1,0:T(8,128)(2,1)S(1)}, u32[]{:S(2)}, u32[]{:S(2)}) %collective-permute-start.66) | collective-permute-done | bytes 196640 | tf_op jit(solution)/shard_map/ppermute | solution.py:642
  (619 shorter events, 232.3 us)
Async XLA Ops:
  8.5 81.9 %collective-permute-start.2 = (bf16[1152,256]{1,0:T(8,128)(2,1)}, bf16[1152,256]{1,0:T(8,128)(2,1)}, u32[]{:S(2)}, u32[]{:S(2)}) collective-permute-start(bf16[1152,256]{1,0:T(8,128)(2,1)} %constant_dynamic-update-slice_fusion), channel_id=1, source_target_pairs={{0,1},{1,0},{2,3},{3,2},{4,5},{5,4},{6,7},{7,6},{8,9},{9,8},{10,11... | collective-permute-start | bytes 1769480 | tf_op jit(solution)/shard_map/ppermute | solution.py:642
  11.5 80.6 %collective-permute-start.3 = (bf16[1152,256]{1,0:T(8,128)(2,1)}, bf16[1152,256]{1,0:T(8,128)(2,1)}, u32[]{:S(2)}, u32[]{:S(2)}) collective-permute-start(bf16[1152,256]{1,0:T(8,128)(2,1)} %constant_dynamic-update-slice_fusion), channel_id=1, source_target_pairs={{0,2},{1,3},{2,0},{3,1},{4,6},{5,7},{6,4},{7,5},{8,10},{9,11},{10,... | collective-permute-start | bytes 1769480 | tf_op jit(solution)/shard_map/ppermute | solution.py:642
  37.7 58.8 %collective-permute-start.1 = (bf16[784,1024]{1,0:T(8,128)(2,1)}, bf16[784,1024]{1,0:T(8,128)(2,1)S(1)}, u32[]{:S(2)}, u32[]{:S(2)}) collective-permute-start(bf16[784,1024]{1,0:T(8,128)(2,1)} %param.17), channel_id=1, source_target_pairs={{0,1},{1,0},{2,3},{3,2},{4,5},{5,4},{6,7},{7,6},{8,9},{9,8},{10,11... | collective-permute-start | bytes 4816904 | tf_op jit(solution)/shard_map/ppermute | solution.py:642
  40.6 37.1 %collective-permute-start.8 = (bf16[128,768]{0,1:T(8,128)(2,1)S(1)}, bf16[128,768]{0,1:T(8,128)(2,1)}, u32[]{:S(2)}, u32[]{:S(2)}) collective-permute-start(bf16[128,768]{0,1:T(8,128)(2,1)S(1)} %constant_dynamic-slice_fusion.19), channel_id=1, source_target_pairs={{0,2},{1,3},{2,0},{3,1},{4,6},{5,7},{6,4},{7,5},{8,10},{9,11},{10,... | collective-permute-start | bytes 589832 | tf_op jit(solution)/shard_map/ppermute | solution.py:642
  41.0 38.2 %collective-permute-start = (bf16[6,512]{1,0:T(8,128)(2,1)S(1)}, bf16[6,512]{1,0:T(8,128)(2,1)S(1)}, u32[]{:S(2)}, u32[]{:S(2)}) collective-permute-start(bf16[6,512]{1,0:T(8,128)(2,1)S(1)} %stack.148), channel_id=1, source_target_pairs={{0,4},{4,0},{1,5},{5,1},{2,6},{6,2},{3,7},{7,3},{8,12},{12,8},{9,1... | collective-permute-start | bytes 18440 | tf_op jit(solution)/shard_map/ppermute | solution.py:642
  90.3 97.4 %collective-permute-start.21 = (bf16[256,512]{1,0:T(8,128)(2,1)}, bf16[256,512]{1,0:T(8,128)(2,1)S(1)}, u32[]{:S(2)}, u32[]{:S(2)}) collective-permute-start(bf16[256,512]{1,0:T(8,128)(2,1)} %param.23), channel_id=1, source_target_pairs={{0,4},{4,0},{1,5},{5,1},{2,6},{6,2},{3,7},{7,3},{8,12},{12,8},{9,1... | collective-permute-start | bytes 786440 | tf_op jit(solution)/shard_map/ppermute | solution.py:642
  154.9 46.4 %collective-permute-start.27 = (bf16[512,1024]{1,0:T(8,128)(2,1)S(1)}, bf16[512,1024]{1,0:T(8,128)(2,1)S(1)}, u32[]{:S(2)}, u32[]{:S(2)}) collective-permute-start(bf16[512,1024]{1,0:T(8,128)(2,1)S(1)} %copy-done.74), channel_id=1, source_target_pairs={{0,4},{4,0},{1,5},{5,1},{2,6},{6,2},{3,7},{7,3},{8,12},{12,8},{9,1... | collective-permute-start | bytes 3145736 | tf_op jit(solution)/shard_map/ppermute | solution.py:642
  155.0 32.3 %collective-permute-start.22 = (bf16[9216,256]{1,0:T(8,128)(2,1)S(1)}, bf16[9216,256]{1,0:T(8,128)(2,1)S(1)}, u32[]{:S(2)}, u32[]{:S(2)}) collective-permute-start(bf16[9216,256]{1,0:T(8,128)(2,1)S(1)} %constant_dynamic-update-slice_fusion.7.two_mine), channel_id=1, source_target_pairs={{0,4},{4,0},{1,5},{5,1},{2,6},{6,2},{3,7},{7,3},{8,12},{12,8},{9,1... | collective-permute-start | bytes 14155784 | tf_op jit(solution)/shard_map/ppermute | solution.py:642
  280.5 57.7 %collective-permute-start.46 = (bf16[784,256]{1,0:T(8,128)(2,1)}, bf16[784,256]{1,0:T(8,128)(2,1)}, u32[]{:S(2)}, u32[]{:S(2)}) collective-permute-start(bf16[784,256]{1,0:T(8,128)(2,1)} %get-tuple-element.259), channel_id=1, source_target_pairs={{0,1},{1,0},{2,3},{3,2},{4,5},{5,4},{6,7},{7,6},{8,9},{9,8},{10,11... | collective-permute-start | bytes 1204232 | tf_op jit(solution)/shard_map/ppermute | solution.py:642
  282.2 82.1 %collective-permute-start.41 = (bf16[784,256]{1,0:T(8,128)(2,1)}, bf16[784,256]{1,0:T(8,128)(2,1)}, u32[]{:S(2)}, u32[]{:S(2)}) collective-permute-start(bf16[784,256]{1,0:T(8,128)(2,1)} %get-tuple-element.260), channel_id=1, source_target_pairs={{0,1},{1,0},{2,3},{3,2},{4,5},{5,4},{6,7},{7,6},{8,9},{9,8},{10,11... | collective-permute-start | bytes 1204232 | tf_op jit(solution)/shard_map/ppermute | solution.py:642
  339.2 32.6 %collective-permute-start.40 = (bf16[2560,256]{1,0:T(8,128)(2,1)}, bf16[2560,256]{1,0:T(8,128)(2,1)}, u32[]{:S(2)}, u32[]{:S(2)}) collective-permute-start(bf16[2560,256]{1,0:T(8,128)(2,1)} %copy-done.56), channel_id=1, source_target_pairs={{0,16},{8,24},{16,0},{24,8},{1,17},{9,25},{17,1},{25,9},{2,18},{10... | collective-permute-start | bytes 3932168 | tf_op jit(solution)/shard_map/ppermute | solution.py:642
  365.4 48.8 %collective-permute-start.38 = (bf16[1024,256]{1,0:T(8,128)(2,1)}, bf16[1024,256]{1,0:T(8,128)(2,1)}, u32[]{:S(2)}, u32[]{:S(2)}) collective-permute-start(bf16[1024,256]{1,0:T(8,128)(2,1)} %add_convert_fusion.18), channel_id=1, source_target_pairs={{0,8},{8,0},{16,24},{24,16},{1,9},{9,1},{17,25},{25,17},{2,10},{10... | collective-permute-start | bytes 1572872 | tf_op jit(solution)/shard_map/ppermute | solution.py:642
  366.3 47.9 %collective-permute-start.37 = (bf16[1024,256]{1,0:T(8,128)(2,1)}, bf16[1024,256]{1,0:T(8,128)(2,1)S(1)}, u32[]{:S(2)}, u32[]{:S(2)}) collective-permute-start(bf16[1024,256]{1,0:T(8,128)(2,1)} %add_convert_fusion.19), channel_id=1, source_target_pairs={{0,16},{8,24},{16,0},{24,8},{1,17},{9,25},{17,1},{25,9},{2,18},{10... | collective-permute-start | bytes 1572872 | tf_op jit(solution)/shard_map/ppermute | solution.py:642
  415.8 53.2 %collective-permute-start.49 = (bf16[256,512]{1,0:T(8,128)(2,1)S(1)}, bf16[256,512]{1,0:T(8,128)(2,1)S(1)}, u32[]{:S(2)}, u32[]{:S(2)}) collective-permute-start(bf16[256,512]{1,0:T(8,128)(2,1)S(1)} %get-tuple-element.283), channel_id=1, source_target_pairs={{0,1},{1,0},{2,3},{3,2},{4,5},{5,4},{6,7},{7,6},{8,9},{9,8},{10,11... | collective-permute-start | bytes 786440 | tf_op jit(solution)/shard_map/ppermute | solution.py:642
  416.2 54.4 %collective-permute-start.50 = (bf16[256,512]{1,0:T(8,128)(2,1)S(1)}, bf16[256,512]{1,0:T(8,128)(2,1)S(1)}, u32[]{:S(2)}, u32[]{:S(2)}) collective-permute-start(bf16[256,512]{1,0:T(8,128)(2,1)S(1)} %get-tuple-element.284), channel_id=1, source_target_pairs={{0,2},{1,3},{2,0},{3,1},{4,6},{5,7},{6,4},{7,5},{8,10},{9,11},{10,... | collective-permute-start | bytes 786440 | tf_op jit(solution)/shard_map/ppermute | solution.py:642
  418.2 54.5 %collective-permute-start.51 = (bf16[256,512]{1,0:T(8,128)(2,1)S(1)}, bf16[256,512]{1,0:T(8,128)(2,1)S(1)}, u32[]{:S(2)}, u32[]{:S(2)}) collective-permute-start(bf16[256,512]{1,0:T(8,128)(2,1)S(1)} %get-tuple-element.285), channel_id=1, source_target_pairs={{0,3},{1,2},{2,1},{3,0},{4,7},{5,6},{6,5},{7,4},{8,11},{9,10},{10,... | collective-permute-start | bytes 786440 | tf_op jit(solution)/shard_map/ppermute | solution.py:642
  429.6 72.7 %collective-permute-start.52 = (bf16[320,512]{1,0:T(8,128)(2,1)S(1)}, bf16[320,512]{1,0:T(8,128)(2,1)S(1)}, u32[]{:S(2)}, u32[]{:S(2)}) collective-permute-start(bf16[320,512]{1,0:T(8,128)(2,1)S(1)} %pad_maximum_fusion.17), channel_id=1, source_target_pairs={{0,1},{1,0},{2,3},{3,2},{4,5},{5,4},{6,7},{7,6},{8,9},{9,8},{10,11... | collective-permute-start | bytes 983048 | tf_op jit(solution)/shard_map/ppermute | solution.py:642
  468.8 38.2 %collective-permute-start.61 = (bf16[512,768]{1,0:T(8,128)(2,1)S(1)}, bf16[512,768]{1,0:T(8,128)(2,1)S(1)}, u32[]{:S(2)}, u32[]{:S(2)}) collective-permute-start(bf16[512,768]{1,0:T(8,128)(2,1)S(1)} %convolution_convert_fusion.4), channel_id=1, source_target_pairs={{0,4},{4,0},{1,5},{5,1},{2,6},{6,2},{3,7},{7,3},{8,12},{12,8},{9,1... | collective-permute-start | bytes 2359304 | tf_op jit(solution)/shard_map/ppermute | solution.py:642
  469.0 34.0 %collective-permute-start.53 = (bf16[320,512]{1,0:T(8,128)(2,1)S(1)}, bf16[320,512]{1,0:T(8,128)(2,1)S(1)}, u32[]{:S(2)}, u32[]{:S(2)}) collective-permute-start(bf16[320,512]{1,0:T(8,128)(2,1)S(1)} %pad_maximum_fusion.18), channel_id=1, source_target_pairs={{0,2},{1,3},{2,0},{3,1},{4,6},{5,7},{6,4},{7,5},{8,10},{9,11},{10,... | collective-permute-start | bytes 983048 | tf_op jit(solution)/shard_map/ppermute | solution.py:642
  470.6 32.8 %collective-permute-start.54 = (bf16[320,512]{1,0:T(8,128)(2,1)S(1)}, bf16[320,512]{1,0:T(8,128)(2,1)S(1)}, u32[]{:S(2)}, u32[]{:S(2)}) collective-permute-start(bf16[320,512]{1,0:T(8,128)(2,1)S(1)} %pad_maximum_fusion.19), channel_id=1, source_target_pairs={{0,3},{1,2},{2,1},{3,0},{4,7},{5,6},{6,5},{7,4},{8,11},{9,10},{10,... | collective-permute-start | bytes 983048 | tf_op jit(solution)/shard_map/ppermute | solution.py:642
  502.4 60.8 %collective-permute-start.48 = (bf16[784,1024]{1,0:T(8,128)(2,1)}, bf16[784,1024]{1,0:T(8,128)(2,1)S(1)}, u32[]{:S(2)}, u32[]{:S(2)}) collective-permute-start(bf16[784,1024]{1,0:T(8,128)(2,1)} %slice.863), channel_id=1, source_target_pairs={{0,1},{1,0},{2,3},{3,2},{4,5},{5,4},{6,7},{7,6},{8,9},{9,8},{10,11... | collective-permute-start | bytes 4816904 | tf_op jit(solution)/shard_map/ppermute | solution.py:642
  524.0 35.2 %collective-permute-start.55 = (bf16[576,512]{1,0:T(8,128)(2,1)}, bf16[576,512]{1,0:T(8,128)(2,1)S(1)}, u32[]{:S(2)}, u32[]{:S(2)}) collective-permute-start(bf16[576,512]{1,0:T(8,128)(2,1)} %pad_maximum_fusion.14.refs_0_), channel_id=1, source_target_pairs={{0,8},{8,0},{16,24},{24,16},{1,9},{9,1},{17,25},{25,17},{2,10},{10... | collective-permute-start | bytes 1769480 | tf_op jit(solution)/shard_map/ppermute | solution.py:642
  525.2 35.7 %collective-permute-start.56 = (bf16[576,512]{1,0:T(8,128)(2,1)}, bf16[576,512]{1,0:T(8,128)(2,1)S(1)}, u32[]{:S(2)}, u32[]{:S(2)}) collective-permute-start(bf16[576,512]{1,0:T(8,128)(2,1)} %pad_maximum_fusion.14.refs_0_), channel_id=1, source_target_pairs={{0,16},{8,24},{16,0},{24,8},{1,17},{9,25},{17,1},{25,9},{2,18},{10... | collective-permute-start | bytes 1769480 | tf_op jit(solution)/shard_map/ppermute | solution.py:642
  525.6 37.1 %collective-permute-start.57 = (bf16[576,512]{1,0:T(8,128)(2,1)}, bf16[576,512]{1,0:T(8,128)(2,1)S(1)}, u32[]{:S(2)}, u32[]{:S(2)}) collective-permute-start(bf16[576,512]{1,0:T(8,128)(2,1)} %pad_maximum_fusion.14.refs_0_), channel_id=1, source_target_pairs={{0,24},{8,16},{16,8},{24,0},{1,25},{9,17},{17,9},{25,1},{2,26},{10... | collective-permute-start | bytes 1769480 | tf_op jit(solution)/shard_map/ppermute | solution.py:642
  (165 other events, 2260.9 us)

commit v3 on v2

--- a/solution.py
+++ b/solution.py
@@ -328,6 +328,10 @@
 
 PAIRED_MESH = (4, 2, 4)
 GROUP = 4
+
+
+def small_cost(flops):
+    return pl.CostEstimate(flops=flops, bytes_accessed=0, transcendentals=0)
 QT = 128
 
 
@@ -387,19 +391,26 @@
     tiles_of(out_ref.shape[0], tile)
 
 
-def attend_back_kernel(first, last, packed_ref, bias_ref, lse_ref, att_ref, up_ref, *refs):
+def attend_back_kernel(
+    first, lane, last, packed_ref, bias_ref, lse_ref, att_ref, up_own_ref, up_far_ref, *refs
+):
     width = GROUP * HD
+    lanes = slice(lane, lane + width)
+    own_rows = up_own_ref.shape[0]
     if last:
-        dq_in, dk_in, dv_in, out_ref, kt_ref, dk_ref, dv_ref = refs
+        dq_in, dk_in, dv_in, out_ref, sum_ref, kt_ref, up_ref, dk_ref, dv_ref = refs
         dk_ref[...] = dk_in[...]
         dv_ref[...] = dv_in[...]
         out_ref[0:first, 0:width] = dq_in[...]
         rows = out_ref.shape[0] - first
+        up_ref[0 : own_rows - first, :] = up_own_ref[first:own_rows, lanes]
+        up_ref[own_rows - first :, :] = up_far_ref[:, lanes]
     else:
-        out_ref, dk_ref, dv_ref, kt_ref = refs
+        out_ref, dk_ref, dv_ref, kt_ref, up_ref = refs
         dk_ref[...] = jnp.zeros_like(dk_ref)
         dv_ref[...] = jnp.zeros_like(dv_ref)
         rows = out_ref.shape[0]
+        up_ref[...] = up_own_ref[0:rows, lanes]
     kt_ref[...] = packed_ref[:, width : 2 * width].T
 
     def tile(start, count, index):
@@ -432,6 +443,9 @@
     if last:
         out_ref[:, width : 2 * width] = dk_ref[...].astype(jnp.bfloat16)
         out_ref[:, 2 * width : 3 * width] = dv_ref[...].astype(jnp.bfloat16)
+        for k in range(3):
+            part = out_ref[:, k * width : (k + 1) * width].astype(jnp.float32)
+            sum_ref[:, k * width : (k + 1) * width] = jnp.sum(part, axis=0, keepdims=True)
 
 
 def attend(packed, bias, first, rows):
@@ -448,58 +462,74 @@
         scratch_shapes=[pltpu.VMEM((width, tokens), jnp.bfloat16)],
         compiler_params=pltpu.CompilerParams(vmem_limit_bytes=32 << 20),
         cost_estimate=pl.CostEstimate(
-            flops=10 * rows * tokens * width * 4, bytes_accessed=6 << 20, transcendentals=0
+            flops=2 * rows * tokens * width * 4, bytes_accessed=6 << 20, transcendentals=0
         ),
         name="attend",
     )(packed, bias)
 
 
-def attend_back(packed, bias, lse, att, upstream, first, before=None):
+def attend_back(packed, bias, lse, att, up_own, up_far, lane, first, before=None):
     tokens, width = packed.shape[0], GROUP * HD
     rows = att.shape[0]
     total = jax.ShapeDtypeStruct((tokens, width), jnp.float32)
     vmem = pl.BlockSpec(memory_space=pltpu.VMEM)
-    turned = pltpu.VMEM((width, tokens), jnp.bfloat16)
+    scratch = [pltpu.VMEM((width, tokens), jnp.bfloat16), pltpu.VMEM((rows, width), jnp.bfloat16)]
     if before is None:
         extra = ()
         out_shape = (jax.ShapeDtypeStruct((rows, width), jnp.bfloat16), total, total)
-        scratch = [turned]
-        out_specs = (vmem,) * 3
+        up_far = up_own
     else:
         extra = before
-        out_shape = jax.ShapeDtypeStruct((tokens, 3 * width), jnp.bfloat16)
-        scratch = [turned] + [pltpu.VMEM((tokens, width), jnp.float32)] * 2
-        out_specs = vmem
+        out_shape = (
+            jax.ShapeDtypeStruct((tokens, 3 * width), jnp.bfloat16),
+            jax.ShapeDtypeStruct((1, 3 * width), jnp.float32),
+        )
+        scratch += [pltpu.VMEM((tokens, width), jnp.float32)] * 2
     return pl.pallas_call(
-        functools.partial(attend_back_kernel, first, before is not None),
+        functools.partial(attend_back_kernel, first, lane, before is not None),
         out_shape=out_shape,
-        in_specs=[vmem] * (5 + len(extra)),
-        out_specs=out_specs,
+        in_specs=[vmem] * (6 + len(extra)),
+        out_specs=(vmem,) * len(out_shape),
         scratch_shapes=scratch,
-        compiler_params=pltpu.CompilerParams(vmem_limit_bytes=48 << 20),
+        compiler_params=pltpu.CompilerParams(vmem_limit_bytes=52 << 20),
         cost_estimate=pl.CostEstimate(
-            flops=20 * rows * tokens * width * 4, bytes_accessed=10 << 20, transcendentals=0
+            flops=4 * rows * tokens * width * 4, bytes_accessed=10 << 20, transcendentals=0
         ),
         name="attend_back",
-    )(packed, bias, lse, att, upstream, *extra)
+    )(packed, bias, lse, att, up_own, up_far, *extra)
 
 
 FF_CHUNK = 512
-
-
-def ffn_kernel(
+ROWS = 112
+
+
+def rows_of(total, body):
+    @pl.loop(0, total // ROWS)
+    def _(index):
+        body(pl.ds(pl.multiple_of(index * ROWS, ROWS), ROWS))
+
+
+def unit_rows(values):
+    centered = values - jnp.mean(values, axis=-1, keepdims=True)
+    spread = lax.rsqrt(jnp.mean(centered * centered, axis=-1, keepdims=True) + EPSILON)
+    return centered * spread, spread
+
+
+def middle_kernel(
     table_ref,
     factor_ref,
-    norm_ref,
-    middle_ref,
+    att_ref,
+    input_ref,
     target_ref,
     valid_ref,
-    bias_one_ref,
-    bias_two_ref,
+    vector_ref,
+    small_ref,
     fc1_own,
     fc1_other,
     fc2_own,
     fc2_other,
+    proj_own,
+    proj_other,
     two_mine,
     two_theirs,
     one_mine,
@@ -507,135 +537,207 @@
     out_ref,
     hidden_ref,
     pre_ref,
-    grad_out_ref,
+    norm_ref,
     grad_low_ref,
-    grad_norm_ref,
+    mid_low_ref,
+    grad_mid_ref,
+    up_own_ref,
+    up_give_ref,
     hidden_sum_ref,
     sums_ref,
     fc1_v,
     fc2_v,
+    proj_v,
+    middle_v,
+    back_v,
     sem_one,
     sem_two,
+    sem_proj,
 ):
+    f32, bf16 = jnp.float32, jnp.bfloat16
+    total_rows = att_ref.shape[0]
     half = fc1_own.shape[0]
     sub = fc1_own.shape[1] // 4
+    heads = proj_own.shape[0]
+    part = heads // 4
     hidden_total = hidden_ref.shape[1]
-    step = one_mine.shape[0] // 4
-
-    def fc1_place(side, at):
-        return fc1_v.at[side * half : (side + 1) * half, pl.ds(pl.multiple_of(at * sub, sub), sub)]
-
-    def fc2_place(side, i, at):
+    chunks = hidden_total // FF_CHUNK
+    unit = half + 2 * sub + 2 * part + 16
+
+    def fc1_copy(source, side, at):
+        lanes = pl.ds(pl.multiple_of(at * sub, sub), sub)
+        pltpu.make_async_copy(
+            source, fc1_v.at[side * half : (side + 1) * half, lanes], sem_one.at[at // 2]
+        ).start()
+
+    def fc2_copy(source, side, i, at):
         lane = side * half + i * sub
-        return fc2_v.at[pl.ds(pl.multiple_of(at * sub, sub), sub), lane : lane + sub]
-
-    def pieces():
-        for a in range(4):
-            at = table_ref[16 + a]
-            rows = slice(a * sub, (a + 1) * sub)
-            for side, (one, two) in enumerate(((fc1_own, fc2_own), (fc1_other, fc2_other))):
-                yield side, at, one.at[:, rows], [two.at[rows, i * sub : (i + 1) * sub] for i in range(2)]
-        for s in range(4):
-            for j in (1, 2, 3):
-                at = table_ref[4 * s + j]
-                for side in range(2):
-                    ref = (one_mine, one_theirs)[side] if j == 3 else (two_mine, two_theirs)[side]
-                    base = s * step if j == 3 else (2 * s + j - 1) * step
-                    low = base + half
-                    yield (
-                        side,
-                        at,
-                        ref.at[base : base + half, :],
-                        [ref.at[low + i * sub : low + (i + 1) * sub, :] for i in range(2)],
-                    )
-
-    listed = list(pieces())
-    for side, at, one, _ in listed:
-        pltpu.make_async_copy(one, fc1_place(side, at), sem_one.at[side, at]).start()
-    for side, at, _, two in listed:
-        for i in range(2):
-            pltpu.make_async_copy(two[i], fc2_place(side, i, at), sem_two.at[side, i, at]).start()
-    grad_norm_ref[...] = jnp.zeros_like(grad_norm_ref)
-
-    @pl.loop(0, hidden_total // FF_CHUNK)
-    def _(k):
-        for i in range(FF_CHUNK // sub):
-            for side in range(2):
-                at = k * (FF_CHUNK // sub) + i
-                pltpu.make_async_copy(
-                    fc1_own.at[:, 0:sub], fc1_place(side, at), sem_one.at[side, at]
-                ).wait()
-        span = pl.ds(pl.multiple_of(k * FF_CHUNK, FF_CHUNK), FF_CHUNK)
-        pre = dot_nn(norm_ref[...], fc1_v[:, span]) + bias_one_ref[0:1, span]
-        cdf = 0.5 * (1.0 + lax.erf(pre * ROOT_HALF))
-        hidden_ref[:, span] = (pre * cdf).astype(jnp.bfloat16)
-        slope = cdf + pre * jnp.exp(-0.5 * pre * pre) * DENSITY_FACTOR
-        pre_ref[:, span] = slope.astype(jnp.bfloat16)
-
-    @pl.loop(0, hidden_total // sub)
-    def _(at):
+        pltpu.make_async_copy(
+            source, fc2_v.at[pl.ds(pl.multiple_of(at * sub, sub), sub), lane : lane + sub], sem_two
+        ).start()
+
+    sources = []
+    for s in range(4):
+        step = two_mine.shape[0] // 4
+        sources.append((s, 2, two_mine, two_theirs, s * step))
+        step = one_mine.shape[0] // 4
+        sources.append((s, 1, one_mine, one_theirs, s * step))
+        sources.append((s, 3, one_mine, one_theirs, s * step + unit))
+
+    for side, ref in enumerate((proj_own, proj_other)):
+        pltpu.make_async_copy(
+            ref, proj_v.at[0:heads, side * half : (side + 1) * half], sem_proj
+        ).start()
+    for s, j, *refs, base in sources:
+        rows = pl.ds(pl.multiple_of(j * heads + table_ref[20 + s] * part, part), part)
         for side in range(2):
             for i in range(2):
+                low = base + half + 2 * sub + i * part
+                lane = side * half + i * sub
                 pltpu.make_async_copy(
-                    fc2_own.at[0:sub, 0:sub], fc2_place(side, i, at), sem_two.at[side, i, at]
-                ).wait()
-
+                    refs[side].at[low : low + part, :], proj_v.at[rows, lane : lane + sub], sem_proj
+                ).start()
+    for a in range(4):
+        for side, ref in enumerate((fc1_own, fc1_other)):
+            fc1_copy(ref.at[:, a * sub : (a + 1) * sub], side, table_ref[16 + a])
+    for s, j, *refs, base in sources:
+        for side in range(2):
+            fc1_copy(refs[side].at[base : base + half, :], side, table_ref[4 * s + j])
+    for a in range(4):
+        for side, ref in enumerate((fc2_own, fc2_other)):
+            for i in range(2):
+                fc2_copy(
+                    ref.at[a * sub : (a + 1) * sub, i * sub : (i + 1) * sub], side, i, table_ref[16 + a]
+                )
+    for s, j, *refs, base in sources:
+        for side in range(2):
+            for i in range(2):
+                low = base + half + i * sub
+                fc2_copy(refs[side].at[low : low + sub, :], side, i, table_ref[4 * s + j])
+    back_v[...] = jnp.zeros_like(back_v)
+
+    def lanes_of(i):
+        return pl.ds(pl.multiple_of((table_ref[28] ^ i) * half, half), half)
+
+    sums_ref[...] = jnp.zeros_like(sums_ref)
+
+    pltpu.make_async_copy(proj_v, proj_v, sem_proj).wait()
     for i in range(2):
         cols = slice(i * half, (i + 1) * half)
-        total = dot_nn(hidden_ref[...], fc2_v[:, cols]) + (middle_ref[:, cols] + bias_two_ref[0:1, cols])
-        out_ref[:, cols] = total.astype(jnp.bfloat16)
-        differ = total - target_ref[:, cols].astype(jnp.float32)
+        middle_v[:, cols] = input_ref[:, lanes_of(i)].astype(f32) + (
+            dot_nn(att_ref[...], proj_v[:, cols]) + vector_ref[2:3, cols]
+        )
+
+    @functools.partial(rows_of, total_rows)
+    def _(rows):
+        normal, _ = unit_rows(middle_v[rows, :])
+        norm_ref[rows, :] = (normal * vector_ref[3:4, :] + vector_ref[4:5, :]).astype(bf16)
+
+    @pl.loop(0, chunks)
+    def _(k):
+        span = pl.ds(pl.multiple_of(k * FF_CHUNK, FF_CHUNK), FF_CHUNK)
+        pltpu.make_async_copy(fc1_v.at[:, span], fc1_v.at[:, span], sem_one.at[k]).wait()
+        a = k // 2
+        bias = jnp.concatenate(
+            [
+                small_ref[table_ref[24 + 2 * (k % 2) + i], pl.ds(a, 1), :]
+                for i in range(FF_CHUNK // sub)
+            ],
+            axis=1,
+        )
+        pre = dot_nn(norm_ref[...], fc1_v[:, span]) + bias
+        cdf = 0.5 * (1.0 + lax.erf(pre * ROOT_HALF))
+        hidden_ref[:, span] = (pre * cdf).astype(bf16)
+        slope = cdf + pre * jnp.exp(-0.5 * pre * pre) * DENSITY_FACTOR
+        pre_ref[:, span] = slope.astype(bf16)
+
+    pltpu.make_async_copy(fc2_v, fc2_v, sem_two).wait()
+    for i in range(2):
+        cols = slice(i * half, (i + 1) * half)
+        total = middle_v[:, cols] + (dot_nn(hidden_ref[...], fc2_v[:, cols]) + vector_ref[5:6, cols])
+        out_ref[:, lanes_of(i)] = total.astype(bf16)
+        differ = total - target_ref[:, lanes_of(i)].astype(f32)
         weighted = valid_ref[...] * differ
         sums_ref[0:1, cols] = jnp.sum(weighted * differ, axis=0, keepdims=True)
         grad = factor_ref[0] * weighted
-        grad_out_ref[:, cols] = grad
-        low = grad.astype(jnp.bfloat16)
+        grad_mid_ref[:, cols] = grad
+        low = grad.astype(bf16)
         grad_low_ref[:, cols] = low
-        sums_ref[1:2, cols] = jnp.sum(low.astype(jnp.float32), axis=0, keepdims=True)
-
-    @pl.loop(0, hidden_total // FF_CHUNK)
+        sums_ref[1:2, cols] = jnp.sum(low.astype(f32), axis=0, keepdims=True)
+
+    @pl.loop(0, chunks)
     def _(k):
         span = pl.ds(pl.multiple_of(k * FF_CHUNK, FF_CHUNK), FF_CHUNK)
         back = dot_nt(grad_low_ref[...], fc2_v[span, :])
-        back = (back * pre_ref[:, span].astype(jnp.float32)).astype(jnp.bfloat16)
+        back = (back * pre_ref[:, span].astype(f32)).astype(bf16)
         pre_ref[:, span] = back
-        hidden_sum_ref[0:1, span] = jnp.sum(back.astype(jnp.float32), axis=0, keepdims=True)
-        grad_norm_ref[...] += dot_nt(back, fc1_v[:, span])
-
-
-def feed_forward(table, factor, norm, middle, target, valid, bias_one, bias_two, pieces):
-    rows, width = norm.shape
-    hidden = bias_one.shape[1]
+        hidden_sum_ref[0:1, span] = jnp.sum(back.astype(f32), axis=0, keepdims=True)
+        back_v[...] += dot_nt(back, fc1_v[:, span])
+
+    @functools.partial(rows_of, total_rows)
+    def _(rows):
+        normal, spread = unit_rows(middle_v[rows, :])
+        upstream = back_v[rows, :]
+        inner = upstream * vector_ref[3:4, :]
+        center = jnp.mean(inner, axis=-1, keepdims=True)
+        slope = jnp.mean(inner * normal, axis=-1, keepdims=True)
+        grad = grad_mid_ref[rows, :] + spread * (inner - center - normal * slope)
+        grad_mid_ref[rows, :] = grad
+        low = grad.astype(bf16)
+        mid_low_ref[rows, :] = low
+        sums_ref[2:3, :] += jnp.sum(upstream * normal, axis=0, keepdims=True)
+        sums_ref[3:4, :] += jnp.sum(upstream, axis=0, keepdims=True)
+        sums_ref[4:5, :] += jnp.sum(low.astype(f32), axis=0, keepdims=True)
+
+    for j, (ref, at) in enumerate(((up_own_ref, 0), (up_give_ref, 0), (up_own_ref, 1), (up_give_ref, 1))):
+        grad = dot_nt(mid_low_ref[...], proj_v[j * heads : (j + 1) * heads, :])
+        ref[:, at * heads : (at + 1) * heads] = grad.astype(bf16)
+
+
+def middle_block(table, factor, att, inputs, target, valid, vectors, smalls, pieces):
+    rows, width = att.shape
+    hidden = 4 * pieces[0].shape[1]
     vmem = pl.BlockSpec(memory_space=pltpu.VMEM)
     smem = pl.BlockSpec(memory_space=pltpu.SMEM)
     anywhere = pl.BlockSpec(memory_space=pl.ANY)
     f32, bf16 = jnp.float32, jnp.bfloat16
+
+    def result(columns, dtype):
+        return jax.ShapeDtypeStruct((rows, columns), dtype)
+
     return pl.pallas_call(
-        ffn_kernel,
+        middle_kernel,
         out_shape=(
-            jax.ShapeDtypeStruct((rows, width), bf16),
-            jax.ShapeDtypeStruct((rows, hidden), bf16),
-            jax.ShapeDtypeStruct((rows, hidden), bf16),
-            jax.ShapeDtypeStruct((rows, width), f32),
-            jax.ShapeDtypeStruct((rows, width), bf16),
-            jax.ShapeDtypeStruct((rows, width), f32),
+            result(width, bf16),
+            result(hidden, bf16),
+            result(hidden, bf16),
+            result(width, bf16),
+            result(width, bf16),
+            result(width, bf16),
+            result(width, f32),
+            result(width // 2, bf16),
+            result(width // 2, bf16),
             jax.ShapeDtypeStruct((1, hidden), f32),
-            jax.ShapeDtypeStruct((2, width), f32),
+            jax.ShapeDtypeStruct((8, width), f32),
         ),
-        in_specs=[smem] * 2 + [vmem] * 6 + [anywhere] * 8,
-        out_specs=[vmem] * 8,
+        in_specs=[smem] * 2 + [vmem] * 6 + [anywhere] * 10,
+        out_specs=[vmem] * 11,
         scratch_shapes=[
             pltpu.VMEM((width, hidden), bf16),
             pltpu.VMEM((hidden, width), bf16),
-            pltpu.SemaphoreType.DMA((2, 16)),
-            pltpu.SemaphoreType.DMA((2, 2, 16)),
+            pltpu.VMEM((width, width), bf16),
+            pltpu.VMEM((rows, width), f32),
+            pltpu.VMEM((rows, width), f32),
+            pltpu.SemaphoreType.DMA((hidden // FF_CHUNK,)),
+            pltpu.SemaphoreType.DMA,
+            pltpu.SemaphoreType.DMA,
         ],
         compiler_params=pltpu.CompilerParams(vmem_limit_bytes=62 << 20),
         cost_estimate=pl.CostEstimate(
-            flops=8 * rows * width * hidden, bytes_accessed=44 << 20, transcendentals=0
+            flops=2 * rows * width * hidden, bytes_accessed=44 << 20, transcendentals=0
         ),
-        name="feed_forward",
-    )(table, factor, norm, middle, target, valid, bias_one, bias_two, *pieces)
+        name="middle_block",
+    )(table, factor, att, inputs, target, valid, vectors, smalls, *pieces)
 
 
 def swap(values, axis, mask, size):
@@ -668,16 +770,343 @@
     return whole
 
 
+def copies(listed, sem_ref):
+    for index, (source, target) in enumerate(listed):
+        pltpu.make_async_copy(source, target, sem_ref.at[index]).start()
+    for index, (source, target) in enumerate(listed):
+        pltpu.make_async_copy(source, target, sem_ref.at[index]).wait()
+
+
+def slab_kernel(places_ref, fc1_ref, fc2_ref, proj_ref, qkv_ref, small_ref, out_ref, sem_ref):
+    half, sub = fc1_ref.shape[0], fc1_ref.shape[1] // 4
+    part, deep = proj_ref.shape[0] // 4, half // 4
+    mine = places_ref[0]
+    fc2 = fc2_ref.at[pl.ds(pl.multiple_of(mine * sub, sub), sub)]
+    proj = proj_ref.at[pl.ds(pl.multiple_of(mine * part, part), part)]
+    listed = [(fc1_ref.at[:, pl.ds(pl.multiple_of(mine * sub, sub), sub)], half)]
+    listed += [(fc2.at[:, i * sub : (i + 1) * sub], sub) for i in range(2)]
+    listed += [(proj.at[:, i * sub : (i + 1) * sub], part) for i in range(2)]
+    listed += [(small_ref, small_ref.shape[0])]
+    rows = pl.ds(pl.multiple_of(mine * deep, deep), deep)
+    listed += [(qkv_ref.at[k, rows], deep) for k in range(3)]
+    pairs, at = [], 0
+    for source, count in listed:
+        pairs.append((source, out_ref.at[at : at + count]))
+        at += count
+    copies(pairs, sem_ref)
+
+
+def make_slab(places, fc1, fc2, proj, qkv, small):
+    half, sub = fc1.shape[0], fc1.shape[1] // 4
+    rows = half + 2 * sub + proj.shape[0] // 2 + small.shape[0] + 3 * (half // 4)
+    anywhere = pl.BlockSpec(memory_space=pl.ANY)
+    return pl.pallas_call(
+        slab_kernel,
+        out_shape=jax.ShapeDtypeStruct((rows, sub), fc1.dtype),
+        in_specs=[pl.BlockSpec(memory_space=pltpu.SMEM)] + [anywhere] * 5,
+        out_specs=pl.BlockSpec(memory_space=pltpu.VMEM),
+        scratch_shapes=[pltpu.SemaphoreType.DMA((9,))],
+        cost_estimate=small_cost(100000000),
+        name="make_slab",
+    )(places, fc1, fc2, proj, qkv, small)
+
+
+def far_qkv_kernel(base, places_ref, mine_ref, theirs_ref, out_ref, sem_ref):
+    sub = mine_ref.shape[1]
+    half = out_ref.shape[0] // 2
+    deep, step = half // 4, mine_ref.shape[0] // 4
+    pairs = []
+    for side, ref in enumerate((mine_ref, theirs_ref)):
+        for s in range(4):
+            rows = pl.ds(pl.multiple_of(side * half + places_ref[s] * deep, deep), deep)
+            for k in range(3):
+                at = s * step + base + k * deep
+                pairs.append((ref.at[at : at + deep], out_ref.at[rows, k * sub : (k + 1) * sub]))
+    copies(pairs, sem_ref)
+
+
+def far_qkv(places, mine, theirs, base, width):
+    anywhere = pl.BlockSpec(memory_space=pl.ANY)
+    return pl.pallas_call(
+        functools.partial(far_qkv_kernel, base),
+        out_shape=jax.ShapeDtypeStruct((width, 3 * mine.shape[1]), mine.dtype),
+        in_specs=[pl.BlockSpec(memory_space=pltpu.SMEM)] + [anywhere] * 2,
+        out_specs=pl.BlockSpec(memory_space=pltpu.VMEM),
+        scratch_shapes=[pltpu.SemaphoreType.DMA((24,))],
+        cost_estimate=small_cost(100000000),
+        name="far_qkv",
+    )(places, mine, theirs)
+
+
+VECTORS = 32
+
+
+def put_split(ref, at, values):
+    high = values.astype(jnp.bfloat16)
+    low = (values - high.astype(jnp.float32)).astype(jnp.bfloat16)
+    columns = values.shape[1]
+    ref[at : at + VECTORS, 0:columns] = high
+    ref[at + VECTORS : at + 2 * VECTORS, 0:columns] = low
+    rest = ref.shape[1] - columns
+    if rest:
+        ref[at : at + 2 * VECTORS, columns:] = jnp.zeros((2 * VECTORS, rest), jnp.bfloat16)
+
+
+def get_split(ref, at, columns):
+    high = ref[at : at + VECTORS, 0:columns].astype(jnp.float32)
+    return high + ref[at + VECTORS : at + 2 * VECTORS, 0:columns].astype(jnp.float32)
+
+
+def framed(ref, rows, flip, half):
+    return jnp.concatenate(
+        [ref[rows, pl.ds(pl.multiple_of((flip ^ i) * half, half), half)] for i in range(2)], axis=1
+    ).astype(jnp.float32)
+
+
+def token_back_kernel(
+    flip_ref, near_ref, far_ref, w_near, w_far, own_states, other_states, own_ref, give_ref, sums_ref, other_v
+):
+    rows_all, half = own_ref.shape[0], own_ref.shape[1] // 2
+    sums_ref[...] = jnp.zeros_like(sums_ref)
+    for start, out_ref in ((rows_all, other_v), (0, own_ref)):
+        rows = slice(start, start + rows_all)
+        out_ref[...] = dot_nt(near_ref[rows, :], w_near[...]) + dot_nt(far_ref[rows, :], w_far[...])
+    for out_ref, states in ((other_v, other_states), (own_ref, own_states)):
+
+        @functools.partial(rows_of, rows_all)
+        def _(rows, out_ref=out_ref, states=states):
+            normal, _ = unit_rows(framed(states, rows, flip_ref[0], half))
+            upstream = out_ref[rows, :]
+            sums_ref[0:1, :] += jnp.sum(upstream * normal, axis=0, keepdims=True)
+            sums_ref[1:2, :] += jnp.sum(upstream, axis=0, keepdims=True)
+            if out_ref is other_v:
+                give_ref[rows, :] = upstream.astype(jnp.bfloat16)
+
+
+def token_back(flip, near, far, w_near, w_far, own_states, other_states):
+    rows, width = own_states.shape
+    vmem = pl.BlockSpec(memory_space=pltpu.VMEM)
+    return pl.pallas_call(
+        token_back_kernel,
+        out_shape=(
+            jax.ShapeDtypeStruct((rows, width), jnp.float32),
+            jax.ShapeDtypeStruct((rows, width), jnp.bfloat16),
+            jax.ShapeDtypeStruct((2, width), jnp.float32),
+        ),
+        in_specs=[pl.BlockSpec(memory_space=pltpu.SMEM)] + [vmem] * 6,
+        out_specs=(vmem,) * 3,
+        scratch_shapes=[pltpu.VMEM((rows, width), jnp.float32)],
+        compiler_params=pltpu.CompilerParams(vmem_limit_bytes=40 << 20),
+        cost_estimate=small_cost(100000000),
+        name="token_back",
+    )(flip, near, far, w_near, w_far, own_states, other_states)
+
+
+def last_kernel(flip_ref, own_ref, taken_ref, states_ref, mid_ref, vector_ref, out_ref):
+    half = own_ref.shape[1] // 2
+    upstream = own_ref[...] + taken_ref[...].astype(jnp.float32)
+    everything = slice(0, own_ref.shape[0])
+    normal, spread = unit_rows(framed(states_ref, everything, flip_ref[0], half))
+    inner = upstream * vector_ref[0:1, :]
+    center = jnp.mean(inner, axis=-1, keepdims=True)
+    slope = jnp.mean(inner * normal, axis=-1, keepdims=True)
+    back = mid_ref[...] + spread * (inner - center - normal * slope)
+    for i in range(2):
+        lanes = pl.ds(pl.multiple_of((flip_ref[0] ^ i) * half, half), half)
+        out_ref[:, lanes] = back[:, i * half : (i + 1) * half].astype(jnp.bfloat16)
+
+
+def last_norm(flip, own, taken, states, mid, vectors):
+    rows, width = own.shape
+    block = pl.BlockSpec((ROWS, width), lambda i: (i, 0))
+    whole = pl.BlockSpec(vectors.shape, lambda i: (0, 0))
+    return pl.pallas_call(
+        last_kernel,
+        grid=(rows // ROWS,),
+        out_shape=jax.ShapeDtypeStruct((rows, width), jnp.bfloat16),
+        in_specs=[pl.BlockSpec(memory_space=pltpu.SMEM)] + [block] * 4 + [whole],
+        out_specs=block,
+        cost_estimate=small_cost(500000000),
+        name="last_norm",
+    )(flip, own, taken, states, mid, vectors)
+
+
+def far_grads_kernel(
+    turned_ref, grad_ref, sums_ref, hidden_ref, norm_ref, near_ref, far_ref, keep_ref, out_ref, kept_ref
+):
+    half = keep_ref.shape[1]
+    width = near_ref.shape[1] // 3
+    shared = [hidden_ref[0:1, i * half : (i + 1) * half] for i in range(8)]
+    for ref in (near_ref, far_ref):
+        shared.append(jnp.concatenate([ref[0:1, 0:width], ref[0:1, 2 * width :]], axis=1))
+    shared.append(sums_ref[0:1, 0:half] + sums_ref[0:1, half:])
+    blank = jnp.zeros((VECTORS - 6 - len(shared), half), jnp.float32)
+
+    def rows(lanes):
+        split = [sums_ref[i : i + 1, lanes] for i in (2, 3, 4, 1)]
+        split += [norm_ref[i : i + 1, lanes] for i in range(2)]
+        return jnp.concatenate(split + shared + [blank], axis=0)
+
+    keep_ref[...] = rows(slice(0, half))
+    put_split(out_ref, half, rows(slice(half, 2 * half)))
+    out_ref[0:half, :] = dot_nn(turned_ref[half:, :], grad_ref[...]).astype(jnp.bfloat16)
+    kept_ref[...] = dot_nn(turned_ref[0:half, :], grad_ref[...])
+
+
+def after_row_kernel(
+    places_ref, kept_ref, taken_ref, keep_ref, near_ref, near_taken, near_own_ref, far_own_ref, sum_ref, *outs
+):
+    deep = far_own_ref.shape[0]
+    vectors = keep_ref[...] + get_split(taken_ref, 4 * deep, keep_ref.shape[1])
+    sum_ref[...] = vectors
+    for s in range(4):
+        rows = pl.ds(pl.multiple_of(places_ref[s] * deep, deep), deep)
+        far = kept_ref[rows, :] + taken_ref[rows, :].astype(jnp.float32)
+        if s == 0:
+            far_own_ref[...] = far
+        else:
+            outs[s - 1][0:deep, :] = far.astype(jnp.bfloat16)
+            put_split(outs[s - 1], deep, vectors)
+        if s % 2 == 0:
+            at = slice(s // 2 * deep, (s // 2 + 1) * deep)
+            near = near_ref[rows, :].astype(jnp.float32) + near_taken[at, :].astype(jnp.float32)
+            if s == 0:
+                near_own_ref[...] = near
+            else:
+                outs[s - 1][deep + 2 * VECTORS :, :] = near.astype(jnp.bfloat16)
+
+
+def after_plane_kernel(near_ref, far_ref, sum_ref, *refs):
+    takes, (keep_ref, vector_ref, give_ref, small_ref) = refs[:3], refs[3:]
+    deep = far_ref.shape[0]
+    vectors, far = sum_ref[...], far_ref[...]
+    keep_ref[...] = near_ref[...] + takes[1][deep + 2 * VECTORS :, :].astype(jnp.float32)
+    for take in takes:
+        vectors = vectors + get_split(take, deep, vectors.shape[1])
+        far = far + take[0:deep, :].astype(jnp.float32)
+    vector_ref[...] = vectors
+    give_ref[0:deep, :] = far.astype(jnp.bfloat16)
+    put_split(give_ref, deep, vectors)
+    put_split(small_ref, 0, vectors)
+
+
+def after_cols_kernel(keep_ref, vector_ref, one_ref, two_ref, three_ref, out_ref, total_ref):
+    deep = keep_ref.shape[0]
+    out_ref[...] = (keep_ref[...] + two_ref[0:deep, :].astype(jnp.float32)).astype(jnp.bfloat16)
+    columns = vector_ref.shape[1]
+    far = get_split(two_ref, deep, columns)
+    total = vector_ref[...] + far
+    total = total + get_split(one_ref, 0, columns) + get_split(three_ref, 0, columns)
+    total_ref[...] = total
+    total_ref[14:15, :] = vector_ref[14:15, :] + far[15:16, :]
+
+
+def on_chip(kernel, shapes, name, *args, tables=0):
+    vmem = pl.BlockSpec(memory_space=pltpu.VMEM)
+    return pl.pallas_call(
+        kernel,
+        out_shape=tuple(jax.ShapeDtypeStruct(*s) for s in shapes),
+        in_specs=[pl.BlockSpec(memory_space=pltpu.SMEM)] * tables + [vmem] * (len(args) - tables),
+        out_specs=(vmem,) * len(shapes),
+        cost_estimate=small_cost(100000000),
+        name=name,
+    )(*args)
+
+
+def wide_kernel(with_proj, places_ref, small_ref, big_ref, taken_ref, *refs):
+    if with_proj:
+        proj_kept, proj_taken, *refs = refs
+    *outs, turned_v = refs
+    half, sub = turned_v.shape[0], turned_v.shape[0] // 2
+    span = big_ref.shape[1] // 4
+    part = 256 // 4 if not with_proj else proj_kept.shape[0] // 16
+    turned_v[...] = small_ref[:, 0:half].T
+    for s in range(4):
+        lanes = pl.ds(pl.multiple_of(places_ref[s] * span, span), span)
+        block = dot_nn(turned_v[...], big_ref[:, lanes]) + taken_ref[:, lanes].astype(jnp.float32)
+        block = block.astype(jnp.bfloat16)
+        for side, (go, slot) in enumerate(((s % 2, s // 2), (s // 2, s % 2))):
+            out = outs[2 * side + go]
+            rows = slice(slot * sub, (slot + 1) * sub)
+            out[rows, 0:span] = block[side * sub : (side + 1) * sub]
+            if with_proj:
+                at = side * sub
+                for j in range(4):
+                    start = pl.multiple_of(4 * j * part + places_ref[s] * part, part)
+                    piece = proj_kept[pl.ds(start, part), at : at + sub] + proj_taken[
+                        pl.ds(start, part), at : at + sub
+                    ].astype(jnp.float32)
+                    low = slot * sub + j * part
+                    out[low : low + part, span:] = piece.astype(jnp.bfloat16)
+
+
+def wide_grads(places, small, big, taken, proj=()):
+    half = small.shape[1] // 2
+    columns = big.shape[1] // 4 + (half // 2 if proj else 0)
+    vmem = pl.BlockSpec(memory_space=pltpu.VMEM)
+    return pl.pallas_call(
+        functools.partial(wide_kernel, bool(proj)),
+        out_shape=(jax.ShapeDtypeStruct((half, columns), jnp.bfloat16),) * 4,
+        in_specs=[pl.BlockSpec(memory_space=pltpu.SMEM)] + [vmem] * (3 + len(proj)),
+        out_specs=(vmem,) * 4,
+        scratch_shapes=[pltpu.VMEM((half, small.shape[0]), jnp.bfloat16)],
+        compiler_params=pltpu.CompilerParams(vmem_limit_bytes=44 << 20),
+        cost_estimate=small_cost(3000000000),
+        name="wide_grads",
+    )(places, small, big, taken, *proj)
+
+
+def plane_sum_kernel(*refs):
+    sub = refs[4].shape[0]
+    for side in range(2):
+        kept, taken = refs[2 * side : 2 * side + 2]
+        for slot in range(2):
+            rows = slice(slot * sub, (slot + 1) * sub)
+            total = kept[rows, :].astype(jnp.float32) + taken[rows, :].astype(jnp.float32)
+            refs[4 + 2 * side + slot][...] = total.astype(jnp.bfloat16)
+
+
+def cols_out_kernel(places_ref, *refs):
+    outs = refs[4:]
+    sub = refs[0].shape[0]
+    columns = refs[0].shape[1]
+    part = (outs[0].shape[0] - 2 * sub) // 2
+    for side in range(2):
+        kept, taken = refs[2 * side : 2 * side + 2]
+        for j in range(4):
+            lanes = pl.ds(pl.multiple_of(places_ref[4 + j] * sub, sub), sub)
+            total = kept[:, lanes].astype(jnp.float32) + taken[:, lanes].astype(jnp.float32)
+            outs[j][side * sub : (side + 1) * sub, :] = total.astype(jnp.bfloat16)
+            if part:
+                rows = slice(j * part, (j + 1) * part)
+                total = kept[rows, columns - sub :].astype(jnp.float32)
+                total = total + taken[rows, columns - sub :].astype(jnp.float32)
+                low = 2 * sub + side * part
+                outs[j][low : low + part, :] = total.astype(jnp.bfloat16)
+
+
+def mine_kernel(*refs):
+    out_ref, at = refs[8], 0
+    for group in (refs[0:4], refs[4:8]):
+        total = group[0][...].astype(jnp.float32)
+        for ref in group[1:]:
+            total = total + ref[...].astype(jnp.float32)
+        out_ref[at : at + total.shape[0], :] = total.astype(jnp.bfloat16)
+        at += total.shape[0]
+
+
 def finish_kernel(part_rows, places_ref, *refs):
     pieces, (fc2_ref, fc1_ref, proj_ref) = refs[:4], refs[4:]
-    sub = fc2_ref.shape[0] // 4
+    half, sub = fc1_ref.shape[0], pieces[0].shape[1]
     for s, piece in enumerate(pieces):
         at = places_ref[s]
         rows = pl.ds(pl.multiple_of(at * sub, sub), sub)
-        fc2_ref[rows, :] = piece[0:sub, :].astype(jnp.float32)
-        fc1_ref[:, rows] = piece[sub : 2 * sub, :].astype(jnp.float32).T
+        fc2_ref[rows, :] = piece[0:half, :].astype(jnp.float32).T
+        fc1_ref[:, rows] = piece[half : 2 * half, :].astype(jnp.float32)
         rows = pl.ds(pl.multiple_of(at * part_rows, part_rows), part_rows)
-        proj_ref[rows, :] = piece[2 * sub :, :].astype(jnp.float32)
+        for i in range(2):
+            low = 2 * half + i * part_rows
+            proj_ref[rows, i * sub : (i + 1) * sub] = piece[low : low + part_rows, :].astype(jnp.float32)
 
 
 def finish_qkv_kernel(places_ref, *refs):
@@ -690,8 +1119,8 @@
 
 
 def finish(places, pieces, part_rows):
-    rows, half = pieces[0].shape
-    sub = (rows - part_rows) // 2
+    rows, sub = pieces[0].shape
+    half = (rows - 2 * part_rows) // 2
     vmem = pl.BlockSpec(memory_space=pltpu.VMEM)
     return pl.pallas_call(
         functools.partial(finish_kernel, part_rows),
@@ -702,6 +1131,7 @@
         ),
         in_specs=[pl.BlockSpec(memory_space=pltpu.SMEM)] + [vmem] * 4,
         out_specs=[vmem] * 3,
+        cost_estimate=small_cost(100000000),
         name="finish",
     )(places, *pieces)
 
@@ -714,6 +1144,7 @@
         out_shape=jax.ShapeDtypeStruct((3, 4 * deep, width // 3), jnp.float32),
         in_specs=[pl.BlockSpec(memory_space=pltpu.SMEM)] + [vmem] * 4,
         out_specs=vmem,
+        cost_estimate=small_cost(100000000),
         name="finish_qkv",
     )(places, *pieces)
 
@@ -770,45 +1201,34 @@
             row == 0, values, jnp.concatenate([values[:, half:], values[:, :half]], axis=1)
         )
 
+    places = jnp.stack([dp ^ s for s in range(4)] + [col ^ j for j in range(4)]).astype(jnp.int32)
+    flip = row.reshape(1).astype(jnp.int32)
     states_other = over_col(states, 1)
-    proj_cut = cut(w_proj, dp, part_rows, 0)
-    fc2_cut = cut(w_fc2, dp, sub, 0)
-    slab = jnp.concatenate(
+    small = jnp.concatenate(
         [
-            cut(w_fc1, dp, sub, 1),
-            fc2_cut[:, :sub],
-            fc2_cut[:, sub:],
-            proj_cut[:, :sub],
-            proj_cut[:, sub:],
+            fc1_bias.reshape(4, sub),
+            q_bias.reshape(1, sub),
+            v_bias.reshape(1, sub),
+            jnp.zeros((10, sub), bf16),
         ],
         axis=0,
     )
-    slab_rows = slab.shape[0]
+    slab = make_slab(places, w_fc1, w_fc2, w_proj, w_qkv.transpose(1, 0, 2), small)
+    unit_rows_total = half + 2 * sub + 2 * part_rows + small.shape[0]
+    small_at = unit_rows_total - small.shape[0]
+    two = over_col(slab, 2)
     w_qkv2 = w_qkv.reshape(half, 3 * head_width)
-    qkv_cut = cut(w_qkv2, dp, half // 4)
-    qkv_quarter = over_col(qkv_cut, 2)
-    two = jnp.concatenate([over_col(slab, 1), over_col(slab, 2)], axis=0)
+    w_qkv2 = tie(w_qkv2, slab)
+    qkv_near = jnp.concatenate([w_qkv2, over_row(w_qkv2)], axis=0)
+    vectors = jnp.stack([ln1_gain, ln1_bias, proj_bias, ln2_gain, ln2_bias, fc2_bias])
+    vectors, states, teacher, loss_mask = lax.optimization_barrier(
+        (vectors, states, teacher, loss_mask, slab)
+    )[:4]
+    vectors = jnp.concatenate([vectors, over_row(vectors)], axis=1).astype(f32)
+    fc1_other, fc2_other, proj_other = over_row(w_fc1), over_row(w_fc2), over_row(w_proj)
+    two = tie(two, fc1_other, fc2_other, proj_other)
     two_x, two_y = over_dp(two, 1), over_dp(two, 2)
     states_other = tie(states_other, two)
-
-    vectors = jnp.stack([ln1_gain, ln1_bias, proj_bias, ln2_gain, ln2_bias, fc2_bias])
-    vectors, fc1_bias, states, teacher, loss_mask = lax.optimization_barrier(
-        (vectors, fc1_bias, states, teacher, loss_mask, slab, qkv_cut)
-    )[:5]
-    vector_full = jnp.concatenate([vectors, over_row(vectors)], axis=1).astype(f32)
-    gain_one, shift_one, bias_proj, gain_two, shift_two, bias_two = (vector_full[i] for i in range(6))
-
-    qkv_near = jnp.concatenate([w_qkv2, over_row(w_qkv2)], axis=0)
-    qkv_pieces = [qkv_quarter] + [over_dp(qkv_quarter, s) for s in (1, 2, 3)]
-    qkv_far = place(qkv_pieces, quarter, 0)
-    qkv_far = jnp.concatenate([qkv_far, over_row(qkv_far)], axis=0)
-    small = jnp.concatenate([fc1_bias, q_bias, v_bias])
-    smalls = [small] + [over_col(small, j) for j in (1, 2, 3)]
-    fc1_other = over_row(w_fc1)
-    fc2_other = over_row(w_fc2)
-    proj_other = over_row(w_proj)
-
-    one = over_col(tie(slab, states_other), 3)
 
     all_clips = lengths.shape[0]
     valid_all = (
@@ -825,9 +1245,9 @@
     key_bias = jnp.where(position < my_length, 0.0, MASKED).astype(f32)
     key_bias = jnp.broadcast_to(key_bias[:, None], (L, 128))
 
-    inputs = frame(states).astype(f32)
-    norm_one, unit_one, spread_one = normalize(inputs, gain_one, shift_one)
-    norm_other, unit_other, _ = normalize(frame(states_other).astype(f32), gain_one, shift_one)
+    gain_one, shift_one = vectors[0], vectors[1]
+    norm_one, _, _ = normalize(frame(states).astype(f32), gain_one, shift_one)
+    norm_other, _, _ = normalize(frame(states_other).astype(f32), gain_one, shift_one)
     tokens_one = jnp.concatenate([norm_one.astype(bf16), norm_other.astype(bf16)], axis=0)
 
     zero_bias = jnp.zeros((head_width,), f32)
@@ -837,56 +1257,42 @@
     later = L - split
     over = local_rows - split
 
-    def project(matrix, extra):
-        q_add = extra[span : span + head_width].astype(f32)
-        v_add = extra[span + head_width :].astype(f32)
+    def project(matrix, q_add, v_add):
         projected = jnp.dot(tokens_one, matrix, preferred_element_type=f32)
-        packed = (projected + jnp.concatenate([q_add, zero_bias, v_add])[None]).astype(bf16)
-        return packed * scale[None]
-
-    packed_near = project(qkv_near, small)
-    near_late, near_late_lse = attend(packed_near, key_bias, split, later)
+        add = jnp.concatenate([q_add.astype(f32), zero_bias, v_add.astype(f32)])
+        return (projected + add[None]).astype(bf16) * scale[None]
+
+    packed_near = project(qkv_near, q_bias, v_bias)
+    cut_at = two.shape[0] // 32 * 16
+    two_x, two_y = tie(two_x, packed_near), tie(two_y, packed_near)
+    two_low, two_high = over_dp(two_y[:cut_at], 1), over_dp(two_x[cut_at:], 2)
+    one_give = jnp.concatenate([slab[:unit_rows_total], two[:unit_rows_total]], axis=0)
+    one = over_col(tie(one_give, states_other), 1)
+    near_late, near_late_lse = attend(tie(packed_near, two_x, two_y, one), key_bias, split, later)
+    two_low, two_high = tie(two_low, near_late), tie(two_high, near_late)
+    two_all = jnp.concatenate([two, two_x, two_y, two_low, two_high], axis=0)
+    two_theirs = over_row(two_all)
     near_other = over_col(near_late[over:], 1)
-    two_x, two_y = tie(two_x, near_late), tie(two_y, near_late)
-    middle_row = two.shape[0] // 2
-    two_low, two_high = over_dp(two_y[:middle_row], 1), over_dp(two_x[middle_row:], 2)
-    near_soon, near_soon_lse = attend(tie(packed_near, two_x, two_y), key_bias, 0, split)
-    one = tie(one, near_soon)
     one_x, one_y = over_dp(one, 1), over_dp(one, 2)
-    packed_far = tie(project(qkv_far, smalls[2]), one, near_other)
+    near_soon, near_soon_lse = attend(
+        tie(packed_near, two_all, near_late, one), key_bias, 0, split
+    )
+    two_theirs = tie(two_theirs, near_soon)
+    qkv_far = far_qkv(places, two_all, two_theirs, unit_rows_total, width)
+    far_small = two_all[small_at : small_at + small.shape[0]]
+    packed_far = project(qkv_far, far_small[4], far_small[5])
+    packed_far = tie(packed_far, one, near_other)
     far_late, far_late_lse = attend(packed_far, key_bias, split, later)
     far_other = over_col(far_late[over:], 1)
-    two_low, two_high = tie(two_low, far_late), tie(two_high, far_late)
-    two_all = jnp.concatenate([two, two_x, two_y, two_low, two_high], axis=0)
-    two_theirs = over_row(two_all)
     one_x, one_y = tie(one_x, far_late), tie(one_y, far_late)
-    middle_row = one.shape[0] // 2
-    one_low, one_high = over_dp(one_y[:middle_row], 1), over_dp(one_x[middle_row:], 2)
-    far_soon, far_soon_lse = attend(tie(packed_far, two_all, one_x, one_y), key_bias, 0, split)
+    cut_at = one.shape[0] // 2
+    one_low, one_high = over_dp(one_y[:cut_at], 1), over_dp(one_x[cut_at:], 2)
+    far_soon, far_soon_lse = attend(tie(packed_far, one_x, one_y, far_late), key_bias, 0, split)
     one_low, one_high = tie(one_low, far_soon), tie(one_high, far_soon)
     one_all = jnp.concatenate([one, one_x, one_y, one_low, one_high], axis=0)
+    one_all = tie(one_all, far_other)
+    turned = tie(tokens_one, far_late).T
     one_theirs = over_row(one_all)
-
-    def proj_rows(block, index, count):
-        rows = []
-        for s in range(4):
-            at = (s * count + index) * slab_rows + half + 2 * sub
-            rows.append(
-                jnp.concatenate(
-                    [block[at : at + part_rows], block[at + part_rows : at + 2 * part_rows]], axis=1
-                )
-            )
-        return place(rows, quarter, 0)
-
-    proj_whole = jnp.concatenate(
-        [
-            jnp.concatenate(
-                [w, proj_rows(b, 0, 2), proj_rows(b, 1, 2), proj_rows(c, 0, 1)], axis=0
-            )
-            for w, b, c in ((w_proj, two_all, one_all), (proj_other, two_theirs, one_theirs))
-        ],
-        axis=1,
-    )
     attended_rows = jnp.concatenate(
         [
             jnp.concatenate([near_soon, near_late[:over]], axis=0),
@@ -896,219 +1302,207 @@
         ],
         axis=1,
     )
-    middle = inputs + (jnp.dot(attended_rows, proj_whole, preferred_element_type=f32) + bias_proj)
-    norm_two, unit_two, spread_two = normalize(middle, gain_two, shift_two)
-    norm_two = norm_two.astype(bf16)
 
     table = jnp.stack(
         [(dp ^ s) * 4 + (col ^ j) for s in range(4) for j in range(4)]
         + [a * 4 + col for a in range(4)]
+        + [dp ^ s for s in range(4)]
+        + [col ^ b for b in range(4)]
+        + [row]
     ).astype(jnp.int32)
-    bias_blocks = jnp.stack([b[:span].reshape(4, sub) for b in smalls], axis=1)
-    bias_blocks = jnp.concatenate(
-        [lax.dynamic_index_in_dim(bias_blocks, col ^ b, 1) for b in range(4)], axis=1
-    )
+    at = unit_rows_total + small_at
+    smalls = jnp.stack(
+        [small, one_all[small_at : small_at + 16], two_all[small_at : small_at + 16], one_all[at : at + 16]]
+    ).astype(f32)
     loss_scale = all_clips * L * width / 2.0
     factor = (loss_scale * 2.0 / (valid_total * width)).reshape(1)
-    outputs, hidden, grad_pre, grad_out, grad_low, grad_norm_two, fc1_bias_sum, sums = feed_forward(
+    (
+        outputs,
+        hidden,
+        grad_pre,
+        norm_two,
+        grad_low,
+        mid_low,
+        grad_mid,
+        up_own,
+        up_give,
+        hidden_sum,
+        sums,
+    ) = middle_block(
         table,
         factor,
-        norm_two,
-        middle,
-        frame(teacher),
+        attended_rows,
+        states,
+        teacher,
         valid[:, None],
-        bias_blocks.reshape(1, 4 * span).astype(f32),
-        bias_two[None],
-        (w_fc1, fc1_other, w_fc2, fc2_other, two_all, two_theirs, one_all, one_theirs),
-    )
-    numerator = jnp.sum(sums[0])
-    back_two, gain_two_grad, shift_two_grad = norm_back(grad_norm_two, unit_two, spread_two, gain_two)
-    grad_mid = grad_out + back_two
-    mid_low = grad_mid.astype(bf16)
-    grad_att_rows = jnp.dot(mid_low, proj_whole.T, preferred_element_type=f32).astype(bf16)
-    ups = [
-        grad_att_rows[:, 0:head_width],
-        over_col(grad_att_rows[:, head_width : 2 * head_width], 1),
-        grad_att_rows[:, 2 * head_width : 3 * head_width],
-        over_col(grad_att_rows[:, 3 * head_width :], 1),
-    ]
+        vectors,
+        smalls,
+        (
+            w_fc1,
+            fc1_other,
+            w_fc2,
+            fc2_other,
+            w_proj,
+            proj_other,
+            two_all,
+            two_theirs,
+            one_all,
+            one_theirs,
+        ),
+    )
+    up_far = over_col(up_give, 1)
 
     def joined(kept, taken):
-        return (kept + taken.astype(f32)).astype(bf16)
-
-    give_fc2 = over_row(dot_tn(hidden, grad_low[:, half:]).astype(bf16))
-    give_fc1 = over_row(dot_tn(grad_pre, norm_two[:, half:]).astype(bf16))
+        return (kept.astype(f32) + taken.astype(f32)).astype(bf16)
+
+    give_fc2 = over_row(dot_tn(grad_low[:, half:], hidden).astype(bf16))
+    give_fc1 = over_row(dot_tn(norm_two[:, half:], grad_pre).astype(bf16))
     give_proj = over_row(dot_tn(attended_rows, mid_low[:, half:]).astype(bf16))
-    wide_fc2 = joined(dot_tn(hidden, grad_low[:, :half]), give_fc2)
-    wide_fc1 = joined(dot_tn(grad_pre, norm_two[:, :half]), give_fc1)
-    wide_proj = joined(dot_tn(attended_rows, mid_low[:, :half]), give_proj)
-
-    def fc2_part(s, side):
-        return cut(wide_fc2[:, side * sub : (side + 1) * sub], quarter(s), span, 0)
-
-    def fc1_part(s, side):
-        lanes = slice(side * sub, (side + 1) * sub)
-        proj = [
-            cut(wide_proj[j * head_width : (j + 1) * head_width, lanes], quarter(s), part_rows, 0)
-            for j in range(4)
-        ]
-        return jnp.concatenate([cut(wide_fc1[:, lanes], quarter(s), span, 0), *proj], axis=0)
-
-    STAY, GO = ((0, 2), (0, 1)), ((1, 3), (2, 3))
-
-    def plane_first(part):
-        give = [jnp.concatenate([part(s, side) for s in GO[side]], axis=0) for side in range(2)]
-        return [over_dp(give[0], 1), over_dp(give[1], 2)], give
-
-    def plane_second(part, taken):
-        rows = taken[0].shape[0] // 2
-        keep, give = [], []
-        for side in range(2):
-            first, second = STAY[side]
-            keep.append(joined(part(first, side).astype(f32), taken[side][:rows]))
-            give.append(joined(part(second, side).astype(f32), taken[side][rows:]))
-        return keep, [over_dp(give[0], 2), over_dp(give[1], 1)], give
-
-    fc2_taken, fc2_give = plane_first(fc2_part)
-    fc1_taken, fc1_give = plane_first(fc1_part)
-
-    def row_half(stacked):
-        return stacked[:, :half].reshape(-1), stacked[:, half:].reshape(-1)
-
-    keep, give = row_half(
-        jnp.stack([gain_two_grad, shift_two_grad, jnp.sum(mid_low, axis=0, dtype=f32), sums[1]])
-    )
-    rest = jnp.concatenate([fc1_bias_sum[0], jnp.full((128,), numerator)])
-    early = jnp.concatenate([keep, rest]) + over_row(jnp.concatenate([give, rest]))
-
-    def cols_out(block_of):
-        return [over_col(block_of(j), j) for j in (1, 2, 3)]
+    kept_proj = dot_tn(attended_rows, mid_low[:, :half])
+
+    def plane_first(wide):
+        keep_x, give_x, keep_y, give_y = wide
+        return (keep_x, keep_y), (give_x, give_y), (over_dp(give_x, 1), over_dp(give_y, 2))
+
+    def plane_second(keep, taken):
+        shape = ((keep[0].shape[0] // 2, keep[0].shape[1]), bf16)
+        keep_x, give_x, keep_y, give_y = on_chip(
+            plane_sum_kernel, [shape] * 4, "plane_sum", keep[0], taken[0], keep[1], taken[1]
+        )
+        return (keep_x, keep_y), (give_x, give_y), (over_dp(give_x, 2), over_dp(give_y, 1))
+
+    def cols_out(keep, taken, rows):
+        blocks = on_chip(
+            cols_out_kernel,
+            [((rows, sub), bf16)] * 4,
+            "cols_out",
+            *(places, keep[0], taken[0], keep[1], taken[1]),
+            tables=1,
+        )
+        return blocks, [over_col(blocks[j], j) for j in (1, 2, 3)]
+
+    def all_tied(values, *others):
+        return [tie(v, *others) for v in values]
+
+    wide = wide_grads(places, grad_low, hidden, give_fc2)
+    fc2_keep, fc2_give, fc2_taken = plane_first(wide)
+    wide = wide_grads(
+        places, tie(norm_two, *fc2_give), grad_pre, give_fc1, (kept_proj, give_proj)
+    )
+    fc1_keep, fc1_give, fc1_taken = plane_first(wide)
 
     packed_near = tie(packed_near, *fc2_give, *fc1_give)
-    part_near = attend_back(packed_near, key_bias, near_soon_lse, near_soon, ups[0][:split], 0)
-    fc2_taken = [tie(t, part_near[0]) for t in fc2_taken]
-    fc2_keep, fc2_taken, fc2_give = plane_second(fc2_part, fc2_taken)
-    early = early + over_dp(tie(early, part_near[0]), 1)
-
-    packed_far = tie(packed_far, *fc2_give, early)
-    part_far = attend_back(packed_far, key_bias, far_soon_lse, far_soon, ups[2][:split], 0)
-    fc2_taken = [tie(t, part_far[0]) for t in fc2_taken]
-    fc2_sum = jnp.concatenate(
-        [joined(k.astype(f32), t) for k, t in zip(fc2_keep, fc2_taken, strict=True)], axis=1
-    )
-    fc2_cols = cols_out(lambda j: cut(fc2_sum, col ^ j, sub, 0))
-    fc1_taken = [tie(t, part_far[0]) for t in fc1_taken]
-    fc1_keep, fc1_taken, fc1_give = plane_second(fc1_part, fc1_taken)
-    early = early + over_dp(tie(early, part_far[0]), 2)
-
-    packed_near = tie(packed_near, fc2_sum, early, *fc1_give)
-    up = jnp.concatenate([ups[0][split:], ups[1]], axis=0)
-    grad_near = attend_back(packed_near, key_bias, near_late_lse, near_late, up, split, part_near)
-    fc1_taken = [tie(t, grad_near) for t in fc1_taken]
-    fc1_sum = jnp.concatenate(
-        [joined(k.astype(f32), t) for k, t in zip(fc1_keep, fc1_taken, strict=True)], axis=1
-    )
-
-    def fc1_block(j):
-        proj = fc1_sum[span + j * part_rows : span + (j + 1) * part_rows]
-        return jnp.concatenate([cut(fc1_sum[:span], col ^ j, sub, 0), proj], axis=0)
-
-    fc1_cols = cols_out(fc1_block)
-    early = early + over_col(tie(early, grad_near), 1)
-
-    def qkv_halves(grad):
-        taken = over_row(dot_tn(tokens_one[:, half:], grad).astype(bf16))
-        return joined(dot_tn(tokens_one[:, :half], grad), taken)
-
+    part_near = attend_back(packed_near, key_bias, near_soon_lse, near_soon, up_own, None, 0, 0)
+    fc2_keep, fc2_give, fc2_taken = plane_second(fc2_keep, all_tied(fc2_taken, part_near[0]))
+
+    packed_far = tie(packed_far, *fc2_give, part_near[0])
+    part_far = attend_back(
+        packed_far, key_bias, far_soon_lse, far_soon, up_own, None, head_width, 0
+    )
+    fc2_blocks, fc2_cols = cols_out(fc2_keep, all_tied(fc2_taken, part_far[0]), 2 * sub)
+    fc1_keep, fc1_give, fc1_taken = plane_second(fc1_keep, all_tied(fc1_taken, part_far[0]))
+
+    packed_near = tie(packed_near, *fc2_blocks, *fc1_give)
+    grad_near, near_sums = attend_back(
+        packed_near, key_bias, near_late_lse, near_late, up_own, up_far, 0, split, part_near
+    )
+    fc2_cols = all_tied(fc2_cols, grad_near)
+    fc1_blocks, fc1_cols = cols_out(
+        fc1_keep, all_tied(fc1_taken, grad_near, *fc2_cols), 2 * sub + 2 * part_rows
+    )
+    near_tied = tie(grad_near, *fc1_blocks)
+    near_row = over_row(dot_tn(tokens_one[:, half:], near_tied).astype(bf16))
+    wide_near = joined(dot_tn(tokens_one[:, :half], near_tied), near_row)
     deep = half // 4
-
-    def plane_out(wide):
-        return cut(wide, dp, deep), [over_dp(cut(wide, quarter(s), deep), s) for s in (1, 2, 3)]
-
-    wide_near = qkv_halves(grad_near)
-    near_keep, near_taken = plane_out(wide_near)
-    norm_near = dot_nt(grad_near, qkv_near)
-
-    packed_far = tie(packed_far, fc1_sum, wide_near, norm_near, early)
-    up = jnp.concatenate([ups[2][split:], ups[3]], axis=0)
-    grad_far = attend_back(packed_far, key_bias, far_late_lse, far_late, up, split, part_far)
-
-    grad_norm_one = norm_near + dot_nt(grad_far, qkv_far)
-    norm_give = grad_norm_one[local_rows:].astype(bf16)
+    near_give = jnp.concatenate([cut(wide_near, quarter(s), deep) for s in (1, 3)], axis=0)
+    near_taken = over_dp(near_give, 1)
+
+    packed_far = tie(packed_far, near_give, *fc1_blocks, *fc2_cols)
+    grad_far, far_sums = attend_back(
+        packed_far, key_bias, far_late_lse, far_late, up_own, up_far, head_width, split, part_far
+    )
+
+    norm_own, norm_give, norm_sums = token_back(
+        flip, grad_near, grad_far, qkv_near, qkv_far, states, states_other
+    )
     norm_taken = over_col(norm_give, 1)
-    grad_far = tie(grad_far, norm_give)
-    taken_far = over_row(dot_tn(tokens_one[:, half:], grad_far).astype(bf16))
-    fc2_cols = [tie(t, grad_far) for t in fc2_cols]
-    fc1_cols = [tie(t, grad_far) for t in fc1_cols]
-    mine = jnp.concatenate(
-        [add_up(cut(fc2_sum, col, sub, 0), fc2_cols), add_up(fc1_block(0), fc1_cols)], axis=0
-    ).astype(bf16)
-    mine_back = [over_dp(mine, s) for s in (1, 2, 3)]
-    near_sum = add_up(near_keep, [tie(t, grad_far) for t in near_taken]).astype(bf16)
-    early = early + over_col(tie(early, grad_far), 2)
-    both = jnp.stack(
+    columns, slots = grad_far.shape[1], 2 * VECTORS
+    vec_keep, row_give, kept = on_chip(
+        far_grads_kernel,
+        [((VECTORS, half), f32), ((half + slots, columns), bf16), ((half, columns), f32)],
+        "far_grads",
+        *(turned, tie(grad_far, norm_give, near_taken), sums, hidden_sum, norm_sums, near_sums, far_sums),
+    )
+    row_taken = over_row(row_give)
+    fc1_cols = all_tied(fc1_cols, row_give)
+    mine_rows = fc2_blocks[0].shape[0] + fc1_blocks[0].shape[0]
+    (mine,) = on_chip(
+        mine_kernel,
+        [((mine_rows, sub), bf16)],
+        "mine",
+        *(fc2_blocks[0], *fc2_cols, fc1_blocks[0], *fc1_cols),
+    )
+    mine_x = over_dp(mine, 1)
+    near_own, far_own, vec_sum, *plane_give = on_chip(
+        after_row_kernel,
+        [((deep, columns), f32)] * 2
+        + [((VECTORS, half), f32)]
+        + [((deep + slots + (deep if s == 2 else 0), columns), bf16) for s in (1, 2, 3)],
+        "after_row",
+        *(places, kept, tie(row_taken, mine), vec_keep, wide_near, tie(near_taken, mine)),
+        tables=1,
+    )
+    plane_taken = [over_dp(plane_give[s - 1], s) for s in (1, 2, 3)]
+    mine_two = jnp.concatenate([mine, tie(mine_x, *plane_give)], axis=0)
+    plane_taken = all_tied(plane_taken, mine_two, norm_taken)
+    near_own, vec_sum, col_give, vec_give = on_chip(
+        after_plane_kernel,
         [
-            jnp.sum(grad_norm_one[:local_rows] * unit_one, axis=0)
-            + jnp.sum(grad_norm_one[local_rows:] * unit_other, axis=0),
-            jnp.sum(grad_norm_one, axis=0),
-        ]
-    )
-    keep, give = row_half(both)
-    heads = [
-        jnp.sum(g[:, i : i + head_width], axis=0, dtype=f32)
-        for g in (grad_near, grad_far)
-        for i in (0, 2 * head_width)
-    ]
-    late_keep, late_give = jnp.concatenate([keep, *heads]), jnp.concatenate([give, *heads])
-    late_taken = over_row(tie(late_give, mine))
-
-    wide_far = joined(dot_tn(tokens_one[:, :half], grad_far), tie(taken_far, mine, late_give))
-    far_keep, far_taken = plane_out(wide_far)
-    late = late_keep + tie(late_taken, wide_far)
-    late_parts = [over_dp(late, s) for s in (1, 2, 3)]
-    far_taken = [tie(t, late) for t in far_taken]
-    far_sum = add_up(far_keep, far_taken).astype(bf16)
-    far_other = over_col(far_sum, 2)
-    late_parts = [tie(t, far_sum) for t in late_parts]
-    late = add_up(late, late_parts)
-    flat, _, theirs = jnp.split(late, [2 * half, 2 * half + 2 * head_width])
-    moved = [over_col(flat, 1), over_col(jnp.concatenate([flat, theirs]), 2), over_col(flat, 3)]
-    qkv_sum = add_up(near_sum, [tie(far_other, flat, theirs)]).astype(bf16)
-    qkv_back = [over_dp(qkv_sum, s) for s in (1, 2, 3)]
-
-    norm_taken, *mine_back = lax.optimization_barrier((norm_taken, *mine_back, qkv_sum))[:4]
-    places = jnp.stack([dp, dp ^ 1, dp ^ 2, dp ^ 3]).astype(jnp.int32)
-    fc2_grad, fc1_grad, proj_grad = finish(places, [mine, *mine_back], part_rows)
-    grad_norm_one = grad_norm_one[:local_rows] + norm_taken.astype(f32)
-    back_one, _, _ = norm_back(grad_norm_one, unit_one, spread_one, gain_one)
-    grad_states = frame((grad_mid + back_one).astype(bf16))
-    moved = [tie(t, grad_states) for t in moved]
-    heads = late[2 * half : 2 * half + 2 * head_width] + moved[1][2 * half :]
-    late = (flat + moved[0] + moved[1][: 2 * half] + moved[2]).reshape(2, half)
-    qkv_back = [tie(t, grad_states) for t in qkv_back]
-    qkv_grad = finish_qkv(places, [qkv_sum, *qkv_back]).transpose(1, 0, 2)
-    flat = early[: 4 * half].reshape(4, half)
-    fc1_bias_grad = lax.dynamic_index_in_dim(
-        early[4 * half : 4 * half + 4 * span].reshape(4, 4, sub), col, 1, False
-    ).reshape(span)
-    loss_value = early[4 * half + 4 * span] / (valid_total * width)
+            ((deep, columns), f32),
+            ((VECTORS, half), f32),
+            ((deep + slots, columns), bf16),
+            ((slots, half), bf16),
+        ],
+        "after_plane",
+        *(near_own, far_own, vec_sum, *plane_taken),
+    )
+    mine_y = over_dp(mine_two, 2)
+    col_taken = [over_col(vec_give, 1), over_col(col_give, 2), over_col(vec_give, 3)]
+    norm_taken = tie(norm_taken, col_give)
+    grad_states = last_norm(flip, norm_own, norm_taken, states, grad_mid, vectors)
+
+    qkv_mine, vec_total = on_chip(
+        after_cols_kernel,
+        [((deep, columns), bf16), ((VECTORS, half), f32)],
+        "after_cols",
+        *(near_own, vec_sum, *all_tied(col_taken, grad_states)),
+    )
+    qkv_back = [over_dp(qkv_mine, s) for s in (1, 2, 3)]
+    mine_y = tie(mine_y, qkv_mine)
+    rows = mine.shape[0]
+    pieces = [mine_two[:rows], mine_two[rows:], mine_y[:rows], mine_y[rows:]]
+    fc2_grad, fc1_grad, proj_grad = finish(places, pieces, part_rows)
+    qkv_grad = finish_qkv(places, [qkv_mine, *all_tied(qkv_back, fc2_grad)]).transpose(1, 0, 2)
+
+    fc1_bias_grad = lax.dynamic_index_in_dim(vec_total[6:14].reshape(4, 4, sub), col, 1, False)
+    loss_value = jnp.sum(vec_total[16]) / (valid_total * width)
     return (
-        frame(outputs),
+        outputs,
         loss_value,
         grad_states,
-        late[0],
-        late[1],
+        vec_total[4],
+        vec_total[5],
         qkv_grad,
-        heads[:head_width],
-        heads[head_width:],
+        vec_total[14, :head_width],
+        vec_total[14, head_width:],
         proj_grad,
-        flat[2],
-        flat[0],
-        flat[1],
+        vec_total[2],
+        vec_total[0],
+        vec_total[1],
         fc1_grad,
-        fc1_bias_grad,
+        fc1_bias_grad.reshape(span),
         fc2_grad,
-        flat[3],
+        vec_total[3],
     )
 
 

time: 597 us -> 520 us (0.87)
  Pallas kernels: 180 us -> 272 us
  waiting for transfers between devices: 151 us -> 63.6 us
  matrix products: 73.9 us -> 34.6 us
  starting transfers between devices: 84.2 us -> 55.4 us
  other arithmetic: 50 us -> 22.4 us
  local copies, waits for them, and re-layouts: 41.9 us -> 57.5 us
    pallas_call x5 -> x20, Pallas kernels: 126 us -> 218 us  [the longest x4 84.2 us: attend_back(): pl.pallas_call(functools.partial(attend_back_kernel, first, lane, before...]
    ppermute x76 -> x53, waiting for transfers between devices: 151 us -> 63.6 us  [swap(): return lax.ppermute(values, axis, [(i, i ^ mask) for i in range(size)])]
    dot_general x4 -> x0, matrix products: 29.5 us -> none  [the longest x2 14.6 us: dot_nt(): lax.dot_general(a, b, (((1,), (1,)), ((), ())), preferred_element_type=jn...]
    ppermute x76 -> x53, starting transfers between devices: 84.2 us -> 55.4 us  [swap(): return lax.ppermute(values, axis, [(i, i ^ mask) for i in range(size)])]
    convert_element_type x17 -> x5, other arithmetic: 18.6 us -> 1.39 us  [the longest x3 0.75 us: project(): add = jnp.concatenate([q_add.astype(f32), zero_bias, v_add.astype(f32)])]
    dot_general x10 -> x6, matrix products: 39 us -> 24.9 us  [dot_tn(): lax.dot_general(a, b, (((0,), (0,)), ((), ())), preferred_element_type=jn...]
    reduce_sum x6 -> x0, other arithmetic: 13 us -> none  [the longest x1 4.28 us: norm_back(): return (back, jnp.sum(upstream * normal, axis=0), jnp.sum(upstream, axis=0))]
    optimization_barrier x0 -> x3, local copies, waits for them, and re-layouts: none -> 6.71 us  [the longest x2 4.27 us: tie(): return lax.optimization_barrier((value, *others))[0]]
  transfers between devices with their start and end apart: 76 -> 53, of which waited for: 23 -> 8; matrix products, arithmetic and copies ran while one was open for 23% -> 17% of each run, Pallas kernels for 21% -> 41%
where the time goes in v3:
time: 520 us; the launch traced here: 510 us
  Pallas kernels  272 us (52%)
  waiting for transfers between devices  63.6 us (12%)
  local copies, waits for them, and re-layouts  57.5 us (11%)
  starting transfers between devices  55.4 us (11%)
  matrix products  34.6 us (7%)
  other arithmetic  22.4 us (4%)
    pallas_call x4, Pallas kernels, attend_back(): pl.pallas_call(functools.partial(attend_back_kernel, first, lane, before...  84.2 us
    ppermute x53, waiting for transfers between devices, swap(): return lax.ppermute(values, axis, [(i, i ^ mask) for i in range(size)])  63.6 us
    pallas_call x1, Pallas kernels, middle_block(): pl.pallas_call(middle_kernel, out_shape=(result(width, bf16), result(hidd...  58.6 us
    ppermute x53, starting transfers between devices, swap(): return lax.ppermute(values, axis, [(i, i ^ mask) for i in range(size)])  55.4 us
    pallas_call x4, Pallas kernels, attend(): pl.pallas_call(functools.partial(attend_kernel, first), out_shape=(jax.Sh...  47 us
    pallas_call x9, Pallas kernels, on_chip(): pl.pallas_call(kernel, out_shape=tuple((jax.ShapeDtypeStruct(*s) for s in...  31 us
    unnamed x141, local copies, waits for them, and re-layouts  28.3 us
    dot_general x6, matrix products, dot_tn(): lax.dot_general(a, b, (((0,), (0,)), ((), ())), preferred_element_type=jn...  24.9 us
  transfers between devices with their start and end apart: 53, of which 8 were waited for; matrix products, arithmetic and copies ran while one was open for 17% of the time, Pallas kernels for 41%

profile of v3, /device:TPU:0, one launch (start us, length us, event | category | flops | bytes accessed | tf_op | source)
XLA Modules:
  0.0 509.6 jit_solution(4760417553022053423)
XLA Ops:
  30.7 16.3 %collective-permute-done.2 = bf16[1552,256]{1,0:T(8,128)(2,1)} collective-permute-done((bf16[1552,256]{1,0:T(8,128)(2,1)}, bf16[1552,256]{1,0:T(8,128)(2,1)}, u32[]{:S(2)}, u32[]{:S(2)}) %collective-permute-start.2) | collective-permute-done | bytes 794656 | tf_op jit(solution)/shard_map/ppermute | solution.py:744
  55.2 9.2 %collective-permute-done.1.other_states = bf16[784,1024]{1,0:T(8,128)(2,1)} collective-permute-done((bf16[784,1024]{1,0:T(8,128)(2,1)S(1)}, bf16[784,1024]{1,0:T(8,128)(2,1)}, u32[]{:S(2)}, u32[]{:S(2)}) %collective-permute-start.1) | collective-permute-done | bytes 1605664 | tf_op jit(solution)/shard_map/ppermute | solution.py:744
  74.4 4.6 fusion.12.packed_ref
  86.9 8.2 %collective-permute-done.10 = bf16[2336,256]{1,0:T(8,128)(2,1)} collective-permute-done((bf16[2336,256]{1,0:T(8,128)(2,1)S(1)}, bf16[2336,256]{1,0:T(8,128)(2,1)}, u32[]{:S(2)}, u32[]{:S(2)}) %collective-permute-start.10) | collective-permute-done | bytes 1196064 | tf_op jit(solution)/shard_map/ppermute | solution.py:744
  95.4 12.5 %attend.4 = (bf16[800,256]{1,0:T(8,128)(2,1)S(1)}, f32[7,8,512]{2,1,0:T(8,128)S(1)}) custom-call(bf16[1568,768]{1,0:T(8,128)(2,1)S(1)} %fusion.12.packed_ref, f32[1568,128]{1,0:T(8,128)S(1)} %broadcast_in_dim.47.bias_ref), custom_call_target="tpu_custom_call" | custom-call | flops 2569011200 | bytes 6291456 | tf_op jit(solution)/shard_map/attend/pallas_call | solution.py:454
  115.3 10.9 %attend.5 = (bf16[768,256]{1,0:T(8,128)(2,1)S(1)}, f32[6,8,512]{2,1,0:T(8,128)S(1)}) custom-call(bf16[1568,768]{1,0:T(8,128)(2,1)S(1)} %fusion.12.packed_ref, f32[1568,128]{1,0:T(8,128)S(1)} %broadcast_in_dim.47.bias_ref), custom_call_target="tpu_custom_call" | custom-call | flops 2466250752 | bytes 6291456 | tf_op jit(solution)/shard_map/attend/pallas_call | solution.py:454
  131.4 5.2 %fusion.13.packed_ref = bf16[1568,768]{1,0:T(8,128)(2,1)S(1)} fusion(bf16[1568,1024]{0,1:T(8,128)(2,1)} %copy-done.31, bf16[1024,768]{1,0:T(8,128)(2,1)} %far_qkv.1.w_far, f32[768]{0:T(1024)S(1)} %get-tuple-element.313, bf16[768]{0:T(1024)(128)(2,1)S(1)} %select_convert_fusion.1), kind=kOutput, calls=%fused_computation.26 | convolution fusion | flops 2469863424 | bytes 7197184 | tf_op jit(solution)/shard_map/dot_general | solution.py:1261
  136.6 12.2 %attend.6 = (bf16[800,256]{1,0:T(8,128)(2,1)S(1)}, f32[7,8,512]{2,1,0:T(8,128)S(1)}) custom-call(bf16[1568,768]{1,0:T(8,128)(2,1)S(1)} %fusion.13.packed_ref, f32[1568,128]{1,0:T(8,128)S(1)} %broadcast_in_dim.47.bias_ref), custom_call_target="tpu_custom_call" | custom-call | flops 2569011200 | bytes 6291456 | tf_op jit(solution)/shard_map/attend/pallas_call | solution.py:454
  155.0 11.3 %attend.7 = (bf16[768,256]{1,0:T(8,128)(2,1)S(1)}, f32[6,8,512]{2,1,0:T(8,128)S(1)}) custom-call(bf16[1568,768]{1,0:T(8,128)(2,1)S(1)} %fusion.13.packed_ref, f32[1568,128]{1,0:T(8,128)S(1)} %broadcast_in_dim.47.bias_ref), custom_call_target="tpu_custom_call" | custom-call | flops 2466250752 | bytes 6291456 | tf_op jit(solution)/shard_map/attend/pallas_call | solution.py:454
  179.5 58.6 %middle_block.1 = (bf16[784,1024]{1,0:T(8,128)(2,1)}, bf16[784,4096]{1,0:T(8,128)(2,1)}, bf16[784,4096]{1,0:T(8,128)(2,1)}, bf16[784,1024]{1,0:T(8,128)(2,1)}, b...) custom-call(s32[29]{0:T(128)} %stack.163.table_ref, ...), custom_call_target="tpu_custom_call" | custom-call | flops 6576668672 | bytes 46137344 | tf_op jit(solution)/shard_map/middle_block/pallas_call | solution.py:708
  238.1 7.8 %convolution_convert_fusion.1 = bf16[512,4096]{1,0:T(8,128)(2,1)S(1)} fusion(bf16[784,4096]{1,0:T(8,128)(2,1)} %get-tuple-element.177.big_ref, bf16[784,1024]{1,0:T(8,128)(2,1)} %get-tuple-element.176.small_ref), kind=kOutput, calls=%fused_computation.1 | convolution fusion | flops 3290431488 | bytes 11419648 | tf_op jit(solution)/shard_map/dot_general | solution.py:347
  246.4 6.5 %convolution_convert_fusion = bf16[512,4096]{1,0:T(8,128)(2,1)} fusion(bf16[784,4096]{1,0:T(8,128)(2,1)S(1)} %copy-done.37, bf16[784,1024]{1,0:T(8,128)(2,1)S(1)} %copy-done.6), kind=kOutput, calls=%fused_computation | convolution fusion | flops 3290431488 | bytes 11419648 | tf_op jit(solution)/shard_map/dot_general | solution.py:347
  257.1 8.7 %wide_grads.2 = (bf16[512,1024]{1,0:T(8,128)(2,1)S(1)}, bf16[512,1024]{1,0:T(8,128)(2,1)}, bf16[512,1024]{1,0:T(8,128)(2,1)S(1)}, bf16[512,1024]{1,0:T(8,128)(2,1)}) custom-call(s32[8]{0:T(128)S(1)} %copy-done.16, bf16[784,1024]{1,0:T(8,128)(2,1)S(1)} %copy-done.7, bf16[784,4096]{1,0:T(8,128)(2,1)} %get-tuple-element.177.big_ref, ...), custom_call_target="tpu_custom_call" | custom-call | flops 3000000000 | tf_op jit(solution)/shard_map/wide_grads/pallas_call | solution.py:1047
  269.9 9.8 %wide_grads.3 = (bf16[512,1280]{1,0:T(8,128)(2,1)S(1)}, bf16[512,1280]{1,0:T(8,128)(2,1)S(1)}, bf16[512,1280]{1,0:T(8,128)(2,1)S(1)}, bf16[512,1280]{1,0:T(8,128)(2,1)}) custom-call(s32[8]{0:T(128)S(1)} %copy-done.16, bf16[784,1024]{1,0:T(8,128)(2,1)S(1)} %copy-done.6, bf16[784,4096]{1,0:T(8,128)(2,1)} %get-tuple-element.183.big_ref, ...), custom_call_target="tpu_custom_call" | custom-call | flops 3000000000 | tf_op jit(solution)/shard_map/wide_grads/pallas_call | solution.py:1047
  284.6 19.4 %attend_back.4 = (bf16[768,256]{1,0:T(8,128)(2,1)S(1)}, f32[1568,256]{1,0:T(8,128)}, f32[1568,256]{1,0:T(8,128)}) custom-call(bf16[1568,768]{1,0:T(8,128)(2,1)} %copy-done.21, f32[1568,128]{1,0:T(8,128)S(1)} %broadcast_in_dim.47.bias_ref, f32[6,8,512]{2,1,0:T(8,128)S(1)} %get-tuple-element.188.lse_ref, bf16[768,256]{1,0:T(8,128)(2,1)S(1)} %get-tuple-element.162.att_ref, ...), custom_call_target="tpu_custom_call" | custom-call | flops 4932501504 | bytes 10485760 | tf_op jit(solution)/shard_map/attend_back/pallas_call | solution.py:488
  311.5 19.7 %attend_back.5 = (bf16[768,256]{1,0:T(8,128)(2,1)S(1)}, f32[1568,256]{1,0:T(8,128)}, f32[1568,256]{1,0:T(8,128)}) custom-call(bf16[1568,768]{1,0:T(8,128)(2,1)} %copy-done.20, f32[1568,128]{1,0:T(8,128)S(1)} %broadcast_in_dim.47.bias_ref, f32[6,8,512]{2,1,0:T(8,128)S(1)} %copy-done.27, bf16[768,256]{1,0:T(8,128)(2,1)S(1)} %copy-done.15, ...), custom_call_target="tpu_custom_call" | custom-call | flops 4932501504 | bytes 10485760 | tf_op jit(solution)/shard_map/attend_back/pallas_call | solution.py:488
  344.3 22.6 %attend_back.6 = (bf16[1568,768]{1,0:T(8,128)(2,1)}, f32[1,768]{1,0:T(1,128)S(1)}) custom-call(bf16[1568,768]{1,0:T(8,128)(2,1)} %copy-done.21, f32[1568,128]{1,0:T(8,128)S(1)} %broadcast_in_dim.47.bias_ref, f32[7,8,512]{2,1,0:T(8,128)S(1)} %get-tuple-element.214.lse_ref, bf16[800,256]{1,0:T(8,128)(2,1)S(1)} %get-tuple-element.158.att_ref, ...), custom_call_target="tpu_custom_call" | custom-call | flops 5138022400 | bytes 10485760 | tf_op jit(solution)/shard_map/attend_back/pallas_call | solution.py:488
  385.3 22.5 %attend_back.7 = (bf16[1568,768]{1,0:T(8,128)(2,1)}, f32[1,768]{1,0:T(1,128)S(1)}) custom-call(bf16[1568,768]{1,0:T(8,128)(2,1)} %copy-done.20, f32[1568,128]{1,0:T(8,128)S(1)} %broadcast_in_dim.47.bias_ref, f32[7,8,512]{2,1,0:T(8,128)S(1)} %get-tuple-element.232.lse_ref, bf16[800,256]{1,0:T(8,128)(2,1)S(1)} %copy-done.13, ...), custom_call_target="tpu_custom_call" | custom-call | flops 5138022400 | bytes 10485760 | tf_op jit(solution)/shard_map/attend_back/pallas_call | solution.py:488
  409.5 11.7 %token_back.1 = (f32[784,1024]{1,0:T(8,128)}, bf16[784,1024]{1,0:T(8,128)(2,1)S(1)}, f32[2,1024]{1,0:T(2,128)S(1)}) custom-call(s32[1]{0:T(128)} %bitcast.27.flip_ref, bf16[1568,768]{1,0:T(8,128)(2,1)S(1)} %copy-done.5, bf16[1568,768]{1,0:T(8,128)(2,1)S(1)} %copy-done.2, bf16[1024,768]{1,0:T(8,128)(2,1)S(1)} %pad_maximum_fusion.2.w_near, ...), custom_call_target="tpu_custom_call" | custom-call | flops 100000000 | tf_op jit(solution)/shard_map/token_back/pallas_call | solution.py:889
  422.5 7.1 %far_grads.1 = (f32[32,512]{1,0:T(8,128)}, bf16[576,768]{1,0:T(8,128)(2,1)}, f32[512,768]{1,0:T(8,128)}) custom-call(bf16[1024,1568]{1,0:T(8,128)(2,1)} %bitcast.64, bf16[1568,768]{1,0:T(8,128)(2,1)} %get-tuple-element.237.far_ref.grad_ref, f32[8,1024]{1,0:T(8,128)} %get-tuple-element.238.sums_ref, f32[1,4096]{1,0:T(1,128)} %get-tuple-element.239.hidden_ref, ...), custom_call_target="tpu_custom_call" | custom-call | flops 100000000 | tf_op jit(solution)/shard_map/far_grads/pallas_call | solution.py:1006
  437.8 10.5 %collective-permute-done.42.refs_1_ = bf16[1152,256]{1,0:T(8,128)(2,1)S(1)} collective-permute-done((bf16[1152,256]{1,0:T(8,128)(2,1)}, bf16[1152,256]{1,0:T(8,128)(2,1)S(1)}, u32[]{:S(2)}, u32[]{:S(2)}) %collective-permute-start.42) | collective-permute-done | bytes 589856 | tf_op jit(solution)/shard_map/ppermute | solution.py:744
  453.0 9.1 %collective-permute-done.45.refs_2_ = bf16[192,768]{1,0:T(8,128)(2,1)S(1)} collective-permute-done((bf16[192,768]{1,0:T(8,128)(2,1)}, bf16[192,768]{1,0:T(8,128)(2,1)S(1)}, u32[]{:S(2)}, u32[]{:S(2)}) %collective-permute-start.45) | collective-permute-done | bytes 294944 | tf_op jit(solution)/shard_map/ppermute | solution.py:744
  473.5 8.0 %last_norm.1 = bf16[784,1024]{1,0:T(8,128)(2,1)} custom-call(s32[1]{0:T(128)} %bitcast.27.flip_ref, f32[784,1024]{1,0:T(8,128)} %get-tuple-element.264.own_ref, bf16[784,1024]{1,0:T(8,128)(2,1)} %collective-permute-done.43.taken_ref, bf16[784,1024]{1,0:T(8,128)(2,1)} %states_ref, f32[784,1024]{1,0:T(8,128)} %get-tuple-element.267.mid_ref, f32[6,1024]{1,0:T(8,128)} %copy-done.45), custom_call_target="tpu_custom_call" | custom-call | flops 500000000 | tf_op jit(solution)/shard_map/last_norm/pallas_call | solution.py:923
  481.6 4.7 collective-permute-done.47.two_ref
  (329 shorter events, 188.1 us)
Async XLA Ops:
  0.7 46.3 %collective-permute-start.3 = (bf16[512,1024]{1,0:T(8,128)(2,1)}, bf16[512,1024]{1,0:T(8,128)(2,1)}, u32[]{:S(2)}, u32[]{:S(2)}) collective-permute-start(bf16[512,1024]{1,0:T(8,128)(2,1)} %fc1_own.1), channel_id=1, source_target_pairs={{0,4},{4,0},{1,5},{5,1},{2,6},{6,2},{3,7},{7,3},{8,12},{12,8},{9,1... | collective-permute-start | bytes 3145736 | tf_op jit(solution)/shard_map/ppermute | solution.py:744
  1.2 45.8 %collective-permute-start.4 = (bf16[1024,512]{1,0:T(8,128)(2,1)}, bf16[1024,512]{1,0:T(8,128)(2,1)}, u32[]{:S(2)}, u32[]{:S(2)}) collective-permute-start(bf16[1024,512]{1,0:T(8,128)(2,1)} %fc2_own.1), channel_id=1, source_target_pairs={{0,4},{4,0},{1,5},{5,1},{2,6},{6,2},{3,7},{7,3},{8,12},{12,8},{9,1... | collective-permute-start | bytes 3145736 | tf_op jit(solution)/shard_map/ppermute | solution.py:744
  7.5 39.5 %collective-permute-start.2 = (bf16[1552,256]{1,0:T(8,128)(2,1)}, bf16[1552,256]{1,0:T(8,128)(2,1)}, u32[]{:S(2)}, u32[]{:S(2)}) collective-permute-start(bf16[1552,256]{1,0:T(8,128)(2,1)} %make_slab.1), channel_id=1, source_target_pairs={{0,2},{1,3},{2,0},{3,1},{4,6},{5,7},{6,4},{7,5},{8,10},{9,11},{10,... | collective-permute-start | bytes 2383880 | tf_op jit(solution)/shard_map/ppermute | solution.py:744
  11.6 52.8 %collective-permute-start.1 = (bf16[784,1024]{1,0:T(8,128)(2,1)S(1)}, bf16[784,1024]{1,0:T(8,128)(2,1)}, u32[]{:S(2)}, u32[]{:S(2)}) collective-permute-start(bf16[784,1024]{1,0:T(8,128)(2,1)S(1)} %copy-done), channel_id=1, source_target_pairs={{0,1},{1,0},{2,3},{3,2},{4,5},{5,4},{6,7},{7,6},{8,9},{9,8},{10,11... | collective-permute-start | bytes 4816904 | tf_op jit(solution)/shard_map/ppermute | solution.py:744
  30.6 43.2 %collective-permute-start.6 = (bf16[512,768]{1,0:T(8,128)(2,1)}, bf16[512,768]{1,0:T(8,128)(2,1)}, u32[]{:S(2)}, u32[]{:S(2)}) collective-permute-start(bf16[512,768]{1,0:T(8,128)(2,1)} %copy.56), channel_id=1, source_target_pairs={{0,4},{4,0},{1,5},{5,1},{2,6},{6,2},{3,7},{7,3},{8,12},{12,8},{9,1... | collective-permute-start | bytes 2359304 | tf_op jit(solution)/shard_map/ppermute | solution.py:744
  48.1 30.9 %collective-permute-start.8 = (bf16[1552,256]{1,0:T(8,128)(2,1)}, bf16[1552,256]{1,0:T(8,128)(2,1)}, u32[]{:S(2)}, u32[]{:S(2)}) collective-permute-start(bf16[1552,256]{1,0:T(8,128)(2,1)} %collective-permute-done.2), channel_id=1, source_target_pairs={{0,16},{8,24},{16,0},{24,8},{1,17},{9,25},{17,1},{25,9},{2,18},{10... | collective-permute-start | bytes 2383880 | tf_op jit(solution)/shard_map/ppermute | solution.py:744
  49.8 29.3 %collective-permute-start.7 = (bf16[1552,256]{1,0:T(8,128)(2,1)}, bf16[1552,256]{1,0:T(8,128)(2,1)}, u32[]{:S(2)}, u32[]{:S(2)}) collective-permute-start(bf16[1552,256]{1,0:T(8,128)(2,1)} %collective-permute-done.2), channel_id=1, source_target_pairs={{0,8},{8,0},{16,24},{24,16},{1,9},{9,1},{17,25},{25,17},{2,10},{10... | collective-permute-start | bytes 2383880 | tf_op jit(solution)/shard_map/ppermute | solution.py:744
  109.8 39.0 %collective-permute-start.15 = (bf16[2336,256]{1,0:T(8,128)(2,1)}, bf16[2336,256]{1,0:T(8,128)(2,1)}, u32[]{:S(2)}, u32[]{:S(2)}) collective-permute-start(bf16[2336,256]{1,0:T(8,128)(2,1)} %collective-permute-done.10), channel_id=1, source_target_pairs={{0,16},{8,24},{16,0},{24,8},{1,17},{9,25},{17,1},{25,9},{2,18},{10... | collective-permute-start | bytes 3588104 | tf_op jit(solution)/shard_map/ppermute | solution.py:744
  111.4 37.5 %collective-permute-start.14 = (bf16[2336,256]{1,0:T(8,128)(2,1)}, bf16[2336,256]{1,0:T(8,128)(2,1)}, u32[]{:S(2)}, u32[]{:S(2)}) collective-permute-start(bf16[2336,256]{1,0:T(8,128)(2,1)} %collective-permute-done.10), channel_id=1, source_target_pairs={{0,8},{8,0},{16,24},{24,16},{1,9},{9,1},{17,25},{25,17},{2,10},{10... | collective-permute-start | bytes 3588104 | tf_op jit(solution)/shard_map/ppermute | solution.py:744
  266.9 37.9 %collective-permute-start.21 = (bf16[512,1024]{1,0:T(8,128)(2,1)}, bf16[512,1024]{1,0:T(8,128)(2,1)}, u32[]{:S(2)}, u32[]{:S(2)}) collective-permute-start(bf16[512,1024]{1,0:T(8,128)(2,1)} %get-tuple-element.179), channel_id=1, source_target_pairs={{0,8},{8,0},{16,24},{24,16},{1,9},{9,1},{17,25},{25,17},{2,10},{10... | collective-permute-start | bytes 3145736 | tf_op jit(solution)/shard_map/ppermute | solution.py:744
  268.3 36.5 %collective-permute-start.24 = (bf16[512,1024]{1,0:T(8,128)(2,1)}, bf16[512,1024]{1,0:T(8,128)(2,1)}, u32[]{:S(2)}, u32[]{:S(2)}) collective-permute-start(bf16[512,1024]{1,0:T(8,128)(2,1)} %get-tuple-element.180), channel_id=1, source_target_pairs={{0,16},{8,24},{16,0},{24,8},{1,17},{9,25},{17,1},{25,9},{2,18},{10... | collective-permute-start | bytes 3145736 | tf_op jit(solution)/shard_map/ppermute | solution.py:744
  281.8 50.1 %collective-permute-start.28 = (bf16[512,1280]{1,0:T(8,128)(2,1)}, bf16[512,1280]{1,0:T(8,128)(2,1)}, u32[]{:S(2)}, u32[]{:S(2)}) collective-permute-start(bf16[512,1280]{1,0:T(8,128)(2,1)} %get-tuple-element.186), channel_id=1, source_target_pairs={{0,16},{8,24},{16,0},{24,8},{1,17},{9,25},{17,1},{25,9},{2,18},{10... | collective-permute-start | bytes 3932168 | tf_op jit(solution)/shard_map/ppermute | solution.py:744
  282.3 49.6 %collective-permute-start.27 = (bf16[512,1280]{1,0:T(8,128)(2,1)S(1)}, bf16[512,1280]{1,0:T(8,128)(2,1)}, u32[]{:S(2)}, u32[]{:S(2)}) collective-permute-start(bf16[512,1280]{1,0:T(8,128)(2,1)S(1)} %get-tuple-element.185), channel_id=1, source_target_pairs={{0,8},{8,0},{16,24},{24,16},{1,9},{9,1},{17,25},{25,17},{2,10},{10... | collective-permute-start | bytes 3932168 | tf_op jit(solution)/shard_map/ppermute | solution.py:744
  282.9 58.9 %collective-permute-start.29 = (bf16[784,512]{1,0:T(8,128)(2,1)}, bf16[784,512]{1,0:T(8,128)(2,1)}, u32[]{:S(2)}, u32[]{:S(2)}) collective-permute-start(bf16[784,512]{1,0:T(8,128)(2,1)} %get-tuple-element.215), channel_id=1, source_target_pairs={{0,1},{1,0},{2,3},{3,2},{4,5},{5,4},{6,7},{7,6},{8,9},{9,8},{10,11... | collective-permute-start | bytes 2408456 | tf_op jit(solution)/shard_map/ppermute | solution.py:744
  308.5 28.7 %collective-permute-start.25 = (bf16[256,1024]{1,0:T(8,128)(2,1)}, bf16[256,1024]{1,0:T(8,128)(2,1)}, u32[]{:S(2)}, u32[]{:S(2)}) collective-permute-start(bf16[256,1024]{1,0:T(8,128)(2,1)} %get-tuple-element.194), channel_id=1, source_target_pairs={{0,16},{8,24},{16,0},{24,8},{1,17},{9,25},{17,1},{25,9},{2,18},{10... | collective-permute-start | bytes 1572872 | tf_op jit(solution)/shard_map/ppermute | solution.py:744
  336.1 31.4 %collective-permute-start.30 = (bf16[256,1280]{1,0:T(8,128)(2,1)}, bf16[256,1280]{1,0:T(8,128)(2,1)}, u32[]{:S(2)}, u32[]{:S(2)}) collective-permute-start(bf16[256,1280]{1,0:T(8,128)(2,1)} %get-tuple-element.211), channel_id=1, source_target_pairs={{0,16},{8,24},{16,0},{24,8},{1,17},{9,25},{17,1},{25,9},{2,18},{10... | collective-permute-start | bytes 1966088 | tf_op jit(solution)/shard_map/ppermute | solution.py:744
  336.6 30.9 %collective-permute-start.34 = (bf16[256,1280]{1,0:T(8,128)(2,1)}, bf16[256,1280]{1,0:T(8,128)(2,1)}, u32[]{:S(2)}, u32[]{:S(2)}) collective-permute-start(bf16[256,1280]{1,0:T(8,128)(2,1)} %get-tuple-element.212), channel_id=1, source_target_pairs={{0,8},{8,0},{16,24},{24,16},{1,9},{9,1},{17,25},{25,17},{2,10},{10... | collective-permute-start | bytes 1966088 | tf_op jit(solution)/shard_map/ppermute | solution.py:744
  376.2 53.5 %collective-permute-start.38 = (bf16[640,256]{1,0:T(8,128)(2,1)}, bf16[640,256]{1,0:T(8,128)(2,1)}, u32[]{:S(2)}, u32[]{:S(2)}) collective-permute-start(bf16[640,256]{1,0:T(8,128)(2,1)} %get-tuple-element.227), channel_id=1, source_target_pairs={{0,1},{1,0},{2,3},{3,2},{4,5},{5,4},{6,7},{7,6},{8,9},{9,8},{10,11... | collective-permute-start | bytes 983048 | tf_op jit(solution)/shard_map/ppermute | solution.py:744
  376.3 53.4 %collective-permute-start.39 = (bf16[640,256]{1,0:T(8,128)(2,1)}, bf16[640,256]{1,0:T(8,128)(2,1)}, u32[]{:S(2)}, u32[]{:S(2)}) collective-permute-start(bf16[640,256]{1,0:T(8,128)(2,1)} %get-tuple-element.228), channel_id=1, source_target_pairs={{0,2},{1,3},{2,0},{3,1},{4,6},{5,7},{6,4},{7,5},{8,10},{9,11},{10,... | collective-permute-start | bytes 983048 | tf_op jit(solution)/shard_map/ppermute | solution.py:744
  378.2 51.5 %collective-permute-start.40 = (bf16[640,256]{1,0:T(8,128)(2,1)}, bf16[640,256]{1,0:T(8,128)(2,1)}, u32[]{:S(2)}, u32[]{:S(2)}) collective-permute-start(bf16[640,256]{1,0:T(8,128)(2,1)} %get-tuple-element.229), channel_id=1, source_target_pairs={{0,3},{1,2},{2,1},{3,0},{4,7},{5,6},{6,5},{7,4},{8,11},{9,10},{10,... | collective-permute-start | bytes 983048 | tf_op jit(solution)/shard_map/ppermute | solution.py:744
  383.8 38.0 %collective-permute-start.36 = (bf16[256,768]{1,0:T(8,128)(2,1)S(1)}, bf16[256,768]{1,0:T(8,128)(2,1)S(1)}, u32[]{:S(2)}, u32[]{:S(2)}) collective-permute-start(bf16[256,768]{1,0:T(8,128)(2,1)S(1)} %pad_maximum_fusion.5), channel_id=1, source_target_pairs={{0,8},{8,0},{16,24},{24,16},{1,9},{9,1},{17,25},{25,17},{2,10},{10... | collective-permute-start | bytes 1179656 | tf_op jit(solution)/shard_map/ppermute | solution.py:744
  421.8 40.4 %collective-permute-start.43 = (bf16[784,1024]{1,0:T(8,128)(2,1)S(1)}, bf16[784,1024]{1,0:T(8,128)(2,1)}, u32[]{:S(2)}, u32[]{:S(2)}) collective-permute-start(bf16[784,1024]{1,0:T(8,128)(2,1)S(1)} %get-tuple-element.236), channel_id=1, source_target_pairs={{0,1},{1,0},{2,3},{3,2},{4,5},{5,4},{6,7},{7,6},{8,9},{9,8},{10,11... | collective-permute-start | bytes 4816904 | tf_op jit(solution)/shard_map/ppermute | solution.py:744
  436.4 29.7 %collective-permute-start.44 = (bf16[320,768]{1,0:T(8,128)(2,1)}, bf16[320,768]{1,0:T(8,128)(2,1)}, u32[]{:S(2)}, u32[]{:S(2)}) collective-permute-start(bf16[320,768]{1,0:T(8,128)(2,1)} %get-tuple-element.255), channel_id=1, source_target_pairs={{0,16},{8,24},{16,0},{24,8},{1,17},{9,25},{17,1},{25,9},{2,18},{10... | collective-permute-start | bytes 1474568 | tf_op jit(solution)/shard_map/ppermute | solution.py:744
  449.6 48.3 %collective-permute-start.50 = (bf16[2304,256]{1,0:T(8,128)(2,1)}, bf16[2304,256]{1,0:T(8,128)(2,1)}, u32[]{:S(2)}, u32[]{:S(2)}) collective-permute-start(bf16[2304,256]{1,0:T(8,128)(2,1)} %pad_maximum_fusion.4), channel_id=1, source_target_pairs={{0,16},{8,24},{16,0},{24,8},{1,17},{9,25},{17,1},{25,9},{2,18},{10... | collective-permute-start | bytes 3538952 | tf_op jit(solution)/shard_map/ppermute | solution.py:744
  (95 other events, 1058.6 us)

commit v4 on v3

--- a/solution.py
+++ b/solution.py
@@ -534,11 +534,11 @@
     two_theirs,
     one_mine,
     one_theirs,
-    out_ref,
-    hidden_ref,
-    pre_ref,
-    norm_ref,
-    grad_low_ref,
+    out_hbm,
+    hidden_hbm,
+    pre_hbm,
+    norm_hbm,
+    grad_low_hbm,
     mid_low_ref,
     grad_mid_ref,
     up_own_ref,
@@ -550,10 +550,28 @@
     proj_v,
     middle_v,
     back_v,
+    out_ref,
+    hidden_ref,
+    pre_ref,
+    norm_ref,
+    grad_low_ref,
     sem_one,
     sem_two,
     sem_proj,
+    sem_out,
 ):
+    stores = [
+        pltpu.make_async_copy(source, target, sem_out.at[i])
+        for i, (source, target) in enumerate(
+            (
+                (norm_ref, norm_hbm),
+                (hidden_ref, hidden_hbm),
+                (out_ref, out_hbm),
+                (grad_low_ref, grad_low_hbm),
+                (pre_ref, pre_hbm),
+            )
+        )
+    ]
     f32, bf16 = jnp.float32, jnp.bfloat16
     total_rows = att_ref.shape[0]
     half = fc1_own.shape[0]
@@ -614,7 +632,6 @@
             for i in range(2):
                 low = base + half + i * sub
                 fc2_copy(refs[side].at[low : low + sub, :], side, i, table_ref[4 * s + j])
-    back_v[...] = jnp.zeros_like(back_v)
 
     def lanes_of(i):
         return pl.ds(pl.multiple_of((table_ref[28] ^ i) * half, half), half)
@@ -632,6 +649,8 @@
     def _(rows):
         normal, _ = unit_rows(middle_v[rows, :])
         norm_ref[rows, :] = (normal * vector_ref[3:4, :] + vector_ref[4:5, :]).astype(bf16)
+
+    stores[0].start()
 
     @pl.loop(0, chunks)
     def _(k):
@@ -651,6 +670,7 @@
         slope = cdf + pre * jnp.exp(-0.5 * pre * pre) * DENSITY_FACTOR
         pre_ref[:, span] = slope.astype(bf16)
 
+    stores[1].start()
     pltpu.make_async_copy(fc2_v, fc2_v, sem_two).wait()
     for i in range(2):
         cols = slice(i * half, (i + 1) * half)
@@ -665,6 +685,9 @@
         grad_low_ref[:, cols] = low
         sums_ref[1:2, cols] = jnp.sum(low.astype(f32), axis=0, keepdims=True)
 
+    stores[2].start()
+    stores[3].start()
+
     @pl.loop(0, chunks)
     def _(k):
         span = pl.ds(pl.multiple_of(k * FF_CHUNK, FF_CHUNK), FF_CHUNK)
@@ -672,7 +695,11 @@
         back = (back * pre_ref[:, span].astype(f32)).astype(bf16)
         pre_ref[:, span] = back
         hidden_sum_ref[0:1, span] = jnp.sum(back.astype(f32), axis=0, keepdims=True)
-        back_v[...] += dot_nt(back, fc1_v[:, span])
+
+    stores[4].start()
+    for i in range(2):
+        cols = slice(i * half, (i + 1) * half)
+        back_v[:, cols] = dot_nt(pre_ref[...], fc1_v[cols, :])
 
     @functools.partial(rows_of, total_rows)
     def _(rows):
@@ -692,6 +719,8 @@
     for j, (ref, at) in enumerate(((up_own_ref, 0), (up_give_ref, 0), (up_own_ref, 1), (up_give_ref, 1))):
         grad = dot_nt(mid_low_ref[...], proj_v[j * heads : (j + 1) * heads, :])
         ref[:, at * heads : (at + 1) * heads] = grad.astype(bf16)
+    for store in stores:
+        store.wait()
 
 
 def middle_block(table, factor, att, inputs, target, valid, vectors, smalls, pieces):
@@ -721,16 +750,22 @@
             jax.ShapeDtypeStruct((8, width), f32),
         ),
         in_specs=[smem] * 2 + [vmem] * 6 + [anywhere] * 10,
-        out_specs=[vmem] * 11,
+        out_specs=[anywhere] * 5 + [vmem] * 6,
         scratch_shapes=[
             pltpu.VMEM((width, hidden), bf16),
             pltpu.VMEM((hidden, width), bf16),
             pltpu.VMEM((width, width), bf16),
             pltpu.VMEM((rows, width), f32),
             pltpu.VMEM((rows, width), f32),
+            pltpu.VMEM((rows, width), bf16),
+            pltpu.VMEM((rows, hidden), bf16),
+            pltpu.VMEM((rows, hidden), bf16),
+            pltpu.VMEM((rows, width), bf16),
+            pltpu.VMEM((rows, width), bf16),
             pltpu.SemaphoreType.DMA((hidden // FF_CHUNK,)),
             pltpu.SemaphoreType.DMA,
             pltpu.SemaphoreType.DMA,
+            pltpu.SemaphoreType.DMA((5,)),
         ],
         compiler_params=pltpu.CompilerParams(vmem_limit_bytes=62 << 20),
         cost_estimate=pl.CostEstimate(
@@ -1096,16 +1131,17 @@
 
 
 def finish_kernel(part_rows, places_ref, *refs):
-    pieces, (fc2_ref, fc1_ref, proj_ref) = refs[:4], refs[4:]
+    pieces, (fc2_ref, fc1_ref, proj_ref) = refs[:2], refs[2:]
     half, sub = fc1_ref.shape[0], pieces[0].shape[1]
-    for s, piece in enumerate(pieces):
+    for s in range(4):
+        piece, base = pieces[s // 2], (s % 2) * (pieces[0].shape[0] // 2)
         at = places_ref[s]
         rows = pl.ds(pl.multiple_of(at * sub, sub), sub)
-        fc2_ref[rows, :] = piece[0:half, :].astype(jnp.float32).T
-        fc1_ref[:, rows] = piece[half : 2 * half, :].astype(jnp.float32)
+        fc2_ref[rows, :] = piece[base : base + half, :].astype(jnp.float32).T
+        fc1_ref[:, rows] = piece[base + half : base + 2 * half, :].astype(jnp.float32)
         rows = pl.ds(pl.multiple_of(at * part_rows, part_rows), part_rows)
         for i in range(2):
-            low = 2 * half + i * part_rows
+            low = base + 2 * half + i * part_rows
             proj_ref[rows, i * sub : (i + 1) * sub] = piece[low : low + part_rows, :].astype(jnp.float32)
 
 
@@ -1120,7 +1156,7 @@
 
 def finish(places, pieces, part_rows):
     rows, sub = pieces[0].shape
-    half = (rows - 2 * part_rows) // 2
+    half = (rows // 2 - 2 * part_rows) // 2
     vmem = pl.BlockSpec(memory_space=pltpu.VMEM)
     return pl.pallas_call(
         functools.partial(finish_kernel, part_rows),
@@ -1129,7 +1165,7 @@
             jax.ShapeDtypeStruct((half, 4 * sub), jnp.float32),
             jax.ShapeDtypeStruct((4 * part_rows, half), jnp.float32),
         ),
-        in_specs=[pl.BlockSpec(memory_space=pltpu.SMEM)] + [vmem] * 4,
+        in_specs=[pl.BlockSpec(memory_space=pltpu.SMEM)] + [vmem] * 2,
         out_specs=[vmem] * 3,
         cost_estimate=small_cost(100000000),
         name="finish",
@@ -1431,7 +1467,7 @@
         far_grads_kernel,
         [((VECTORS, half), f32), ((half + slots, columns), bf16), ((half, columns), f32)],
         "far_grads",
-        *(turned, tie(grad_far, norm_give, near_taken), sums, hidden_sum, norm_sums, near_sums, far_sums),
+        *(turned, tie(grad_far, norm_give, near_taken, *fc1_cols), sums, hidden_sum, norm_sums, near_sums, far_sums),
     )
     row_taken = over_row(row_give)
     fc1_cols = all_tied(fc1_cols, row_give)
@@ -1466,7 +1502,7 @@
         "after_plane",
         *(near_own, far_own, vec_sum, *plane_taken),
     )
-    mine_y = over_dp(mine_two, 2)
+    mine_y = over_dp(tie(mine_two, col_give), 2)
     col_taken = [over_col(vec_give, 1), over_col(col_give, 2), over_col(vec_give, 3)]
     norm_taken = tie(norm_taken, col_give)
     grad_states = last_norm(flip, norm_own, norm_taken, states, grad_mid, vectors)
@@ -1478,10 +1514,7 @@
         *(near_own, vec_sum, *all_tied(col_taken, grad_states)),
     )
     qkv_back = [over_dp(qkv_mine, s) for s in (1, 2, 3)]
-    mine_y = tie(mine_y, qkv_mine)
-    rows = mine.shape[0]
-    pieces = [mine_two[:rows], mine_two[rows:], mine_y[:rows], mine_y[rows:]]
-    fc2_grad, fc1_grad, proj_grad = finish(places, pieces, part_rows)
+    fc2_grad, fc1_grad, proj_grad = finish(places, [mine_two, tie(mine_y, qkv_mine)], part_rows)
     qkv_grad = finish_qkv(places, [qkv_mine, *all_tied(qkv_back, fc2_grad)]).transpose(1, 0, 2)
 
     fc1_bias_grad = lax.dynamic_index_in_dim(vec_total[6:14].reshape(4, 4, sub), col, 1, False)

time: 520 us -> 516 us (level)
    unnamed x141 -> x147, local copies, waits for them, and re-layouts: 28.3 us -> 30.5 us
  transfers between devices with their start and end apart: 53 -> 53, of which waited for: 8 -> 9; matrix products, arithmetic and copies ran while one was open for 17% -> 17% of each run, Pallas kernels for 41% -> 40%
where the time goes in v4:
time: 516 us; the launch traced here: 507 us
  Pallas kernels  269 us (52%)
  waiting for transfers between devices  63.9 us (12%)
  local copies, waits for them, and re-layouts  57.4 us (11%)
  starting transfers between devices  54.4 us (11%)
  matrix products  34.8 us (7%)
  other arithmetic  22.6 us (4%)
    pallas_call x4, Pallas kernels, attend_back(): pl.pallas_call(functools.partial(attend_back_kernel, first, lane, before...  83.9 us
    ppermute x53, waiting for transfers between devices, swap(): return lax.ppermute(values, axis, [(i, i ^ mask) for i in range(size)])  63.9 us
    pallas_call x1, Pallas kernels, middle_block(): pl.pallas_call(middle_kernel, out_shape=(result(width, bf16), result(hidd...  56 us
    ppermute x53, starting transfers between devices, swap(): return lax.ppermute(values, axis, [(i, i ^ mask) for i in range(size)])  54.4 us
    pallas_call x4, Pallas kernels, attend(): pl.pallas_call(functools.partial(attend_kernel, first), out_shape=(jax.Sh...  47 us
    pallas_call x9, Pallas kernels, on_chip(): pl.pallas_call(kernel, out_shape=tuple((jax.ShapeDtypeStruct(*s) for s in...  31 us
    unnamed x147, local copies, waits for them, and re-layouts  30.5 us
    dot_general x6, matrix products, dot_tn(): lax.dot_general(a, b, (((0,), (0,)), ((), ())), preferred_element_type=jn...  25.1 us
  transfers between devices with their start and end apart: 53, of which 9 were waited for; matrix products, arithmetic and copies ran while one was open for 17% of the time, Pallas kernels for 40%

profile of v4, /device:TPU:0, one launch (start us, length us, event | category | flops | bytes accessed | tf_op | source)
XLA Modules:
  0.0 506.5 jit_solution(12120920072644320703)
XLA Ops:
  30.7 16.3 %collective-permute-done.2 = bf16[1552,256]{1,0:T(8,128)(2,1)} collective-permute-done((bf16[1552,256]{1,0:T(8,128)(2,1)}, bf16[1552,256]{1,0:T(8,128)(2,1)}, u32[]{:S(2)}, u32[]{:S(2)}) %collective-permute-start.2) | collective-permute-done | bytes 794656 | tf_op jit(solution)/shard_map/ppermute | solution.py:779
  55.2 9.2 %collective-permute-done.1.other_states = bf16[784,1024]{1,0:T(8,128)(2,1)} collective-permute-done((bf16[784,1024]{1,0:T(8,128)(2,1)S(1)}, bf16[784,1024]{1,0:T(8,128)(2,1)}, u32[]{:S(2)}, u32[]{:S(2)}) %collective-permute-start.1) | collective-permute-done | bytes 1605664 | tf_op jit(solution)/shard_map/ppermute | solution.py:779
  74.4 4.6 fusion.12.packed_ref
  86.9 8.2 %collective-permute-done.10 = bf16[2336,256]{1,0:T(8,128)(2,1)} collective-permute-done((bf16[2336,256]{1,0:T(8,128)(2,1)S(1)}, bf16[2336,256]{1,0:T(8,128)(2,1)}, u32[]{:S(2)}, u32[]{:S(2)}) %collective-permute-start.10) | collective-permute-done | bytes 1196064 | tf_op jit(solution)/shard_map/ppermute | solution.py:779
  95.4 12.7 %attend.4 = (bf16[800,256]{1,0:T(8,128)(2,1)S(1)}, f32[7,8,512]{2,1,0:T(8,128)S(1)}) custom-call(bf16[1568,768]{1,0:T(8,128)(2,1)S(1)} %fusion.12.packed_ref, f32[1568,128]{1,0:T(8,128)S(1)} %broadcast_in_dim.47.bias_ref), custom_call_target="tpu_custom_call" | custom-call | flops 2569011200 | bytes 6291456 | tf_op jit(solution)/shard_map/attend/pallas_call | solution.py:454
  115.5 10.9 %attend.5 = (bf16[768,256]{1,0:T(8,128)(2,1)S(1)}, f32[6,8,512]{2,1,0:T(8,128)S(1)}) custom-call(bf16[1568,768]{1,0:T(8,128)(2,1)S(1)} %fusion.12.packed_ref, f32[1568,128]{1,0:T(8,128)S(1)} %broadcast_in_dim.47.bias_ref), custom_call_target="tpu_custom_call" | custom-call | flops 2466250752 | bytes 6291456 | tf_op jit(solution)/shard_map/attend/pallas_call | solution.py:454
  131.7 5.2 %fusion.13.packed_ref = bf16[1568,768]{1,0:T(8,128)(2,1)S(1)} fusion(bf16[1568,1024]{0,1:T(8,128)(2,1)} %copy-done.31, bf16[1024,768]{1,0:T(8,128)(2,1)} %far_qkv.1.w_far, f32[768]{0:T(1024)S(1)} %get-tuple-element.313, bf16[768]{0:T(1024)(128)(2,1)S(1)} %select_convert_fusion.1), kind=kOutput, calls=%fused_computation.26 | convolution fusion | flops 2469863424 | bytes 7197184 | tf_op jit(solution)/shard_map/dot_general | solution.py:1297
  136.8 12.2 %attend.6 = (bf16[800,256]{1,0:T(8,128)(2,1)S(1)}, f32[7,8,512]{2,1,0:T(8,128)S(1)}) custom-call(bf16[1568,768]{1,0:T(8,128)(2,1)S(1)} %fusion.13.packed_ref, f32[1568,128]{1,0:T(8,128)S(1)} %broadcast_in_dim.47.bias_ref), custom_call_target="tpu_custom_call" | custom-call | flops 2569011200 | bytes 6291456 | tf_op jit(solution)/shard_map/attend/pallas_call | solution.py:454
  155.3 11.1 %attend.7 = (bf16[768,256]{1,0:T(8,128)(2,1)S(1)}, f32[6,8,512]{2,1,0:T(8,128)S(1)}) custom-call(bf16[1568,768]{1,0:T(8,128)(2,1)S(1)} %fusion.13.packed_ref, f32[1568,128]{1,0:T(8,128)S(1)} %broadcast_in_dim.47.bias_ref), custom_call_target="tpu_custom_call" | custom-call | flops 2466250752 | bytes 6291456 | tf_op jit(solution)/shard_map/attend/pallas_call | solution.py:454
  179.5 56.0 %middle_block.1 = (bf16[784,1024]{1,0:T(8,128)(2,1)}, bf16[784,4096]{1,0:T(8,128)(2,1)}, bf16[784,4096]{1,0:T(8,128)(2,1)}, bf16[784,1024]{1,0:T(8,128)(2,1)}, b...) custom-call(s32[29]{0:T(128)} %stack.163.table_ref, ...), custom_call_target="tpu_custom_call" | custom-call | flops 6576668672 | bytes 46137344 | tf_op jit(solution)/shard_map/middle_block/pallas_call | solution.py:737
  235.6 7.8 %convolution_convert_fusion.1 = bf16[512,4096]{1,0:T(8,128)(2,1)S(1)} fusion(bf16[784,4096]{1,0:T(8,128)(2,1)} %get-tuple-element.178.big_ref, bf16[784,1024]{1,0:T(8,128)(2,1)} %get-tuple-element.177.small_ref), kind=kOutput, calls=%fused_computation.1 | convolution fusion | flops 3290431488 | bytes 11419648 | tf_op jit(solution)/shard_map/dot_general | solution.py:347
  243.9 6.8 %convolution_convert_fusion = bf16[512,4096]{1,0:T(8,128)(2,1)} fusion(bf16[784,4096]{1,0:T(8,128)(2,1)S(1)} %copy-done.37, bf16[784,1024]{1,0:T(8,128)(2,1)S(1)} %copy-done.6), kind=kOutput, calls=%fused_computation | convolution fusion | flops 3290431488 | bytes 11419648 | tf_op jit(solution)/shard_map/dot_general | solution.py:347
  254.7 8.7 %wide_grads.2 = (bf16[512,1024]{1,0:T(8,128)(2,1)S(1)}, bf16[512,1024]{1,0:T(8,128)(2,1)}, bf16[512,1024]{1,0:T(8,128)(2,1)S(1)}, bf16[512,1024]{1,0:T(8,128)(2,1)}) custom-call(s32[8]{0:T(128)S(1)} %copy-done.16, bf16[784,1024]{1,0:T(8,128)(2,1)S(1)} %copy-done.7, bf16[784,4096]{1,0:T(8,128)(2,1)} %get-tuple-element.178.big_ref, ...), custom_call_target="tpu_custom_call" | custom-call | flops 3000000000 | tf_op jit(solution)/shard_map/wide_grads/pallas_call | solution.py:1082
  267.5 9.8 %wide_grads.3 = (bf16[512,1280]{1,0:T(8,128)(2,1)S(1)}, bf16[512,1280]{1,0:T(8,128)(2,1)S(1)}, bf16[512,1280]{1,0:T(8,128)(2,1)S(1)}, bf16[512,1280]{1,0:T(8,128)(2,1)}) custom-call(s32[8]{0:T(128)S(1)} %copy-done.16, bf16[784,1024]{1,0:T(8,128)(2,1)S(1)} %copy-done.6, bf16[784,4096]{1,0:T(8,128)(2,1)} %get-tuple-element.184.big_ref, ...), custom_call_target="tpu_custom_call" | custom-call | flops 3000000000 | tf_op jit(solution)/shard_map/wide_grads/pallas_call | solution.py:1082
  282.2 19.6 %attend_back.4 = (bf16[768,256]{1,0:T(8,128)(2,1)S(1)}, f32[1568,256]{1,0:T(8,128)}, f32[1568,256]{1,0:T(8,128)}) custom-call(bf16[1568,768]{1,0:T(8,128)(2,1)} %copy-done.21, f32[1568,128]{1,0:T(8,128)S(1)} %broadcast_in_dim.47.bias_ref, f32[6,8,512]{2,1,0:T(8,128)S(1)} %get-tuple-element.189.lse_ref, bf16[768,256]{1,0:T(8,128)(2,1)S(1)} %get-tuple-element.163.att_ref, ...), custom_call_target="tpu_custom_call" | custom-call | flops 4932501504 | bytes 10485760 | tf_op jit(solution)/shard_map/attend_back/pallas_call | solution.py:488
  309.3 19.4 %attend_back.5 = (bf16[768,256]{1,0:T(8,128)(2,1)S(1)}, f32[1568,256]{1,0:T(8,128)}, f32[1568,256]{1,0:T(8,128)}) custom-call(bf16[1568,768]{1,0:T(8,128)(2,1)} %copy-done.20, f32[1568,128]{1,0:T(8,128)S(1)} %broadcast_in_dim.47.bias_ref, f32[6,8,512]{2,1,0:T(8,128)S(1)} %copy-done.27, bf16[768,256]{1,0:T(8,128)(2,1)S(1)} %copy-done.15, ...), custom_call_target="tpu_custom_call" | custom-call | flops 4932501504 | bytes 10485760 | tf_op jit(solution)/shard_map/attend_back/pallas_call | solution.py:488
  341.8 22.4 %attend_back.6 = (bf16[1568,768]{1,0:T(8,128)(2,1)}, f32[1,768]{1,0:T(1,128)S(1)}) custom-call(bf16[1568,768]{1,0:T(8,128)(2,1)} %copy-done.21, f32[1568,128]{1,0:T(8,128)S(1)} %broadcast_in_dim.47.bias_ref, f32[7,8,512]{2,1,0:T(8,128)S(1)} %get-tuple-element.215.lse_ref, bf16[800,256]{1,0:T(8,128)(2,1)S(1)} %get-tuple-element.159.att_ref, ...), custom_call_target="tpu_custom_call" | custom-call | flops 5138022400 | bytes 10485760 | tf_op jit(solution)/shard_map/attend_back/pallas_call | solution.py:488
  382.6 22.6 %attend_back.7 = (bf16[1568,768]{1,0:T(8,128)(2,1)}, f32[1,768]{1,0:T(1,128)S(1)}) custom-call(bf16[1568,768]{1,0:T(8,128)(2,1)} %copy-done.20, f32[1568,128]{1,0:T(8,128)S(1)} %broadcast_in_dim.47.bias_ref, f32[7,8,512]{2,1,0:T(8,128)S(1)} %get-tuple-element.233.lse_ref, bf16[800,256]{1,0:T(8,128)(2,1)S(1)} %copy-done.13, ...), custom_call_target="tpu_custom_call" | custom-call | flops 5138022400 | bytes 10485760 | tf_op jit(solution)/shard_map/attend_back/pallas_call | solution.py:488
  406.9 11.7 %token_back.1 = (f32[784,1024]{1,0:T(8,128)}, bf16[784,1024]{1,0:T(8,128)(2,1)S(1)}, f32[2,1024]{1,0:T(2,128)S(1)}) custom-call(s32[1]{0:T(128)} %bitcast.27.flip_ref, bf16[1568,768]{1,0:T(8,128)(2,1)S(1)} %copy-done.5, bf16[1568,768]{1,0:T(8,128)(2,1)S(1)} %copy-done.2, bf16[1024,768]{1,0:T(8,128)(2,1)S(1)} %pad_maximum_fusion.2.w_near, ...), custom_call_target="tpu_custom_call" | custom-call | flops 100000000 | tf_op jit(solution)/shard_map/token_back/pallas_call | solution.py:924
  420.1 7.1 %far_grads.1 = (f32[32,512]{1,0:T(8,128)}, bf16[576,768]{1,0:T(8,128)(2,1)}, f32[512,768]{1,0:T(8,128)}) custom-call(bf16[1024,1568]{1,0:T(8,128)(2,1)} %bitcast.64, bf16[1568,768]{1,0:T(8,128)(2,1)} %get-tuple-element.238.far_ref.grad_ref, f32[8,1024]{1,0:T(8,128)} %get-tuple-element.239.sums_ref, f32[1,4096]{1,0:T(1,128)} %get-tuple-element.240.hidden_ref, ...), custom_call_target="tpu_custom_call" | custom-call | flops 100000000 | tf_op jit(solution)/shard_map/far_grads/pallas_call | solution.py:1041
  438.3 8.2 %collective-permute-done.42 = bf16[1152,256]{1,0:T(8,128)(2,1)} collective-permute-done((bf16[1152,256]{1,0:T(8,128)(2,1)}, bf16[1152,256]{1,0:T(8,128)(2,1)}, u32[]{:S(2)}, u32[]{:S(2)}) %collective-permute-start.42) | collective-permute-done | bytes 589856 | tf_op jit(solution)/shard_map/ppermute | solution.py:779
  447.8 11.8 %collective-permute-done.45.refs_2_ = bf16[192,768]{1,0:T(8,128)(2,1)S(1)} collective-permute-done((bf16[192,768]{1,0:T(8,128)(2,1)}, bf16[192,768]{1,0:T(8,128)(2,1)S(1)}, u32[]{:S(2)}, u32[]{:S(2)}) %collective-permute-start.45) | collective-permute-done | bytes 294944 | tf_op jit(solution)/shard_map/ppermute | solution.py:779
  467.6 8.0 %last_norm.1 = bf16[784,1024]{1,0:T(8,128)(2,1)} custom-call(s32[1]{0:T(128)} %bitcast.27.flip_ref, f32[784,1024]{1,0:T(8,128)} %get-tuple-element.265.own_ref, bf16[784,1024]{1,0:T(8,128)(2,1)} %collective-permute-done.43.taken_ref, bf16[784,1024]{1,0:T(8,128)(2,1)} %states_ref, f32[784,1024]{1,0:T(8,128)} %get-tuple-element.268.mid_ref, f32[6,1024]{1,0:T(8,128)} %copy-done.46), custom_call_target="tpu_custom_call" | custom-call | flops 500000000 | tf_op jit(solution)/shard_map/last_norm/pallas_call | solution.py:958
  476.3 4.8 collective-permute-done.47.two_ref
  (334 shorter events, 187.0 us)
Async XLA Ops:
  0.7 46.3 %collective-permute-start.3 = (bf16[512,1024]{1,0:T(8,128)(2,1)}, bf16[512,1024]{1,0:T(8,128)(2,1)}, u32[]{:S(2)}, u32[]{:S(2)}) collective-permute-start(bf16[512,1024]{1,0:T(8,128)(2,1)} %fc1_own.1), channel_id=1, source_target_pairs={{0,4},{4,0},{1,5},{5,1},{2,6},{6,2},{3,7},{7,3},{8,12},{12,8},{9,1... | collective-permute-start | bytes 3145736 | tf_op jit(solution)/shard_map/ppermute | solution.py:779
  1.2 45.8 %collective-permute-start.4 = (bf16[1024,512]{1,0:T(8,128)(2,1)}, bf16[1024,512]{1,0:T(8,128)(2,1)}, u32[]{:S(2)}, u32[]{:S(2)}) collective-permute-start(bf16[1024,512]{1,0:T(8,128)(2,1)} %fc2_own.1), channel_id=1, source_target_pairs={{0,4},{4,0},{1,5},{5,1},{2,6},{6,2},{3,7},{7,3},{8,12},{12,8},{9,1... | collective-permute-start | bytes 3145736 | tf_op jit(solution)/shard_map/ppermute | solution.py:779
  7.5 39.5 %collective-permute-start.2 = (bf16[1552,256]{1,0:T(8,128)(2,1)}, bf16[1552,256]{1,0:T(8,128)(2,1)}, u32[]{:S(2)}, u32[]{:S(2)}) collective-permute-start(bf16[1552,256]{1,0:T(8,128)(2,1)} %make_slab.1), channel_id=1, source_target_pairs={{0,2},{1,3},{2,0},{3,1},{4,6},{5,7},{6,4},{7,5},{8,10},{9,11},{10,... | collective-permute-start | bytes 2383880 | tf_op jit(solution)/shard_map/ppermute | solution.py:779
  11.6 52.8 %collective-permute-start.1 = (bf16[784,1024]{1,0:T(8,128)(2,1)S(1)}, bf16[784,1024]{1,0:T(8,128)(2,1)}, u32[]{:S(2)}, u32[]{:S(2)}) collective-permute-start(bf16[784,1024]{1,0:T(8,128)(2,1)S(1)} %copy-done), channel_id=1, source_target_pairs={{0,1},{1,0},{2,3},{3,2},{4,5},{5,4},{6,7},{7,6},{8,9},{9,8},{10,11... | collective-permute-start | bytes 4816904 | tf_op jit(solution)/shard_map/ppermute | solution.py:779
  30.6 43.2 %collective-permute-start.6 = (bf16[512,768]{1,0:T(8,128)(2,1)}, bf16[512,768]{1,0:T(8,128)(2,1)}, u32[]{:S(2)}, u32[]{:S(2)}) collective-permute-start(bf16[512,768]{1,0:T(8,128)(2,1)} %copy.56), channel_id=1, source_target_pairs={{0,4},{4,0},{1,5},{5,1},{2,6},{6,2},{3,7},{7,3},{8,12},{12,8},{9,1... | collective-permute-start | bytes 2359304 | tf_op jit(solution)/shard_map/ppermute | solution.py:779
  48.1 30.9 %collective-permute-start.8 = (bf16[1552,256]{1,0:T(8,128)(2,1)}, bf16[1552,256]{1,0:T(8,128)(2,1)}, u32[]{:S(2)}, u32[]{:S(2)}) collective-permute-start(bf16[1552,256]{1,0:T(8,128)(2,1)} %collective-permute-done.2), channel_id=1, source_target_pairs={{0,16},{8,24},{16,0},{24,8},{1,17},{9,25},{17,1},{25,9},{2,18},{10... | collective-permute-start | bytes 2383880 | tf_op jit(solution)/shard_map/ppermute | solution.py:779
  49.8 29.3 %collective-permute-start.7 = (bf16[1552,256]{1,0:T(8,128)(2,1)}, bf16[1552,256]{1,0:T(8,128)(2,1)}, u32[]{:S(2)}, u32[]{:S(2)}) collective-permute-start(bf16[1552,256]{1,0:T(8,128)(2,1)} %collective-permute-done.2), channel_id=1, source_target_pairs={{0,8},{8,0},{16,24},{24,16},{1,9},{9,1},{17,25},{25,17},{2,10},{10... | collective-permute-start | bytes 2383880 | tf_op jit(solution)/shard_map/ppermute | solution.py:779
  108.3 28.6 %collective-permute-start.12 = (bf16[784,256]{1,0:T(8,128)(2,1)S(1)}, bf16[784,256]{1,0:T(8,128)(2,1)}, u32[]{:S(2)}, u32[]{:S(2)}) collective-permute-start(bf16[784,256]{1,0:T(8,128)(2,1)S(1)} %slice.125), channel_id=1, source_target_pairs={{0,1},{1,0},{2,3},{3,2},{4,5},{5,4},{6,7},{7,6},{8,9},{9,8},{10,11... | collective-permute-start | bytes 1204232 | tf_op jit(solution)/shard_map/ppermute | solution.py:779
  110.1 39.1 %collective-permute-start.15 = (bf16[2336,256]{1,0:T(8,128)(2,1)}, bf16[2336,256]{1,0:T(8,128)(2,1)}, u32[]{:S(2)}, u32[]{:S(2)}) collective-permute-start(bf16[2336,256]{1,0:T(8,128)(2,1)} %collective-permute-done.10), channel_id=1, source_target_pairs={{0,16},{8,24},{16,0},{24,8},{1,17},{9,25},{17,1},{25,9},{2,18},{10... | collective-permute-start | bytes 3588104 | tf_op jit(solution)/shard_map/ppermute | solution.py:779
  111.6 37.5 %collective-permute-start.14 = (bf16[2336,256]{1,0:T(8,128)(2,1)}, bf16[2336,256]{1,0:T(8,128)(2,1)}, u32[]{:S(2)}, u32[]{:S(2)}) collective-permute-start(bf16[2336,256]{1,0:T(8,128)(2,1)} %collective-permute-done.10), channel_id=1, source_target_pairs={{0,8},{8,0},{16,24},{24,16},{1,9},{9,1},{17,25},{25,17},{2,10},{10... | collective-permute-start | bytes 3588104 | tf_op jit(solution)/shard_map/ppermute | solution.py:779
  264.5 38.1 %collective-permute-start.21 = (bf16[512,1024]{1,0:T(8,128)(2,1)}, bf16[512,1024]{1,0:T(8,128)(2,1)}, u32[]{:S(2)}, u32[]{:S(2)}) collective-permute-start(bf16[512,1024]{1,0:T(8,128)(2,1)} %get-tuple-element.180), channel_id=1, source_target_pairs={{0,8},{8,0},{16,24},{24,16},{1,9},{9,1},{17,25},{25,17},{2,10},{10... | collective-permute-start | bytes 3145736 | tf_op jit(solution)/shard_map/ppermute | solution.py:779
  266.0 36.6 %collective-permute-start.24 = (bf16[512,1024]{1,0:T(8,128)(2,1)}, bf16[512,1024]{1,0:T(8,128)(2,1)}, u32[]{:S(2)}, u32[]{:S(2)}) collective-permute-start(bf16[512,1024]{1,0:T(8,128)(2,1)} %get-tuple-element.181), channel_id=1, source_target_pairs={{0,16},{8,24},{16,0},{24,8},{1,17},{9,25},{17,1},{25,9},{2,18},{10... | collective-permute-start | bytes 3145736 | tf_op jit(solution)/shard_map/ppermute | solution.py:779
  279.4 50.0 %collective-permute-start.28 = (bf16[512,1280]{1,0:T(8,128)(2,1)}, bf16[512,1280]{1,0:T(8,128)(2,1)}, u32[]{:S(2)}, u32[]{:S(2)}) collective-permute-start(bf16[512,1280]{1,0:T(8,128)(2,1)} %get-tuple-element.187), channel_id=1, source_target_pairs={{0,16},{8,24},{16,0},{24,8},{1,17},{9,25},{17,1},{25,9},{2,18},{10... | collective-permute-start | bytes 3932168 | tf_op jit(solution)/shard_map/ppermute | solution.py:779
  280.0 49.5 %collective-permute-start.27 = (bf16[512,1280]{1,0:T(8,128)(2,1)S(1)}, bf16[512,1280]{1,0:T(8,128)(2,1)}, u32[]{:S(2)}, u32[]{:S(2)}) collective-permute-start(bf16[512,1280]{1,0:T(8,128)(2,1)S(1)} %get-tuple-element.186), channel_id=1, source_target_pairs={{0,8},{8,0},{16,24},{24,16},{1,9},{9,1},{17,25},{25,17},{2,10},{10... | collective-permute-start | bytes 3932168 | tf_op jit(solution)/shard_map/ppermute | solution.py:779
  280.5 58.8 %collective-permute-start.29 = (bf16[784,512]{1,0:T(8,128)(2,1)}, bf16[784,512]{1,0:T(8,128)(2,1)}, u32[]{:S(2)}, u32[]{:S(2)}) collective-permute-start(bf16[784,512]{1,0:T(8,128)(2,1)} %get-tuple-element.216), channel_id=1, source_target_pairs={{0,1},{1,0},{2,3},{3,2},{4,5},{5,4},{6,7},{7,6},{8,9},{9,8},{10,11... | collective-permute-start | bytes 2408456 | tf_op jit(solution)/shard_map/ppermute | solution.py:779
  306.3 28.4 %collective-permute-start.25 = (bf16[256,1024]{1,0:T(8,128)(2,1)}, bf16[256,1024]{1,0:T(8,128)(2,1)}, u32[]{:S(2)}, u32[]{:S(2)}) collective-permute-start(bf16[256,1024]{1,0:T(8,128)(2,1)} %get-tuple-element.195), channel_id=1, source_target_pairs={{0,16},{8,24},{16,0},{24,8},{1,17},{9,25},{17,1},{25,9},{2,18},{10... | collective-permute-start | bytes 1572872 | tf_op jit(solution)/shard_map/ppermute | solution.py:779
  333.7 31.1 %collective-permute-start.30 = (bf16[256,1280]{1,0:T(8,128)(2,1)}, bf16[256,1280]{1,0:T(8,128)(2,1)}, u32[]{:S(2)}, u32[]{:S(2)}) collective-permute-start(bf16[256,1280]{1,0:T(8,128)(2,1)} %get-tuple-element.212), channel_id=1, source_target_pairs={{0,16},{8,24},{16,0},{24,8},{1,17},{9,25},{17,1},{25,9},{2,18},{10... | collective-permute-start | bytes 1966088 | tf_op jit(solution)/shard_map/ppermute | solution.py:779
  334.1 30.7 %collective-permute-start.34 = (bf16[256,1280]{1,0:T(8,128)(2,1)}, bf16[256,1280]{1,0:T(8,128)(2,1)}, u32[]{:S(2)}, u32[]{:S(2)}) collective-permute-start(bf16[256,1280]{1,0:T(8,128)(2,1)} %get-tuple-element.213), channel_id=1, source_target_pairs={{0,8},{8,0},{16,24},{24,16},{1,9},{9,1},{17,25},{25,17},{2,10},{10... | collective-permute-start | bytes 1966088 | tf_op jit(solution)/shard_map/ppermute | solution.py:779
  373.4 45.7 %collective-permute-start.37 = (bf16[640,256]{1,0:T(8,128)(2,1)}, bf16[640,256]{1,0:T(8,128)(2,1)S(1)}, u32[]{:S(2)}, u32[]{:S(2)}) collective-permute-start(bf16[640,256]{1,0:T(8,128)(2,1)} %get-tuple-element.228), channel_id=1, source_target_pairs={{0,1},{1,0},{2,3},{3,2},{4,5},{5,4},{6,7},{7,6},{8,9},{9,8},{10,11... | collective-permute-start | bytes 983048 | tf_op jit(solution)/shard_map/ppermute | solution.py:779
  373.5 45.6 %collective-permute-start.38 = (bf16[640,256]{1,0:T(8,128)(2,1)}, bf16[640,256]{1,0:T(8,128)(2,1)S(1)}, u32[]{:S(2)}, u32[]{:S(2)}) collective-permute-start(bf16[640,256]{1,0:T(8,128)(2,1)} %get-tuple-element.229), channel_id=1, source_target_pairs={{0,2},{1,3},{2,0},{3,1},{4,6},{5,7},{6,4},{7,5},{8,10},{9,11},{10,... | collective-permute-start | bytes 983048 | tf_op jit(solution)/shard_map/ppermute | solution.py:779
  375.4 43.7 %collective-permute-start.39 = (bf16[640,256]{1,0:T(8,128)(2,1)}, bf16[640,256]{1,0:T(8,128)(2,1)}, u32[]{:S(2)}, u32[]{:S(2)}) collective-permute-start(bf16[640,256]{1,0:T(8,128)(2,1)} %get-tuple-element.230), channel_id=1, source_target_pairs={{0,3},{1,2},{2,1},{3,0},{4,7},{5,6},{6,5},{7,4},{8,11},{9,10},{10,... | collective-permute-start | bytes 983048 | tf_op jit(solution)/shard_map/ppermute | solution.py:779
  381.0 38.2 %collective-permute-start.36 = (bf16[256,768]{1,0:T(8,128)(2,1)S(1)}, bf16[256,768]{1,0:T(8,128)(2,1)S(1)}, u32[]{:S(2)}, u32[]{:S(2)}) collective-permute-start(bf16[256,768]{1,0:T(8,128)(2,1)S(1)} %pad_maximum_fusion.5), channel_id=1, source_target_pairs={{0,8},{8,0},{16,24},{24,16},{1,9},{9,1},{17,25},{25,17},{2,10},{10... | collective-permute-start | bytes 1179656 | tf_op jit(solution)/shard_map/ppermute | solution.py:779
  419.1 40.4 %collective-permute-start.43 = (bf16[784,1024]{1,0:T(8,128)(2,1)S(1)}, bf16[784,1024]{1,0:T(8,128)(2,1)}, u32[]{:S(2)}, u32[]{:S(2)}) collective-permute-start(bf16[784,1024]{1,0:T(8,128)(2,1)S(1)} %get-tuple-element.237), channel_id=1, source_target_pairs={{0,1},{1,0},{2,3},{3,2},{4,5},{5,4},{6,7},{7,6},{8,9},{9,8},{10,11... | collective-permute-start | bytes 4816904 | tf_op jit(solution)/shard_map/ppermute | solution.py:779
  462.8 33.1 %collective-permute-start.50 = (bf16[2304,256]{1,0:T(8,128)(2,1)S(1)}, bf16[2304,256]{1,0:T(8,128)(2,1)S(1)}, u32[]{:S(2)}, u32[]{:S(2)}) collective-permute-start(bf16[2304,256]{1,0:T(8,128)(2,1)S(1)} %pad_maximum_fusion.4.refs_0_), channel_id=1, source_target_pairs={{0,16},{8,24},{16,0},{24,8},{1,17},{9,25},{17,1},{25,9},{2,18},{10... | collective-permute-start | bytes 3538952 | tf_op jit(solution)/shard_map/ppermute | solution.py:779
  (98 other events, 1061.7 us)

commit v5 on v4

--- a/solution.py
+++ b/solution.py
@@ -518,7 +518,6 @@
 def middle_kernel(
     table_ref,
     factor_ref,
-    att_ref,
     input_ref,
     target_ref,
     valid_ref,
@@ -532,34 +531,39 @@
     proj_other,
     two_mine,
     two_theirs,
-    one_mine,
-    one_theirs,
-    out_hbm,
-    hidden_hbm,
-    pre_hbm,
-    norm_hbm,
-    grad_low_hbm,
-    mid_low_ref,
-    grad_mid_ref,
-    up_own_ref,
-    up_give_ref,
-    hidden_sum_ref,
-    sums_ref,
-    fc1_v,
-    fc2_v,
-    proj_v,
-    middle_v,
-    back_v,
-    out_ref,
-    hidden_ref,
-    pre_ref,
-    norm_ref,
-    grad_low_ref,
-    sem_one,
-    sem_two,
-    sem_proj,
-    sem_out,
+    *refs,
 ):
+    one_mine, one_theirs, att_parts, refs = refs[:5], refs[5:10], refs[10:16], refs[16:]
+    (
+        att_hbm,
+        out_hbm,
+        hidden_hbm,
+        pre_hbm,
+        norm_hbm,
+        grad_low_hbm,
+        mid_low_ref,
+        grad_mid_ref,
+        up_own_ref,
+        up_give_ref,
+        hidden_sum_ref,
+        sums_ref,
+        fc1_v,
+        fc2_v,
+        proj_v,
+        middle_v,
+        back_v,
+        out_ref,
+        hidden_ref,
+        pre_ref,
+        norm_ref,
+        grad_low_ref,
+        att_ref,
+        sem_one,
+        sem_two,
+        sem_proj,
+        sem_att,
+        sem_out,
+    ) = refs
     stores = [
         pltpu.make_async_copy(source, target, sem_out.at[i])
         for i, (source, target) in enumerate(
@@ -569,11 +573,12 @@
                 (out_ref, out_hbm),
                 (grad_low_ref, grad_low_hbm),
                 (pre_ref, pre_hbm),
+                (att_ref, att_hbm),
             )
         )
     ]
     f32, bf16 = jnp.float32, jnp.bfloat16
-    total_rows = att_ref.shape[0]
+    total_rows = input_ref.shape[0]
     half = fc1_own.shape[0]
     sub = fc1_own.shape[1] // 4
     heads = proj_own.shape[0]
@@ -598,10 +603,20 @@
     for s in range(4):
         step = two_mine.shape[0] // 4
         sources.append((s, 2, two_mine, two_theirs, s * step))
-        step = one_mine.shape[0] // 4
-        sources.append((s, 1, one_mine, one_theirs, s * step))
-        sources.append((s, 3, one_mine, one_theirs, s * step + unit))
-
+        low, high = (3, 4) if s == 3 else (s, s)
+        sources.append((s, 1, one_mine[low], one_theirs[low], 0))
+        sources.append((s, 3, one_mine[high], one_theirs[high], 0 if s == 3 else unit))
+
+    early_rows = att_parts[0].shape[0]
+    for at in range(2):
+        soon, late, other = att_parts[3 * at : 3 * at + 3]
+        lanes = slice(2 * at * heads, (2 * at + 1) * heads)
+        pltpu.make_async_copy(soon, att_ref.at[0:early_rows, lanes], sem_att).start()
+        pltpu.make_async_copy(
+            late.at[0 : total_rows - early_rows], att_ref.at[early_rows:total_rows, lanes], sem_att
+        ).start()
+        lanes = slice((2 * at + 1) * heads, (2 * at + 2) * heads)
+        pltpu.make_async_copy(other, att_ref.at[:, lanes], sem_att).start()
     for side, ref in enumerate((proj_own, proj_other)):
         pltpu.make_async_copy(
             ref, proj_v.at[0:heads, side * half : (side + 1) * half], sem_proj
@@ -638,6 +653,8 @@
 
     sums_ref[...] = jnp.zeros_like(sums_ref)
 
+    pltpu.make_async_copy(att_ref, att_ref, sem_att).wait()
+    stores[5].start()
     pltpu.make_async_copy(proj_v, proj_v, sem_proj).wait()
     for i in range(2):
         cols = slice(i * half, (i + 1) * half)
@@ -723,8 +740,8 @@
         store.wait()
 
 
-def middle_block(table, factor, att, inputs, target, valid, vectors, smalls, pieces):
-    rows, width = att.shape
+def middle_block(table, factor, inputs, target, valid, vectors, smalls, pieces):
+    rows, width = inputs.shape
     hidden = 4 * pieces[0].shape[1]
     vmem = pl.BlockSpec(memory_space=pltpu.VMEM)
     smem = pl.BlockSpec(memory_space=pltpu.SMEM)
@@ -737,6 +754,7 @@
     return pl.pallas_call(
         middle_kernel,
         out_shape=(
+            result(width, bf16),
             result(width, bf16),
             result(hidden, bf16),
             result(hidden, bf16),
@@ -749,8 +767,8 @@
             jax.ShapeDtypeStruct((1, hidden), f32),
             jax.ShapeDtypeStruct((8, width), f32),
         ),
-        in_specs=[smem] * 2 + [vmem] * 6 + [anywhere] * 10,
-        out_specs=[anywhere] * 5 + [vmem] * 6,
+        in_specs=[smem] * 2 + [vmem] * 5 + [anywhere] * len(pieces),
+        out_specs=[anywhere] * 6 + [vmem] * 6,
         scratch_shapes=[
             pltpu.VMEM((width, hidden), bf16),
             pltpu.VMEM((hidden, width), bf16),
@@ -762,17 +780,19 @@
             pltpu.VMEM((rows, hidden), bf16),
             pltpu.VMEM((rows, width), bf16),
             pltpu.VMEM((rows, width), bf16),
+            pltpu.VMEM((rows, width), bf16),
             pltpu.SemaphoreType.DMA((hidden // FF_CHUNK,)),
             pltpu.SemaphoreType.DMA,
             pltpu.SemaphoreType.DMA,
-            pltpu.SemaphoreType.DMA((5,)),
+            pltpu.SemaphoreType.DMA,
+            pltpu.SemaphoreType.DMA((6,)),
         ],
         compiler_params=pltpu.CompilerParams(vmem_limit_bytes=62 << 20),
         cost_estimate=pl.CostEstimate(
             flops=2 * rows * width * hidden, bytes_accessed=44 << 20, transcendentals=0
         ),
         name="middle_block",
-    )(table, factor, att, inputs, target, valid, vectors, smalls, *pieces)
+    )(table, factor, inputs, target, valid, vectors, smalls, *pieces)
 
 
 def swap(values, axis, mask, size):
@@ -1298,7 +1318,17 @@
         add = jnp.concatenate([q_add.astype(f32), zero_bias, v_add.astype(f32)])
         return (projected + add[None]).astype(bf16) * scale[None]
 
-    packed_near = project(qkv_near, q_bias, v_bias)
+    table = jnp.stack(
+        [(dp ^ s) * 4 + (col ^ j) for s in range(4) for j in range(4)]
+        + [a * 4 + col for a in range(4)]
+        + [dp ^ s for s in range(4)]
+        + [col ^ b for b in range(4)]
+        + [row]
+    ).astype(jnp.int32)
+    loss_scale = all_clips * L * width / 2.0
+    factor = (loss_scale * 2.0 / (valid_total * width)).reshape(1)
+    valid = valid[:, None]
+    packed_near = tie(project(qkv_near, q_bias, v_bias), table, factor, valid)
     cut_at = two.shape[0] // 32 * 16
     two_x, two_y = tie(two_x, packed_near), tie(two_y, packed_near)
     two_low, two_high = over_dp(two_y[:cut_at], 1), over_dp(two_x[cut_at:], 2)
@@ -1310,6 +1340,7 @@
     two_theirs = over_row(two_all)
     near_other = over_col(near_late[over:], 1)
     one_x, one_y = over_dp(one, 1), over_dp(one, 2)
+    one_other = over_row(tie(one, near_late))
     near_soon, near_soon_lse = attend(
         tie(packed_near, two_all, near_late, one), key_bias, 0, split
     )
@@ -1323,36 +1354,20 @@
     one_x, one_y = tie(one_x, far_late), tie(one_y, far_late)
     cut_at = one.shape[0] // 2
     one_low, one_high = over_dp(one_y[:cut_at], 1), over_dp(one_x[cut_at:], 2)
-    far_soon, far_soon_lse = attend(tie(packed_far, one_x, one_y, far_late), key_bias, 0, split)
-    one_low, one_high = tie(one_low, far_soon), tie(one_high, far_soon)
-    one_all = jnp.concatenate([one, one_x, one_y, one_low, one_high], axis=0)
-    one_all = tie(one_all, far_other)
+    one_theirs = [over_row(one_x), over_row(one_y)]
+    far_soon, far_soon_lse = attend(
+        tie(packed_far, one_x, one_y, far_late, one_other), key_bias, 0, split
+    )
+    one_low, one_high = tie(one_low, far_soon, far_other), tie(one_high, far_soon, far_other)
+    one_mine = [one, one_x, one_y, one_low, one_high]
+    one_theirs = [one_other, *one_theirs, over_row(one_low), over_row(one_high)]
     turned = tie(tokens_one, far_late).T
-    one_theirs = over_row(one_all)
-    attended_rows = jnp.concatenate(
-        [
-            jnp.concatenate([near_soon, near_late[:over]], axis=0),
-            near_other,
-            jnp.concatenate([far_soon, far_late[:over]], axis=0),
-            far_other,
-        ],
-        axis=1,
-    )
-
-    table = jnp.stack(
-        [(dp ^ s) * 4 + (col ^ j) for s in range(4) for j in range(4)]
-        + [a * 4 + col for a in range(4)]
-        + [dp ^ s for s in range(4)]
-        + [col ^ b for b in range(4)]
-        + [row]
-    ).astype(jnp.int32)
     at = unit_rows_total + small_at
     smalls = jnp.stack(
-        [small, one_all[small_at : small_at + 16], two_all[small_at : small_at + 16], one_all[at : at + 16]]
+        [small, one[small_at : small_at + 16], two_all[small_at : small_at + 16], one[at : at + 16]]
     ).astype(f32)
-    loss_scale = all_clips * L * width / 2.0
-    factor = (loss_scale * 2.0 / (valid_total * width)).reshape(1)
     (
+        attended_rows,
         outputs,
         hidden,
         grad_pre,
@@ -1367,10 +1382,9 @@
     ) = middle_block(
         table,
         factor,
-        attended_rows,
         states,
         teacher,
-        valid[:, None],
+        valid,
         vectors,
         smalls,
         (
@@ -1382,8 +1396,14 @@
             proj_other,
             two_all,
             two_theirs,
-            one_all,
-            one_theirs,
+            *one_mine,
+            *one_theirs,
+            near_soon,
+            near_late,
+            near_other,
+            far_soon,
+            far_late,
+            far_other,
         ),
     )
     up_far = over_col(up_give, 1)

time: 516 us -> 504 us (0.977)
  local copies, waits for them, and re-layouts: 57.4 us -> 49.8 us
    unnamed x147 -> x159, local copies, waits for them, and re-layouts: 30.5 us -> 23.8 us
    ppermute x53 -> x57, waiting for transfers between devices: 63.9 us -> 62.9 us  [swap(): return lax.ppermute(values, axis, [(i, i ^ mask) for i in range(size)])]
    ppermute x53 -> x57, starting transfers between devices: 54.4 us -> 53.9 us  [swap(): return lax.ppermute(values, axis, [(i, i ^ mask) for i in range(size)])]
  transfers between devices with their start and end apart: 53 -> 57, of which waited for: 9 -> 11; matrix products, arithmetic and copies ran while one was open for 17% -> 15% of each run, Pallas kernels for 40% -> 41%
where the time goes in v5:
time: 504 us; the launch traced here: 495 us
  Pallas kernels  269 us (53%)
  waiting for transfers between devices  62.9 us (12%)
  starting transfers between devices  53.9 us (11%)
  local copies, waits for them, and re-layouts  49.8 us (10%)
  matrix products  34.8 us (7%)
  other arithmetic  19.2 us (4%)
    pallas_call x4, Pallas kernels, attend_back(): pl.pallas_call(functools.partial(attend_back_kernel, first, lane, before...  84 us
    ppermute x57, waiting for transfers between devices, swap(): return lax.ppermute(values, axis, [(i, i ^ mask) for i in range(size)])  62.9 us
    pallas_call x1, Pallas kernels, middle_block(): pl.pallas_call(middle_kernel, out_shape=(result(width, bf16), result(widt...  56.2 us
    ppermute x57, starting transfers between devices, swap(): return lax.ppermute(values, axis, [(i, i ^ mask) for i in range(size)])  53.9 us
    pallas_call x4, Pallas kernels, attend(): pl.pallas_call(functools.partial(attend_kernel, first), out_shape=(jax.Sh...  47 us
    pallas_call x9, Pallas kernels, on_chip(): pl.pallas_call(kernel, out_shape=tuple((jax.ShapeDtypeStruct(*s) for s in...  31.1 us
    dot_general x6, matrix products, dot_tn(): lax.dot_general(a, b, (((0,), (0,)), ((), ())), preferred_element_type=jn...  25.1 us
    unnamed x159, local copies, waits for them, and re-layouts  23.8 us
  transfers between devices with their start and end apart: 57, of which 11 were waited for; matrix products, arithmetic and copies ran while one was open for 15% of the time, Pallas kernels for 41%

profile of v5, /device:TPU:0, one launch (start us, length us, event | category | flops | bytes accessed | tf_op | source)
XLA Modules:
  0.0 494.5 jit_solution(12408536917261072960)
XLA Ops:
  33.0 14.0 %collective-permute-done.1 = bf16[1552,256]{1,0:T(8,128)(2,1)} collective-permute-done((bf16[1552,256]{1,0:T(8,128)(2,1)}, bf16[1552,256]{1,0:T(8,128)(2,1)}, u32[]{:S(2)}, u32[]{:S(2)}) %collective-permute-start.1) | collective-permute-done | bytes 794656 | tf_op jit(solution)/shard_map/ppermute | solution.py:799
  55.2 9.2 %collective-permute-done.5.other_states = bf16[784,1024]{1,0:T(8,128)(2,1)} collective-permute-done((bf16[784,1024]{1,0:T(8,128)(2,1)S(1)}, bf16[784,1024]{1,0:T(8,128)(2,1)}, u32[]{:S(2)}, u32[]{:S(2)}) %collective-permute-start.5) | collective-permute-done | bytes 1605664 | tf_op jit(solution)/shard_map/ppermute | solution.py:799
  74.4 4.6 fusion.12.packed_ref
  86.9 8.2 %collective-permute-done.6.refs_0_ = bf16[2336,256]{1,0:T(8,128)(2,1)} collective-permute-done((bf16[2336,256]{1,0:T(8,128)(2,1)S(1)}, bf16[2336,256]{1,0:T(8,128)(2,1)}, u32[]{:S(2)}, u32[]{:S(2)}) %collective-permute-start.6) | collective-permute-done | bytes 1196064 | tf_op jit(solution)/shard_map/ppermute | solution.py:799
  95.4 12.7 %attend.4 = (bf16[800,256]{1,0:T(8,128)(2,1)S(1)}, f32[7,8,512]{2,1,0:T(8,128)S(1)}) custom-call(bf16[1568,768]{1,0:T(8,128)(2,1)S(1)} %fusion.12.packed_ref, f32[1568,128]{1,0:T(8,128)S(1)} %broadcast_in_dim.48.bias_ref), custom_call_target="tpu_custom_call" | custom-call | flops 2569011200 | bytes 6291456 | tf_op jit(solution)/shard_map/attend/pallas_call | solution.py:454
  113.2 10.9 %attend.5 = (bf16[768,256]{1,0:T(8,128)(2,1)S(1)}, f32[6,8,512]{2,1,0:T(8,128)S(1)}) custom-call(bf16[1568,768]{1,0:T(8,128)(2,1)S(1)} %fusion.12.packed_ref, f32[1568,128]{1,0:T(8,128)S(1)} %broadcast_in_dim.48.bias_ref), custom_call_target="tpu_custom_call" | custom-call | flops 2466250752 | bytes 6291456 | tf_op jit(solution)/shard_map/attend/pallas_call | solution.py:454
  129.3 5.2 %fusion.13.packed_ref = bf16[1568,768]{1,0:T(8,128)(2,1)S(1)} fusion(bf16[1568,1024]{0,1:T(8,128)(2,1)} %copy-done.35, bf16[1024,768]{1,0:T(8,128)(2,1)} %far_qkv.1.w_far, f32[768]{0:T(1024)S(1)} %get-tuple-element.317, bf16[768]{0:T(1024)(128)(2,1)S(1)} %select_convert_fusion.1), kind=kOutput, calls=%fused_computation.26 | convolution fusion | flops 2469863424 | bytes 7197184 | tf_op jit(solution)/shard_map/dot_general | solution.py:1317
  134.5 12.2 %attend.6 = (bf16[800,256]{1,0:T(8,128)(2,1)S(1)}, f32[7,8,512]{2,1,0:T(8,128)S(1)}) custom-call(bf16[1568,768]{1,0:T(8,128)(2,1)S(1)} %fusion.13.packed_ref, f32[1568,128]{1,0:T(8,128)S(1)} %broadcast_in_dim.48.bias_ref), custom_call_target="tpu_custom_call" | custom-call | flops 2569011200 | bytes 6291456 | tf_op jit(solution)/shard_map/attend/pallas_call | solution.py:454
  151.2 11.1 %attend.7 = (bf16[768,256]{1,0:T(8,128)(2,1)S(1)}, f32[6,8,512]{2,1,0:T(8,128)S(1)}) custom-call(bf16[1568,768]{1,0:T(8,128)(2,1)S(1)} %fusion.13.packed_ref, f32[1568,128]{1,0:T(8,128)S(1)} %broadcast_in_dim.48.bias_ref), custom_call_target="tpu_custom_call" | custom-call | flops 2466250752 | bytes 6291456 | tf_op jit(solution)/shard_map/attend/pallas_call | solution.py:454
  169.3 56.2 %middle_block.1 = (bf16[784,1024]{1,0:T(8,128)(2,1)}, bf16[784,1024]{1,0:T(8,128)(2,1)}, bf16[784,4096]{1,0:T(8,128)(2,1)}, bf16[784,4096]{1,0:T(8,128)(2,1)}, b...) custom-call(s32[29]{0:T(128)} %stack.163.table_ref, ...), custom_call_target="tpu_custom_call" | custom-call | flops 6576668672 | bytes 46137344 | tf_op jit(solution)/shard_map/middle_block/pallas_call | solution.py:754
  225.5 7.8 %convolution_convert_fusion.1 = bf16[512,4096]{1,0:T(8,128)(2,1)S(1)} fusion(bf16[784,4096]{1,0:T(8,128)(2,1)} %get-tuple-element.181.big_ref, bf16[784,1024]{1,0:T(8,128)(2,1)} %get-tuple-element.180.small_ref), kind=kOutput, calls=%fused_computation.1 | convolution fusion | flops 3290431488 | bytes 11419648 | tf_op jit(solution)/shard_map/dot_general | solution.py:347
  233.9 6.8 %convolution_convert_fusion = bf16[512,4096]{1,0:T(8,128)(2,1)} fusion(bf16[784,4096]{1,0:T(8,128)(2,1)S(1)} %copy-done.40, bf16[784,1024]{1,0:T(8,128)(2,1)S(1)} %copy-done.10), kind=kOutput, calls=%fused_computation | convolution fusion | flops 3290431488 | bytes 11419648 | tf_op jit(solution)/shard_map/dot_general | solution.py:347
  244.8 8.7 %wide_grads.2 = (bf16[512,1024]{1,0:T(8,128)(2,1)S(1)}, bf16[512,1024]{1,0:T(8,128)(2,1)}, bf16[512,1024]{1,0:T(8,128)(2,1)S(1)}, bf16[512,1024]{1,0:T(8,128)(2,1)}) custom-call(s32[8]{0:T(128)S(1)} %copy-done.22, bf16[784,1024]{1,0:T(8,128)(2,1)S(1)} %copy-done.11, bf16[784,4096]{1,0:T(8,128)(2,1)} %get-tuple-element.181.big_ref, ...), custom_call_target="tpu_custom_call" | custom-call | flops 3000000000 | tf_op jit(solution)/shard_map/wide_grads/pallas_call | solution.py:1102
  256.4 9.7 %wide_grads.3 = (bf16[512,1280]{1,0:T(8,128)(2,1)S(1)}, bf16[512,1280]{1,0:T(8,128)(2,1)S(1)}, bf16[512,1280]{1,0:T(8,128)(2,1)S(1)}, bf16[512,1280]{1,0:T(8,128)(2,1)}) custom-call(s32[8]{0:T(128)S(1)} %copy-done.22, bf16[784,1024]{1,0:T(8,128)(2,1)S(1)} %copy-done.10, bf16[784,4096]{1,0:T(8,128)(2,1)} %get-tuple-element.187.big_ref, ...), custom_call_target="tpu_custom_call" | custom-call | flops 3000000000 | tf_op jit(solution)/shard_map/wide_grads/pallas_call | solution.py:1102
  270.6 19.6 %attend_back.4 = (bf16[768,256]{1,0:T(8,128)(2,1)S(1)}, f32[1568,256]{1,0:T(8,128)}, f32[1568,256]{1,0:T(8,128)}) custom-call(bf16[1568,768]{1,0:T(8,128)(2,1)} %copy-done.27, f32[1568,128]{1,0:T(8,128)S(1)} %copy-done.17, f32[6,8,512]{2,1,0:T(8,128)S(1)} %get-tuple-element.193.lse_ref, bf16[768,256]{1,0:T(8,128)(2,1)S(1)} %copy-done.19, ...), custom_call_target="tpu_custom_call" | custom-call | flops 4932501504 | bytes 10485760 | tf_op jit(solution)/shard_map/attend_back/pallas_call | solution.py:488
  297.7 19.4 %attend_back.5 = (bf16[768,256]{1,0:T(8,128)(2,1)S(1)}, f32[1568,256]{1,0:T(8,128)}, f32[1568,256]{1,0:T(8,128)}) custom-call(bf16[1568,768]{1,0:T(8,128)(2,1)} %copy-done.26, f32[1568,128]{1,0:T(8,128)S(1)} %copy-done.17, f32[6,8,512]{2,1,0:T(8,128)S(1)} %get-tuple-element.203.lse_ref, bf16[768,256]{1,0:T(8,128)(2,1)S(1)} %copy-done.21, ...), custom_call_target="tpu_custom_call" | custom-call | flops 4932501504 | bytes 10485760 | tf_op jit(solution)/shard_map/attend_back/pallas_call | solution.py:488
  329.6 22.4 %attend_back.6 = (bf16[1568,768]{1,0:T(8,128)(2,1)}, f32[1,768]{1,0:T(1,128)S(1)}) custom-call(bf16[1568,768]{1,0:T(8,128)(2,1)} %copy-done.27, f32[1568,128]{1,0:T(8,128)S(1)} %copy-done.17, f32[7,8,512]{2,1,0:T(8,128)S(1)} %get-tuple-element.219.lse_ref, bf16[800,256]{1,0:T(8,128)(2,1)S(1)} %copy-done.9, ...), custom_call_target="tpu_custom_call" | custom-call | flops 5138022400 | bytes 10485760 | tf_op jit(solution)/shard_map/attend_back/pallas_call | solution.py:488
  370.4 22.6 %attend_back.7 = (bf16[1568,768]{1,0:T(8,128)(2,1)}, f32[1,768]{1,0:T(1,128)S(1)}) custom-call(bf16[1568,768]{1,0:T(8,128)(2,1)} %copy-done.26, f32[1568,128]{1,0:T(8,128)S(1)} %copy-done.17, f32[7,8,512]{2,1,0:T(8,128)S(1)} %get-tuple-element.237.lse_ref, bf16[800,256]{1,0:T(8,128)(2,1)S(1)} %copy-done.7, ...), custom_call_target="tpu_custom_call" | custom-call | flops 5138022400 | bytes 10485760 | tf_op jit(solution)/shard_map/attend_back/pallas_call | solution.py:488
  394.7 11.7 %token_back.1 = (f32[784,1024]{1,0:T(8,128)}, bf16[784,1024]{1,0:T(8,128)(2,1)S(1)}, f32[2,1024]{1,0:T(2,128)S(1)}) custom-call(s32[1]{0:T(128)} %bitcast.27.flip_ref, bf16[1568,768]{1,0:T(8,128)(2,1)S(1)} %copy-done.5, bf16[1568,768]{1,0:T(8,128)(2,1)S(1)} %copy-done.2, bf16[1024,768]{1,0:T(8,128)(2,1)S(1)} %pad_maximum_fusion.1.w_near, ...), custom_call_target="tpu_custom_call" | custom-call | flops 100000000 | tf_op jit(solution)/shard_map/token_back/pallas_call | solution.py:944
  408.1 7.1 %far_grads.1 = (f32[32,512]{1,0:T(8,128)}, bf16[576,768]{1,0:T(8,128)(2,1)}, f32[512,768]{1,0:T(8,128)}) custom-call(bf16[1024,1568]{1,0:T(8,128)(2,1)} %bitcast.64, bf16[1568,768]{1,0:T(8,128)(2,1)} %get-tuple-element.242.far_ref.grad_ref, f32[8,1024]{1,0:T(8,128)} %get-tuple-element.243.sums_ref, f32[1,4096]{1,0:T(1,128)} %get-tuple-element.244.hidden_ref, ...), custom_call_target="tpu_custom_call" | custom-call | flops 100000000 | tf_op jit(solution)/shard_map/far_grads/pallas_call | solution.py:1061
  426.4 8.0 %collective-permute-done.46 = bf16[1152,256]{1,0:T(8,128)(2,1)} collective-permute-done((bf16[1152,256]{1,0:T(8,128)(2,1)}, bf16[1152,256]{1,0:T(8,128)(2,1)}, u32[]{:S(2)}, u32[]{:S(2)}) %collective-permute-start.46) | collective-permute-done | bytes 589856 | tf_op jit(solution)/shard_map/ppermute | solution.py:799
  435.8 11.8 %collective-permute-done.49.refs_2_ = bf16[192,768]{1,0:T(8,128)(2,1)S(1)} collective-permute-done((bf16[192,768]{1,0:T(8,128)(2,1)}, bf16[192,768]{1,0:T(8,128)(2,1)S(1)}, u32[]{:S(2)}, u32[]{:S(2)}) %collective-permute-start.49) | collective-permute-done | bytes 294944 | tf_op jit(solution)/shard_map/ppermute | solution.py:799
  455.6 8.0 %last_norm.1 = bf16[784,1024]{1,0:T(8,128)(2,1)} custom-call(s32[1]{0:T(128)} %bitcast.27.flip_ref, f32[784,1024]{1,0:T(8,128)} %get-tuple-element.269.own_ref, bf16[784,1024]{1,0:T(8,128)(2,1)} %collective-permute-done.47.taken_ref, bf16[784,1024]{1,0:T(8,128)(2,1)} %states_ref, f32[784,1024]{1,0:T(8,128)} %get-tuple-element.272.mid_ref, f32[6,1024]{1,0:T(8,128)} %copy-done.52), custom_call_target="tpu_custom_call" | custom-call | flops 500000000 | tf_op jit(solution)/shard_map/last_norm/pallas_call | solution.py:978
  464.3 5.0 %collective-permute-done.51.two_ref = bf16[192,768]{1,0:T(8,128)(2,1)S(1)} collective-permute-done((bf16[192,768]{1,0:T(8,128)(2,1)}, bf16[192,768]{1,0:T(8,128)(2,1)S(1)}, u32[]{:S(2)}, u32[]{:S(2)}) %collective-permute-start.51) | collective-permute-done | bytes 294944 | tf_op jit(solution)/shard_map/ppermute | solution.py:799
  (351 shorter events, 177.0 us)
Async XLA Ops:
  0.7 46.3 %collective-permute-start.2 = (bf16[512,1024]{1,0:T(8,128)(2,1)}, bf16[512,1024]{1,0:T(8,128)(2,1)}, u32[]{:S(2)}, u32[]{:S(2)}) collective-permute-start(bf16[512,1024]{1,0:T(8,128)(2,1)} %fc1_own.1), channel_id=1, source_target_pairs={{0,4},{4,0},{1,5},{5,1},{2,6},{6,2},{3,7},{7,3},{8,12},{12,8},{9,1... | collective-permute-start | bytes 3145736 | tf_op jit(solution)/shard_map/ppermute | solution.py:799
  1.2 45.8 %collective-permute-start.3 = (bf16[1024,512]{1,0:T(8,128)(2,1)}, bf16[1024,512]{1,0:T(8,128)(2,1)}, u32[]{:S(2)}, u32[]{:S(2)}) collective-permute-start(bf16[1024,512]{1,0:T(8,128)(2,1)} %fc2_own.1), channel_id=1, source_target_pairs={{0,4},{4,0},{1,5},{5,1},{2,6},{6,2},{3,7},{7,3},{8,12},{12,8},{9,1... | collective-permute-start | bytes 3145736 | tf_op jit(solution)/shard_map/ppermute | solution.py:799
  7.5 39.5 %collective-permute-start.1 = (bf16[1552,256]{1,0:T(8,128)(2,1)}, bf16[1552,256]{1,0:T(8,128)(2,1)}, u32[]{:S(2)}, u32[]{:S(2)}) collective-permute-start(bf16[1552,256]{1,0:T(8,128)(2,1)} %make_slab.1), channel_id=1, source_target_pairs={{0,2},{1,3},{2,0},{3,1},{4,6},{5,7},{6,4},{7,5},{8,10},{9,11},{10,... | collective-permute-start | bytes 2383880 | tf_op jit(solution)/shard_map/ppermute | solution.py:799
  11.6 52.8 %collective-permute-start.5 = (bf16[784,1024]{1,0:T(8,128)(2,1)S(1)}, bf16[784,1024]{1,0:T(8,128)(2,1)}, u32[]{:S(2)}, u32[]{:S(2)}) collective-permute-start(bf16[784,1024]{1,0:T(8,128)(2,1)S(1)} %copy-done), channel_id=1, source_target_pairs={{0,1},{1,0},{2,3},{3,2},{4,5},{5,4},{6,7},{7,6},{8,9},{9,8},{10,11... | collective-permute-start | bytes 4816904 | tf_op jit(solution)/shard_map/ppermute | solution.py:799
  32.9 40.9 %collective-permute-start.8 = (bf16[512,768]{1,0:T(8,128)(2,1)}, bf16[512,768]{1,0:T(8,128)(2,1)}, u32[]{:S(2)}, u32[]{:S(2)}) collective-permute-start(bf16[512,768]{1,0:T(8,128)(2,1)} %copy.56), channel_id=1, source_target_pairs={{0,4},{4,0},{1,5},{5,1},{2,6},{6,2},{3,7},{7,3},{8,12},{12,8},{9,1... | collective-permute-start | bytes 2359304 | tf_op jit(solution)/shard_map/ppermute | solution.py:799
  48.1 30.9 %collective-permute-start.9 = (bf16[1552,256]{1,0:T(8,128)(2,1)}, bf16[1552,256]{1,0:T(8,128)(2,1)}, u32[]{:S(2)}, u32[]{:S(2)}) collective-permute-start(bf16[1552,256]{1,0:T(8,128)(2,1)} %collective-permute-done.1), channel_id=1, source_target_pairs={{0,16},{8,24},{16,0},{24,8},{1,17},{9,25},{17,1},{25,9},{2,18},{10... | collective-permute-start | bytes 2383880 | tf_op jit(solution)/shard_map/ppermute | solution.py:799
  49.8 29.3 %collective-permute-start.7 = (bf16[1552,256]{1,0:T(8,128)(2,1)}, bf16[1552,256]{1,0:T(8,128)(2,1)}, u32[]{:S(2)}, u32[]{:S(2)}) collective-permute-start(bf16[1552,256]{1,0:T(8,128)(2,1)} %collective-permute-done.1), channel_id=1, source_target_pairs={{0,8},{8,0},{16,24},{24,16},{1,9},{9,1},{17,25},{25,17},{2,10},{10... | collective-permute-start | bytes 2383880 | tf_op jit(solution)/shard_map/ppermute | solution.py:799
  108.3 38.5 %collective-permute-start.15 = (bf16[2336,256]{1,0:T(8,128)(2,1)}, bf16[2336,256]{1,0:T(8,128)(2,1)}, u32[]{:S(2)}, u32[]{:S(2)}) collective-permute-start(bf16[2336,256]{1,0:T(8,128)(2,1)} %collective-permute-done.6.refs_0_), channel_id=1, source_target_pairs={{0,16},{8,24},{16,0},{24,8},{1,17},{9,25},{17,1},{25,9},{2,18},{10... | collective-permute-start | bytes 3588104 | tf_op jit(solution)/shard_map/ppermute | solution.py:799
  109.8 38.7 %collective-permute-start.13 = (bf16[2336,256]{1,0:T(8,128)(2,1)}, bf16[2336,256]{1,0:T(8,128)(2,1)}, u32[]{:S(2)}, u32[]{:S(2)}) collective-permute-start(bf16[2336,256]{1,0:T(8,128)(2,1)} %collective-permute-done.6.refs_0_), channel_id=1, source_target_pairs={{0,8},{8,0},{16,24},{24,16},{1,9},{9,1},{17,25},{25,17},{2,10},{10... | collective-permute-start | bytes 3588104 | tf_op jit(solution)/shard_map/ppermute | solution.py:799
  113.2 37.6 %collective-permute-start.17 = (bf16[2336,256]{1,0:T(8,128)(2,1)}, bf16[2336,256]{1,0:T(8,128)(2,1)}, u32[]{:S(2)}, u32[]{:S(2)}) collective-permute-start(bf16[2336,256]{1,0:T(8,128)(2,1)} %collective-permute-done.6.refs_0_), channel_id=1, source_target_pairs={{0,4},{4,0},{1,5},{5,1},{2,6},{6,2},{3,7},{7,3},{8,12},{12,8},{9,1... | collective-permute-start | bytes 3588104 | tf_op jit(solution)/shard_map/ppermute | solution.py:799
  254.4 36.6 %collective-permute-start.25 = (bf16[512,1024]{1,0:T(8,128)(2,1)}, bf16[512,1024]{1,0:T(8,128)(2,1)}, u32[]{:S(2)}, u32[]{:S(2)}) collective-permute-start(bf16[512,1024]{1,0:T(8,128)(2,1)} %get-tuple-element.183), channel_id=1, source_target_pairs={{0,8},{8,0},{16,24},{24,16},{1,9},{9,1},{17,25},{25,17},{2,10},{10... | collective-permute-start | bytes 3145736 | tf_op jit(solution)/shard_map/ppermute | solution.py:799
  255.9 35.1 %collective-permute-start.28 = (bf16[512,1024]{1,0:T(8,128)(2,1)}, bf16[512,1024]{1,0:T(8,128)(2,1)}, u32[]{:S(2)}, u32[]{:S(2)}) collective-permute-start(bf16[512,1024]{1,0:T(8,128)(2,1)} %get-tuple-element.184), channel_id=1, source_target_pairs={{0,16},{8,24},{16,0},{24,8},{1,17},{9,25},{17,1},{25,9},{2,18},{10... | collective-permute-start | bytes 3145736 | tf_op jit(solution)/shard_map/ppermute | solution.py:799
  268.3 48.8 %collective-permute-start.32 = (bf16[512,1280]{1,0:T(8,128)(2,1)}, bf16[512,1280]{1,0:T(8,128)(2,1)}, u32[]{:S(2)}, u32[]{:S(2)}) collective-permute-start(bf16[512,1280]{1,0:T(8,128)(2,1)} %get-tuple-element.191), channel_id=1, source_target_pairs={{0,16},{8,24},{16,0},{24,8},{1,17},{9,25},{17,1},{25,9},{2,18},{10... | collective-permute-start | bytes 3932168 | tf_op jit(solution)/shard_map/ppermute | solution.py:799
  269.8 47.3 %collective-permute-start.31 = (bf16[512,1280]{1,0:T(8,128)(2,1)S(1)}, bf16[512,1280]{1,0:T(8,128)(2,1)}, u32[]{:S(2)}, u32[]{:S(2)}) collective-permute-start(bf16[512,1280]{1,0:T(8,128)(2,1)S(1)} %get-tuple-element.190), channel_id=1, source_target_pairs={{0,8},{8,0},{16,24},{24,16},{1,9},{9,1},{17,25},{25,17},{2,10},{10... | collective-permute-start | bytes 3932168 | tf_op jit(solution)/shard_map/ppermute | solution.py:799
  270.3 57.7 %collective-permute-start.33 = (bf16[784,512]{1,0:T(8,128)(2,1)}, bf16[784,512]{1,0:T(8,128)(2,1)}, u32[]{:S(2)}, u32[]{:S(2)}) collective-permute-start(bf16[784,512]{1,0:T(8,128)(2,1)} %get-tuple-element.220), channel_id=1, source_target_pairs={{0,1},{1,0},{2,3},{3,2},{4,5},{5,4},{6,7},{7,6},{8,9},{9,8},{10,11... | collective-permute-start | bytes 2408456 | tf_op jit(solution)/shard_map/ppermute | solution.py:799
  294.7 27.8 %collective-permute-start.29 = (bf16[256,1024]{1,0:T(8,128)(2,1)}, bf16[256,1024]{1,0:T(8,128)(2,1)}, u32[]{:S(2)}, u32[]{:S(2)}) collective-permute-start(bf16[256,1024]{1,0:T(8,128)(2,1)} %get-tuple-element.199), channel_id=1, source_target_pairs={{0,16},{8,24},{16,0},{24,8},{1,17},{9,25},{17,1},{25,9},{2,18},{10... | collective-permute-start | bytes 1572872 | tf_op jit(solution)/shard_map/ppermute | solution.py:799
  321.4 31.1 %collective-permute-start.34 = (bf16[256,1280]{1,0:T(8,128)(2,1)}, bf16[256,1280]{1,0:T(8,128)(2,1)}, u32[]{:S(2)}, u32[]{:S(2)}) collective-permute-start(bf16[256,1280]{1,0:T(8,128)(2,1)} %get-tuple-element.216), channel_id=1, source_target_pairs={{0,16},{8,24},{16,0},{24,8},{1,17},{9,25},{17,1},{25,9},{2,18},{10... | collective-permute-start | bytes 1966088 | tf_op jit(solution)/shard_map/ppermute | solution.py:799
  321.9 30.7 %collective-permute-start.38 = (bf16[256,1280]{1,0:T(8,128)(2,1)}, bf16[256,1280]{1,0:T(8,128)(2,1)}, u32[]{:S(2)}, u32[]{:S(2)}) collective-permute-start(bf16[256,1280]{1,0:T(8,128)(2,1)} %get-tuple-element.217), channel_id=1, source_target_pairs={{0,8},{8,0},{16,24},{24,16},{1,9},{9,1},{17,25},{25,17},{2,10},{10... | collective-permute-start | bytes 1966088 | tf_op jit(solution)/shard_map/ppermute | solution.py:799
  361.2 45.8 %collective-permute-start.41 = (bf16[640,256]{1,0:T(8,128)(2,1)}, bf16[640,256]{1,0:T(8,128)(2,1)S(1)}, u32[]{:S(2)}, u32[]{:S(2)}) collective-permute-start(bf16[640,256]{1,0:T(8,128)(2,1)} %get-tuple-element.232), channel_id=1, source_target_pairs={{0,1},{1,0},{2,3},{3,2},{4,5},{5,4},{6,7},{7,6},{8,9},{9,8},{10,11... | collective-permute-start | bytes 983048 | tf_op jit(solution)/shard_map/ppermute | solution.py:799
  362.1 44.9 %collective-permute-start.42 = (bf16[640,256]{1,0:T(8,128)(2,1)}, bf16[640,256]{1,0:T(8,128)(2,1)S(1)}, u32[]{:S(2)}, u32[]{:S(2)}) collective-permute-start(bf16[640,256]{1,0:T(8,128)(2,1)} %get-tuple-element.233), channel_id=1, source_target_pairs={{0,2},{1,3},{2,0},{3,1},{4,6},{5,7},{6,4},{7,5},{8,10},{9,11},{10,... | collective-permute-start | bytes 983048 | tf_op jit(solution)/shard_map/ppermute | solution.py:799
  364.2 42.9 %collective-permute-start.43 = (bf16[640,256]{1,0:T(8,128)(2,1)}, bf16[640,256]{1,0:T(8,128)(2,1)S(1)}, u32[]{:S(2)}, u32[]{:S(2)}) collective-permute-start(bf16[640,256]{1,0:T(8,128)(2,1)} %get-tuple-element.234), channel_id=1, source_target_pairs={{0,3},{1,2},{2,1},{3,0},{4,7},{5,6},{6,5},{7,4},{8,11},{9,10},{10,... | collective-permute-start | bytes 983048 | tf_op jit(solution)/shard_map/ppermute | solution.py:799
  368.8 38.2 %collective-permute-start.40 = (bf16[256,768]{1,0:T(8,128)(2,1)S(1)}, bf16[256,768]{1,0:T(8,128)(2,1)S(1)}, u32[]{:S(2)}, u32[]{:S(2)}) collective-permute-start(bf16[256,768]{1,0:T(8,128)(2,1)S(1)} %pad_maximum_fusion.4), channel_id=1, source_target_pairs={{0,8},{8,0},{16,24},{24,16},{1,9},{9,1},{17,25},{25,17},{2,10},{10... | collective-permute-start | bytes 1179656 | tf_op jit(solution)/shard_map/ppermute | solution.py:799
  407.0 40.5 %collective-permute-start.47 = (bf16[784,1024]{1,0:T(8,128)(2,1)S(1)}, bf16[784,1024]{1,0:T(8,128)(2,1)}, u32[]{:S(2)}, u32[]{:S(2)}) collective-permute-start(bf16[784,1024]{1,0:T(8,128)(2,1)S(1)} %get-tuple-element.241), channel_id=1, source_target_pairs={{0,1},{1,0},{2,3},{3,2},{4,5},{5,4},{6,7},{7,6},{8,9},{9,8},{10,11... | collective-permute-start | bytes 4816904 | tf_op jit(solution)/shard_map/ppermute | solution.py:799
  450.7 33.1 %collective-permute-start.54 = (bf16[2304,256]{1,0:T(8,128)(2,1)S(1)}, bf16[2304,256]{1,0:T(8,128)(2,1)S(1)}, u32[]{:S(2)}, u32[]{:S(2)}) collective-permute-start(bf16[2304,256]{1,0:T(8,128)(2,1)S(1)} %pad_maximum_fusion.3.refs_0_), channel_id=1, source_target_pairs={{0,16},{8,24},{16,0},{24,8},{1,17},{9,25},{17,1},{25,9},{2,18},{10... | collective-permute-start | bytes 3538952 | tf_op jit(solution)/shard_map/ppermute | solution.py:799
  (110 other events, 1182.9 us)

commit v6 on v5

--- a/solution.py
+++ b/solution.py
@@ -987,7 +987,7 @@
 
 
 def far_grads_kernel(
-    turned_ref, grad_ref, sums_ref, hidden_ref, norm_ref, near_ref, far_ref, keep_ref, out_ref, kept_ref
+    turned_ref, grad_ref, sums_ref, hidden_ref, near_ref, far_ref, keep_ref, out_ref, kept_ref
 ):
     half = keep_ref.shape[1]
     width = near_ref.shape[1] // 3
@@ -999,7 +999,7 @@
 
     def rows(lanes):
         split = [sums_ref[i : i + 1, lanes] for i in (2, 3, 4, 1)]
-        split += [norm_ref[i : i + 1, lanes] for i in range(2)]
+        split += [jnp.zeros((2, half), jnp.float32)]
         return jnp.concatenate(split + shared + [blank], axis=0)
 
     keep_ref[...] = rows(slice(0, half))
@@ -1009,10 +1009,24 @@
 
 
 def after_row_kernel(
-    places_ref, kept_ref, taken_ref, keep_ref, near_ref, near_taken, near_own_ref, far_own_ref, sum_ref, *outs
+    places_ref,
+    kept_ref,
+    taken_ref,
+    keep_ref,
+    norm_ref,
+    near_ref,
+    near_taken,
+    near_own_ref,
+    far_own_ref,
+    sum_ref,
+    *outs,
 ):
     deep = far_own_ref.shape[0]
-    vectors = keep_ref[...] + get_split(taken_ref, 4 * deep, keep_ref.shape[1])
+    half = keep_ref.shape[1]
+    vectors = keep_ref[...] + get_split(taken_ref, 4 * deep, half)
+    vectors = jnp.concatenate(
+        [vectors[0:4], norm_ref[:, 0:half], vectors[6:17], norm_ref[:, half:], vectors[19:]], axis=0
+    )
     sum_ref[...] = vectors
     for s in range(4):
         rows = pl.ds(pl.multiple_of(places_ref[s] * deep, deep), deep)
@@ -1478,34 +1492,34 @@
         packed_far, key_bias, far_late_lse, far_late, up_own, up_far, head_width, split, part_far
     )
 
-    norm_own, norm_give, norm_sums = token_back(
-        flip, grad_near, grad_far, qkv_near, qkv_far, states, states_other
-    )
-    norm_taken = over_col(norm_give, 1)
     columns, slots = grad_far.shape[1], 2 * VECTORS
     vec_keep, row_give, kept = on_chip(
         far_grads_kernel,
         [((VECTORS, half), f32), ((half + slots, columns), bf16), ((half, columns), f32)],
         "far_grads",
-        *(turned, tie(grad_far, norm_give, near_taken, *fc1_cols), sums, hidden_sum, norm_sums, near_sums, far_sums),
+        *(turned, tie(grad_far, near_taken, *fc1_cols), sums, hidden_sum, near_sums, far_sums),
     )
     row_taken = over_row(row_give)
-    fc1_cols = all_tied(fc1_cols, row_give)
     mine_rows = fc2_blocks[0].shape[0] + fc1_blocks[0].shape[0]
     (mine,) = on_chip(
         mine_kernel,
         [((mine_rows, sub), bf16)],
         "mine",
-        *(fc2_blocks[0], *fc2_cols, fc1_blocks[0], *fc1_cols),
+        *(fc2_blocks[0], *fc2_cols, fc1_blocks[0], *all_tied(fc1_cols, row_give)),
     )
     mine_x = over_dp(mine, 1)
+    norm_own, norm_give, norm_sums = token_back(
+        flip, grad_near, tie(grad_far, mine), qkv_near, qkv_far, states, states_other
+    )
+    norm_give = tie(norm_give, row_taken, mine_x)
+    norm_taken = over_col(norm_give, 1)
     near_own, far_own, vec_sum, *plane_give = on_chip(
         after_row_kernel,
         [((deep, columns), f32)] * 2
         + [((VECTORS, half), f32)]
         + [((deep + slots + (deep if s == 2 else 0), columns), bf16) for s in (1, 2, 3)],
         "after_row",
-        *(places, kept, tie(row_taken, mine), vec_keep, wide_near, tie(near_taken, mine)),
+        *(places, kept, tie(row_taken, norm_give), vec_keep, norm_sums, wide_near, near_taken),
         tables=1,
     )
     plane_taken = [over_dp(plane_give[s - 1], s) for s in (1, 2, 3)]
@@ -1534,6 +1548,7 @@
         *(near_own, vec_sum, *all_tied(col_taken, grad_states)),
     )
     qkv_back = [over_dp(qkv_mine, s) for s in (1, 2, 3)]
+    norm_total = vec_total[4:6] + over_row(vec_total[17:19])
     fc2_grad, fc1_grad, proj_grad = finish(places, [mine_two, tie(mine_y, qkv_mine)], part_rows)
     qkv_grad = finish_qkv(places, [qkv_mine, *all_tied(qkv_back, fc2_grad)]).transpose(1, 0, 2)
 
@@ -1543,8 +1558,8 @@
         outputs,
         loss_value,
         grad_states,
-        vec_total[4],
-        vec_total[5],
+        norm_total[0],
+        norm_total[1],
         qkv_grad,
         vec_total[14, :head_width],
         vec_total[14, head_width:],

time: 504 us -> 519 us (1.030)
  waiting for transfers between devices: 62.9 us -> 84.5 us
  local copies, waits for them, and re-layouts: 49.8 us -> 43.2 us
    ppermute x57 -> x58, waiting for transfers between devices: 62.9 us -> 84.5 us  [swap(): return lax.ppermute(values, axis, [(i, i ^ mask) for i in range(size)])]
    transpose x0 -> x1, local copies, waits for them, and re-layouts: none -> 5.51 us  [local_paired(): turned = tie(tokens_one, far_late).T]
    unnamed x159 -> x153, local copies, waits for them, and re-layouts: 23.8 us -> 18.4 us
    ppermute x57 -> x58, starting transfers between devices: 53.9 us -> 56.4 us  [swap(): return lax.ppermute(values, axis, [(i, i ^ mask) for i in range(size)])]
  transfers between devices with their start and end apart: 57 -> 58, of which waited for: 11 -> 10; matrix products, arithmetic and copies ran while one was open for 15% -> 14% of each run, Pallas kernels for 41% -> 39%
where the time goes in v6:
time: 519 us; the launch traced here: 514 us
  Pallas kernels  270 us (52%)
  waiting for transfers between devices  84.5 us (16%)
  starting transfers between devices  56.4 us (11%)
  local copies, waits for them, and re-layouts  43.2 us (8%)
  matrix products  33 us (6%)
  other arithmetic  22.2 us (4%)
    ppermute x58, waiting for transfers between devices, swap(): return lax.ppermute(values, axis, [(i, i ^ mask) for i in range(size)])  84.5 us
    pallas_call x4, Pallas kernels, attend_back(): pl.pallas_call(functools.partial(attend_back_kernel, first, lane, before...  83.5 us
    ppermute x58, starting transfers between devices, swap(): return lax.ppermute(values, axis, [(i, i ^ mask) for i in range(size)])  56.4 us
    pallas_call x1, Pallas kernels, middle_block(): pl.pallas_call(middle_kernel, out_shape=(result(width, bf16), result(widt...  56.2 us
    pallas_call x4, Pallas kernels, attend(): pl.pallas_call(functools.partial(attend_kernel, first), out_shape=(jax.Sh...  46.9 us
    pallas_call x9, Pallas kernels, on_chip(): pl.pallas_call(kernel, out_shape=tuple((jax.ShapeDtypeStruct(*s) for s in...  31.8 us
    dot_general x6, matrix products, dot_tn(): lax.dot_general(a, b, (((0,), (0,)), ((), ())), preferred_element_type=jn...  25.2 us
    pallas_call x2, Pallas kernels, wide_grads(): pl.pallas_call(functools.partial(wide_kernel, bool(proj)), out_shape=(jax...  18.4 us
  transfers between devices with their start and end apart: 58, of which 10 were waited for; matrix products, arithmetic and copies ran while one was open for 14% of the time, Pallas kernels for 39%

profile of v6, /device:TPU:0, one launch (start us, length us, event | category | flops | bytes accessed | tf_op | source)
XLA Modules:
  0.0 513.9 jit_solution(5522708111221326903)
XLA Ops:
  28.6 18.4 %collective-permute-done.1 = bf16[1552,256]{1,0:T(8,128)(2,1)} collective-permute-done((bf16[1552,256]{1,0:T(8,128)(2,1)}, bf16[1552,256]{1,0:T(8,128)(2,1)}, u32[]{:S(2)}, u32[]{:S(2)}) %collective-permute-start.1) | collective-permute-done | bytes 794656 | tf_op jit(solution)/shard_map/ppermute | solution.py:799
  53.3 11.1 %collective-permute-done.5.other_states = bf16[784,1024]{1,0:T(8,128)(2,1)} collective-permute-done((bf16[784,1024]{1,0:T(8,128)(2,1)S(1)}, bf16[784,1024]{1,0:T(8,128)(2,1)}, u32[]{:S(2)}, u32[]{:S(2)}) %collective-permute-start.5) | collective-permute-done | bytes 1605664 | tf_op jit(solution)/shard_map/ppermute | solution.py:799
  78.2 15.9 %collective-permute-done.6.refs_0_ = bf16[2336,256]{1,0:T(8,128)(2,1)} collective-permute-done((bf16[2336,256]{1,0:T(8,128)(2,1)S(1)}, bf16[2336,256]{1,0:T(8,128)(2,1)}, u32[]{:S(2)}, u32[]{:S(2)}) %collective-permute-start.6) | collective-permute-done | bytes 1196064 | tf_op jit(solution)/shard_map/ppermute | solution.py:799
  94.3 12.3 %attend.4 = (bf16[800,256]{1,0:T(8,128)(2,1)S(1)}, f32[7,8,512]{2,1,0:T(8,128)S(1)}) custom-call(bf16[1568,768]{1,0:T(8,128)(2,1)S(1)} %fusion.12.packed_ref, f32[1568,128]{1,0:T(8,128)S(1)} %broadcast_in_dim.48.bias_ref), custom_call_target="tpu_custom_call" | custom-call | flops 2569011200 | bytes 6291456 | tf_op jit(solution)/shard_map/attend/pallas_call | solution.py:454
  111.7 10.9 %attend.5 = (bf16[768,256]{1,0:T(8,128)(2,1)S(1)}, f32[6,8,512]{2,1,0:T(8,128)S(1)}) custom-call(bf16[1568,768]{1,0:T(8,128)(2,1)S(1)} %fusion.12.packed_ref, f32[1568,128]{1,0:T(8,128)S(1)} %broadcast_in_dim.48.bias_ref), custom_call_target="tpu_custom_call" | custom-call | flops 2466250752 | bytes 6291456 | tf_op jit(solution)/shard_map/attend/pallas_call | solution.py:454
  127.8 5.0 fusion.13.packed_ref
  132.8 12.8 %attend.6 = (bf16[800,256]{1,0:T(8,128)(2,1)S(1)}, f32[7,8,512]{2,1,0:T(8,128)S(1)}) custom-call(bf16[1568,768]{1,0:T(8,128)(2,1)S(1)} %fusion.13.packed_ref, f32[1568,128]{1,0:T(8,128)S(1)} %broadcast_in_dim.48.bias_ref), custom_call_target="tpu_custom_call" | custom-call | flops 2569011200 | bytes 6291456 | tf_op jit(solution)/shard_map/attend/pallas_call | solution.py:454
  150.1 10.9 %attend.7 = (bf16[768,256]{1,0:T(8,128)(2,1)S(1)}, f32[6,8,512]{2,1,0:T(8,128)S(1)}) custom-call(bf16[1568,768]{1,0:T(8,128)(2,1)S(1)} %fusion.13.packed_ref, f32[1568,128]{1,0:T(8,128)S(1)} %broadcast_in_dim.48.bias_ref), custom_call_target="tpu_custom_call" | custom-call | flops 2466250752 | bytes 6291456 | tf_op jit(solution)/shard_map/attend/pallas_call | solution.py:454
  168.2 56.2 %middle_block.1 = (bf16[784,1024]{1,0:T(8,128)(2,1)}, bf16[784,1024]{1,0:T(8,128)(2,1)}, bf16[784,4096]{1,0:T(8,128)(2,1)}, bf16[784,4096]{1,0:T(8,128)(2,1)}, b...) custom-call(s32[29]{0:T(128)} %stack.163.table_ref, ...), custom_call_target="tpu_custom_call" | custom-call | flops 6576668672 | bytes 46137344 | tf_op jit(solution)/shard_map/middle_block/pallas_call | solution.py:754
  224.5 7.8 %convolution_convert_fusion.1 = bf16[512,4096]{1,0:T(8,128)(2,1)S(1)} fusion(bf16[784,4096]{1,0:T(8,128)(2,1)} %get-tuple-element.182.big_ref, bf16[784,1024]{1,0:T(8,128)(2,1)} %get-tuple-element.181.small_ref), kind=kOutput, calls=%fused_computation.1 | convolution fusion | flops 3290431488 | bytes 11419648 | tf_op jit(solution)/shard_map/dot_general | solution.py:347
  232.9 6.7 %convolution_convert_fusion = bf16[512,4096]{1,0:T(8,128)(2,1)} fusion(bf16[784,4096]{1,0:T(8,128)(2,1)S(1)} %copy-done.35, bf16[784,1024]{1,0:T(8,128)(2,1)S(1)} %copy-done.10), kind=kOutput, calls=%fused_computation | convolution fusion | flops 3290431488 | bytes 11419648 | tf_op jit(solution)/shard_map/dot_general | solution.py:347
  243.7 8.7 %wide_grads.2 = (bf16[512,1024]{1,0:T(8,128)(2,1)S(1)}, bf16[512,1024]{1,0:T(8,128)(2,1)}, bf16[512,1024]{1,0:T(8,128)(2,1)S(1)}, bf16[512,1024]{1,0:T(8,128)(2,1)}) custom-call(s32[8]{0:T(128)S(1)} %copy-done.22, bf16[784,1024]{1,0:T(8,128)(2,1)S(1)} %copy-done.11, bf16[784,4096]{1,0:T(8,128)(2,1)} %get-tuple-element.182.big_ref, ...), custom_call_target="tpu_custom_call" | custom-call | flops 3000000000 | tf_op jit(solution)/shard_map/wide_grads/pallas_call | solution.py:1116
  255.5 9.7 %wide_grads.3 = (bf16[512,1280]{1,0:T(8,128)(2,1)S(1)}, bf16[512,1280]{1,0:T(8,128)(2,1)S(1)}, bf16[512,1280]{1,0:T(8,128)(2,1)S(1)}, bf16[512,1280]{1,0:T(8,128)(2,1)}) custom-call(s32[8]{0:T(128)S(1)} %copy-done.22, bf16[784,1024]{1,0:T(8,128)(2,1)S(1)} %copy-done.10, bf16[784,4096]{1,0:T(8,128)(2,1)} %get-tuple-element.188.big_ref, ...), custom_call_target="tpu_custom_call" | custom-call | flops 3000000000 | tf_op jit(solution)/shard_map/wide_grads/pallas_call | solution.py:1116
  269.8 19.4 %attend_back.4 = (bf16[768,256]{1,0:T(8,128)(2,1)S(1)}, f32[1568,256]{1,0:T(8,128)}, f32[1568,256]{1,0:T(8,128)}) custom-call(bf16[1568,768]{1,0:T(8,128)(2,1)} %copy-done.27, f32[1568,128]{1,0:T(8,128)S(1)} %copy-done.17, f32[6,8,512]{2,1,0:T(8,128)S(1)} %get-tuple-element.194.lse_ref, bf16[768,256]{1,0:T(8,128)(2,1)S(1)} %copy-done.19, ...), custom_call_target="tpu_custom_call" | custom-call | flops 4932501504 | bytes 10485760 | tf_op jit(solution)/shard_map/attend_back/pallas_call | solution.py:488
  296.5 19.6 %attend_back.5 = (bf16[768,256]{1,0:T(8,128)(2,1)S(1)}, f32[1568,256]{1,0:T(8,128)}, f32[1568,256]{1,0:T(8,128)}) custom-call(bf16[1568,768]{1,0:T(8,128)(2,1)} %copy-done.26, f32[1568,128]{1,0:T(8,128)S(1)} %copy-done.17, f32[6,8,512]{2,1,0:T(8,128)S(1)} %get-tuple-element.204.lse_ref, bf16[768,256]{1,0:T(8,128)(2,1)S(1)} %copy-done.21, ...), custom_call_target="tpu_custom_call" | custom-call | flops 4932501504 | bytes 10485760 | tf_op jit(solution)/shard_map/attend_back/pallas_call | solution.py:488
  328.8 22.2 %attend_back.6 = (bf16[1568,768]{1,0:T(8,128)(2,1)}, f32[1,768]{1,0:T(1,128)S(1)}) custom-call(bf16[1568,768]{1,0:T(8,128)(2,1)} %copy-done.27, f32[1568,128]{1,0:T(8,128)S(1)} %copy-done.17, f32[7,8,512]{2,1,0:T(8,128)S(1)} %get-tuple-element.220.lse_ref, bf16[800,256]{1,0:T(8,128)(2,1)S(1)} %copy-done.9, ...), custom_call_target="tpu_custom_call" | custom-call | flops 5138022400 | bytes 10485760 | tf_op jit(solution)/shard_map/attend_back/pallas_call | solution.py:488
  362.5 5.5 %copy.39.turned_ref = bf16[1024,1568]{1,0:T(8,128)(2,1)} copy(bf16[1024,1568]{0,1:T(8,128)(2,1)} %bitcast.62) | data formatting | bytes 6422528 | tf_op jit(solution)/shard_map/transpose | solution.py:1378
  377.3 22.2 %attend_back.7 = (bf16[1568,768]{1,0:T(8,128)(2,1)}, f32[1,768]{1,0:T(1,128)S(1)}) custom-call(bf16[1568,768]{1,0:T(8,128)(2,1)} %copy-done.26, f32[1568,128]{1,0:T(8,128)S(1)} %copy-done.17, f32[7,8,512]{2,1,0:T(8,128)S(1)} %get-tuple-element.238.lse_ref, bf16[800,256]{1,0:T(8,128)(2,1)S(1)} %copy-done.7, ...), custom_call_target="tpu_custom_call" | custom-call | flops 5138022400 | bytes 10485760 | tf_op jit(solution)/shard_map/attend_back/pallas_call | solution.py:488
  401.2 7.1 %far_grads.1 = (f32[32,512]{1,0:T(8,128)}, bf16[576,768]{1,0:T(8,128)(2,1)}, f32[512,768]{1,0:T(8,128)}) custom-call(bf16[1024,1568]{1,0:T(8,128)(2,1)} %copy.39.turned_ref, bf16[1568,768]{1,0:T(8,128)(2,1)} %get-tuple-element.252.grad_ref.far_ref, f32[8,1024]{1,0:T(8,128)} %get-tuple-element.243.sums_ref, f32[1,4096]{1,0:T(1,128)} %get-tuple-element.244.hidden_ref, ...), custom_call_target="tpu_custom_call" | custom-call | flops 100000000 | tf_op jit(solution)/shard_map/far_grads/pallas_call | solution.py:1075
  415.1 12.4 %token_back.1 = (f32[784,1024]{1,0:T(8,128)}, bf16[784,1024]{1,0:T(8,128)(2,1)}, f32[2,1024]{1,0:T(2,128)S(1)}) custom-call(s32[1]{0:T(128)} %bitcast.27.flip_ref, bf16[1568,768]{1,0:T(8,128)(2,1)S(1)} %copy-done.5, bf16[1568,768]{1,0:T(8,128)(2,1)S(1)} %copy-done.2, bf16[1024,768]{1,0:T(8,128)(2,1)S(1)} %pad_maximum_fusion.1.w_near, ...), custom_call_target="tpu_custom_call" | custom-call | flops 100000000 | tf_op jit(solution)/shard_map/token_back/pallas_call | solution.py:944
  438.3 7.9 %collective-permute-done.49.refs_2_ = bf16[192,768]{1,0:T(8,128)(2,1)S(1)} collective-permute-done((bf16[192,768]{1,0:T(8,128)(2,1)}, bf16[192,768]{1,0:T(8,128)(2,1)S(1)}, u32[]{:S(2)}, u32[]{:S(2)}) %collective-permute-start.49) | collective-permute-done | bytes 294944 | tf_op jit(solution)/shard_map/ppermute | solution.py:799
  446.2 20.2 %collective-permute-done.47.taken_ref = bf16[784,1024]{1,0:T(8,128)(2,1)S(1)} collective-permute-done((bf16[784,1024]{1,0:T(8,128)(2,1)}, bf16[784,1024]{1,0:T(8,128)(2,1)S(1)}, u32[]{:S(2)}, u32[]{:S(2)}) %collective-permute-start.47) | collective-permute-done | bytes 1605664 | tf_op jit(solution)/shard_map/ppermute | solution.py:799
  474.6 8.0 %last_norm.1 = bf16[784,1024]{1,0:T(8,128)(2,1)} custom-call(s32[1]{0:T(128)} %bitcast.27.flip_ref, f32[784,1024]{1,0:T(8,128)} %get-tuple-element.271.own_ref, bf16[784,1024]{1,0:T(8,128)(2,1)} %copy-done.42, bf16[784,1024]{1,0:T(8,128)(2,1)} %states_ref, f32[784,1024]{1,0:T(8,128)} %get-tuple-element.274.mid_ref, f32[6,1024]{1,0:T(8,128)} %copy-done.50), custom_call_target="tpu_custom_call" | custom-call | flops 500000000 | tf_op jit(solution)/shard_map/last_norm/pallas_call | solution.py:978
  482.7 4.6 collective-permute-done.51.two_ref
  (349 shorter events, 173.8 us)
Async XLA Ops:
  0.7 46.3 %collective-permute-start.2 = (bf16[512,1024]{1,0:T(8,128)(2,1)}, bf16[512,1024]{1,0:T(8,128)(2,1)}, u32[]{:S(2)}, u32[]{:S(2)}) collective-permute-start(bf16[512,1024]{1,0:T(8,128)(2,1)} %fc1_own.1), channel_id=1, source_target_pairs={{0,4},{4,0},{1,5},{5,1},{2,6},{6,2},{3,7},{7,3},{8,12},{12,8},{9,1... | collective-permute-start | bytes 3145736 | tf_op jit(solution)/shard_map/ppermute | solution.py:799
  1.2 45.8 %collective-permute-start.3 = (bf16[1024,512]{1,0:T(8,128)(2,1)}, bf16[1024,512]{1,0:T(8,128)(2,1)}, u32[]{:S(2)}, u32[]{:S(2)}) collective-permute-start(bf16[1024,512]{1,0:T(8,128)(2,1)} %fc2_own.1), channel_id=1, source_target_pairs={{0,4},{4,0},{1,5},{5,1},{2,6},{6,2},{3,7},{7,3},{8,12},{12,8},{9,1... | collective-permute-start | bytes 3145736 | tf_op jit(solution)/shard_map/ppermute | solution.py:799
  7.5 39.5 %collective-permute-start.1 = (bf16[1552,256]{1,0:T(8,128)(2,1)}, bf16[1552,256]{1,0:T(8,128)(2,1)}, u32[]{:S(2)}, u32[]{:S(2)}) collective-permute-start(bf16[1552,256]{1,0:T(8,128)(2,1)} %make_slab.1), channel_id=1, source_target_pairs={{0,2},{1,3},{2,0},{3,1},{4,6},{5,7},{6,4},{7,5},{8,10},{9,11},{10,... | collective-permute-start | bytes 2383880 | tf_op jit(solution)/shard_map/ppermute | solution.py:799
  11.6 52.8 %collective-permute-start.5 = (bf16[784,1024]{1,0:T(8,128)(2,1)S(1)}, bf16[784,1024]{1,0:T(8,128)(2,1)}, u32[]{:S(2)}, u32[]{:S(2)}) collective-permute-start(bf16[784,1024]{1,0:T(8,128)(2,1)S(1)} %copy-done), channel_id=1, source_target_pairs={{0,1},{1,0},{2,3},{3,2},{4,5},{5,4},{6,7},{7,6},{8,9},{9,8},{10,11... | collective-permute-start | bytes 4816904 | tf_op jit(solution)/shard_map/ppermute | solution.py:799
  28.2 43.9 %collective-permute-start.8 = (bf16[512,768]{1,0:T(8,128)(2,1)}, bf16[512,768]{1,0:T(8,128)(2,1)S(1)}, u32[]{:S(2)}, u32[]{:S(2)}) collective-permute-start(bf16[512,768]{1,0:T(8,128)(2,1)} %copy.37), channel_id=1, source_target_pairs={{0,4},{4,0},{1,5},{5,1},{2,6},{6,2},{3,7},{7,3},{8,12},{12,8},{9,1... | collective-permute-start | bytes 2359304 | tf_op jit(solution)/shard_map/ppermute | solution.py:799
  74.9 31.7 %collective-permute-start.11 = (bf16[784,256]{1,0:T(8,128)(2,1)S(1)}, bf16[784,256]{1,0:T(8,128)(2,1)S(1)}, u32[]{:S(2)}, u32[]{:S(2)}) collective-permute-start(bf16[784,256]{1,0:T(8,128)(2,1)S(1)} %slice.126), channel_id=1, source_target_pairs={{0,16},{8,24},{16,0},{24,8},{1,17},{9,25},{17,1},{25,9},{2,18},{10... | collective-permute-start | bytes 1204232 | tf_op jit(solution)/shard_map/ppermute | solution.py:799
  76.5 30.1 %collective-permute-start.10 = (bf16[768,256]{1,0:T(8,128)(2,1)S(1)}, bf16[768,256]{1,0:T(8,128)(2,1)S(1)}, u32[]{:S(2)}, u32[]{:S(2)}) collective-permute-start(bf16[768,256]{1,0:T(8,128)(2,1)S(1)} %slice.125), channel_id=1, source_target_pairs={{0,8},{8,0},{16,24},{24,16},{1,9},{9,1},{17,25},{25,17},{2,10},{10... | collective-permute-start | bytes 1179656 | tf_op jit(solution)/shard_map/ppermute | solution.py:799
  106.8 38.8 %collective-permute-start.13 = (bf16[2336,256]{1,0:T(8,128)(2,1)}, bf16[2336,256]{1,0:T(8,128)(2,1)}, u32[]{:S(2)}, u32[]{:S(2)}) collective-permute-start(bf16[2336,256]{1,0:T(8,128)(2,1)} %collective-permute-done.6.refs_0_), channel_id=1, source_target_pairs={{0,8},{8,0},{16,24},{24,16},{1,9},{9,1},{17,25},{25,17},{2,10},{10... | collective-permute-start | bytes 3588104 | tf_op jit(solution)/shard_map/ppermute | solution.py:799
  108.3 39.2 %collective-permute-start.15 = (bf16[2336,256]{1,0:T(8,128)(2,1)}, bf16[2336,256]{1,0:T(8,128)(2,1)}, u32[]{:S(2)}, u32[]{:S(2)}) collective-permute-start(bf16[2336,256]{1,0:T(8,128)(2,1)} %collective-permute-done.6.refs_0_), channel_id=1, source_target_pairs={{0,16},{8,24},{16,0},{24,8},{1,17},{9,25},{17,1},{25,9},{2,18},{10... | collective-permute-start | bytes 3588104 | tf_op jit(solution)/shard_map/ppermute | solution.py:799
  111.7 38.0 %collective-permute-start.17 = (bf16[2336,256]{1,0:T(8,128)(2,1)}, bf16[2336,256]{1,0:T(8,128)(2,1)}, u32[]{:S(2)}, u32[]{:S(2)}) collective-permute-start(bf16[2336,256]{1,0:T(8,128)(2,1)} %collective-permute-done.6.refs_0_), channel_id=1, source_target_pairs={{0,4},{4,0},{1,5},{5,1},{2,6},{6,2},{3,7},{7,3},{8,12},{12,8},{9,1... | collective-permute-start | bytes 3588104 | tf_op jit(solution)/shard_map/ppermute | solution.py:799
  253.4 36.5 %collective-permute-start.28 = (bf16[512,1024]{1,0:T(8,128)(2,1)}, bf16[512,1024]{1,0:T(8,128)(2,1)}, u32[]{:S(2)}, u32[]{:S(2)}) collective-permute-start(bf16[512,1024]{1,0:T(8,128)(2,1)} %get-tuple-element.185), channel_id=1, source_target_pairs={{0,16},{8,24},{16,0},{24,8},{1,17},{9,25},{17,1},{25,9},{2,18},{10... | collective-permute-start | bytes 3145736 | tf_op jit(solution)/shard_map/ppermute | solution.py:799
  254.9 35.0 %collective-permute-start.25 = (bf16[512,1024]{1,0:T(8,128)(2,1)}, bf16[512,1024]{1,0:T(8,128)(2,1)}, u32[]{:S(2)}, u32[]{:S(2)}) collective-permute-start(bf16[512,1024]{1,0:T(8,128)(2,1)} %get-tuple-element.184), channel_id=1, source_target_pairs={{0,8},{8,0},{16,24},{24,16},{1,9},{9,1},{17,25},{25,17},{2,10},{10... | collective-permute-start | bytes 3145736 | tf_op jit(solution)/shard_map/ppermute | solution.py:799
  267.5 48.6 %collective-permute-start.32 = (bf16[512,1280]{1,0:T(8,128)(2,1)}, bf16[512,1280]{1,0:T(8,128)(2,1)}, u32[]{:S(2)}, u32[]{:S(2)}) collective-permute-start(bf16[512,1280]{1,0:T(8,128)(2,1)} %get-tuple-element.192), channel_id=1, source_target_pairs={{0,16},{8,24},{16,0},{24,8},{1,17},{9,25},{17,1},{25,9},{2,18},{10... | collective-permute-start | bytes 3932168 | tf_op jit(solution)/shard_map/ppermute | solution.py:799
  268.0 48.1 %collective-permute-start.31 = (bf16[512,1280]{1,0:T(8,128)(2,1)S(1)}, bf16[512,1280]{1,0:T(8,128)(2,1)}, u32[]{:S(2)}, u32[]{:S(2)}) collective-permute-start(bf16[512,1280]{1,0:T(8,128)(2,1)S(1)} %get-tuple-element.191), channel_id=1, source_target_pairs={{0,8},{8,0},{16,24},{24,16},{1,9},{9,1},{17,25},{25,17},{2,10},{10... | collective-permute-start | bytes 3932168 | tf_op jit(solution)/shard_map/ppermute | solution.py:799
  269.5 58.1 %collective-permute-start.33 = (bf16[784,512]{1,0:T(8,128)(2,1)}, bf16[784,512]{1,0:T(8,128)(2,1)}, u32[]{:S(2)}, u32[]{:S(2)}) collective-permute-start(bf16[784,512]{1,0:T(8,128)(2,1)} %get-tuple-element.221), channel_id=1, source_target_pairs={{0,1},{1,0},{2,3},{3,2},{4,5},{5,4},{6,7},{7,6},{8,9},{9,8},{10,11... | collective-permute-start | bytes 2408456 | tf_op jit(solution)/shard_map/ppermute | solution.py:799
  320.4 31.2 %collective-permute-start.38 = (bf16[256,1280]{1,0:T(8,128)(2,1)}, bf16[256,1280]{1,0:T(8,128)(2,1)}, u32[]{:S(2)}, u32[]{:S(2)}) collective-permute-start(bf16[256,1280]{1,0:T(8,128)(2,1)} %get-tuple-element.218), channel_id=1, source_target_pairs={{0,8},{8,0},{16,24},{24,16},{1,9},{9,1},{17,25},{25,17},{2,10},{10... | collective-permute-start | bytes 1966088 | tf_op jit(solution)/shard_map/ppermute | solution.py:799
  321.1 30.5 %collective-permute-start.34 = (bf16[256,1280]{1,0:T(8,128)(2,1)}, bf16[256,1280]{1,0:T(8,128)(2,1)}, u32[]{:S(2)}, u32[]{:S(2)}) collective-permute-start(bf16[256,1280]{1,0:T(8,128)(2,1)} %get-tuple-element.217), channel_id=1, source_target_pairs={{0,16},{8,24},{16,0},{24,8},{1,17},{9,25},{17,1},{25,9},{2,18},{10... | collective-permute-start | bytes 1966088 | tf_op jit(solution)/shard_map/ppermute | solution.py:799
  368.1 32.0 %collective-permute-start.41 = (bf16[640,256]{1,0:T(8,128)(2,1)}, bf16[640,256]{1,0:T(8,128)(2,1)S(1)}, u32[]{:S(2)}, u32[]{:S(2)}) collective-permute-start(bf16[640,256]{1,0:T(8,128)(2,1)} %get-tuple-element.233), channel_id=1, source_target_pairs={{0,1},{1,0},{2,3},{3,2},{4,5},{5,4},{6,7},{7,6},{8,9},{9,8},{10,11... | collective-permute-start | bytes 983048 | tf_op jit(solution)/shard_map/ppermute | solution.py:799
  368.9 31.2 %collective-permute-start.42 = (bf16[640,256]{1,0:T(8,128)(2,1)}, bf16[640,256]{1,0:T(8,128)(2,1)S(1)}, u32[]{:S(2)}, u32[]{:S(2)}) collective-permute-start(bf16[640,256]{1,0:T(8,128)(2,1)} %get-tuple-element.234), channel_id=1, source_target_pairs={{0,2},{1,3},{2,0},{3,1},{4,6},{5,7},{6,4},{7,5},{8,10},{9,11},{10,... | collective-permute-start | bytes 983048 | tf_op jit(solution)/shard_map/ppermute | solution.py:799
  371.0 29.1 %collective-permute-start.43 = (bf16[640,256]{1,0:T(8,128)(2,1)}, bf16[640,256]{1,0:T(8,128)(2,1)S(1)}, u32[]{:S(2)}, u32[]{:S(2)}) collective-permute-start(bf16[640,256]{1,0:T(8,128)(2,1)} %get-tuple-element.235), channel_id=1, source_target_pairs={{0,3},{1,2},{2,1},{3,0},{4,7},{5,6},{6,5},{7,4},{8,11},{9,10},{10,... | collective-permute-start | bytes 983048 | tf_op jit(solution)/shard_map/ppermute | solution.py:799
  428.9 37.5 %collective-permute-start.47 = (bf16[784,1024]{1,0:T(8,128)(2,1)}, bf16[784,1024]{1,0:T(8,128)(2,1)S(1)}, u32[]{:S(2)}, u32[]{:S(2)}) collective-permute-start(bf16[784,1024]{1,0:T(8,128)(2,1)} %get-tuple-element.254), channel_id=1, source_target_pairs={{0,1},{1,0},{2,3},{3,2},{4,5},{5,4},{6,7},{7,6},{8,9},{9,8},{10,11... | collective-permute-start | bytes 4816904 | tf_op jit(solution)/shard_map/ppermute | solution.py:799
  433.7 32.7 %collective-permute-start.48 = (bf16[320,768]{1,0:T(8,128)(2,1)}, bf16[320,768]{1,0:T(8,128)(2,1)}, u32[]{:S(2)}, u32[]{:S(2)}) collective-permute-start(bf16[320,768]{1,0:T(8,128)(2,1)} %get-tuple-element.262), channel_id=1, source_target_pairs={{0,16},{8,24},{16,0},{24,8},{1,17},{9,25},{17,1},{25,9},{2,18},{10... | collective-permute-start | bytes 1474568 | tf_op jit(solution)/shard_map/ppermute | solution.py:799
  436.2 30.1 %collective-permute-start.46 = (bf16[192,768]{1,0:T(8,128)(2,1)}, bf16[192,768]{1,0:T(8,128)(2,1)}, u32[]{:S(2)}, u32[]{:S(2)}) collective-permute-start(bf16[192,768]{1,0:T(8,128)(2,1)} %get-tuple-element.261), channel_id=1, source_target_pairs={{0,8},{8,0},{16,24},{24,16},{1,9},{9,1},{17,25},{25,17},{2,10},{10... | collective-permute-start | bytes 884744 | tf_op jit(solution)/shard_map/ppermute | solution.py:799
  471.1 33.2 %collective-permute-start.55 = (bf16[2304,256]{1,0:T(8,128)(2,1)S(1)}, bf16[2304,256]{1,0:T(8,128)(2,1)}, u32[]{:S(2)}, u32[]{:S(2)}) collective-permute-start(bf16[2304,256]{1,0:T(8,128)(2,1)S(1)} %pad_maximum_fusion.3.refs_0_), channel_id=1, source_target_pairs={{0,16},{8,24},{16,0},{24,8},{1,17},{9,25},{17,1},{25,9},{2,18},{10... | collective-permute-start | bytes 3538952 | tf_op jit(solution)/shard_map/ppermute | solution.py:799
  (108 other events, 1196.3 us)

commit v7 on v6

--- a/solution.py
+++ b/solution.py
@@ -1524,7 +1524,7 @@
     )
     plane_taken = [over_dp(plane_give[s - 1], s) for s in (1, 2, 3)]
     mine_two = jnp.concatenate([mine, tie(mine_x, *plane_give)], axis=0)
-    plane_taken = all_tied(plane_taken, mine_two, norm_taken)
+    plane_taken = all_tied(plane_taken, mine_two)
     near_own, vec_sum, col_give, vec_give = on_chip(
         after_plane_kernel,
         [
@@ -1538,18 +1538,16 @@
     )
     mine_y = over_dp(tie(mine_two, col_give), 2)
     col_taken = [over_col(vec_give, 1), over_col(col_give, 2), over_col(vec_give, 3)]
-    norm_taken = tie(norm_taken, col_give)
-    grad_states = last_norm(flip, norm_own, norm_taken, states, grad_mid, vectors)
-
     qkv_mine, vec_total = on_chip(
         after_cols_kernel,
         [((deep, columns), bf16), ((VECTORS, half), f32)],
         "after_cols",
-        *(near_own, vec_sum, *all_tied(col_taken, grad_states)),
+        *(near_own, vec_sum, *col_taken),
     )
     qkv_back = [over_dp(qkv_mine, s) for s in (1, 2, 3)]
     norm_total = vec_total[4:6] + over_row(vec_total[17:19])
-    fc2_grad, fc1_grad, proj_grad = finish(places, [mine_two, tie(mine_y, qkv_mine)], part_rows)
+    grad_states = last_norm(flip, norm_own, tie(norm_taken, qkv_mine), states, grad_mid, vectors)
+    fc2_grad, fc1_grad, proj_grad = finish(places, [mine_two, tie(mine_y, grad_states)], part_rows)
     qkv_grad = finish_qkv(places, [qkv_mine, *all_tied(qkv_back, fc2_grad)]).transpose(1, 0, 2)
 
     fc1_bias_grad = lax.dynamic_index_in_dim(vec_total[6:14].reshape(4, 4, sub), col, 1, False)

time: 519 us -> 518 us (level)
    unnamed x153 -> x151, local copies, waits for them, and re-layouts: 18.4 us -> 18.8 us
  transfers between devices with their start and end apart: 58 -> 58, of which waited for: 10 -> 11; matrix products, arithmetic and copies ran while one was open for 14% -> 14% of each run, Pallas kernels for 39% -> 38%
where the time goes in v7:
time: 518 us; the launch traced here: 512 us
  Pallas kernels  269 us (52%)
  waiting for transfers between devices  82.8 us (16%)
  starting transfers between devices  57 us (11%)
  local copies, waits for them, and re-layouts  43.6 us (8%)
  matrix products  33 us (6%)
  other arithmetic  22.2 us (4%)
    pallas_call x4, Pallas kernels, attend_back(): pl.pallas_call(functools.partial(attend_back_kernel, first, lane, before...  83.4 us
    ppermute x58, waiting for transfers between devices, swap(): return lax.ppermute(values, axis, [(i, i ^ mask) for i in range(size)])  82.8 us
    ppermute x58, starting transfers between devices, swap(): return lax.ppermute(values, axis, [(i, i ^ mask) for i in range(size)])  57 us
    pallas_call x1, Pallas kernels, middle_block(): pl.pallas_call(middle_kernel, out_shape=(result(width, bf16), result(widt...  56.2 us
    pallas_call x4, Pallas kernels, attend(): pl.pallas_call(functools.partial(attend_kernel, first), out_shape=(jax.Sh...  46.9 us
    pallas_call x9, Pallas kernels, on_chip(): pl.pallas_call(kernel, out_shape=tuple((jax.ShapeDtypeStruct(*s) for s in...  31.5 us
    dot_general x6, matrix products, dot_tn(): lax.dot_general(a, b, (((0,), (0,)), ((), ())), preferred_element_type=jn...  25.2 us
    unnamed x151, local copies, waits for them, and re-layouts  18.8 us
  transfers between devices with their start and end apart: 58, of which 11 were waited for; matrix products, arithmetic and copies ran while one was open for 14% of the time, Pallas kernels for 38%

profile of v7, /device:TPU:0, one launch (start us, length us, event | category | flops | bytes accessed | tf_op | source)
XLA Modules:
  0.0 512.4 jit_solution(16853733804305630991)
XLA Ops:
  28.7 18.3 %collective-permute-done.1 = bf16[1552,256]{1,0:T(8,128)(2,1)} collective-permute-done((bf16[1552,256]{1,0:T(8,128)(2,1)}, bf16[1552,256]{1,0:T(8,128)(2,1)}, u32[]{:S(2)}, u32[]{:S(2)}) %collective-permute-start.1) | collective-permute-done | bytes 794656 | tf_op jit(solution)/shard_map/ppermute | solution.py:799
  53.3 11.1 %collective-permute-done.5.other_states = bf16[784,1024]{1,0:T(8,128)(2,1)} collective-permute-done((bf16[784,1024]{1,0:T(8,128)(2,1)S(1)}, bf16[784,1024]{1,0:T(8,128)(2,1)}, u32[]{:S(2)}, u32[]{:S(2)}) %collective-permute-start.5) | collective-permute-done | bytes 1605664 | tf_op jit(solution)/shard_map/ppermute | solution.py:799
  78.2 15.8 %collective-permute-done.6.refs_0_ = bf16[2336,256]{1,0:T(8,128)(2,1)} collective-permute-done((bf16[2336,256]{1,0:T(8,128)(2,1)S(1)}, bf16[2336,256]{1,0:T(8,128)(2,1)}, u32[]{:S(2)}, u32[]{:S(2)}) %collective-permute-start.6) | collective-permute-done | bytes 1196064 | tf_op jit(solution)/shard_map/ppermute | solution.py:799
  94.3 12.2 %attend.4 = (bf16[800,256]{1,0:T(8,128)(2,1)S(1)}, f32[7,8,512]{2,1,0:T(8,128)S(1)}) custom-call(bf16[1568,768]{1,0:T(8,128)(2,1)S(1)} %fusion.12.packed_ref, f32[1568,128]{1,0:T(8,128)S(1)} %broadcast_in_dim.48.bias_ref), custom_call_target="tpu_custom_call" | custom-call | flops 2569011200 | bytes 6291456 | tf_op jit(solution)/shard_map/attend/pallas_call | solution.py:454
  111.7 10.9 %attend.5 = (bf16[768,256]{1,0:T(8,128)(2,1)S(1)}, f32[6,8,512]{2,1,0:T(8,128)S(1)}) custom-call(bf16[1568,768]{1,0:T(8,128)(2,1)S(1)} %fusion.12.packed_ref, f32[1568,128]{1,0:T(8,128)S(1)} %broadcast_in_dim.48.bias_ref), custom_call_target="tpu_custom_call" | custom-call | flops 2466250752 | bytes 6291456 | tf_op jit(solution)/shard_map/attend/pallas_call | solution.py:454
  127.8 5.1 fusion.13.packed_ref
  132.9 12.8 %attend.6 = (bf16[800,256]{1,0:T(8,128)(2,1)S(1)}, f32[7,8,512]{2,1,0:T(8,128)S(1)}) custom-call(bf16[1568,768]{1,0:T(8,128)(2,1)S(1)} %fusion.13.packed_ref, f32[1568,128]{1,0:T(8,128)S(1)} %broadcast_in_dim.48.bias_ref), custom_call_target="tpu_custom_call" | custom-call | flops 2569011200 | bytes 6291456 | tf_op jit(solution)/shard_map/attend/pallas_call | solution.py:454
  150.1 10.9 %attend.7 = (bf16[768,256]{1,0:T(8,128)(2,1)S(1)}, f32[6,8,512]{2,1,0:T(8,128)S(1)}) custom-call(bf16[1568,768]{1,0:T(8,128)(2,1)S(1)} %fusion.13.packed_ref, f32[1568,128]{1,0:T(8,128)S(1)} %broadcast_in_dim.48.bias_ref), custom_call_target="tpu_custom_call" | custom-call | flops 2466250752 | bytes 6291456 | tf_op jit(solution)/shard_map/attend/pallas_call | solution.py:454
  168.2 56.2 %middle_block.1 = (bf16[784,1024]{1,0:T(8,128)(2,1)}, bf16[784,1024]{1,0:T(8,128)(2,1)}, bf16[784,4096]{1,0:T(8,128)(2,1)}, bf16[784,4096]{1,0:T(8,128)(2,1)}, b...) custom-call(s32[29]{0:T(128)} %stack.163.table_ref, ...), custom_call_target="tpu_custom_call" | custom-call | flops 6576668672 | bytes 46137344 | tf_op jit(solution)/shard_map/middle_block/pallas_call | solution.py:754
  224.5 7.8 %convolution_convert_fusion.1 = bf16[512,4096]{1,0:T(8,128)(2,1)S(1)} fusion(bf16[784,4096]{1,0:T(8,128)(2,1)} %get-tuple-element.179.big_ref, bf16[784,1024]{1,0:T(8,128)(2,1)} %get-tuple-element.178.small_ref), kind=kOutput, calls=%fused_computation.1 | convolution fusion | flops 3290431488 | bytes 11419648 | tf_op jit(solution)/shard_map/dot_general | solution.py:347
  232.9 6.7 %convolution_convert_fusion = bf16[512,4096]{1,0:T(8,128)(2,1)} fusion(bf16[784,4096]{1,0:T(8,128)(2,1)S(1)} %copy-done.37, bf16[784,1024]{1,0:T(8,128)(2,1)S(1)} %copy-done.10), kind=kOutput, calls=%fused_computation | convolution fusion | flops 3290431488 | bytes 11419648 | tf_op jit(solution)/shard_map/dot_general | solution.py:347
  243.7 8.7 %wide_grads.2 = (bf16[512,1024]{1,0:T(8,128)(2,1)S(1)}, bf16[512,1024]{1,0:T(8,128)(2,1)}, bf16[512,1024]{1,0:T(8,128)(2,1)S(1)}, bf16[512,1024]{1,0:T(8,128)(2,1)}) custom-call(s32[8]{0:T(128)S(1)} %copy-done.22, bf16[784,1024]{1,0:T(8,128)(2,1)S(1)} %copy-done.11, bf16[784,4096]{1,0:T(8,128)(2,1)} %get-tuple-element.179.big_ref, ...), custom_call_target="tpu_custom_call" | custom-call | flops 3000000000 | tf_op jit(solution)/shard_map/wide_grads/pallas_call | solution.py:1116
  255.5 9.7 %wide_grads.3 = (bf16[512,1280]{1,0:T(8,128)(2,1)S(1)}, bf16[512,1280]{1,0:T(8,128)(2,1)S(1)}, bf16[512,1280]{1,0:T(8,128)(2,1)S(1)}, bf16[512,1280]{1,0:T(8,128)(2,1)}) custom-call(s32[8]{0:T(128)S(1)} %copy-done.22, bf16[784,1024]{1,0:T(8,128)(2,1)S(1)} %copy-done.10, bf16[784,4096]{1,0:T(8,128)(2,1)} %get-tuple-element.185.big_ref, ...), custom_call_target="tpu_custom_call" | custom-call | flops 3000000000 | tf_op jit(solution)/shard_map/wide_grads/pallas_call | solution.py:1116
  269.8 19.4 %attend_back.4 = (bf16[768,256]{1,0:T(8,128)(2,1)S(1)}, f32[1568,256]{1,0:T(8,128)}, f32[1568,256]{1,0:T(8,128)}) custom-call(bf16[1568,768]{1,0:T(8,128)(2,1)} %copy-done.29, f32[1568,128]{1,0:T(8,128)S(1)} %copy-done.17, f32[6,8,512]{2,1,0:T(8,128)S(1)} %get-tuple-element.191.lse_ref, bf16[768,256]{1,0:T(8,128)(2,1)S(1)} %copy-done.19, ...), custom_call_target="tpu_custom_call" | custom-call | flops 4932501504 | bytes 10485760 | tf_op jit(solution)/shard_map/attend_back/pallas_call | solution.py:488
  296.5 19.6 %attend_back.5 = (bf16[768,256]{1,0:T(8,128)(2,1)S(1)}, f32[1568,256]{1,0:T(8,128)}, f32[1568,256]{1,0:T(8,128)}) custom-call(bf16[1568,768]{1,0:T(8,128)(2,1)} %copy-done.28, f32[1568,128]{1,0:T(8,128)S(1)} %copy-done.17, f32[6,8,512]{2,1,0:T(8,128)S(1)} %get-tuple-element.201.lse_ref, bf16[768,256]{1,0:T(8,128)(2,1)S(1)} %copy-done.21, ...), custom_call_target="tpu_custom_call" | custom-call | flops 4932501504 | bytes 10485760 | tf_op jit(solution)/shard_map/attend_back/pallas_call | solution.py:488
  316.1 4.3 plane_sum.3
  328.7 22.2 %attend_back.6 = (bf16[1568,768]{1,0:T(8,128)(2,1)}, f32[1,768]{1,0:T(1,128)S(1)}) custom-call(bf16[1568,768]{1,0:T(8,128)(2,1)} %copy-done.29, f32[1568,128]{1,0:T(8,128)S(1)} %copy-done.17, f32[7,8,512]{2,1,0:T(8,128)S(1)} %get-tuple-element.217.lse_ref, bf16[800,256]{1,0:T(8,128)(2,1)S(1)} %copy-done.9, ...), custom_call_target="tpu_custom_call" | custom-call | flops 5138022400 | bytes 10485760 | tf_op jit(solution)/shard_map/attend_back/pallas_call | solution.py:488
  362.5 5.5 %copy.39.turned_ref = bf16[1024,1568]{1,0:T(8,128)(2,1)} copy(bf16[1024,1568]{0,1:T(8,128)(2,1)} %bitcast.62) | data formatting | bytes 6422528 | tf_op jit(solution)/shard_map/transpose | solution.py:1378
  377.3 22.2 %attend_back.7 = (bf16[1568,768]{1,0:T(8,128)(2,1)}, f32[1,768]{1,0:T(1,128)S(1)}) custom-call(bf16[1568,768]{1,0:T(8,128)(2,1)} %copy-done.28, f32[1568,128]{1,0:T(8,128)S(1)} %copy-done.17, f32[7,8,512]{2,1,0:T(8,128)S(1)} %get-tuple-element.235.lse_ref, bf16[800,256]{1,0:T(8,128)(2,1)S(1)} %copy-done.7, ...), custom_call_target="tpu_custom_call" | custom-call | flops 5138022400 | bytes 10485760 | tf_op jit(solution)/shard_map/attend_back/pallas_call | solution.py:488
  401.2 7.1 %far_grads.1 = (f32[32,512]{1,0:T(8,128)}, bf16[576,768]{1,0:T(8,128)(2,1)}, f32[512,768]{1,0:T(8,128)}) custom-call(bf16[1024,1568]{1,0:T(8,128)(2,1)} %copy.39.turned_ref, bf16[1568,768]{1,0:T(8,128)(2,1)} %get-tuple-element.249.grad_ref.far_ref, f32[8,1024]{1,0:T(8,128)} %get-tuple-element.240.sums_ref, f32[1,4096]{1,0:T(1,128)} %get-tuple-element.241.hidden_ref, ...), custom_call_target="tpu_custom_call" | custom-call | flops 100000000 | tf_op jit(solution)/shard_map/far_grads/pallas_call | solution.py:1075
  415.1 11.9 %token_back.1 = (f32[784,1024]{1,0:T(8,128)}, bf16[784,1024]{1,0:T(8,128)(2,1)S(1)}, f32[2,1024]{1,0:T(2,128)S(1)}) custom-call(s32[1]{0:T(128)} %bitcast.27.flip_ref, bf16[1568,768]{1,0:T(8,128)(2,1)S(1)} %copy-done.5, bf16[1568,768]{1,0:T(8,128)(2,1)S(1)} %copy-done.2, bf16[1024,768]{1,0:T(8,128)(2,1)S(1)} %pad_maximum_fusion.1.w_near, ...), custom_call_target="tpu_custom_call" | custom-call | flops 100000000 | tf_op jit(solution)/shard_map/token_back/pallas_call | solution.py:944
  438.4 8.0 %collective-permute-done.48.refs_2_ = bf16[192,768]{1,0:T(8,128)(2,1)} collective-permute-done((bf16[192,768]{1,0:T(8,128)(2,1)}, bf16[192,768]{1,0:T(8,128)(2,1)}, u32[]{:S(2)}, u32[]{:S(2)}) %collective-permute-start.48) | collective-permute-done | bytes 294944 | tf_op jit(solution)/shard_map/ppermute | solution.py:799
  460.6 17.9 %collective-permute-done.49.one_ref = bf16[64,512]{1,0:T(8,128)(2,1)S(1)} collective-permute-done((bf16[64,512]{1,0:T(8,128)(2,1)}, bf16[64,512]{1,0:T(8,128)(2,1)S(1)}, u32[]{:S(2)}, u32[]{:S(2)}) %collective-permute-start.49) | collective-permute-done | bytes 65568 | tf_op jit(solution)/shard_map/ppermute | solution.py:799
  494.8 8.0 %last_norm.1 = bf16[784,1024]{1,0:T(8,128)(2,1)} custom-call(s32[1]{0:T(128)} %bitcast.27.flip_ref, f32[784,1024]{1,0:T(8,128)} %get-tuple-element.270.own_ref, bf16[784,1024]{1,0:T(8,128)(2,1)} %collective-permute-done.52.taken_ref, bf16[784,1024]{1,0:T(8,128)(2,1)} %states_ref, f32[784,1024]{1,0:T(8,128)} %get-tuple-element.273.mid_ref, f32[6,1024]{1,0:T(8,128)} %copy-done.50), custom_call_target="tpu_custom_call" | custom-call | flops 500000000 | tf_op jit(solution)/shard_map/last_norm/pallas_call | solution.py:978
  (347 shorter events, 175.2 us)
Async XLA Ops:
  0.7 46.3 %collective-permute-start.2 = (bf16[512,1024]{1,0:T(8,128)(2,1)}, bf16[512,1024]{1,0:T(8,128)(2,1)}, u32[]{:S(2)}, u32[]{:S(2)}) collective-permute-start(bf16[512,1024]{1,0:T(8,128)(2,1)} %fc1_own.1), channel_id=1, source_target_pairs={{0,4},{4,0},{1,5},{5,1},{2,6},{6,2},{3,7},{7,3},{8,12},{12,8},{9,1... | collective-permute-start | bytes 3145736 | tf_op jit(solution)/shard_map/ppermute | solution.py:799
  1.2 45.8 %collective-permute-start.3 = (bf16[1024,512]{1,0:T(8,128)(2,1)}, bf16[1024,512]{1,0:T(8,128)(2,1)}, u32[]{:S(2)}, u32[]{:S(2)}) collective-permute-start(bf16[1024,512]{1,0:T(8,128)(2,1)} %fc2_own.1), channel_id=1, source_target_pairs={{0,4},{4,0},{1,5},{5,1},{2,6},{6,2},{3,7},{7,3},{8,12},{12,8},{9,1... | collective-permute-start | bytes 3145736 | tf_op jit(solution)/shard_map/ppermute | solution.py:799
  7.5 39.5 %collective-permute-start.1 = (bf16[1552,256]{1,0:T(8,128)(2,1)}, bf16[1552,256]{1,0:T(8,128)(2,1)}, u32[]{:S(2)}, u32[]{:S(2)}) collective-permute-start(bf16[1552,256]{1,0:T(8,128)(2,1)} %make_slab.1), channel_id=1, source_target_pairs={{0,2},{1,3},{2,0},{3,1},{4,6},{5,7},{6,4},{7,5},{8,10},{9,11},{10,... | collective-permute-start | bytes 2383880 | tf_op jit(solution)/shard_map/ppermute | solution.py:799
  11.6 52.8 %collective-permute-start.5 = (bf16[784,1024]{1,0:T(8,128)(2,1)S(1)}, bf16[784,1024]{1,0:T(8,128)(2,1)}, u32[]{:S(2)}, u32[]{:S(2)}) collective-permute-start(bf16[784,1024]{1,0:T(8,128)(2,1)S(1)} %copy-done), channel_id=1, source_target_pairs={{0,1},{1,0},{2,3},{3,2},{4,5},{5,4},{6,7},{7,6},{8,9},{9,8},{10,11... | collective-permute-start | bytes 4816904 | tf_op jit(solution)/shard_map/ppermute | solution.py:799
  28.3 43.8 %collective-permute-start.8 = (bf16[512,768]{1,0:T(8,128)(2,1)}, bf16[512,768]{1,0:T(8,128)(2,1)S(1)}, u32[]{:S(2)}, u32[]{:S(2)}) collective-permute-start(bf16[512,768]{1,0:T(8,128)(2,1)} %copy.37), channel_id=1, source_target_pairs={{0,4},{4,0},{1,5},{5,1},{2,6},{6,2},{3,7},{7,3},{8,12},{12,8},{9,1... | collective-permute-start | bytes 2359304 | tf_op jit(solution)/shard_map/ppermute | solution.py:799
  47.0 27.8 %collective-permute-start.9 = (bf16[1552,256]{1,0:T(8,128)(2,1)}, bf16[1552,256]{1,0:T(8,128)(2,1)S(1)}, u32[]{:S(2)}, u32[]{:S(2)}) collective-permute-start(bf16[1552,256]{1,0:T(8,128)(2,1)} %collective-permute-done.1), channel_id=1, source_target_pairs={{0,16},{8,24},{16,0},{24,8},{1,17},{9,25},{17,1},{25,9},{2,18},{10... | collective-permute-start | bytes 2383880 | tf_op jit(solution)/shard_map/ppermute | solution.py:799
  74.9 31.7 %collective-permute-start.11 = (bf16[784,256]{1,0:T(8,128)(2,1)S(1)}, bf16[784,256]{1,0:T(8,128)(2,1)S(1)}, u32[]{:S(2)}, u32[]{:S(2)}) collective-permute-start(bf16[784,256]{1,0:T(8,128)(2,1)S(1)} %slice.126), channel_id=1, source_target_pairs={{0,16},{8,24},{16,0},{24,8},{1,17},{9,25},{17,1},{25,9},{2,18},{10... | collective-permute-start | bytes 1204232 | tf_op jit(solution)/shard_map/ppermute | solution.py:799
  76.5 30.1 %collective-permute-start.10 = (bf16[768,256]{1,0:T(8,128)(2,1)S(1)}, bf16[768,256]{1,0:T(8,128)(2,1)S(1)}, u32[]{:S(2)}, u32[]{:S(2)}) collective-permute-start(bf16[768,256]{1,0:T(8,128)(2,1)S(1)} %slice.125), channel_id=1, source_target_pairs={{0,8},{8,0},{16,24},{24,16},{1,9},{9,1},{17,25},{25,17},{2,10},{10... | collective-permute-start | bytes 1179656 | tf_op jit(solution)/shard_map/ppermute | solution.py:799
  106.8 38.9 %collective-permute-start.13 = (bf16[2336,256]{1,0:T(8,128)(2,1)}, bf16[2336,256]{1,0:T(8,128)(2,1)}, u32[]{:S(2)}, u32[]{:S(2)}) collective-permute-start(bf16[2336,256]{1,0:T(8,128)(2,1)} %collective-permute-done.6.refs_0_), channel_id=1, source_target_pairs={{0,8},{8,0},{16,24},{24,16},{1,9},{9,1},{17,25},{25,17},{2,10},{10... | collective-permute-start | bytes 3588104 | tf_op jit(solution)/shard_map/ppermute | solution.py:799
  108.3 39.2 %collective-permute-start.15 = (bf16[2336,256]{1,0:T(8,128)(2,1)}, bf16[2336,256]{1,0:T(8,128)(2,1)}, u32[]{:S(2)}, u32[]{:S(2)}) collective-permute-start(bf16[2336,256]{1,0:T(8,128)(2,1)} %collective-permute-done.6.refs_0_), channel_id=1, source_target_pairs={{0,16},{8,24},{16,0},{24,8},{1,17},{9,25},{17,1},{25,9},{2,18},{10... | collective-permute-start | bytes 3588104 | tf_op jit(solution)/shard_map/ppermute | solution.py:799
  111.7 38.1 %collective-permute-start.17 = (bf16[2336,256]{1,0:T(8,128)(2,1)}, bf16[2336,256]{1,0:T(8,128)(2,1)}, u32[]{:S(2)}, u32[]{:S(2)}) collective-permute-start(bf16[2336,256]{1,0:T(8,128)(2,1)} %collective-permute-done.6.refs_0_), channel_id=1, source_target_pairs={{0,4},{4,0},{1,5},{5,1},{2,6},{6,2},{3,7},{7,3},{8,12},{12,8},{9,1... | collective-permute-start | bytes 3588104 | tf_op jit(solution)/shard_map/ppermute | solution.py:799
  253.4 36.5 %collective-permute-start.28 = (bf16[512,1024]{1,0:T(8,128)(2,1)}, bf16[512,1024]{1,0:T(8,128)(2,1)}, u32[]{:S(2)}, u32[]{:S(2)}) collective-permute-start(bf16[512,1024]{1,0:T(8,128)(2,1)} %get-tuple-element.182), channel_id=1, source_target_pairs={{0,16},{8,24},{16,0},{24,8},{1,17},{9,25},{17,1},{25,9},{2,18},{10... | collective-permute-start | bytes 3145736 | tf_op jit(solution)/shard_map/ppermute | solution.py:799
  254.9 35.0 %collective-permute-start.25 = (bf16[512,1024]{1,0:T(8,128)(2,1)}, bf16[512,1024]{1,0:T(8,128)(2,1)}, u32[]{:S(2)}, u32[]{:S(2)}) collective-permute-start(bf16[512,1024]{1,0:T(8,128)(2,1)} %get-tuple-element.181), channel_id=1, source_target_pairs={{0,8},{8,0},{16,24},{24,16},{1,9},{9,1},{17,25},{25,17},{2,10},{10... | collective-permute-start | bytes 3145736 | tf_op jit(solution)/shard_map/ppermute | solution.py:799
  267.5 48.6 %collective-permute-start.32 = (bf16[512,1280]{1,0:T(8,128)(2,1)}, bf16[512,1280]{1,0:T(8,128)(2,1)}, u32[]{:S(2)}, u32[]{:S(2)}) collective-permute-start(bf16[512,1280]{1,0:T(8,128)(2,1)} %get-tuple-element.189), channel_id=1, source_target_pairs={{0,16},{8,24},{16,0},{24,8},{1,17},{9,25},{17,1},{25,9},{2,18},{10... | collective-permute-start | bytes 3932168 | tf_op jit(solution)/shard_map/ppermute | solution.py:799
  268.0 48.1 %collective-permute-start.31 = (bf16[512,1280]{1,0:T(8,128)(2,1)S(1)}, bf16[512,1280]{1,0:T(8,128)(2,1)}, u32[]{:S(2)}, u32[]{:S(2)}) collective-permute-start(bf16[512,1280]{1,0:T(8,128)(2,1)S(1)} %get-tuple-element.188), channel_id=1, source_target_pairs={{0,8},{8,0},{16,24},{24,16},{1,9},{9,1},{17,25},{25,17},{2,10},{10... | collective-permute-start | bytes 3932168 | tf_op jit(solution)/shard_map/ppermute | solution.py:799
  269.5 58.1 %collective-permute-start.33 = (bf16[784,512]{1,0:T(8,128)(2,1)}, bf16[784,512]{1,0:T(8,128)(2,1)}, u32[]{:S(2)}, u32[]{:S(2)}) collective-permute-start(bf16[784,512]{1,0:T(8,128)(2,1)} %get-tuple-element.218), channel_id=1, source_target_pairs={{0,1},{1,0},{2,3},{3,2},{4,5},{5,4},{6,7},{7,6},{8,9},{9,8},{10,11... | collective-permute-start | bytes 2408456 | tf_op jit(solution)/shard_map/ppermute | solution.py:799
  293.6 28.0 %collective-permute-start.30 = (bf16[256,1024]{1,0:T(8,128)(2,1)}, bf16[256,1024]{1,0:T(8,128)(2,1)}, u32[]{:S(2)}, u32[]{:S(2)}) collective-permute-start(bf16[256,1024]{1,0:T(8,128)(2,1)} %get-tuple-element.198), channel_id=1, source_target_pairs={{0,8},{8,0},{16,24},{24,16},{1,9},{9,1},{17,25},{25,17},{2,10},{10... | collective-permute-start | bytes 1572872 | tf_op jit(solution)/shard_map/ppermute | solution.py:799
  320.4 31.1 %collective-permute-start.38 = (bf16[256,1280]{1,0:T(8,128)(2,1)}, bf16[256,1280]{1,0:T(8,128)(2,1)}, u32[]{:S(2)}, u32[]{:S(2)}) collective-permute-start(bf16[256,1280]{1,0:T(8,128)(2,1)} %get-tuple-element.215), channel_id=1, source_target_pairs={{0,8},{8,0},{16,24},{24,16},{1,9},{9,1},{17,25},{25,17},{2,10},{10... | collective-permute-start | bytes 1966088 | tf_op jit(solution)/shard_map/ppermute | solution.py:799
  321.1 30.5 %collective-permute-start.34 = (bf16[256,1280]{1,0:T(8,128)(2,1)}, bf16[256,1280]{1,0:T(8,128)(2,1)}, u32[]{:S(2)}, u32[]{:S(2)}) collective-permute-start(bf16[256,1280]{1,0:T(8,128)(2,1)} %get-tuple-element.214), channel_id=1, source_target_pairs={{0,16},{8,24},{16,0},{24,8},{1,17},{9,25},{17,1},{25,9},{2,18},{10... | collective-permute-start | bytes 1966088 | tf_op jit(solution)/shard_map/ppermute | solution.py:799
  368.0 32.1 %collective-permute-start.41 = (bf16[640,256]{1,0:T(8,128)(2,1)}, bf16[640,256]{1,0:T(8,128)(2,1)S(1)}, u32[]{:S(2)}, u32[]{:S(2)}) collective-permute-start(bf16[640,256]{1,0:T(8,128)(2,1)} %get-tuple-element.230), channel_id=1, source_target_pairs={{0,1},{1,0},{2,3},{3,2},{4,5},{5,4},{6,7},{7,6},{8,9},{9,8},{10,11... | collective-permute-start | bytes 983048 | tf_op jit(solution)/shard_map/ppermute | solution.py:799
  369.0 31.2 %collective-permute-start.42 = (bf16[640,256]{1,0:T(8,128)(2,1)}, bf16[640,256]{1,0:T(8,128)(2,1)S(1)}, u32[]{:S(2)}, u32[]{:S(2)}) collective-permute-start(bf16[640,256]{1,0:T(8,128)(2,1)} %get-tuple-element.231), channel_id=1, source_target_pairs={{0,2},{1,3},{2,0},{3,1},{4,6},{5,7},{6,4},{7,5},{8,10},{9,11},{10,... | collective-permute-start | bytes 983048 | tf_op jit(solution)/shard_map/ppermute | solution.py:799
  371.0 29.2 %collective-permute-start.43 = (bf16[640,256]{1,0:T(8,128)(2,1)}, bf16[640,256]{1,0:T(8,128)(2,1)S(1)}, u32[]{:S(2)}, u32[]{:S(2)}) collective-permute-start(bf16[640,256]{1,0:T(8,128)(2,1)} %get-tuple-element.232), channel_id=1, source_target_pairs={{0,3},{1,2},{2,1},{3,0},{4,7},{5,6},{6,5},{7,4},{8,11},{9,10},{10,... | collective-permute-start | bytes 983048 | tf_op jit(solution)/shard_map/ppermute | solution.py:799
  433.8 61.0 %collective-permute-start.52 = (bf16[784,1024]{1,0:T(8,128)(2,1)S(1)}, bf16[784,1024]{1,0:T(8,128)(2,1)}, u32[]{:S(2)}, u32[]{:S(2)}) collective-permute-start(bf16[784,1024]{1,0:T(8,128)(2,1)S(1)} %copy-done.27), channel_id=1, source_target_pairs={{0,1},{1,0},{2,3},{3,2},{4,5},{5,4},{6,7},{7,6},{8,9},{9,8},{10,11... | collective-permute-start | bytes 4816904 | tf_op jit(solution)/shard_map/ppermute | solution.py:799
  456.5 46.4 %collective-permute-start.55 = (bf16[2304,256]{1,0:T(8,128)(2,1)S(1)}, bf16[2304,256]{1,0:T(8,128)(2,1)}, u32[]{:S(2)}, u32[]{:S(2)}) collective-permute-start(bf16[2304,256]{1,0:T(8,128)(2,1)S(1)} %pad_maximum_fusion.3.refs_0_), channel_id=1, source_target_pairs={{0,16},{8,24},{16,0},{24,8},{1,17},{9,25},{17,1},{25,9},{2,18},{10... | collective-permute-start | bytes 3538952 | tf_op jit(solution)/shard_map/ppermute | solution.py:799
  (107 other events, 1208.0 us)
